TPU v7x, 512 devices: a whole 4x4x16 slice. The times are simulated.
512 devices in a mesh: row: 16 (over x, z_hi, core), col: 32 (over y, z_lo).
Axes of the slice: x: 4, y: 4, z: 16 (z_hi: 2, z_lo: 8; z = z_hi * 8 + z_lo), core: 2. Of those that a mesh axis runs over, the one named last changes fastest.
Arguments:
- a_blocks: float32 [384, 16, 128, 128], P('col', 'row'), may hold values from -0.25 to 0.25
- a_cols: int32 [384, 16], P('col'), may hold values from 0 to 63, as said below
- a_lengths: int32 [384], P('col'), may hold values from 1 to 16, as said below
- b_blocks: float32 [64, 16, 128, 128], P('col', 'row'), may hold values from -6 to 6
- b_cols: int32 [64, 16], P(None, 'row'), may hold values from 0 to 7
- c_cols: int32 [384, 64], P('col', 'row'), may hold values from 0 to 7, as said below
- order: int32 [64], replicated, may hold values from 0 to 63, each once
Outputs:
- c_blocks: float32 [384, 64, 128, 128], P('col', 'row')
Inputs may be any that keep to these rules, and one draw needn't show every extreme that they name: `a_cols`: the 16 entries of one row are distinct. `a_lengths`: the first row has 16 live slots; slots at or after a row's length hold blocks that are not used. `c_cols`: the 4 entries of one row in one row group are distinct. `order`: each number once.
All inputs are finite; a program needn't handle non-finite values.
Results may differ from a plain program's by a relative error of at most 0.0003.
Values sent between devices are 32-bit elements; how exact they have to be, the bound alone decides.
No kernel may reach another device: no remote copies, remote signals or barrier semaphores. Data moves between devices by JAX's collectives and lax.ppermute only.
A program may use at most 64 MiB of HBM per device.

v0:
```python
import jax
import jax.numpy as jnp
from jax import lax
from jax.sharding import PartitionSpec as P


def lookup(values_table, indices):
    matched = indices[..., None] == jnp.arange(values_table.shape[0], dtype=jnp.int32)
    return jnp.sum(jnp.where(matched, values_table, 0), axis=-1)


def local(a_blocks, a_cols, a_lengths, b_blocks, b_cols, c_cols, order):
    panels = lax.all_gather(b_blocks, "col", axis=0, tiled=True)[:, 0]
    rows_here, slot_all = a_cols.shape
    pattern_slots = c_cols.shape[1]
    block_size = panels.shape[-1]
    position = lookup(order, a_cols)
    window_col = lookup(b_cols[:, 0], position)
    live_slots = jnp.arange(slot_all, dtype=jnp.int32)[None, :] < a_lengths[:, None]
    weights = ((window_col[:, :, None] == c_cols[:, None, :]) & live_slots[:, :, None]).astype(
        jnp.float32
    )
    zero_sums = jnp.zeros((rows_here, pattern_slots, block_size, block_size), jnp.float32)
    whole_slots = lax.all_gather(a_blocks, "row", axis=1, tiled=True)

    def per_row(row_index, running):
        chosen = jnp.take(panels, position[row_index], axis=0)
        products = jnp.einsum(
            "jab,jbc->jac", whole_slots[row_index], chosen, precision=lax.Precision.HIGHEST
        )
        landed = jnp.einsum(
            "js,jac->sac", weights[row_index], products, precision=lax.Precision.HIGHEST
        )
        return running.at[row_index].add(landed)

    return lax.fori_loop(0, rows_here, per_row, zero_sums)


def solution(mesh):
    return jax.shard_map(
        local,
        mesh=mesh,
        in_specs=(
            P("col", "row", None, None),
            P("col", None),
            P("col"),
            P("col", "row", None, None),
            P(None, "row"),
            P("col", "row"),
            P(),
        ),
        out_specs=P("col", "row", None, None),
        check_vma=False,
    )
```

profile of v0, /device:TPU:113, one launch (start us, length us, event | category | flops | bytes accessed | tf_op | source)
XLA Modules:
  0.0 615.3 jit_solution(10681453512464985414)
XLA Ops:
  8.0 0.8 copy.14
  8.8 1.1 select_reduce_fusion.1
  9.8 1.0 select_reduce_fusion
  10.9 0.7 iota_compare_fusion.2
  11.7 190.2 %all-gather.5.cloned.1.call-done = f32[64,1,128,128]{3,2,1,0:T(8,128)} async-done(((f32[2,1,128,128]{3,2,1,0:T(8,128)}), f32[64,1,128,128]{3,2,1,0:T(8,128)}) %all-gather.5.cloned.1.call-update) | async-done | bytes 4194320 | tf_op jit(solution)/shard_map/all_gather | solution.py:13
  201.9 290.0 %all-gather.3.cloned.1.call-done = f32[12,16,128,128]{3,2,1,0:T(8,128)} async-done(((f32[12,1,128,128]{3,2,1,0:T(8,128)}), f32[12,16,128,128]{3,2,1,0:T(8,128)}) %all-gather.3.cloned.1.call-update) | async-done | bytes 12582928 | tf_op jit(solution)/shard_map/all_gather | solution.py:24
  491.9 2.0 broadcast_in_dim.47.clone
  493.9 114.5 %while.14 = (s32[]{:T(128)}, f32[12,4,128,128]{3,2,1,0:T(8,128)}, f32[12,16,4]{1,2,0:T(4,128)S(1)}, f32[12,16,128,128]{3,2,1,0:T(8,128)}, s32[12,16]{1,0:T(8,128...) while((s32[]{:T(128)}, f32[12,4,128,128]{3,2,1,0:T(8,128)}, ...), condition=%wide.region_4.5_spmd, body=%wide.region_2.4_spmd.sunk | while | flops 415630528 | bytes 7871975 | solution.py:36
  494.0 2.8 gather_fusion
  496.8 2.4 fusion.27
  499.9 1.0 constant_dynamic-slice_fusion.3
  500.9 1.8 fusion.28
  502.7 0.7 copy_dynamic-update-slice_fusion.2
  503.5 2.8 gather_fusion
  506.3 2.4 fusion.27
  509.5 1.0 constant_dynamic-slice_fusion.3
  510.4 1.8 fusion.28
  512.3 0.7 copy_dynamic-update-slice_fusion.2
  513.0 2.8 gather_fusion
  515.9 2.4 fusion.27
  519.0 1.0 constant_dynamic-slice_fusion.3
  520.0 1.8 fusion.28
  521.8 0.7 copy_dynamic-update-slice_fusion.2
  522.6 2.8 gather_fusion
  525.4 2.4 fusion.27
  528.5 1.0 constant_dynamic-slice_fusion.3
  529.5 1.8 fusion.28
  531.4 0.7 copy_dynamic-update-slice_fusion.2
  532.1 2.8 gather_fusion
  534.9 2.4 fusion.27
  538.1 1.0 constant_dynamic-slice_fusion.3
  539.1 1.8 fusion.28
  540.9 0.7 copy_dynamic-update-slice_fusion.2
  541.7 2.8 gather_fusion
  544.5 2.4 fusion.27
  547.6 1.0 constant_dynamic-slice_fusion.3
  548.6 1.8 fusion.28
  550.4 0.7 copy_dynamic-update-slice_fusion.2
  551.2 2.8 gather_fusion
  554.0 2.4 fusion.27
  557.2 1.0 constant_dynamic-slice_fusion.3
  558.1 1.8 fusion.28
  560.0 0.7 copy_dynamic-update-slice_fusion.2
  560.7 2.8 gather_fusion
  563.6 2.4 fusion.27
  566.7 1.0 constant_dynamic-slice_fusion.3
  567.7 1.8 fusion.28
  569.5 0.7 copy_dynamic-update-slice_fusion.2
  570.3 2.8 gather_fusion
  573.1 2.4 fusion.27
  576.2 1.0 constant_dynamic-slice_fusion.3
  577.2 1.8 fusion.28
  579.8 2.8 gather_fusion
  582.6 2.4 fusion.27
  585.8 1.0 constant_dynamic-slice_fusion.3
  586.7 1.8 fusion.28
  589.4 2.8 gather_fusion
  592.2 2.4 fusion.27
  595.3 1.0 constant_dynamic-slice_fusion.3
  596.3 1.8 fusion.28
  598.9 2.8 gather_fusion
  601.7 2.4 fusion.27
  604.9 1.0 constant_dynamic-slice_fusion.3
  605.8 1.8 fusion.28
  (59 shorter events, 13.3 us)
Async XLA Ops:
  6.5 487.4 %copy-start = (s32[4]{0:T(128)S(1)}, s32[4]{0:T(128)}, u32[]{:S(2)}) copy-start(s32[4]{0:T(128)} %constant.90.clone.1) | copy-start | bytes 52
  6.5 195.4 %all-gather.5.cloned.1.call-start = ((), (), s32[]{:S(2)}) async-start(), calls=%async_computation.1 | async-start | bytes 4325376 | tf_op jit(solution)/shard_map/all_gather | solution.py:13
  7.3 484.6 %all-gather.3.cloned.1.call-start = ((), (), s32[]{:S(2)}) async-start(), calls=%async_computation | async-start | bytes 13369344 | tf_op jit(solution)/shard_map/all_gather | solution.py:24
Sparse Core Ops, SparseCore 0:
  9.4 192.4 all-gather.4
  205.2 286.6 all-gather.2
where the time goes:
time: 617 us; the launch traced here: 615 us
  waiting for transfers between devices  482 us (78%)
  local copies, waits for them, and re-layouts  56.7 us (9%)
  matrix products  51.2 us (8%)
  between operations  13.4 us (2%)
  other arithmetic  11.8 us (2%)
    all_gather x1, waiting for transfers between devices, local(): whole_slots = lax.all_gather(a_blocks, 'row', axis=1, tiled=True)  290 us
    all_gather x1, waiting for transfers between devices, local(): panels = lax.all_gather(b_blocks, 'col', axis=0, tiled=True)[:, 0]  190 us
    gather x12, local copies, waits for them, and re-layouts, per_row(): chosen = jnp.take(panels, position[row_index], axis=0)  33.6 us
    dot_general x12, matrix products, per_row(): jnp.einsum('jab,jbc->jac', whole_slots[row_index], chosen, precision=lax....  29.1 us
    dot_general x12, matrix products, per_row(): jnp.einsum('js,jac->sac', weights[row_index], products, precision=lax.Pre...  22.2 us
  transfers between devices with their start and end apart: 2, of which 2 were waited for; matrix products, arithmetic and copies ran while one was open for 1% of the time, Pallas kernels for 0%

commit v1 on v0

--- a/solution.py
+++ b/solution.py
@@ -1,3 +1,5 @@
+import functools
+
 import jax
 import jax.numpy as jnp
 from jax import lax
@@ -9,22 +11,69 @@
     return jnp.sum(jnp.where(matched, values_table, 0), axis=-1)
 
 
-def local(a_blocks, a_cols, a_lengths, b_blocks, b_cols, c_cols, order):
-    panels = lax.all_gather(b_blocks, "col", axis=0, tiled=True)[:, 0]
+def row_gather(chunk, n_row):
+    n_x = n_row // 4
+    swap_z = [(r, r ^ 2) for r in range(n_row)]
+    held = jnp.concatenate([chunk, lax.ppermute(chunk, "row", swap_z)], axis=1)
+    parts = [held]
+    for k in range(1, n_x):
+        shift = [(r, ((r // 4 + k) % n_x) * 4 + r % 4) for r in range(n_row)]
+        parts.append(lax.ppermute(held, "row", shift))
+    held = jnp.concatenate(parts, axis=1)
+    swap_core = [(r, r ^ 1) for r in range(n_row)]
+    return jnp.concatenate([held, lax.ppermute(held, "row", swap_core)], axis=1)
+
+
+def row_slot_of_held(n_row):
+    n_x = n_row // 4
+    r = lax.axis_index("row")
+    x, zh, core = r // 4, (r // 2) % 2, r % 2
+    h = jnp.arange(n_row, dtype=jnp.int32)
+    cb, k, zb = h // (2 * n_x), (h // 2) % n_x, h % 2
+    return ((x - k) % n_x) * 4 + (zh ^ zb) * 2 + (core ^ cb)
+
+
+def col_gather(chunk, n_col):
+    n_y = n_col // 8
+    parts = [chunk]
+    for k in range(1, 8):
+        shift = [(c, (c // 8) * 8 + (c % 8 + k) % 8) for c in range(n_col)]
+        parts.append(lax.ppermute(chunk, "col", shift))
+    held = jnp.concatenate(parts, axis=0)
+    parts = [held]
+    for k in range(1, n_y):
+        shift = [(c, ((c // 8 + k) % n_y) * 8 + c % 8) for c in range(n_col)]
+        parts.append(lax.ppermute(held, "col", shift))
+    return jnp.concatenate(parts, axis=0)
+
+
+def col_held_index(grid_pos, per_dev, n_col):
+    n_y = n_col // 8
+    c = lax.axis_index("col")
+    y, zl = c // 8, c % 8
+    src = grid_pos // per_dev
+    return ((y - src // 8) % n_y) * (8 * per_dev) + ((zl - src % 8) % 8) * per_dev + grid_pos % per_dev
+
+
+def local(a_blocks, a_cols, a_lengths, b_blocks, b_cols, c_cols, order, n_row, n_col):
+    per_dev = b_blocks.shape[0]
+    panels = col_gather(b_blocks[:, 0], n_col)
     rows_here, slot_all = a_cols.shape
     pattern_slots = c_cols.shape[1]
     block_size = panels.shape[-1]
-    position = lookup(order, a_cols)
+    slot_of_held = row_slot_of_held(n_row)
+    position = jnp.take(lookup(order, a_cols), slot_of_held, axis=1)
     window_col = lookup(b_cols[:, 0], position)
-    live_slots = jnp.arange(slot_all, dtype=jnp.int32)[None, :] < a_lengths[:, None]
+    panel_index = col_held_index(position, per_dev, n_col)
+    live_slots = slot_of_held[None, :] < a_lengths[:, None]
     weights = ((window_col[:, :, None] == c_cols[:, None, :]) & live_slots[:, :, None]).astype(
         jnp.float32
     )
     zero_sums = jnp.zeros((rows_here, pattern_slots, block_size, block_size), jnp.float32)
-    whole_slots = lax.all_gather(a_blocks, "row", axis=1, tiled=True)
+    whole_slots = row_gather(a_blocks, n_row)
 
     def per_row(row_index, running):
-        chosen = jnp.take(panels, position[row_index], axis=0)
+        chosen = jnp.take(panels, panel_index[row_index], axis=0)
         products = jnp.einsum(
             "jab,jbc->jac", whole_slots[row_index], chosen, precision=lax.Precision.HIGHEST
         )
@@ -37,8 +86,9 @@
 
 
 def solution(mesh):
+    sizes = dict(n_row=mesh.shape["row"], n_col=mesh.shape["col"])
     return jax.shard_map(
-        local,
+        functools.partial(local, **sizes),
         mesh=mesh,
         in_specs=(
             P("col", "row", None, None),

time: 617 us -> 399 us (0.65)
  the two profiles are of different devices: /device:TPU:113 before, /device:TPU:107 now
where the time goes in v1:
time: 399 us; the launch traced here: 397 us
  waiting for transfers between devices  168 us (42%)
  starting transfers between devices  83.9 us (21%)
  local copies, waits for them, and re-layouts  82 us (21%)
  matrix products  51.9 us (13%)
  other arithmetic  10.6 us (3%)
    ppermute x3, waiting for transfers between devices, row_gather(): parts.append(lax.ppermute(held, 'row', shift))  62.8 us
    ppermute x1, waiting for transfers between devices, row_gather(): held = jnp.concatenate([chunk, lax.ppermute(chunk, 'row', swap_z)], axis=1)  52.5 us
    ppermute x7, starting transfers between devices, col_gather(): parts.append(lax.ppermute(chunk, 'col', shift))  49.4 us
    ppermute x3, waiting for transfers between devices, col_gather(): parts.append(lax.ppermute(held, 'col', shift))  40.8 us
    gather x12, local copies, waits for them, and re-layouts, per_row(): chosen = jnp.take(panels, panel_index[row_index], axis=0)  33.6 us
    dot_general x12, matrix products, per_row(): jnp.einsum('jab,jbc->jac', whole_slots[row_index], chosen, precision=lax....  29.1 us
    dot_general x12, matrix products, per_row(): jnp.einsum('js,jac->sac', weights[row_index], products, precision=lax.Pre...  22.9 us
    unnamed x28, local copies, waits for them, and re-layouts  15.1 us
  transfers between devices with their start and end apart: 15, of which 9 were waited for; matrix products, arithmetic and copies ran while one was open for 4% of the time, Pallas kernels for 0%

profile of v1, /device:TPU:107, one launch (start us, length us, event | category | flops | bytes accessed | tf_op | source)
XLA Modules:
  0.0 397.3 jit_solution(5443844370406495623)
XLA Ops:
  0.0 12.7 %collective-permute-start = (f32[12,1,128,128]{3,2,1,0:T(8,128)}, f32[12,1,128,128]{3,2,1,0:T(8,128)S(1)}, u32[]{:S(2)}, u32[]{:S(2)}) collective-permute-start(f32[12,1,128,128]{3,2,1,0:T(8,128)} %param.11), channel_id=1, source_target_pairs={{0,64},{32,96},{64,0},{96,32},{128,192},{160,224},{192,128},{224,1... | collective-permute-start | bytes 2359304 | tf_op jit(solution)/shard_map/ppermute | solution.py:17
  12.7 2.5 constant_dynamic-update-slice_fusion.6
  15.2 52.5 %collective-permute-done = f32[12,1,128,128]{3,2,1,0:T(8,128)S(1)} collective-permute-done((f32[12,1,128,128]{3,2,1,0:T(8,128)}, f32[12,1,128,128]{3,2,1,0:T(8,128)S(1)}, u32[]{:S(2)}, u32[]{:S(2)}) %collective-permute-start) | collective-permute-done | bytes 786464 | tf_op jit(solution)/shard_map/ppermute | solution.py:17
  69.1 3.1 collective-permute-start.1
  72.2 2.7 collective-permute-start.2
  74.9 3.8 collective-permute-start.3
  78.7 26.6 %collective-permute-done.1 = f32[12,2,128,128]{3,2,1,0:T(8,128)S(1)} collective-permute-done((f32[12,2,128,128]{3,2,1,0:T(8,128)S(1)}, f32[12,2,128,128]{3,2,1,0:T(8,128)S(1)}, u32[]{:S(2)}, u32[]{:S(2)}) %collective-permute-start.1) | collective-permute-done | bytes 1572896 | tf_op jit(solution)/shard_map/ppermute | solution.py:21
  105.3 2.0 constant_dynamic-update-slice_fusion.4
  107.3 2.4 collective-permute-done.2
  109.7 2.0 constant_dynamic-update-slice_fusion.3
  111.7 33.9 %collective-permute-done.3 = f32[12,2,128,128]{3,2,1,0:T(8,128)S(1)} collective-permute-done((f32[12,2,128,128]{3,2,1,0:T(8,128)S(1)}, f32[12,2,128,128]{3,2,1,0:T(8,128)S(1)}, u32[]{:S(2)}, u32[]{:S(2)}) %collective-permute-start.3) | collective-permute-done | bytes 1572896 | tf_op jit(solution)/shard_map/ppermute | solution.py:21
  145.6 2.0 constant_dynamic-update-slice_fusion.2
  147.7 2.4 collective-permute-start.4
  150.1 6.9 %collective-permute-start.5 = (f32[2,128,128]{2,1,0:T(8,128)S(1)}, f32[2,128,128]{2,1,0:T(8,128)S(1)}, u32[]{:S(2)}, u32[]{:S(2)}) collective-permute-start(f32[2,128,128]{2,1,0:T(8,128)S(1)} %bitcast.43), channel_id=1, source_target_pairs={{0,1},{1,2},{2,3},{3,4},{4,5},{5,6},{6,7},{7,0},{8,9},{9,10},{10,1... | collective-permute-start | bytes 393224 | tf_op jit(solution)/shard_map/ppermute | solution.py:41
  157.0 15.0 %collective-permute-start.6 = (f32[2,128,128]{2,1,0:T(8,128)S(1)}, f32[2,128,128]{2,1,0:T(8,128)S(1)}, u32[]{:S(2)}, u32[]{:S(2)}) collective-permute-start(f32[2,128,128]{2,1,0:T(8,128)S(1)} %bitcast.44), channel_id=1, source_target_pairs={{0,2},{1,3},{2,4},{3,5},{4,6},{5,7},{6,0},{7,1},{8,10},{9,11},{10,... | collective-permute-start | bytes 393224 | tf_op jit(solution)/shard_map/ppermute | solution.py:41
  172.0 3.6 collective-permute-start.7
  175.7 1.9 collective-permute-start.8
  178.7 4.9 %collective-permute-start.9 = (f32[2,128,128]{2,1,0:T(8,128)S(1)}, f32[2,128,128]{2,1,0:T(8,128)S(1)}, u32[]{:S(2)}, u32[]{:S(2)}) collective-permute-start(f32[2,128,128]{2,1,0:T(8,128)S(1)} %bitcast.47), channel_id=1, source_target_pairs={{0,5},{1,6},{2,7},{3,0},{4,1},{5,2},{6,3},{7,4},{8,13},{9,14},{10,... | collective-permute-start | bytes 393224 | tf_op jit(solution)/shard_map/ppermute | solution.py:41
  184.3 4.7 %collective-permute-start.10 = (f32[2,128,128]{2,1,0:T(8,128)S(1)}, f32[2,128,128]{2,1,0:T(8,128)S(1)}, u32[]{:S(2)}, u32[]{:S(2)}) collective-permute-start(f32[2,128,128]{2,1,0:T(8,128)S(1)} %bitcast.48), channel_id=1, source_target_pairs={{0,6},{1,7},{2,0},{3,1},{4,2},{5,3},{6,4},{7,5},{8,14},{9,15},{10,... | collective-permute-start | bytes 393224 | tf_op jit(solution)/shard_map/ppermute | solution.py:41
  189.7 12.3 %collective-permute-start.11 = (f32[2,128,128]{2,1,0:T(8,128)S(1)}, f32[2,128,128]{2,1,0:T(8,128)S(1)}, u32[]{:S(2)}, u32[]{:S(2)}) collective-permute-start(f32[2,128,128]{2,1,0:T(8,128)S(1)} %bitcast.49), channel_id=1, source_target_pairs={{0,7},{1,0},{2,1},{3,2},{4,3},{5,4},{6,5},{7,6},{8,15},{9,8},{10,9... | collective-permute-start | bytes 393224 | tf_op jit(solution)/shard_map/ppermute | solution.py:41
  202.8 9.1 %collective-permute-done.8 = f32[2,128,128]{2,1,0:T(8,128)S(1)} collective-permute-done((f32[2,128,128]{2,1,0:T(8,128)S(1)}, f32[2,128,128]{2,1,0:T(8,128)S(1)}, u32[]{:S(2)}, u32[]{:S(2)}) %collective-permute-start.8) | collective-permute-done | bytes 131104 | tf_op jit(solution)/shard_map/ppermute | solution.py:41
  214.0 2.9 collective-permute-done.11
  217.6 3.2 collective-permute-start.12
  220.9 2.6 collective-permute-start.13
  224.3 4.0 collective-permute-start.14
  229.1 14.9 %collective-permute-done.12 = f32[16,128,128]{2,1,0:T(8,128)S(1)} collective-permute-done((f32[16,128,128]{2,1,0:T(8,128)}, f32[16,128,128]{2,1,0:T(8,128)S(1)}, u32[]{:S(2)}, u32[]{:S(2)}) %collective-permute-start.12) | collective-permute-done | bytes 1048608 | tf_op jit(solution)/shard_map/ppermute | solution.py:46
  245.0 3.4 collective-permute-done.13
  249.5 22.6 %collective-permute-done.14 = f32[16,128,128]{2,1,0:T(8,128)S(1)} collective-permute-done((f32[16,128,128]{2,1,0:T(8,128)}, f32[16,128,128]{2,1,0:T(8,128)S(1)}, u32[]{:S(2)}, u32[]{:S(2)}) %collective-permute-start.14) | collective-permute-done | bytes 1048608 | tf_op jit(solution)/shard_map/ppermute | solution.py:46
  273.1 6.2 %constant_dynamic-update-slice_fusion.7 = f32[12,16,128,128]{3,2,1,0:T(8,128)} fusion(f32[12,16,128,128]{3,2,1,0:T(8,128)} %get-tuple-element.166, f32[12,8,128,128]{3,2,1,0:T(8,128)} %collective-permute-done.4), kind=kLoop, calls=%fused_computation.37 | loop fusion | bytes 12582912 | tf_op jit(solution)/shard_map/concatenate | solution.py:24
  279.3 2.0 broadcast_in_dim.57.clone
  281.4 115.9 %while.14 = (s32[]{:T(128)}, f32[12,4,128,128]{3,2,1,0:T(8,128)}, f32[12,16,4]{1,2,0:T(4,128)S(1)}, f32[12,16,128,128]{3,2,1,0:T(8,128)}, s32[12,16]{1,0:T(8,128...) while((s32[]{:T(128)}, f32[12,4,128,128]{3,2,1,0:T(8,128)}, ...), condition=%wide.region_4.5_spmd, body=%wide.region_2.4_spmd.sunk | while | flops 415630528 | bytes 7871983 | solution.py:85
  281.4 2.8 gather_fusion
  284.2 2.4 fusion.57
  288.4 1.9 fusion.58
  291.0 2.8 gather_fusion
  293.9 2.4 fusion.57
  298.0 1.9 fusion.58
  300.7 2.8 gather_fusion
  303.5 2.4 fusion.57
  307.7 1.9 fusion.58
  310.4 2.8 gather_fusion
  313.2 2.4 fusion.57
  317.4 1.9 fusion.58
  320.0 2.8 gather_fusion
  322.9 2.4 fusion.57
  329.7 2.8 gather_fusion
  332.5 2.4 fusion.57
  336.7 1.9 fusion.58
  339.3 2.8 gather_fusion
  342.2 2.4 fusion.57
  346.4 1.9 fusion.58
  349.0 2.8 gather_fusion
  351.8 2.4 fusion.57
  356.0 1.9 fusion.58
  358.7 2.8 gather_fusion
  361.5 2.4 fusion.57
  368.3 2.8 gather_fusion
  371.2 2.4 fusion.57
  375.3 1.9 fusion.58
  378.0 2.8 gather_fusion
  380.8 2.4 fusion.57
  385.0 1.9 fusion.58
  387.7 2.8 gather_fusion
  390.5 2.4 fusion.57
  (120 shorter events, 47.9 us)
Async XLA Ops:
  0.0 67.7 %collective-permute-start = (f32[12,1,128,128]{3,2,1,0:T(8,128)}, f32[12,1,128,128]{3,2,1,0:T(8,128)S(1)}, u32[]{:S(2)}, u32[]{:S(2)}) collective-permute-start(f32[12,1,128,128]{3,2,1,0:T(8,128)} %param.11), channel_id=1, source_target_pairs={{0,64},{32,96},{64,0},{96,32},{128,192},{160,224},{192,128},{224,1... | collective-permute-start | bytes 2359304 | tf_op jit(solution)/shard_map/ppermute | solution.py:17
  69.1 36.2 %collective-permute-start.1 = (f32[12,2,128,128]{3,2,1,0:T(8,128)S(1)}, f32[12,2,128,128]{3,2,1,0:T(8,128)S(1)}, u32[]{:S(2)}, u32[]{:S(2)}) collective-permute-start(f32[12,2,128,128]{3,2,1,0:T(8,128)S(1)} %get-tuple-element.173), channel_id=1, source_target_pairs={{0,128},{32,160},{64,192},{96,224},{128,256},{160,288},{192,320},{... | collective-permute-start | bytes 4718600 | tf_op jit(solution)/shard_map/ppermute | solution.py:21
  72.2 37.5 %collective-permute-start.2 = (f32[12,2,128,128]{3,2,1,0:T(8,128)S(1)}, f32[12,2,128,128]{3,2,1,0:T(8,128)S(1)}, u32[]{:S(2)}, u32[]{:S(2)}) collective-permute-start(f32[12,2,128,128]{3,2,1,0:T(8,128)S(1)} %get-tuple-element.173), channel_id=1, source_target_pairs={{0,256},{32,288},{64,320},{96,352},{128,384},{160,416},{192,448},{... | collective-permute-start | bytes 4718600 | tf_op jit(solution)/shard_map/ppermute | solution.py:21
  74.9 70.7 %collective-permute-start.3 = (f32[12,2,128,128]{3,2,1,0:T(8,128)S(1)}, f32[12,2,128,128]{3,2,1,0:T(8,128)S(1)}, u32[]{:S(2)}, u32[]{:S(2)}) collective-permute-start(f32[12,2,128,128]{3,2,1,0:T(8,128)S(1)} %get-tuple-element.173), channel_id=1, source_target_pairs={{0,384},{32,416},{64,448},{96,480},{128,0},{160,32},{192,64},{224,... | collective-permute-start | bytes 4718600 | tf_op jit(solution)/shard_map/ppermute | solution.py:21
  109.7 40.4 %copy-start = (f32[2,1,128,128]{3,2,1,0:T(8,128)S(1)}, f32[2,1,128,128]{3,2,1,0:T(8,128)}, u32[]{:S(2)}) copy-start(f32[2,1,128,128]{3,2,1,0:T(8,128)} %param.14) | copy-start | bytes 393220
  109.7 68.6 %copy-start.2 = (s32[12,16]{1,0:T(8,128)S(1)}, s32[12,16]{1,0:T(8,128)}, u32[]{:S(2)}) copy-start(s32[12,16]{1,0:T(8,128)} %param.12) | copy-start | bytes 2308
  109.7 68.6 %copy-start.4 = (s32[64]{0:T(128)S(1)}, s32[64]{0:T(128)}, u32[]{:S(2)}) copy-start(s32[64]{0:T(128)} %param.17) | copy-start | bytes 772
  111.7 111.8 %copy-start.3 = (s32[12,4]{0,1:T(4,128)S(1)}, s32[12,4]{0,1:T(4,128)}, u32[]{:S(2)}) copy-start(s32[12,4]{0,1:T(4,128)} %param.16) | copy-start | bytes 580
  111.7 116.8 %copy-start.5 = (s32[64,1]{0,1:T(1,128)S(1)}, s32[64,1]{0,1:T(1,128)}, u32[]{:S(2)}) copy-start(s32[64,1]{0,1:T(1,128)} %param.15) | copy-start | bytes 772
  111.7 117.2 %copy-start.6 = (s32[12]{0:T(128)S(1)}, s32[12]{0:T(128)}, u32[]{:S(2)}) copy-start(s32[12]{0:T(128)} %param.13) | copy-start | bytes 148
  147.7 125.4 %collective-permute-start.4 = (f32[12,8,128,128]{3,2,1,0:T(8,128)}, f32[12,8,128,128]{3,2,1,0:T(8,128)}, u32[]{:S(2)}, u32[]{:S(2)}) collective-permute-start(f32[12,8,128,128]{3,2,1,0:T(8,128)} %get-tuple-element.165), channel_id=1, source_target_pairs={{0,32},{32,0},{64,96},{96,64},{128,160},{160,128},{192,224},{224,1... | collective-permute-start | bytes 18874376 | tf_op jit(solution)/shard_map/ppermute | solution.py:24
  150.1 28.7 %collective-permute-start.5 = (f32[2,128,128]{2,1,0:T(8,128)S(1)}, f32[2,128,128]{2,1,0:T(8,128)S(1)}, u32[]{:S(2)}, u32[]{:S(2)}) collective-permute-start(f32[2,128,128]{2,1,0:T(8,128)S(1)} %bitcast.43), channel_id=1, source_target_pairs={{0,1},{1,2},{2,3},{3,4},{4,5},{5,6},{6,7},{7,0},{8,9},{9,10},{10,1... | collective-permute-start | bytes 393224 | tf_op jit(solution)/shard_map/ppermute | solution.py:41
  157.0 27.3 %collective-permute-start.6 = (f32[2,128,128]{2,1,0:T(8,128)S(1)}, f32[2,128,128]{2,1,0:T(8,128)S(1)}, u32[]{:S(2)}, u32[]{:S(2)}) collective-permute-start(f32[2,128,128]{2,1,0:T(8,128)S(1)} %bitcast.44), channel_id=1, source_target_pairs={{0,2},{1,3},{2,4},{3,5},{4,6},{5,7},{6,0},{7,1},{8,10},{9,11},{10,... | collective-permute-start | bytes 393224 | tf_op jit(solution)/shard_map/ppermute | solution.py:41
  172.0 17.7 %collective-permute-start.7 = (f32[2,128,128]{2,1,0:T(8,128)S(1)}, f32[2,128,128]{2,1,0:T(8,128)S(1)}, u32[]{:S(2)}, u32[]{:S(2)}) collective-permute-start(f32[2,128,128]{2,1,0:T(8,128)S(1)} %bitcast.45), channel_id=1, source_target_pairs={{0,3},{1,4},{2,5},{3,6},{4,7},{5,0},{6,1},{7,2},{8,11},{9,12},{10,... | collective-permute-start | bytes 393224 | tf_op jit(solution)/shard_map/ppermute | solution.py:41
  175.7 36.2 %collective-permute-start.8 = (f32[2,128,128]{2,1,0:T(8,128)S(1)}, f32[2,128,128]{2,1,0:T(8,128)S(1)}, u32[]{:S(2)}, u32[]{:S(2)}) collective-permute-start(f32[2,128,128]{2,1,0:T(8,128)S(1)} %bitcast.46), channel_id=1, source_target_pairs={{0,4},{1,5},{2,6},{3,7},{4,0},{5,1},{6,2},{7,3},{8,12},{9,13},{10,... | collective-permute-start | bytes 393224 | tf_op jit(solution)/shard_map/ppermute | solution.py:41
  178.7 33.8 %collective-permute-start.9 = (f32[2,128,128]{2,1,0:T(8,128)S(1)}, f32[2,128,128]{2,1,0:T(8,128)S(1)}, u32[]{:S(2)}, u32[]{:S(2)}) collective-permute-start(f32[2,128,128]{2,1,0:T(8,128)S(1)} %bitcast.47), channel_id=1, source_target_pairs={{0,5},{1,6},{2,7},{3,0},{4,1},{5,2},{6,3},{7,4},{8,13},{9,14},{10,... | collective-permute-start | bytes 393224 | tf_op jit(solution)/shard_map/ppermute | solution.py:41
  184.3 28.9 %collective-permute-start.10 = (f32[2,128,128]{2,1,0:T(8,128)S(1)}, f32[2,128,128]{2,1,0:T(8,128)S(1)}, u32[]{:S(2)}, u32[]{:S(2)}) collective-permute-start(f32[2,128,128]{2,1,0:T(8,128)S(1)} %bitcast.48), channel_id=1, source_target_pairs={{0,6},{1,7},{2,0},{3,1},{4,2},{5,3},{6,4},{7,5},{8,14},{9,15},{10,... | collective-permute-start | bytes 393224 | tf_op jit(solution)/shard_map/ppermute | solution.py:41
  189.7 27.2 %collective-permute-start.11 = (f32[2,128,128]{2,1,0:T(8,128)S(1)}, f32[2,128,128]{2,1,0:T(8,128)S(1)}, u32[]{:S(2)}, u32[]{:S(2)}) collective-permute-start(f32[2,128,128]{2,1,0:T(8,128)S(1)} %bitcast.49), channel_id=1, source_target_pairs={{0,7},{1,0},{2,1},{3,2},{4,3},{5,4},{6,5},{7,6},{8,15},{9,8},{10,9... | collective-permute-start | bytes 393224 | tf_op jit(solution)/shard_map/ppermute | solution.py:41
  217.6 26.3 %collective-permute-start.12 = (f32[16,128,128]{2,1,0:T(8,128)}, f32[16,128,128]{2,1,0:T(8,128)S(1)}, u32[]{:S(2)}, u32[]{:S(2)}) collective-permute-start(f32[16,128,128]{2,1,0:T(8,128)} %get-tuple-element.177), channel_id=1, source_target_pairs={{0,8},{1,9},{2,10},{3,11},{4,12},{5,13},{6,14},{7,15},{8,16},{9,17... | collective-permute-start | bytes 3145736 | tf_op jit(solution)/shard_map/ppermute | solution.py:46
  220.9 27.6 %collective-permute-start.13 = (f32[16,128,128]{2,1,0:T(8,128)}, f32[16,128,128]{2,1,0:T(8,128)S(1)}, u32[]{:S(2)}, u32[]{:S(2)}) collective-permute-start(f32[16,128,128]{2,1,0:T(8,128)} %get-tuple-element.177), channel_id=1, source_target_pairs={{0,16},{1,17},{2,18},{3,19},{4,20},{5,21},{6,22},{7,23},{8,24},{9,... | collective-permute-start | bytes 3145736 | tf_op jit(solution)/shard_map/ppermute | solution.py:46
  224.3 47.7 %collective-permute-start.14 = (f32[16,128,128]{2,1,0:T(8,128)}, f32[16,128,128]{2,1,0:T(8,128)S(1)}, u32[]{:S(2)}, u32[]{:S(2)}) collective-permute-start(f32[16,128,128]{2,1,0:T(8,128)} %get-tuple-element.177), channel_id=1, source_target_pairs={{0,24},{1,25},{2,26},{3,27},{4,28},{5,29},{6,30},{7,31},{8,0},{9,1... | collective-permute-start | bytes 3145736 | tf_op jit(solution)/shard_map/ppermute | solution.py:46
  273.1 8.3 %copy-start.1 = (s32[4]{0:T(128)S(1)}, s32[4]{0:T(128)}, u32[]{:S(2)}) copy-start(s32[4]{0:T(128)} %constant.264.clone.1) | copy-start | bytes 52

commit v2 on v1

v2 whole, which is shorter than its diff:
```python
import functools

import jax
import jax.numpy as jnp
from jax import lax
from jax.experimental import pallas as pl
from jax.experimental.pallas import tpu as pltpu
from jax.sharding import PartitionSpec as P


def lookup(values_table, indices):
    matched = indices[..., None] == jnp.arange(values_table.shape[0], dtype=jnp.int32)
    return jnp.sum(jnp.where(matched, values_table, 0), axis=-1)


def row_stages(n_row):
    n_x = n_row // 4

    def swap_z(chunk):
        pairs = [(r, r ^ 2) for r in range(n_row)]
        return jnp.concatenate([chunk, lax.ppermute(chunk, "row", pairs)], axis=1)

    def ring_x(held):
        parts = [held]
        for k in range(1, n_x):
            shift = [(r, ((r // 4 + k) % n_x) * 4 + r % 4) for r in range(n_row)]
            parts.append(lax.ppermute(held, "row", shift))
        return jnp.concatenate(parts, axis=1)

    def swap_core(held):
        pairs = [(r, r ^ 1) for r in range(n_row)]
        return jnp.concatenate([held, lax.ppermute(held, "row", pairs)], axis=1)

    return swap_z, ring_x, swap_core


def row_slot_of_held(n_row):
    n_x = n_row // 4
    r = lax.axis_index("row")
    x, zh, core = r // 4, (r // 2) % 2, r % 2
    h = jnp.arange(n_row, dtype=jnp.int32)
    cb, k, zb = h // (2 * n_x), (h // 2) % n_x, h % 2
    return ((x - k) % n_x) * 4 + (zh ^ zb) * 2 + (core ^ cb)


def col_stages(n_col):
    n_y = n_col // 8

    def line_z(chunk):
        parts = [chunk]
        for k in range(1, 8):
            shift = [(c, (c // 8) * 8 + (c % 8 + k) % 8) for c in range(n_col)]
            parts.append(lax.ppermute(chunk, "col", shift))
        return jnp.concatenate(parts, axis=0)

    def ring_y(held):
        parts = [held]
        for k in range(1, n_y):
            shift = [(c, ((c // 8 + k) % n_y) * 8 + c % 8) for c in range(n_col)]
            parts.append(lax.ppermute(held, "col", shift))
        return jnp.concatenate(parts, axis=0)

    return line_z, ring_y


def col_held_index(grid_pos, per_dev, n_col):
    n_y = n_col // 8
    c = lax.axis_index("col")
    y, zl = c // 8, c % 8
    src = grid_pos // per_dev
    return ((y - src // 8) % n_y) * (8 * per_dev) + ((zl - src % 8) % 8) * per_dev + grid_pos % per_dev


def local(a_blocks, a_cols, a_lengths, b_blocks, b_cols, c_cols, order, n_row, n_col):
    per_dev = b_blocks.shape[0]
    swap_z, ring_x, swap_core = row_stages(n_row)
    line_z, ring_y = col_stages(n_col)
    a_held, b_held = lax.optimization_barrier((swap_z(a_blocks), line_z(b_blocks[:, 0])))
    a_held, panels = lax.optimization_barrier((ring_x(a_held), ring_y(b_held)))
    whole_slots = swap_core(a_held)
    rows_here, slot_all = a_cols.shape
    pattern_slots = c_cols.shape[1]
    block_size = panels.shape[-1]
    slot_of_held = row_slot_of_held(n_row)
    position = jnp.take(lookup(order, a_cols), slot_of_held, axis=1)
    window_col = lookup(b_cols[:, 0], position)
    panel_index = col_held_index(position, per_dev, n_col)
    live_slots = slot_of_held[None, :] < a_lengths[:, None]
    weights = ((window_col[:, :, None] == c_cols[:, None, :]) & live_slots[:, :, None]).astype(
        jnp.float32
    )
    target = jnp.where(jnp.any(weights > 0, axis=-1), jnp.argmax(weights, axis=-1), -1)
    return row_products(whole_slots, panels, panel_index.reshape(-1), target.astype(jnp.int32).reshape(-1), pattern_slots)


def product_kernel(pidx_ref, sidx_ref, a_ref, b_ref, o_ref):
    i = pl.program_id(0)
    n_slots = a_ref.shape[1]
    o_ref[...] = jnp.zeros_like(o_ref)

    def body(j, carry):
        s = sidx_ref[i * n_slots + j]

        @pl.when(s >= 0)
        def _():
            p = pidx_ref[i * n_slots + j]
            prod = jnp.dot(a_ref[0, j], b_ref[p], precision=lax.Precision.HIGHEST,
                           preferred_element_type=jnp.float32)
            o_ref[0, s] += prod

        return carry

    lax.fori_loop(0, n_slots, body, 0)


def row_products(whole_slots, panels, panel_index, target, pattern_slots, interpret=False):
    rows, slots, bs, _ = whole_slots.shape
    grid_spec = pltpu.PrefetchScalarGridSpec(
        num_scalar_prefetch=2,
        grid=(rows,),
        in_specs=[
            pl.BlockSpec((1, slots, bs, bs), lambda i, pidx, sidx: (i, 0, 0, 0)),
            pl.BlockSpec(panels.shape, lambda i, pidx, sidx: (0, 0, 0)),
        ],
        out_specs=pl.BlockSpec((1, pattern_slots, bs, bs), lambda i, pidx, sidx: (i, 0, 0, 0)),
    )
    return pl.pallas_call(
        product_kernel,
        grid_spec=grid_spec,
        out_shape=jax.ShapeDtypeStruct((rows, pattern_slots, bs, bs), jnp.float32),
        interpret=interpret,
    )(panel_index, target, whole_slots, panels)


def solution(mesh):
    sizes = dict(n_row=mesh.shape["row"], n_col=mesh.shape["col"])
    return jax.shard_map(
        functools.partial(local, **sizes),
        mesh=mesh,
        in_specs=(
            P("col", "row", None, None),
            P("col", None),
            P("col"),
            P("col", "row", None, None),
            P(None, "row"),
            P("col", "row"),
            P(),
        ),
        out_specs=P("col", "row", None, None),
        check_vma=False,
    )
```

time: 399 us -> 259 us (0.65)
  the two profiles are of different devices: /device:TPU:107 before, /device:TPU:88 now
where the time goes in v2:
time: 259 us; the launch traced here: 258 us
  waiting for transfers between devices  123 us (47%)
  starting transfers between devices  83.6 us (32%)
  Pallas kernels  28.1 us (11%)
  other arithmetic  20.5 us (8%)
    ppermute x7, waiting for transfers between devices, line_z(): parts.append(lax.ppermute(chunk, 'col', shift))  81.1 us
    ppermute x3, starting transfers between devices, ring_y(): parts.append(lax.ppermute(held, 'col', shift))  29.9 us
    ppermute x7, starting transfers between devices, line_z(): parts.append(lax.ppermute(chunk, 'col', shift))  28.4 us
    pallas_call x1, Pallas kernels, row_products(): pl.pallas_call(product_kernel, grid_spec=grid_spec, out_shape=jax.ShapeDt...  28.1 us
    ppermute x3, waiting for transfers between devices, ring_y(): parts.append(lax.ppermute(held, 'col', shift))  22.8 us
    ppermute x1, starting transfers between devices, swap_z(): return jnp.concatenate([chunk, lax.ppermute(chunk, 'row', pairs)], axis=1)  12.6 us
    ppermute x3, waiting for transfers between devices, ring_x(): parts.append(lax.ppermute(held, 'row', shift))  12.6 us
    concatenate x1, other arithmetic, swap_core(): return jnp.concatenate([held, lax.ppermute(held, 'row', pairs)], axis=1)  11.4 us
  transfers between devices with their start and end apart: 15, of which 10 were waited for; matrix products, arithmetic and copies ran while one was open for 3% of the time, Pallas kernels for 0%

profile of v2, /device:TPU:88, one launch (start us, length us, event | category | flops | bytes accessed | tf_op | source)
XLA Modules:
  0.0 258.0 jit_solution(8242451019884466968)
XLA Ops:
  0.0 3.8 %collective-permute-start.1 = (f32[2,128,128]{2,1,0:T(8,128)}, f32[2,128,128]{2,1,0:T(8,128)S(1)}, u32[]{:S(2)}, u32[]{:S(2)}) collective-permute-start(f32[2,128,128]{2,1,0:T(8,128)} %bitcast.7), channel_id=1, source_target_pairs={{0,1},{1,2},{2,3},{3,4},{4,5},{5,6},{6,7},{7,0},{8,9},{9,10},{10,1... | collective-permute-start | bytes 393224 | tf_op jit(solution)/shard_map/ppermute | solution.py:53
  3.8 6.4 %collective-permute-start.2 = (f32[2,128,128]{2,1,0:T(8,128)}, f32[2,128,128]{2,1,0:T(8,128)S(1)}, u32[]{:S(2)}, u32[]{:S(2)}) collective-permute-start(f32[2,128,128]{2,1,0:T(8,128)} %bitcast.8), channel_id=1, source_target_pairs={{0,2},{1,3},{2,4},{3,5},{4,6},{5,7},{6,0},{7,1},{8,10},{9,11},{10,... | collective-permute-start | bytes 393224 | tf_op jit(solution)/shard_map/ppermute | solution.py:53
  10.2 4.6 %collective-permute-start.3 = (f32[2,128,128]{2,1,0:T(8,128)}, f32[2,128,128]{2,1,0:T(8,128)S(1)}, u32[]{:S(2)}, u32[]{:S(2)}) collective-permute-start(f32[2,128,128]{2,1,0:T(8,128)} %bitcast.9), channel_id=1, source_target_pairs={{0,3},{1,4},{2,5},{3,6},{4,7},{5,0},{6,1},{7,2},{8,11},{9,12},{10,... | collective-permute-start | bytes 393224 | tf_op jit(solution)/shard_map/ppermute | solution.py:53
  14.9 4.7 %collective-permute-start.4 = (f32[2,128,128]{2,1,0:T(8,128)}, f32[2,128,128]{2,1,0:T(8,128)S(1)}, u32[]{:S(2)}, u32[]{:S(2)}) collective-permute-start(f32[2,128,128]{2,1,0:T(8,128)} %bitcast.10), channel_id=1, source_target_pairs={{0,4},{1,5},{2,6},{3,7},{4,0},{5,1},{6,2},{7,3},{8,12},{9,13},{10,... | collective-permute-start | bytes 393224 | tf_op jit(solution)/shard_map/ppermute | solution.py:53
  19.5 5.1 %collective-permute-start.5 = (f32[2,128,128]{2,1,0:T(8,128)}, f32[2,128,128]{2,1,0:T(8,128)S(1)}, u32[]{:S(2)}, u32[]{:S(2)}) collective-permute-start(f32[2,128,128]{2,1,0:T(8,128)} %bitcast.11), channel_id=1, source_target_pairs={{0,5},{1,6},{2,7},{3,0},{4,1},{5,2},{6,3},{7,4},{8,13},{9,14},{10,... | collective-permute-start | bytes 393224 | tf_op jit(solution)/shard_map/ppermute | solution.py:53
  24.6 0.9 constant_dynamic-update-slice_fusion.7
  25.6 0.0 collective-permute-done.1
  25.6 12.6 %collective-permute-start = (f32[12,1,128,128]{3,2,1,0:T(8,128)}, f32[12,1,128,128]{3,2,1,0:T(8,128)S(1)}, u32[]{:S(2)}, u32[]{:S(2)}) collective-permute-start(f32[12,1,128,128]{3,2,1,0:T(8,128)} %param.7), channel_id=1, source_target_pairs={{0,64},{32,96},{64,0},{96,32},{128,192},{160,224},{192,128},{224,1... | collective-permute-start | bytes 2359304 | tf_op jit(solution)/shard_map/ppermute | solution.py:21
  38.2 0.0 collective-permute-done.2
  38.3 1.9 collective-permute-start.6
  40.2 40.5 %collective-permute-done.3 = f32[2,128,128]{2,1,0:T(8,128)S(1)} collective-permute-done((f32[2,128,128]{2,1,0:T(8,128)}, f32[2,128,128]{2,1,0:T(8,128)S(1)}, u32[]{:S(2)}, u32[]{:S(2)}) %collective-permute-start.3) | collective-permute-done | bytes 131104 | tf_op jit(solution)/shard_map/ppermute | solution.py:53
  80.7 1.9 collective-permute-start.7
  82.7 0.9 collective-permute-done.4
  83.6 5.0 %collective-permute-done.5 = f32[2,128,128]{2,1,0:T(8,128)S(1)} collective-permute-done((f32[2,128,128]{2,1,0:T(8,128)}, f32[2,128,128]{2,1,0:T(8,128)S(1)}, u32[]{:S(2)}, u32[]{:S(2)}) %collective-permute-start.5) | collective-permute-done | bytes 131104 | tf_op jit(solution)/shard_map/ppermute | solution.py:53
  88.6 31.5 %collective-permute-done.6 = f32[2,128,128]{2,1,0:T(8,128)S(1)} collective-permute-done((f32[2,128,128]{2,1,0:T(8,128)}, f32[2,128,128]{2,1,0:T(8,128)S(1)}, u32[]{:S(2)}, u32[]{:S(2)}) %collective-permute-start.6) | collective-permute-done | bytes 131104 | tf_op jit(solution)/shard_map/ppermute | solution.py:53
  120.1 3.2 %collective-permute-done.7 = f32[2,128,128]{2,1,0:T(8,128)S(1)} collective-permute-done((f32[2,128,128]{2,1,0:T(8,128)}, f32[2,128,128]{2,1,0:T(8,128)S(1)}, u32[]{:S(2)}, u32[]{:S(2)}) %collective-permute-start.7) | collective-permute-done | bytes 131104 | tf_op jit(solution)/shard_map/ppermute | solution.py:53
  123.3 0.0 collective-permute-done
  123.3 1.3 pad_maximum_fusion.3
  124.6 2.1 collective-permute-start.11
  126.7 4.7 %collective-permute-start.10 = (f32[12,2,128,128]{3,2,1,0:T(8,128)S(1)}, f32[12,2,128,128]{3,2,1,0:T(8,128)S(1)}, u32[]{:S(2)}, u32[]{:S(2)}) collective-permute-start(f32[12,2,128,128]{3,2,1,0:T(8,128)S(1)} %pad_maximum_fusion.3), channel_id=1, source_target_pairs={{0,384},{32,416},{64,448},{96,480},{128,0},{160,32},{192,64},{224,... | collective-permute-start | bytes 4718600 | tf_op jit(solution)/shard_map/ppermute | solution.py:27
  131.4 1.9 collective-permute-start.8
  133.3 4.2 %collective-permute-start.9 = (f32[12,2,128,128]{3,2,1,0:T(8,128)S(1)}, f32[12,2,128,128]{3,2,1,0:T(8,128)S(1)}, u32[]{:S(2)}, u32[]{:S(2)}) collective-permute-start(f32[12,2,128,128]{3,2,1,0:T(8,128)S(1)} %pad_maximum_fusion.3), channel_id=1, source_target_pairs={{0,256},{32,288},{64,320},{96,352},{128,384},{160,416},{192,448},{... | collective-permute-start | bytes 4718600 | tf_op jit(solution)/shard_map/ppermute | solution.py:27
  137.5 4.5 %collective-permute-start.12 = (f32[16,128,128]{2,1,0:T(8,128)S(1)}, f32[16,128,128]{2,1,0:T(8,128)S(1)}, u32[]{:S(2)}, u32[]{:S(2)}) collective-permute-start(f32[16,128,128]{2,1,0:T(8,128)S(1)} %constant_dynamic-update-slice_fusion), channel_id=1, source_target_pairs={{0,16},{1,17},{2,18},{3,19},{4,20},{5,21},{6,22},{7,23},{8,24},{9,... | collective-permute-start | bytes 3145736 | tf_op jit(solution)/shard_map/ppermute | solution.py:60
  142.0 10.5 %collective-permute-done.11 = f32[16,128,128]{2,1,0:T(8,128)S(1)} collective-permute-done((f32[16,128,128]{2,1,0:T(8,128)S(1)}, f32[16,128,128]{2,1,0:T(8,128)S(1)}, u32[]{:S(2)}, u32[]{:S(2)}) %collective-permute-start.11) | collective-permute-done | bytes 1048608 | tf_op jit(solution)/shard_map/ppermute | solution.py:60
  152.6 23.2 %collective-permute-start.13 = (f32[16,128,128]{2,1,0:T(8,128)S(1)}, f32[16,128,128]{2,1,0:T(8,128)S(1)}, u32[]{:S(2)}, u32[]{:S(2)}) collective-permute-start(f32[16,128,128]{2,1,0:T(8,128)S(1)} %constant_dynamic-update-slice_fusion), channel_id=1, source_target_pairs={{0,24},{1,25},{2,26},{3,27},{4,28},{5,29},{6,30},{7,31},{8,0},{9,1... | collective-permute-start | bytes 3145736 | tf_op jit(solution)/shard_map/ppermute | solution.py:60
  175.8 0.0 collective-permute-done.12
  175.8 12.3 %collective-permute-done.13 = f32[16,128,128]{2,1,0:T(8,128)S(1)} collective-permute-done((f32[16,128,128]{2,1,0:T(8,128)S(1)}, f32[16,128,128]{2,1,0:T(8,128)S(1)}, u32[]{:S(2)}, u32[]{:S(2)}) %collective-permute-start.13) | collective-permute-done | bytes 1048608 | tf_op jit(solution)/shard_map/ppermute | solution.py:60
  188.1 2.5 pad_maximum_fusion.2.b_ref
  190.6 0.0 copy-start
  190.6 0.0 copy-start.2
  190.6 0.0 copy-start.1
  190.6 0.0 copy-start.3
  190.6 0.0 copy-start.4
  190.6 7.3 %collective-permute-done.10 = f32[12,2,128,128]{3,2,1,0:T(8,128)S(1)} collective-permute-done((f32[12,2,128,128]{3,2,1,0:T(8,128)S(1)}, f32[12,2,128,128]{3,2,1,0:T(8,128)S(1)}, u32[]{:S(2)}, u32[]{:S(2)}) %collective-permute-start.10) | collective-permute-done | bytes 1572896 | tf_op jit(solution)/shard_map/ppermute | solution.py:27
  197.9 5.3 %collective-permute-done.8 = f32[12,2,128,128]{3,2,1,0:T(8,128)S(1)} collective-permute-done((f32[12,2,128,128]{3,2,1,0:T(8,128)S(1)}, f32[12,2,128,128]{3,2,1,0:T(8,128)S(1)}, u32[]{:S(2)}, u32[]{:S(2)}) %collective-permute-start.8) | collective-permute-done | bytes 1572896 | tf_op jit(solution)/shard_map/ppermute | solution.py:27
  203.2 0.0 collective-permute-done.9
  203.2 3.0 %pad_maximum_fusion.1 = f32[12,8,128,128]{3,2,1,0:T(8,128)} fusion(f32[12,2,128,128]{3,2,1,0:T(8,128)S(1)} %collective-permute-done.10, f32[12,2,128,128]{3,2,1,0:T(8,128)S(1)} %collective-permute-done.9, f32[12,2,128,128]{3,2,1,0:T(8,128)S(1)} %collective-permute-done.8, f32[12,2,128,128]{3,2,1,0:T(8,128)S(1)} %pad_maximum_fusion.3), kind=kLoop, calls=%fused_computation.2 | loop fusion | flops 4718592 | bytes 12582912 | tf_op jit(solution)/shard_map/concatenate | solution.py:28
  206.2 1.9 collective-permute-start.14
  208.1 0.0 copy-done
  208.1 0.0 copy-done.2
  208.2 0.4 select_reduce_fusion.1
  208.5 0.1 copy.13
  208.6 0.6 gather_fusion
  209.2 0.1 select_bitcast_fusion
  209.3 0.1 copy.14
  209.4 0.0 copy-done.1
  209.4 0.1 copy.16
  209.5 0.1 select_n.215
  209.6 0.0 copy-done.3
  209.6 0.4 select_reduce_fusion
  209.9 0.0 copy-done.4
  209.9 0.1 broadcast_compare_fusion
  210.0 0.1 fusion
  210.1 0.8 convert_reduce_fusion
  210.9 0.7 reshape.282.sidx_ref
  211.6 0.6 fusion.3.pidx_ref
  212.2 6.4 %collective-permute-done.14 = f32[12,8,128,128]{3,2,1,0:T(8,128)} collective-permute-done((f32[12,8,128,128]{3,2,1,0:T(8,128)}, f32[12,8,128,128]{3,2,1,0:T(8,128)}, u32[]{:S(2)}, u32[]{:S(2)}) %collective-permute-start.14) | collective-permute-done | bytes 6291488 | tf_op jit(solution)/shard_map/ppermute | solution.py:32
  218.5 11.4 %pad_maximum_fusion.a_ref = f32[12,16,128,128]{3,2,1,0:T(8,128)} fusion(f32[12,8,128,128]{3,2,1,0:T(8,128)} %collective-permute-done.14, f32[12,8,128,128]{3,2,1,0:T(8,128)} %pad_maximum_fusion.1), kind=kLoop, calls=%fused_computation.1 | loop fusion | flops 3145728 | bytes 25165824 | tf_op jit(solution)/shard_map/concatenate | solution.py:32
  229.9 28.1 %shard_map.73 = f32[12,4,128,128]{3,2,1,0:T(8,128)} custom-call(s32[192]{0:T(256)} %fusion.3.pidx_ref, s32[192]{0:T(256)} %reshape.282.sidx_ref, f32[12,16,128,128]{3,2,1,0:T(8,128)} %pad_maximum_fusion.a_ref, f32[64,128,128]{2,1,0:T(8,128)} %pad_maximum_fusion.2.b_ref), custom_call_target="tpu_custom_call" | custom-call | tf_op jit(solution)/shard_map/pallas_call | solution.py:127
  (11 shorter events, 0.1 us)
Async XLA Ops:
  0.0 25.6 %collective-permute-start.1 = (f32[2,128,128]{2,1,0:T(8,128)}, f32[2,128,128]{2,1,0:T(8,128)S(1)}, u32[]{:S(2)}, u32[]{:S(2)}) collective-permute-start(f32[2,128,128]{2,1,0:T(8,128)} %bitcast.7), channel_id=1, source_target_pairs={{0,1},{1,2},{2,3},{3,4},{4,5},{5,6},{6,7},{7,0},{8,9},{9,10},{10,1... | collective-permute-start | bytes 393224 | tf_op jit(solution)/shard_map/ppermute | solution.py:53
  3.8 34.4 %collective-permute-start.2 = (f32[2,128,128]{2,1,0:T(8,128)}, f32[2,128,128]{2,1,0:T(8,128)S(1)}, u32[]{:S(2)}, u32[]{:S(2)}) collective-permute-start(f32[2,128,128]{2,1,0:T(8,128)} %bitcast.8), channel_id=1, source_target_pairs={{0,2},{1,3},{2,4},{3,5},{4,6},{5,7},{6,0},{7,1},{8,10},{9,11},{10,... | collective-permute-start | bytes 393224 | tf_op jit(solution)/shard_map/ppermute | solution.py:53
  10.2 70.5 %collective-permute-start.3 = (f32[2,128,128]{2,1,0:T(8,128)}, f32[2,128,128]{2,1,0:T(8,128)S(1)}, u32[]{:S(2)}, u32[]{:S(2)}) collective-permute-start(f32[2,128,128]{2,1,0:T(8,128)} %bitcast.9), channel_id=1, source_target_pairs={{0,3},{1,4},{2,5},{3,6},{4,7},{5,0},{6,1},{7,2},{8,11},{9,12},{10,... | collective-permute-start | bytes 393224 | tf_op jit(solution)/shard_map/ppermute | solution.py:53
  14.9 68.7 %collective-permute-start.4 = (f32[2,128,128]{2,1,0:T(8,128)}, f32[2,128,128]{2,1,0:T(8,128)S(1)}, u32[]{:S(2)}, u32[]{:S(2)}) collective-permute-start(f32[2,128,128]{2,1,0:T(8,128)} %bitcast.10), channel_id=1, source_target_pairs={{0,4},{1,5},{2,6},{3,7},{4,0},{5,1},{6,2},{7,3},{8,12},{9,13},{10,... | collective-permute-start | bytes 393224 | tf_op jit(solution)/shard_map/ppermute | solution.py:53
  19.5 69.0 %collective-permute-start.5 = (f32[2,128,128]{2,1,0:T(8,128)}, f32[2,128,128]{2,1,0:T(8,128)S(1)}, u32[]{:S(2)}, u32[]{:S(2)}) collective-permute-start(f32[2,128,128]{2,1,0:T(8,128)} %bitcast.11), channel_id=1, source_target_pairs={{0,5},{1,6},{2,7},{3,0},{4,1},{5,2},{6,3},{7,4},{8,13},{9,14},{10,... | collective-permute-start | bytes 393224 | tf_op jit(solution)/shard_map/ppermute | solution.py:53
  25.6 97.7 %collective-permute-start = (f32[12,1,128,128]{3,2,1,0:T(8,128)}, f32[12,1,128,128]{3,2,1,0:T(8,128)S(1)}, u32[]{:S(2)}, u32[]{:S(2)}) collective-permute-start(f32[12,1,128,128]{3,2,1,0:T(8,128)} %param.7), channel_id=1, source_target_pairs={{0,64},{32,96},{64,0},{96,32},{128,192},{160,224},{192,128},{224,1... | collective-permute-start | bytes 2359304 | tf_op jit(solution)/shard_map/ppermute | solution.py:21
  38.3 81.8 %collective-permute-start.6 = (f32[2,128,128]{2,1,0:T(8,128)}, f32[2,128,128]{2,1,0:T(8,128)S(1)}, u32[]{:S(2)}, u32[]{:S(2)}) collective-permute-start(f32[2,128,128]{2,1,0:T(8,128)} %bitcast.12), channel_id=1, source_target_pairs={{0,6},{1,7},{2,0},{3,1},{4,2},{5,3},{6,4},{7,5},{8,14},{9,15},{10,... | collective-permute-start | bytes 393224 | tf_op jit(solution)/shard_map/ppermute | solution.py:53
  80.7 42.6 %collective-permute-start.7 = (f32[2,128,128]{2,1,0:T(8,128)}, f32[2,128,128]{2,1,0:T(8,128)S(1)}, u32[]{:S(2)}, u32[]{:S(2)}) collective-permute-start(f32[2,128,128]{2,1,0:T(8,128)} %bitcast.13), channel_id=1, source_target_pairs={{0,7},{1,0},{2,1},{3,2},{4,3},{5,4},{6,5},{7,6},{8,15},{9,8},{10,9... | collective-permute-start | bytes 393224 | tf_op jit(solution)/shard_map/ppermute | solution.py:53
  124.6 28.0 %collective-permute-start.11 = (f32[16,128,128]{2,1,0:T(8,128)S(1)}, f32[16,128,128]{2,1,0:T(8,128)S(1)}, u32[]{:S(2)}, u32[]{:S(2)}) collective-permute-start(f32[16,128,128]{2,1,0:T(8,128)S(1)} %constant_dynamic-update-slice_fusion), channel_id=1, source_target_pairs={{0,8},{1,9},{2,10},{3,11},{4,12},{5,13},{6,14},{7,15},{8,16},{9,17... | collective-permute-start | bytes 3145736 | tf_op jit(solution)/shard_map/ppermute | solution.py:60
  126.7 71.2 %collective-permute-start.10 = (f32[12,2,128,128]{3,2,1,0:T(8,128)S(1)}, f32[12,2,128,128]{3,2,1,0:T(8,128)S(1)}, u32[]{:S(2)}, u32[]{:S(2)}) collective-permute-start(f32[12,2,128,128]{3,2,1,0:T(8,128)S(1)} %pad_maximum_fusion.3), channel_id=1, source_target_pairs={{0,384},{32,416},{64,448},{96,480},{128,0},{160,32},{192,64},{224,... | collective-permute-start | bytes 4718600 | tf_op jit(solution)/shard_map/ppermute | solution.py:27
  131.4 71.8 %collective-permute-start.8 = (f32[12,2,128,128]{3,2,1,0:T(8,128)S(1)}, f32[12,2,128,128]{3,2,1,0:T(8,128)S(1)}, u32[]{:S(2)}, u32[]{:S(2)}) collective-permute-start(f32[12,2,128,128]{3,2,1,0:T(8,128)S(1)} %pad_maximum_fusion.3), channel_id=1, source_target_pairs={{0,128},{32,160},{64,192},{96,224},{128,256},{160,288},{192,320},{... | collective-permute-start | bytes 4718600 | tf_op jit(solution)/shard_map/ppermute | solution.py:27
  133.3 69.9 %collective-permute-start.9 = (f32[12,2,128,128]{3,2,1,0:T(8,128)S(1)}, f32[12,2,128,128]{3,2,1,0:T(8,128)S(1)}, u32[]{:S(2)}, u32[]{:S(2)}) collective-permute-start(f32[12,2,128,128]{3,2,1,0:T(8,128)S(1)} %pad_maximum_fusion.3), channel_id=1, source_target_pairs={{0,256},{32,288},{64,320},{96,352},{128,384},{160,416},{192,448},{... | collective-permute-start | bytes 4718600 | tf_op jit(solution)/shard_map/ppermute | solution.py:27
  137.5 38.3 %collective-permute-start.12 = (f32[16,128,128]{2,1,0:T(8,128)S(1)}, f32[16,128,128]{2,1,0:T(8,128)S(1)}, u32[]{:S(2)}, u32[]{:S(2)}) collective-permute-start(f32[16,128,128]{2,1,0:T(8,128)S(1)} %constant_dynamic-update-slice_fusion), channel_id=1, source_target_pairs={{0,16},{1,17},{2,18},{3,19},{4,20},{5,21},{6,22},{7,23},{8,24},{9,... | collective-permute-start | bytes 3145736 | tf_op jit(solution)/shard_map/ppermute | solution.py:60
  152.6 35.5 %collective-permute-start.13 = (f32[16,128,128]{2,1,0:T(8,128)S(1)}, f32[16,128,128]{2,1,0:T(8,128)S(1)}, u32[]{:S(2)}, u32[]{:S(2)}) collective-permute-start(f32[16,128,128]{2,1,0:T(8,128)S(1)} %constant_dynamic-update-slice_fusion), channel_id=1, source_target_pairs={{0,24},{1,25},{2,26},{3,27},{4,28},{5,29},{6,30},{7,31},{8,0},{9,1... | collective-permute-start | bytes 3145736 | tf_op jit(solution)/shard_map/ppermute | solution.py:60
  190.6 17.5 %copy-start = (s32[12,16]{1,0:T(8,128)S(1)}, s32[12,16]{1,0:T(8,128)}, u32[]{:S(2)}) copy-start(s32[12,16]{1,0:T(8,128)} %param.8) | copy-start | bytes 2308
  190.6 17.5 %copy-start.2 = (s32[64]{0:T(128)S(1)}, s32[64]{0:T(128)}, u32[]{:S(2)}) copy-start(s32[64]{0:T(128)} %param.13) | copy-start | bytes 772
  190.6 18.8 %copy-start.1 = (s32[12,4]{0,1:T(4,128)S(1)}, s32[12,4]{0,1:T(4,128)}, u32[]{:S(2)}) copy-start(s32[12,4]{0,1:T(4,128)} %param.12) | copy-start | bytes 580
  190.6 19.0 %copy-start.3 = (s32[64,1]{0,1:T(1,128)S(1)}, s32[64,1]{0,1:T(1,128)}, u32[]{:S(2)}) copy-start(s32[64,1]{0,1:T(1,128)} %param.11) | copy-start | bytes 772
  190.6 19.3 %copy-start.4 = (s32[12]{0:T(128)S(1)}, s32[12]{0:T(128)}, u32[]{:S(2)}) copy-start(s32[12]{0:T(128)} %param.9) | copy-start | bytes 148
  206.2 12.4 %collective-permute-start.14 = (f32[12,8,128,128]{3,2,1,0:T(8,128)}, f32[12,8,128,128]{3,2,1,0:T(8,128)}, u32[]{:S(2)}, u32[]{:S(2)}) collective-permute-start(f32[12,8,128,128]{3,2,1,0:T(8,128)} %pad_maximum_fusion.1), channel_id=1, source_target_pairs={{0,32},{32,0},{64,96},{96,64},{128,160},{160,128},{192,224},{224,1... | collective-permute-start | bytes 18874376 | tf_op jit(solution)/shard_map/ppermute | solution.py:32

commit v3 on v2

--- a/solution.py
+++ b/solution.py
@@ -29,7 +29,7 @@
 
     def swap_core(held):
         pairs = [(r, r ^ 1) for r in range(n_row)]
-        return jnp.concatenate([held, lax.ppermute(held, "row", pairs)], axis=1)
+        return lax.ppermute(held, "row", pairs)
 
     return swap_z, ring_x, swap_core
 
@@ -47,11 +47,21 @@
     n_y = n_col // 8
 
     def line_z(chunk):
-        parts = [chunk]
-        for k in range(1, 8):
-            shift = [(c, (c // 8) * 8 + (c % 8 + k) % 8) for c in range(n_col)]
-            parts.append(lax.ppermute(chunk, "col", shift))
-        return jnp.concatenate(parts, axis=0)
+        c = lax.axis_index("col")
+        zl = c % 8
+        right = [(c, c + 1) for c in range(n_col) if c % 8 < 7]
+        left = [(c, c - 1) for c in range(n_col) if c % 8 > 0]
+        from_left, from_right = [chunk], []
+        going_right, going_left = chunk, chunk
+        for _ in range(7):
+            going_right = lax.ppermute(going_right, "col", right)
+            going_left = lax.ppermute(going_left, "col", left)
+            from_left.append(going_right)
+            from_right.append(going_left)
+        pieces = jnp.stack(from_left + from_right, axis=0)
+        src = jnp.arange(8, dtype=jnp.int32)
+        pick = jnp.where(src <= zl, zl - src, 7 + src - zl)
+        return jnp.take(pieces, pick, axis=0).reshape((-1,) + chunk.shape[1:])
 
     def ring_y(held):
         parts = [held]
@@ -66,9 +76,9 @@
 def col_held_index(grid_pos, per_dev, n_col):
     n_y = n_col // 8
     c = lax.axis_index("col")
-    y, zl = c // 8, c % 8
+    y = c // 8
     src = grid_pos // per_dev
-    return ((y - src // 8) % n_y) * (8 * per_dev) + ((zl - src % 8) % 8) * per_dev + grid_pos % per_dev
+    return ((y - src // 8) % n_y) * (8 * per_dev) + (src % 8) * per_dev + grid_pos % per_dev
 
 
 def local(a_blocks, a_cols, a_lengths, b_blocks, b_cols, c_cols, order, n_row, n_col):
@@ -77,7 +87,6 @@
     line_z, ring_y = col_stages(n_col)
     a_held, b_held = lax.optimization_barrier((swap_z(a_blocks), line_z(b_blocks[:, 0])))
     a_held, panels = lax.optimization_barrier((ring_x(a_held), ring_y(b_held)))
-    whole_slots = swap_core(a_held)
     rows_here, slot_all = a_cols.shape
     pattern_slots = c_cols.shape[1]
     block_size = panels.shape[-1]
@@ -90,13 +99,22 @@
         jnp.float32
     )
     target = jnp.where(jnp.any(weights > 0, axis=-1), jnp.argmax(weights, axis=-1), -1)
-    return row_products(whole_slots, panels, panel_index.reshape(-1), target.astype(jnp.int32).reshape(-1), pattern_slots)
+    target = target.astype(jnp.int32)
+    half = a_held.shape[1]
+    mine = row_products(a_held, panels, panel_index[:, :half].reshape(-1),
+                        target[:, :half].reshape(-1), pattern_slots)
+    return row_products(swap_core(a_held), panels, panel_index[:, half:].reshape(-1),
+                        target[:, half:].reshape(-1), pattern_slots, mine)
 
 
-def product_kernel(pidx_ref, sidx_ref, a_ref, b_ref, o_ref):
+def product_kernel(pidx_ref, sidx_ref, a_ref, b_ref, *rest):
     i = pl.program_id(0)
     n_slots = a_ref.shape[1]
-    o_ref[...] = jnp.zeros_like(o_ref)
+    o_ref = rest[-1]
+    if len(rest) == 2:
+        o_ref[...] = rest[0][...]
+    else:
+        o_ref[...] = jnp.zeros_like(o_ref)
 
     def body(j, carry):
         s = sidx_ref[i * n_slots + j]
@@ -113,23 +131,26 @@
     lax.fori_loop(0, n_slots, body, 0)
 
 
-def row_products(whole_slots, panels, panel_index, target, pattern_slots, interpret=False):
+def row_products(whole_slots, panels, panel_index, target, pattern_slots, acc=None, interpret=False):
     rows, slots, bs, _ = whole_slots.shape
+    out_spec = pl.BlockSpec((1, pattern_slots, bs, bs), lambda i, pidx, sidx: (i, 0, 0, 0))
+    extra = [] if acc is None else [acc]
     grid_spec = pltpu.PrefetchScalarGridSpec(
         num_scalar_prefetch=2,
         grid=(rows,),
         in_specs=[
             pl.BlockSpec((1, slots, bs, bs), lambda i, pidx, sidx: (i, 0, 0, 0)),
             pl.BlockSpec(panels.shape, lambda i, pidx, sidx: (0, 0, 0)),
-        ],
-        out_specs=pl.BlockSpec((1, pattern_slots, bs, bs), lambda i, pidx, sidx: (i, 0, 0, 0)),
+        ] + [out_spec] * len(extra),
+        out_specs=out_spec,
     )
     return pl.pallas_call(
         product_kernel,
         grid_spec=grid_spec,
         out_shape=jax.ShapeDtypeStruct((rows, pattern_slots, bs, bs), jnp.float32),
+        input_output_aliases={} if acc is None else {4: 0},
         interpret=interpret,
-    )(panel_index, target, whole_slots, panels)
+    )(panel_index, target, whole_slots, panels, *extra)
 
 
 def solution(mesh):

time: 259 us -> 263 us (1.015)
  the two profiles are of different devices: /device:TPU:88 before, /device:TPU:97 now
where the time goes in v3:
time: 263 us; the launch traced here: 261 us
  waiting for transfers between devices  125 us (48%)
  starting transfers between devices  77 us (29%)
  Pallas kernels  33.8 us (13%)
  local copies, waits for them, and re-layouts  17.2 us (7%)
  other arithmetic  7.54 us (3%)
    ppermute x7, waiting for transfers between devices, line_z(): going_right = lax.ppermute(going_right, 'col', right)  63.7 us
    ppermute x3, waiting for transfers between devices, ring_y(): parts.append(lax.ppermute(held, 'col', shift))  35.6 us
    pallas_call x2, Pallas kernels, row_products(): pl.pallas_call(product_kernel, grid_spec=grid_spec, out_shape=jax.ShapeDt...  33.8 us
    ppermute x7, starting transfers between devices, line_z(): going_right = lax.ppermute(going_right, 'col', right)  31.7 us
    ppermute x3, waiting for transfers between devices, ring_x(): parts.append(lax.ppermute(held, 'row', shift))  26.2 us
    ppermute x7, starting transfers between devices, line_z(): going_left = lax.ppermute(going_left, 'col', left)  13.4 us
    ppermute x1, starting transfers between devices, swap_z(): return jnp.concatenate([chunk, lax.ppermute(chunk, 'row', pairs)], axis=1)  11.4 us
    unnamed x27, local copies, waits for them, and re-layouts  10.3 us
  transfers between devices with their start and end apart: 22, of which 5 were waited for; matrix products, arithmetic and copies ran while one was open for 7% of the time, Pallas kernels for 6%

profile of v3, /device:TPU:97, one launch (start us, length us, event | category | flops | bytes accessed | tf_op | source)
XLA Modules:
  0.0 261.5 jit_solution(16222686459509324762)
XLA Ops:
  0.0 4.9 %collective-permute-start.1 = (f32[2,128,128]{2,1,0:T(8,128)}, f32[2,128,128]{2,1,0:T(8,128)S(1)}, u32[]{:S(2)}, u32[]{:S(2)}) collective-permute-start(f32[2,128,128]{2,1,0:T(8,128)} %bitcast.41), channel_id=1, source_target_pairs={{0,1},{1,2},{2,3},{3,4},{4,5},{5,6},{6,7},{8,9},{9,10},{10,11},{11... | collective-permute-start | bytes 393224 | tf_op jit(solution)/shard_map/ppermute | solution.py:57
  4.9 1.9 collective-permute-start.8
  6.8 11.4 %collective-permute-start = (f32[12,1,128,128]{3,2,1,0:T(8,128)}, f32[12,1,128,128]{3,2,1,0:T(8,128)S(1)}, u32[]{:S(2)}, u32[]{:S(2)}) collective-permute-start(f32[12,1,128,128]{3,2,1,0:T(8,128)} %param.7), channel_id=1, source_target_pairs={{0,64},{32,96},{64,0},{96,32},{128,192},{160,224},{192,128},{224,1... | collective-permute-start | bytes 2359304 | tf_op jit(solution)/shard_map/ppermute | solution.py:21
  18.2 1.6 bitcast_dynamic-update-slice_fusion.14
  19.8 0.1 broadcast_in_dim.53
  19.9 3.9 %collective-permute-start.2 = (f32[2,128,128]{2,1,0:T(8,128)S(1)}, f32[2,128,128]{2,1,0:T(8,128)S(1)}, u32[]{:S(2)}, u32[]{:S(2)}) collective-permute-start(f32[2,128,128]{2,1,0:T(8,128)S(1)} %collective-permute-done.1), channel_id=1, source_target_pairs={{0,1},{1,2},{2,3},{3,4},{4,5},{5,6},{6,7},{8,9},{9,10},{10,11},{11... | collective-permute-start | bytes 393224 | tf_op jit(solution)/shard_map/ppermute | solution.py:57
  23.8 1.9 collective-permute-start.9
  25.8 0.7 bitcast_dynamic-update-slice_fusion.13
  26.4 63.6 %collective-permute-done.2 = f32[2,128,128]{2,1,0:T(8,128)S(1)} collective-permute-done((f32[2,128,128]{2,1,0:T(8,128)S(1)}, f32[2,128,128]{2,1,0:T(8,128)S(1)}, u32[]{:S(2)}, u32[]{:S(2)}) %collective-permute-start.2) | collective-permute-done | bytes 131104 | tf_op jit(solution)/shard_map/ppermute | solution.py:57
  90.1 4.3 %collective-permute-start.3 = (f32[2,128,128]{2,1,0:T(8,128)S(1)}, f32[2,128,128]{2,1,0:T(8,128)S(1)}, u32[]{:S(2)}, u32[]{:S(2)}) collective-permute-start(f32[2,128,128]{2,1,0:T(8,128)S(1)} %collective-permute-done.2), channel_id=1, source_target_pairs={{0,1},{1,2},{2,3},{3,4},{4,5},{5,6},{6,7},{8,9},{9,10},{10,11},{11... | collective-permute-start | bytes 393224 | tf_op jit(solution)/shard_map/ppermute | solution.py:57
  94.3 1.9 collective-permute-start.10
  96.3 0.7 bitcast_dynamic-update-slice_fusion.12
  96.9 5.0 %collective-permute-start.4 = (f32[2,128,128]{2,1,0:T(8,128)S(1)}, f32[2,128,128]{2,1,0:T(8,128)S(1)}, u32[]{:S(2)}, u32[]{:S(2)}) collective-permute-start(f32[2,128,128]{2,1,0:T(8,128)S(1)} %collective-permute-done.3), channel_id=1, source_target_pairs={{0,1},{1,2},{2,3},{3,4},{4,5},{5,6},{6,7},{8,9},{9,10},{10,11},{11... | collective-permute-start | bytes 393224 | tf_op jit(solution)/shard_map/ppermute | solution.py:57
  102.0 1.9 collective-permute-start.11
  103.9 0.7 bitcast_dynamic-update-slice_fusion.11
  104.6 4.6 %collective-permute-start.5 = (f32[2,128,128]{2,1,0:T(8,128)S(1)}, f32[2,128,128]{2,1,0:T(8,128)S(1)}, u32[]{:S(2)}, u32[]{:S(2)}) collective-permute-start(f32[2,128,128]{2,1,0:T(8,128)S(1)} %collective-permute-done.4), channel_id=1, source_target_pairs={{0,1},{1,2},{2,3},{3,4},{4,5},{5,6},{6,7},{8,9},{9,10},{10,11},{11... | collective-permute-start | bytes 393224 | tf_op jit(solution)/shard_map/ppermute | solution.py:57
  109.2 1.9 collective-permute-start.12
  111.1 0.7 bitcast_dynamic-update-slice_fusion.10
  111.8 4.6 %collective-permute-start.6 = (f32[2,128,128]{2,1,0:T(8,128)S(1)}, f32[2,128,128]{2,1,0:T(8,128)S(1)}, u32[]{:S(2)}, u32[]{:S(2)}) collective-permute-start(f32[2,128,128]{2,1,0:T(8,128)S(1)} %collective-permute-done.5), channel_id=1, source_target_pairs={{0,1},{1,2},{2,3},{3,4},{4,5},{5,6},{6,7},{8,9},{9,10},{10,11},{11... | collective-permute-start | bytes 393224 | tf_op jit(solution)/shard_map/ppermute | solution.py:57
  116.4 1.9 collective-permute-start.13
  118.3 0.7 bitcast_dynamic-update-slice_fusion.9
  119.0 4.6 %collective-permute-start.7 = (f32[2,128,128]{2,1,0:T(8,128)S(1)}, f32[2,128,128]{2,1,0:T(8,128)S(1)}, u32[]{:S(2)}, u32[]{:S(2)}) collective-permute-start(f32[2,128,128]{2,1,0:T(8,128)S(1)} %collective-permute-done.6), channel_id=1, source_target_pairs={{0,1},{1,2},{2,3},{3,4},{4,5},{5,6},{6,7},{8,9},{9,10},{10,11},{11... | collective-permute-start | bytes 393224 | tf_op jit(solution)/shard_map/ppermute | solution.py:57
  123.5 1.9 collective-permute-start.14
  125.5 0.7 bitcast_dynamic-update-slice_fusion.8
  126.1 0.1 pad_maximum_fusion.2
  126.3 0.7 bitcast_dynamic-update-slice_fusion.7
  127.0 0.7 bitcast_dynamic-update-slice_fusion.6
  127.6 0.7 bitcast_dynamic-update-slice_fusion.5
  128.3 0.7 bitcast_dynamic-update-slice_fusion.4
  129.0 0.7 bitcast_dynamic-update-slice_fusion.3
  129.6 0.7 bitcast_dynamic-update-slice_fusion.2
  130.3 0.7 bitcast_dynamic-update-slice_fusion.1
  131.0 0.7 bitcast_dynamic-update-slice_fusion
  131.6 2.2 gather_fusion.1
  133.8 0.1 bitcast_select_fusion
  133.9 4.6 %collective-permute-start.20 = (f32[16,128,128]{2,1,0:T(8,128)S(1)}, f32[16,128,128]{2,1,0:T(8,128)S(1)}, u32[]{:S(2)}, u32[]{:S(2)}) collective-permute-start(f32[16,128,128]{2,1,0:T(8,128)S(1)} %bitcast_select_fusion), channel_id=1, source_target_pairs={{0,24},{1,25},{2,26},{3,27},{4,28},{5,29},{6,30},{7,31},{8,0},{9,1... | collective-permute-start | bytes 3145736 | tf_op jit(solution)/shard_map/ppermute | solution.py:70
  138.6 4.4 %collective-permute-start.17 = (f32[12,2,128,128]{3,2,1,0:T(8,128)S(1)}, f32[12,2,128,128]{3,2,1,0:T(8,128)S(1)}, u32[]{:S(2)}, u32[]{:S(2)}) collective-permute-start(f32[12,2,128,128]{3,2,1,0:T(8,128)S(1)} %pad_maximum_fusion.2), channel_id=1, source_target_pairs={{0,384},{32,416},{64,448},{96,480},{128,0},{160,32},{192,64},{224,... | collective-permute-start | bytes 4718600 | tf_op jit(solution)/shard_map/ppermute | solution.py:27
  143.0 2.4 collective-permute-start.16
  145.4 2.5 collective-permute-start.15
  147.9 2.3 collective-permute-start.19
  150.2 6.9 %collective-permute-done.20 = f32[16,128,128]{2,1,0:T(8,128)S(1)} collective-permute-done((f32[16,128,128]{2,1,0:T(8,128)S(1)}, f32[16,128,128]{2,1,0:T(8,128)S(1)}, u32[]{:S(2)}, u32[]{:S(2)}) %collective-permute-start.20) | collective-permute-done | bytes 1048608 | tf_op jit(solution)/shard_map/ppermute | solution.py:70
  157.2 1.9 collective-permute-start.18
  159.1 10.9 %collective-permute-done.19 = f32[16,128,128]{2,1,0:T(8,128)S(1)} collective-permute-done((f32[16,128,128]{2,1,0:T(8,128)S(1)}, f32[16,128,128]{2,1,0:T(8,128)S(1)}, u32[]{:S(2)}, u32[]{:S(2)}) %collective-permute-start.19) | collective-permute-done | bytes 1048608 | tf_op jit(solution)/shard_map/ppermute | solution.py:70
  170.0 17.7 %collective-permute-done.18 = f32[16,128,128]{2,1,0:T(8,128)S(1)} collective-permute-done((f32[16,128,128]{2,1,0:T(8,128)S(1)}, f32[16,128,128]{2,1,0:T(8,128)S(1)}, u32[]{:S(2)}, u32[]{:S(2)}) %collective-permute-start.18) | collective-permute-done | bytes 1048608 | tf_op jit(solution)/shard_map/ppermute | solution.py:70
  187.8 2.4 pad_maximum_fusion.1.b_ref
  190.2 26.2 %collective-permute-done.15 = f32[12,2,128,128]{3,2,1,0:T(8,128)S(1)} collective-permute-done((f32[12,2,128,128]{3,2,1,0:T(8,128)S(1)}, f32[12,2,128,128]{3,2,1,0:T(8,128)S(1)}, u32[]{:S(2)}, u32[]{:S(2)}) %collective-permute-start.15) | collective-permute-done | bytes 1572896 | tf_op jit(solution)/shard_map/ppermute | solution.py:27
  216.4 3.0 %pad_maximum_fusion.a_ref = f32[12,8,128,128]{3,2,1,0:T(8,128)} fusion(f32[12,2,128,128]{3,2,1,0:T(8,128)S(1)} %collective-permute-done.17, f32[12,2,128,128]{3,2,1,0:T(8,128)S(1)} %collective-permute-done.16, f32[12,2,128,128]{3,2,1,0:T(8,128)S(1)} %collective-permute-done.15, f32[12,2,128,128]{3,2,1,0:T(8,128)S(1)} %pad_maximum_fusion.2), kind=kLoop, calls=%fused_computation.2 | loop fusion | flops 4718592 | bytes 12582912 | tf_op jit(solution)/shard_map/concatenate | solution.py:28
  219.4 2.4 collective-permute-start.21
  221.9 0.4 select_reduce_fusion.1
  222.3 0.6 gather_fusion
  222.9 0.1 fusion.5
  223.1 0.1 copy.24
  223.1 0.7 reshape.328.pidx_ref
  223.8 0.1 copy.26
  224.0 0.4 select_reduce_fusion
  224.4 0.1 fusion
  224.5 0.1 copy.27
  224.6 0.8 convert_reduce_fusion
  225.5 0.1 copy.29
  225.6 0.6 reshape.329.sidx_ref
  226.3 0.7 reshape.330.pidx_ref
  227.0 0.7 reshape.331.sidx_ref
  227.7 16.0 %shard_map.73.rest_0_ = f32[12,4,128,128]{3,2,1,0:T(8,128)} custom-call(s32[96]{0:T(128)} %reshape.330.pidx_ref, s32[96]{0:T(128)} %reshape.331.sidx_ref, f32[12,8,128,128]{3,2,1,0:T(8,128)} %pad_maximum_fusion.a_ref, f32[64,128,128]{2,1,0:T(8,128)} %pad_maximum_fusion.1.b_ref), custom_call_target="tpu_custom_call" | custom-call | tf_op jit(solution)/shard_map/pallas_call | solution.py:147
  243.7 17.8 %shard_map.74 = f32[12,4,128,128]{3,2,1,0:T(8,128)} custom-call(s32[96]{0:T(128)} %reshape.328.pidx_ref, s32[96]{0:T(128)} %reshape.329.sidx_ref, f32[12,8,128,128]{3,2,1,0:T(8,128)} %collective-permute-done.21.a_ref, f32[64,128,128]{2,1,0:T(8,128)} %pad_maximum_fusion.1.b_ref, f32[12,4,128,128]{3,2,1,0:T(8,128)} %shard_map.73.rest_0_), custom_call_target="tpu_custom_call", output_to_operand_aliasing={{}: (4, {})} | custom-call | tf_op jit(solution)/shard_map/pallas_call | solution.py:147
  (45 shorter events, 0.7 us)
Async XLA Ops:
  0.0 126.1 %copy-start = (f32[12,1,128,128]{3,2,1,0:T(8,128)S(1)}, f32[12,1,128,128]{3,2,1,0:T(8,128)}, u32[]{:S(2)}) copy-start(f32[12,1,128,128]{3,2,1,0:T(8,128)} %param.7) | copy-start | bytes 2359300
  0.0 19.9 %collective-permute-start.1 = (f32[2,128,128]{2,1,0:T(8,128)}, f32[2,128,128]{2,1,0:T(8,128)S(1)}, u32[]{:S(2)}, u32[]{:S(2)}) collective-permute-start(f32[2,128,128]{2,1,0:T(8,128)} %bitcast.41), channel_id=1, source_target_pairs={{0,1},{1,2},{2,3},{3,4},{4,5},{5,6},{6,7},{8,9},{9,10},{10,11},{11... | collective-permute-start | bytes 393224 | tf_op jit(solution)/shard_map/ppermute | solution.py:57
  4.9 18.9 %collective-permute-start.8 = (f32[2,128,128]{2,1,0:T(8,128)}, f32[2,128,128]{2,1,0:T(8,128)S(1)}, u32[]{:S(2)}, u32[]{:S(2)}) collective-permute-start(f32[2,128,128]{2,1,0:T(8,128)} %bitcast.42), channel_id=1, source_target_pairs={{1,0},{2,1},{3,2},{4,3},{5,4},{6,5},{7,6},{9,8},{10,9},{11,10},{12... | collective-permute-start | bytes 393224 | tf_op jit(solution)/shard_map/ppermute | solution.py:58
  6.8 119.3 %collective-permute-start = (f32[12,1,128,128]{3,2,1,0:T(8,128)}, f32[12,1,128,128]{3,2,1,0:T(8,128)S(1)}, u32[]{:S(2)}, u32[]{:S(2)}) collective-permute-start(f32[12,1,128,128]{3,2,1,0:T(8,128)} %param.7), channel_id=1, source_target_pairs={{0,64},{32,96},{64,0},{96,32},{128,192},{160,224},{192,128},{224,1... | collective-permute-start | bytes 2359304 | tf_op jit(solution)/shard_map/ppermute | solution.py:21
  19.9 70.1 %collective-permute-start.2 = (f32[2,128,128]{2,1,0:T(8,128)S(1)}, f32[2,128,128]{2,1,0:T(8,128)S(1)}, u32[]{:S(2)}, u32[]{:S(2)}) collective-permute-start(f32[2,128,128]{2,1,0:T(8,128)S(1)} %collective-permute-done.1), channel_id=1, source_target_pairs={{0,1},{1,2},{2,3},{3,4},{4,5},{5,6},{6,7},{8,9},{9,10},{10,11},{11... | collective-permute-start | bytes 393224 | tf_op jit(solution)/shard_map/ppermute | solution.py:57
  23.8 70.5 %collective-permute-start.9 = (f32[2,128,128]{2,1,0:T(8,128)S(1)}, f32[2,128,128]{2,1,0:T(8,128)S(1)}, u32[]{:S(2)}, u32[]{:S(2)}) collective-permute-start(f32[2,128,128]{2,1,0:T(8,128)S(1)} %collective-permute-done.8), channel_id=1, source_target_pairs={{1,0},{2,1},{3,2},{4,3},{5,4},{6,5},{7,6},{9,8},{10,9},{11,10},{12... | collective-permute-start | bytes 393224 | tf_op jit(solution)/shard_map/ppermute | solution.py:58
  90.1 6.9 %collective-permute-start.3 = (f32[2,128,128]{2,1,0:T(8,128)S(1)}, f32[2,128,128]{2,1,0:T(8,128)S(1)}, u32[]{:S(2)}, u32[]{:S(2)}) collective-permute-start(f32[2,128,128]{2,1,0:T(8,128)S(1)} %collective-permute-done.2), channel_id=1, source_target_pairs={{0,1},{1,2},{2,3},{3,4},{4,5},{5,6},{6,7},{8,9},{9,10},{10,11},{11... | collective-permute-start | bytes 393224 | tf_op jit(solution)/shard_map/ppermute | solution.py:57
  94.3 7.7 %collective-permute-start.10 = (f32[2,128,128]{2,1,0:T(8,128)S(1)}, f32[2,128,128]{2,1,0:T(8,128)S(1)}, u32[]{:S(2)}, u32[]{:S(2)}) collective-permute-start(f32[2,128,128]{2,1,0:T(8,128)S(1)} %collective-permute-done.9), channel_id=1, source_target_pairs={{1,0},{2,1},{3,2},{4,3},{5,4},{6,5},{7,6},{9,8},{10,9},{11,10},{12... | collective-permute-start | bytes 393224 | tf_op jit(solution)/shard_map/ppermute | solution.py:58
  96.9 7.7 %collective-permute-start.4 = (f32[2,128,128]{2,1,0:T(8,128)S(1)}, f32[2,128,128]{2,1,0:T(8,128)S(1)}, u32[]{:S(2)}, u32[]{:S(2)}) collective-permute-start(f32[2,128,128]{2,1,0:T(8,128)S(1)} %collective-permute-done.3), channel_id=1, source_target_pairs={{0,1},{1,2},{2,3},{3,4},{4,5},{5,6},{6,7},{8,9},{9,10},{10,11},{11... | collective-permute-start | bytes 393224 | tf_op jit(solution)/shard_map/ppermute | solution.py:57
  102.0 7.2 %collective-permute-start.11 = (f32[2,128,128]{2,1,0:T(8,128)S(1)}, f32[2,128,128]{2,1,0:T(8,128)S(1)}, u32[]{:S(2)}, u32[]{:S(2)}) collective-permute-start(f32[2,128,128]{2,1,0:T(8,128)S(1)} %collective-permute-done.10), channel_id=1, source_target_pairs={{1,0},{2,1},{3,2},{4,3},{5,4},{6,5},{7,6},{9,8},{10,9},{11,10},{12... | collective-permute-start | bytes 393224 | tf_op jit(solution)/shard_map/ppermute | solution.py:58
  104.6 7.2 %collective-permute-start.5 = (f32[2,128,128]{2,1,0:T(8,128)S(1)}, f32[2,128,128]{2,1,0:T(8,128)S(1)}, u32[]{:S(2)}, u32[]{:S(2)}) collective-permute-start(f32[2,128,128]{2,1,0:T(8,128)S(1)} %collective-permute-done.4), channel_id=1, source_target_pairs={{0,1},{1,2},{2,3},{3,4},{4,5},{5,6},{6,7},{8,9},{9,10},{10,11},{11... | collective-permute-start | bytes 393224 | tf_op jit(solution)/shard_map/ppermute | solution.py:57
  109.2 7.2 %collective-permute-start.12 = (f32[2,128,128]{2,1,0:T(8,128)S(1)}, f32[2,128,128]{2,1,0:T(8,128)S(1)}, u32[]{:S(2)}, u32[]{:S(2)}) collective-permute-start(f32[2,128,128]{2,1,0:T(8,128)S(1)} %collective-permute-done.11), channel_id=1, source_target_pairs={{1,0},{2,1},{3,2},{4,3},{5,4},{6,5},{7,6},{9,8},{10,9},{11,10},{12... | collective-permute-start | bytes 393224 | tf_op jit(solution)/shard_map/ppermute | solution.py:58
  111.8 7.2 %collective-permute-start.6 = (f32[2,128,128]{2,1,0:T(8,128)S(1)}, f32[2,128,128]{2,1,0:T(8,128)S(1)}, u32[]{:S(2)}, u32[]{:S(2)}) collective-permute-start(f32[2,128,128]{2,1,0:T(8,128)S(1)} %collective-permute-done.5), channel_id=1, source_target_pairs={{0,1},{1,2},{2,3},{3,4},{4,5},{5,6},{6,7},{8,9},{9,10},{10,11},{11... | collective-permute-start | bytes 393224 | tf_op jit(solution)/shard_map/ppermute | solution.py:57
  116.4 7.2 %collective-permute-start.13 = (f32[2,128,128]{2,1,0:T(8,128)S(1)}, f32[2,128,128]{2,1,0:T(8,128)S(1)}, u32[]{:S(2)}, u32[]{:S(2)}) collective-permute-start(f32[2,128,128]{2,1,0:T(8,128)S(1)} %collective-permute-done.12), channel_id=1, source_target_pairs={{1,0},{2,1},{3,2},{4,3},{5,4},{6,5},{7,6},{9,8},{10,9},{11,10},{12... | collective-permute-start | bytes 393224 | tf_op jit(solution)/shard_map/ppermute | solution.py:58
  119.0 7.3 %collective-permute-start.7 = (f32[2,128,128]{2,1,0:T(8,128)S(1)}, f32[2,128,128]{2,1,0:T(8,128)S(1)}, u32[]{:S(2)}, u32[]{:S(2)}) collective-permute-start(f32[2,128,128]{2,1,0:T(8,128)S(1)} %collective-permute-done.6), channel_id=1, source_target_pairs={{0,1},{1,2},{2,3},{3,4},{4,5},{5,6},{6,7},{8,9},{9,10},{10,11},{11... | collective-permute-start | bytes 393224 | tf_op jit(solution)/shard_map/ppermute | solution.py:57
  123.5 7.4 %collective-permute-start.14 = (f32[2,128,128]{2,1,0:T(8,128)S(1)}, f32[2,128,128]{2,1,0:T(8,128)S(1)}, u32[]{:S(2)}, u32[]{:S(2)}) collective-permute-start(f32[2,128,128]{2,1,0:T(8,128)S(1)} %collective-permute-done.13), channel_id=1, source_target_pairs={{1,0},{2,1},{3,2},{4,3},{5,4},{6,5},{7,6},{9,8},{10,9},{11,10},{12... | collective-permute-start | bytes 393224 | tf_op jit(solution)/shard_map/ppermute | solution.py:58
  133.9 23.2 %collective-permute-start.20 = (f32[16,128,128]{2,1,0:T(8,128)S(1)}, f32[16,128,128]{2,1,0:T(8,128)S(1)}, u32[]{:S(2)}, u32[]{:S(2)}) collective-permute-start(f32[16,128,128]{2,1,0:T(8,128)S(1)} %bitcast_select_fusion), channel_id=1, source_target_pairs={{0,24},{1,25},{2,26},{3,27},{4,28},{5,29},{6,30},{7,31},{8,0},{9,1... | collective-permute-start | bytes 3145736 | tf_op jit(solution)/shard_map/ppermute | solution.py:70
  138.6 51.6 %collective-permute-start.17 = (f32[12,2,128,128]{3,2,1,0:T(8,128)S(1)}, f32[12,2,128,128]{3,2,1,0:T(8,128)S(1)}, u32[]{:S(2)}, u32[]{:S(2)}) collective-permute-start(f32[12,2,128,128]{3,2,1,0:T(8,128)S(1)} %pad_maximum_fusion.2), channel_id=1, source_target_pairs={{0,384},{32,416},{64,448},{96,480},{128,0},{160,32},{192,64},{224,... | collective-permute-start | bytes 4718600 | tf_op jit(solution)/shard_map/ppermute | solution.py:27
  143.0 47.2 %collective-permute-start.16 = (f32[12,2,128,128]{3,2,1,0:T(8,128)S(1)}, f32[12,2,128,128]{3,2,1,0:T(8,128)S(1)}, u32[]{:S(2)}, u32[]{:S(2)}) collective-permute-start(f32[12,2,128,128]{3,2,1,0:T(8,128)S(1)} %pad_maximum_fusion.2), channel_id=1, source_target_pairs={{0,256},{32,288},{64,320},{96,352},{128,384},{160,416},{192,448},{... | collective-permute-start | bytes 4718600 | tf_op jit(solution)/shard_map/ppermute | solution.py:27
  145.4 71.0 %collective-permute-start.15 = (f32[12,2,128,128]{3,2,1,0:T(8,128)S(1)}, f32[12,2,128,128]{3,2,1,0:T(8,128)S(1)}, u32[]{:S(2)}, u32[]{:S(2)}) collective-permute-start(f32[12,2,128,128]{3,2,1,0:T(8,128)S(1)} %pad_maximum_fusion.2), channel_id=1, source_target_pairs={{0,128},{32,160},{64,192},{96,224},{128,256},{160,288},{192,320},{... | collective-permute-start | bytes 4718600 | tf_op jit(solution)/shard_map/ppermute | solution.py:27
  147.9 22.1 %collective-permute-start.19 = (f32[16,128,128]{2,1,0:T(8,128)S(1)}, f32[16,128,128]{2,1,0:T(8,128)S(1)}, u32[]{:S(2)}, u32[]{:S(2)}) collective-permute-start(f32[16,128,128]{2,1,0:T(8,128)S(1)} %bitcast_select_fusion), channel_id=1, source_target_pairs={{0,16},{1,17},{2,18},{3,19},{4,20},{5,21},{6,22},{7,23},{8,24},{9,... | collective-permute-start | bytes 3145736 | tf_op jit(solution)/shard_map/ppermute | solution.py:70
  157.2 30.6 %collective-permute-start.18 = (f32[16,128,128]{2,1,0:T(8,128)S(1)}, f32[16,128,128]{2,1,0:T(8,128)S(1)}, u32[]{:S(2)}, u32[]{:S(2)}) collective-permute-start(f32[16,128,128]{2,1,0:T(8,128)S(1)} %bitcast_select_fusion), channel_id=1, source_target_pairs={{0,8},{1,9},{2,10},{3,11},{4,12},{5,13},{6,14},{7,15},{8,16},{9,17... | collective-permute-start | bytes 3145736 | tf_op jit(solution)/shard_map/ppermute | solution.py:70
  190.2 31.7 %copy-start.1 = (s32[12,16]{1,0:T(8,128)S(1)}, s32[12,16]{1,0:T(8,128)}, u32[]{:S(2)}) copy-start(s32[12,16]{1,0:T(8,128)} %param.8) | copy-start | bytes 2308
  190.2 31.7 %copy-start.3 = (s32[64]{0:T(128)S(1)}, s32[64]{0:T(128)}, u32[]{:S(2)}) copy-start(s32[64]{0:T(128)} %param.13) | copy-start | bytes 772
  190.2 33.6 %copy-start.2 = (s32[12,4]{0,1:T(4,128)S(1)}, s32[12,4]{0,1:T(4,128)}, u32[]{:S(2)}) copy-start(s32[12,4]{0,1:T(4,128)} %param.12) | copy-start | bytes 580
  190.2 33.8 %copy-start.4 = (s32[64,1]{0,1:T(1,128)S(1)}, s32[64,1]{0,1:T(1,128)}, u32[]{:S(2)}) copy-start(s32[64,1]{0,1:T(1,128)} %param.11) | copy-start | bytes 772
  190.2 34.1 %copy-start.5 = (s32[12]{0:T(128)S(1)}, s32[12]{0:T(128)}, u32[]{:S(2)}) copy-start(s32[12]{0:T(128)} %param.9) | copy-start | bytes 148
  219.4 24.3 %collective-permute-start.21 = (f32[12,8,128,128]{3,2,1,0:T(8,128)}, f32[12,8,128,128]{3,2,1,0:T(8,128)}, u32[]{:S(2)}, u32[]{:S(2)}) collective-permute-start(f32[12,8,128,128]{3,2,1,0:T(8,128)} %pad_maximum_fusion.a_ref), channel_id=1, source_target_pairs={{0,32},{32,0},{64,96},{96,64},{128,160},{160,128},{192,224},{224,1... | collective-permute-start | bytes 18874376 | tf_op jit(solution)/shard_map/ppermute | solution.py:32

commit v4 on v3

--- a/solution.py
+++ b/solution.py
@@ -78,15 +78,15 @@
     c = lax.axis_index("col")
     y = c // 8
     src = grid_pos // per_dev
-    return ((y - src // 8) % n_y) * (8 * per_dev) + (src % 8) * per_dev + grid_pos % per_dev
+    return (src % 8) * (n_y * per_dev) + ((y - src // 8) % n_y) * per_dev + grid_pos % per_dev
 
 
 def local(a_blocks, a_cols, a_lengths, b_blocks, b_cols, c_cols, order, n_row, n_col):
     per_dev = b_blocks.shape[0]
     swap_z, ring_x, swap_core = row_stages(n_row)
     line_z, ring_y = col_stages(n_col)
-    a_held, b_held = lax.optimization_barrier((swap_z(a_blocks), line_z(b_blocks[:, 0])))
-    a_held, panels = lax.optimization_barrier((ring_x(a_held), ring_y(b_held)))
+    a_held, b_held = lax.optimization_barrier((swap_z(a_blocks), ring_y(b_blocks[:, 0])))
+    a_held, panels = lax.optimization_barrier((ring_x(a_held), line_z(b_held)))
     rows_here, slot_all = a_cols.shape
     pattern_slots = c_cols.shape[1]
     block_size = panels.shape[-1]

time: 263 us -> 282 us (1.072)
  the two profiles are of different devices: /device:TPU:97 before, /device:TPU:203 now
where the time goes in v4:
time: 282 us; the launch traced here: 280 us
  waiting for transfers between devices  132 us (47%)
  starting transfers between devices  70.3 us (25%)
  Pallas kernels  33.5 us (12%)
  local copies, waits for them, and re-layouts  30.1 us (11%)
  other arithmetic  13.2 us (5%)
    ppermute x1, waiting for transfers between devices, swap_z(): return jnp.concatenate([chunk, lax.ppermute(chunk, 'row', pairs)], axis=1)  56.2 us
    ppermute x3, waiting for transfers between devices, ring_x(): parts.append(lax.ppermute(held, 'row', shift))  38.8 us
    pallas_call x2, Pallas kernels, row_products(): pl.pallas_call(product_kernel, grid_spec=grid_spec, out_shape=jax.ShapeDt...  33.5 us
    ppermute x7, waiting for transfers between devices, line_z(): going_right = lax.ppermute(going_right, 'col', right)  26.9 us
    ppermute x7, starting transfers between devices, line_z(): going_right = lax.ppermute(going_right, 'col', right)  21 us
    unnamed x29, local copies, waits for them, and re-layouts  19.3 us
    ppermute x7, starting transfers between devices, line_z(): going_left = lax.ppermute(going_left, 'col', left)  16.8 us
    ppermute x3, starting transfers between devices, ring_y(): parts.append(lax.ppermute(held, 'col', shift))  9.81 us
  transfers between devices with their start and end apart: 22, of which 12 were waited for; matrix products, arithmetic and copies ran while one was open for 11% of the time, Pallas kernels for 6%

profile of v4, /device:TPU:203, one launch (start us, length us, event | category | flops | bytes accessed | tf_op | source)
XLA Modules:
  0.0 280.0 jit_solution(14914272713970701894)
XLA Ops:
  0.0 8.8 %collective-permute-start = (f32[12,1,128,128]{3,2,1,0:T(8,128)}, f32[12,1,128,128]{3,2,1,0:T(8,128)S(1)}, u32[]{:S(2)}, u32[]{:S(2)}) collective-permute-start(f32[12,1,128,128]{3,2,1,0:T(8,128)} %param.7), channel_id=1, source_target_pairs={{0,64},{32,96},{64,0},{96,32},{128,192},{160,224},{192,128},{224,1... | collective-permute-start | bytes 2359304 | tf_op jit(solution)/shard_map/ppermute | solution.py:21
  8.8 3.2 %collective-permute-start.1 = (f32[2,128,128]{2,1,0:T(8,128)}, f32[2,128,128]{2,1,0:T(8,128)S(1)}, u32[]{:S(2)}, u32[]{:S(2)}) collective-permute-start(f32[2,128,128]{2,1,0:T(8,128)} %bitcast.41), channel_id=1, source_target_pairs={{0,8},{1,9},{2,10},{3,11},{4,12},{5,13},{6,14},{7,15},{8,16},{9,17... | collective-permute-start | bytes 393224 | tf_op jit(solution)/shard_map/ppermute | solution.py:70
  12.0 2.6 collective-permute-start.2
  14.7 4.0 %collective-permute-start.3 = (f32[2,128,128]{2,1,0:T(8,128)}, f32[2,128,128]{2,1,0:T(8,128)S(1)}, u32[]{:S(2)}, u32[]{:S(2)}) collective-permute-start(f32[2,128,128]{2,1,0:T(8,128)} %bitcast.43), channel_id=1, source_target_pairs={{0,24},{1,25},{2,26},{3,27},{4,28},{5,29},{6,30},{7,31},{8,0},{9,1... | collective-permute-start | bytes 393224 | tf_op jit(solution)/shard_map/ppermute | solution.py:70
  18.7 0.8 collective-permute-done.2
  19.5 3.6 %collective-permute-done.3 = f32[2,128,128]{2,1,0:T(8,128)S(1)} collective-permute-done((f32[2,128,128]{2,1,0:T(8,128)}, f32[2,128,128]{2,1,0:T(8,128)S(1)}, u32[]{:S(2)}, u32[]{:S(2)}) %collective-permute-start.3) | collective-permute-done | bytes 131104 | tf_op jit(solution)/shard_map/ppermute | solution.py:70
  23.1 0.9 pad_maximum_fusion.2
  24.0 56.2 %collective-permute-done = f32[12,1,128,128]{3,2,1,0:T(8,128)S(1)} collective-permute-done((f32[12,1,128,128]{3,2,1,0:T(8,128)}, f32[12,1,128,128]{3,2,1,0:T(8,128)S(1)}, u32[]{:S(2)}, u32[]{:S(2)}) %collective-permute-start) | collective-permute-done | bytes 786464 | tf_op jit(solution)/shard_map/ppermute | solution.py:21
  80.2 1.2 pad_maximum_fusion.1
  81.4 1.9 collective-permute-start.7
  83.4 3.4 %collective-permute-start.14 = (f32[8,128,128]{2,1,0:T(8,128)S(1)}, f32[8,128,128]{2,1,0:T(8,128)S(1)}, u32[]{:S(2)}, u32[]{:S(2)}) collective-permute-start(f32[8,128,128]{2,1,0:T(8,128)S(1)} %pad_maximum_fusion.2), channel_id=1, source_target_pairs={{1,0},{2,1},{3,2},{4,3},{5,4},{6,5},{7,6},{9,8},{10,9},{11,10},{12... | collective-permute-start | bytes 1572872 | tf_op jit(solution)/shard_map/ppermute | solution.py:58
  86.7 9.2 %collective-permute-done.7 = f32[8,128,128]{2,1,0:T(8,128)S(1)} collective-permute-done((f32[8,128,128]{2,1,0:T(8,128)S(1)}, f32[8,128,128]{2,1,0:T(8,128)S(1)}, u32[]{:S(2)}, u32[]{:S(2)}) %collective-permute-start.7) | collective-permute-done | bytes 524320 | tf_op jit(solution)/shard_map/ppermute | solution.py:57
  96.0 2.2 collective-permute-start.8
  98.2 3.0 %collective-permute-start.15 = (f32[8,128,128]{2,1,0:T(8,128)S(1)}, f32[8,128,128]{2,1,0:T(8,128)S(1)}, u32[]{:S(2)}, u32[]{:S(2)}) collective-permute-start(f32[8,128,128]{2,1,0:T(8,128)S(1)} %collective-permute-done.14), channel_id=1, source_target_pairs={{1,0},{2,1},{3,2},{4,3},{5,4},{6,5},{7,6},{9,8},{10,9},{11,10},{12... | collective-permute-start | bytes 1572872 | tf_op jit(solution)/shard_map/ppermute | solution.py:58
  101.3 8.3 %collective-permute-done.8 = f32[8,128,128]{2,1,0:T(8,128)S(1)} collective-permute-done((f32[8,128,128]{2,1,0:T(8,128)S(1)}, f32[8,128,128]{2,1,0:T(8,128)S(1)}, u32[]{:S(2)}, u32[]{:S(2)}) %collective-permute-start.8) | collective-permute-done | bytes 524320 | tf_op jit(solution)/shard_map/ppermute | solution.py:57
  109.6 2.5 collective-permute-start.9
  112.2 2.7 collective-permute-start.16
  114.9 3.1 %collective-permute-start.4 = (f32[12,2,128,128]{3,2,1,0:T(8,128)S(1)}, f32[12,2,128,128]{3,2,1,0:T(8,128)}, u32[]{:S(2)}, u32[]{:S(2)}) collective-permute-start(f32[12,2,128,128]{3,2,1,0:T(8,128)S(1)} %pad_maximum_fusion.1), channel_id=1, source_target_pairs={{0,128},{32,160},{64,192},{96,224},{128,256},{160,288},{192,320},{... | collective-permute-start | bytes 4718600 | tf_op jit(solution)/shard_map/ppermute | solution.py:27
  118.0 2.7 collective-permute-start.5
  120.8 3.8 %collective-permute-start.6 = (f32[12,2,128,128]{3,2,1,0:T(8,128)S(1)}, f32[12,2,128,128]{3,2,1,0:T(8,128)}, u32[]{:S(2)}, u32[]{:S(2)}) collective-permute-start(f32[12,2,128,128]{3,2,1,0:T(8,128)S(1)} %pad_maximum_fusion.1), channel_id=1, source_target_pairs={{0,384},{32,416},{64,448},{96,480},{128,0},{160,32},{192,64},{224,... | collective-permute-start | bytes 4718600 | tf_op jit(solution)/shard_map/ppermute | solution.py:27
  124.6 3.3 %collective-permute-start.10 = (f32[8,128,128]{2,1,0:T(8,128)}, f32[8,128,128]{2,1,0:T(8,128)}, u32[]{:S(2)}, u32[]{:S(2)}) collective-permute-start(f32[8,128,128]{2,1,0:T(8,128)} %collective-permute-done.9), channel_id=1, source_target_pairs={{0,1},{1,2},{2,3},{3,4},{4,5},{5,6},{6,7},{8,9},{9,10},{10,11},{11... | collective-permute-start | bytes 1572872 | tf_op jit(solution)/shard_map/ppermute | solution.py:57
  128.0 2.0 collective-permute-start.17
  129.9 6.3 %collective-permute-done.10 = f32[8,128,128]{2,1,0:T(8,128)} collective-permute-done((f32[8,128,128]{2,1,0:T(8,128)}, f32[8,128,128]{2,1,0:T(8,128)}, u32[]{:S(2)}, u32[]{:S(2)}) %collective-permute-start.10) | collective-permute-done | bytes 524320 | tf_op jit(solution)/shard_map/ppermute | solution.py:57
  136.2 3.6 %collective-permute-start.11 = (f32[8,128,128]{2,1,0:T(8,128)}, f32[8,128,128]{2,1,0:T(8,128)}, u32[]{:S(2)}, u32[]{:S(2)}) collective-permute-start(f32[8,128,128]{2,1,0:T(8,128)} %collective-permute-done.10), channel_id=1, source_target_pairs={{0,1},{1,2},{2,3},{3,4},{4,5},{5,6},{6,7},{8,9},{9,10},{10,11},{11... | collective-permute-start | bytes 1572872 | tf_op jit(solution)/shard_map/ppermute | solution.py:57
  140.0 0.9 bitcast_dynamic-update-slice_fusion.14
  140.9 1.9 collective-permute-start.18
  142.8 1.9 bitcast_dynamic-update-slice_fusion.13
  144.7 2.2 collective-permute-done.11
  146.9 4.0 %collective-permute-start.12 = (f32[8,128,128]{2,1,0:T(8,128)}, f32[8,128,128]{2,1,0:T(8,128)S(1)}, u32[]{:S(2)}, u32[]{:S(2)}) collective-permute-start(f32[8,128,128]{2,1,0:T(8,128)} %collective-permute-done.11), channel_id=1, source_target_pairs={{0,1},{1,2},{2,3},{3,4},{4,5},{5,6},{6,7},{8,9},{9,10},{10,11},{11... | collective-permute-start | bytes 1572872 | tf_op jit(solution)/shard_map/ppermute | solution.py:57
  150.9 1.9 bitcast_dynamic-update-slice_fusion.12
  152.8 1.3 collective-permute-done.5
  154.1 37.5 %collective-permute-done.6 = f32[12,2,128,128]{3,2,1,0:T(8,128)} collective-permute-done((f32[12,2,128,128]{3,2,1,0:T(8,128)S(1)}, f32[12,2,128,128]{3,2,1,0:T(8,128)}, u32[]{:S(2)}, u32[]{:S(2)}) %collective-permute-start.6) | collective-permute-done | bytes 1572896 | tf_op jit(solution)/shard_map/ppermute | solution.py:27
  191.6 4.6 %pad_maximum_fusion.a_ref = f32[12,8,128,128]{3,2,1,0:T(8,128)} fusion(f32[12,2,128,128]{3,2,1,0:T(8,128)} %collective-permute-done.6, f32[12,2,128,128]{3,2,1,0:T(8,128)} %collective-permute-done.5, f32[12,2,128,128]{3,2,1,0:T(8,128)} %collective-permute-done.4, f32[12,2,128,128]{3,2,1,0:T(8,128)S(1)} %pad_maximum_fusion.1), kind=kLoop, calls=%fused_computation.2 | loop fusion | flops 4718592 | bytes 12582912 | tf_op jit(solution)/shard_map/concatenate | solution.py:28
  196.2 1.9 collective-permute-start.19
  198.1 1.9 bitcast_dynamic-update-slice_fusion.11
  200.0 3.4 %collective-permute-start.13 = (f32[8,128,128]{2,1,0:T(8,128)S(1)}, f32[8,128,128]{2,1,0:T(8,128)S(1)}, u32[]{:S(2)}, u32[]{:S(2)}) collective-permute-start(f32[8,128,128]{2,1,0:T(8,128)S(1)} %collective-permute-done.12), channel_id=1, source_target_pairs={{0,1},{1,2},{2,3},{3,4},{4,5},{5,6},{6,7},{8,9},{9,10},{10,11},{11... | collective-permute-start | bytes 1572872 | tf_op jit(solution)/shard_map/ppermute | solution.py:57
  203.4 1.9 bitcast_dynamic-update-slice_fusion.10
  205.3 1.9 bitcast_dynamic-update-slice_fusion.9
  207.2 3.8 %collective-permute-done.19 = f32[8,128,128]{2,1,0:T(8,128)S(1)} collective-permute-done((f32[8,128,128]{2,1,0:T(8,128)S(1)}, f32[8,128,128]{2,1,0:T(8,128)S(1)}, u32[]{:S(2)}, u32[]{:S(2)}) %collective-permute-start.19) | collective-permute-done | bytes 524320 | tf_op jit(solution)/shard_map/ppermute | solution.py:58
  211.0 1.9 collective-permute-start.20
  213.0 0.8 bitcast_dynamic-update-slice_fusion.8
  213.8 0.8 collective-permute-done.13
  214.6 0.8 bitcast_dynamic-update-slice_fusion.7
  215.5 0.8 bitcast_dynamic-update-slice_fusion.6
  216.3 0.8 bitcast_dynamic-update-slice_fusion.5
  217.1 1.9 bitcast_dynamic-update-slice_fusion.4
  219.0 1.9 bitcast_dynamic-update-slice_fusion.3
  220.9 0.9 bitcast_dynamic-update-slice_fusion.2
  221.7 0.8 bitcast_dynamic-update-slice_fusion.1
  222.6 2.4 collective-permute-done.20
  225.0 0.8 bitcast_dynamic-update-slice_fusion
  225.9 6.1 %gather_fusion.1 = f32[8,8,128,128]{3,2,1,0:T(8,128)} fusion(f32[15,8,128,128]{3,2,1,0:T(8,128)} %bitcast_dynamic-update-slice_fusion, s32[1024]{0:T(1024)S(1)} %pad_clamp_fusion), kind=kCustom, calls=%fused_computation.1 | custom fusion | bytes 8388640 | tf_op jit(solution)/shard_map/jit(_take)/gather | solution.py:64
  231.9 4.6 %bitcast_select_fusion.b_ref = f32[64,128,128]{2,1,0:T(8,128)} fusion(f32[8,8,128,128]{3,2,1,0:T(8,128)} %gather_fusion.1, pred[64]{0:T(512)(128)(4,1)S(1)} %broadcast_in_dim.53), kind=kLoop, calls=%fused_computation.3 | loop fusion | flops 1048576 | bytes 8388672 | tf_op jit(solution)/shard_map/jit(_take)/select_n | solution.py:64
  236.5 4.2 %collective-permute-start.21 = (f32[12,8,128,128]{3,2,1,0:T(8,128)}, f32[12,8,128,128]{3,2,1,0:T(8,128)}, u32[]{:S(2)}, u32[]{:S(2)}) collective-permute-start(f32[12,8,128,128]{3,2,1,0:T(8,128)} %pad_maximum_fusion.a_ref), channel_id=1, source_target_pairs={{0,32},{32,0},{64,96},{96,64},{128,160},{160,128},{192,224},{224,1... | collective-permute-start | bytes 18874376 | tf_op jit(solution)/shard_map/ppermute | solution.py:32
  240.7 0.4 select_reduce_fusion.1
  241.2 0.6 gather_fusion
  242.1 0.4 select_reduce_fusion
  242.5 0.8 convert_reduce_fusion
  243.7 0.6 reshape.331.sidx_ref
  244.4 0.7 reshape.330.pidx_ref
  245.1 0.7 reshape.329.sidx_ref
  245.9 0.6 reshape.328.pidx_ref
  246.5 15.9 %shard_map.73.rest_0_ = f32[12,4,128,128]{3,2,1,0:T(8,128)} custom-call(s32[96]{0:T(128)} %reshape.330.pidx_ref, s32[96]{0:T(128)} %reshape.331.sidx_ref, f32[12,8,128,128]{3,2,1,0:T(8,128)} %pad_maximum_fusion.a_ref, f32[64,128,128]{2,1,0:T(8,128)} %bitcast_select_fusion.b_ref), custom_call_target="tpu_custom_call" | custom-call | tf_op jit(solution)/shard_map/pallas_call | solution.py:147
  262.4 17.6 %shard_map.74 = f32[12,4,128,128]{3,2,1,0:T(8,128)} custom-call(s32[96]{0:T(128)} %reshape.328.pidx_ref, s32[96]{0:T(128)} %reshape.329.sidx_ref, f32[12,8,128,128]{3,2,1,0:T(8,128)} %collective-permute-done.21.a_ref, f32[64,128,128]{2,1,0:T(8,128)} %bitcast_select_fusion.b_ref, f32[12,4,128,128]{3,2,1,0:T(8,128)} %shard_map.73.rest_0_), custom_call_target="tpu_custom_call", output_to_operand_aliasing={{}: (4, {})} | custom-call | tf_op jit(solution)/shard_map/pallas_call | solution.py:147
  (47 shorter events, 1.4 us)
Async XLA Ops:
  0.0 80.2 %collective-permute-start = (f32[12,1,128,128]{3,2,1,0:T(8,128)}, f32[12,1,128,128]{3,2,1,0:T(8,128)S(1)}, u32[]{:S(2)}, u32[]{:S(2)}) collective-permute-start(f32[12,1,128,128]{3,2,1,0:T(8,128)} %param.7), channel_id=1, source_target_pairs={{0,64},{32,96},{64,0},{96,32},{128,192},{160,224},{192,128},{224,1... | collective-permute-start | bytes 2359304 | tf_op jit(solution)/shard_map/ppermute | solution.py:21
  8.8 9.8 %collective-permute-start.1 = (f32[2,128,128]{2,1,0:T(8,128)}, f32[2,128,128]{2,1,0:T(8,128)S(1)}, u32[]{:S(2)}, u32[]{:S(2)}) collective-permute-start(f32[2,128,128]{2,1,0:T(8,128)} %bitcast.41), channel_id=1, source_target_pairs={{0,8},{1,9},{2,10},{3,11},{4,12},{5,13},{6,14},{7,15},{8,16},{9,17... | collective-permute-start | bytes 393224 | tf_op jit(solution)/shard_map/ppermute | solution.py:70
  12.0 7.5 %collective-permute-start.2 = (f32[2,128,128]{2,1,0:T(8,128)}, f32[2,128,128]{2,1,0:T(8,128)S(1)}, u32[]{:S(2)}, u32[]{:S(2)}) collective-permute-start(f32[2,128,128]{2,1,0:T(8,128)} %bitcast.42), channel_id=1, source_target_pairs={{0,16},{1,17},{2,18},{3,19},{4,20},{5,21},{6,22},{7,23},{8,24},{9,... | collective-permute-start | bytes 393224 | tf_op jit(solution)/shard_map/ppermute | solution.py:70
  14.7 8.4 %collective-permute-start.3 = (f32[2,128,128]{2,1,0:T(8,128)}, f32[2,128,128]{2,1,0:T(8,128)S(1)}, u32[]{:S(2)}, u32[]{:S(2)}) collective-permute-start(f32[2,128,128]{2,1,0:T(8,128)} %bitcast.43), channel_id=1, source_target_pairs={{0,24},{1,25},{2,26},{3,27},{4,28},{5,29},{6,30},{7,31},{8,0},{9,1... | collective-permute-start | bytes 393224 | tf_op jit(solution)/shard_map/ppermute | solution.py:70
  81.4 14.5 %collective-permute-start.7 = (f32[8,128,128]{2,1,0:T(8,128)S(1)}, f32[8,128,128]{2,1,0:T(8,128)S(1)}, u32[]{:S(2)}, u32[]{:S(2)}) collective-permute-start(f32[8,128,128]{2,1,0:T(8,128)S(1)} %pad_maximum_fusion.2), channel_id=1, source_target_pairs={{0,1},{1,2},{2,3},{3,4},{4,5},{5,6},{6,7},{8,9},{9,10},{10,11},{11... | collective-permute-start | bytes 1572872 | tf_op jit(solution)/shard_map/ppermute | solution.py:57
  83.4 14.9 %collective-permute-start.14 = (f32[8,128,128]{2,1,0:T(8,128)S(1)}, f32[8,128,128]{2,1,0:T(8,128)S(1)}, u32[]{:S(2)}, u32[]{:S(2)}) collective-permute-start(f32[8,128,128]{2,1,0:T(8,128)S(1)} %pad_maximum_fusion.2), channel_id=1, source_target_pairs={{1,0},{2,1},{3,2},{4,3},{5,4},{6,5},{7,6},{9,8},{10,9},{11,10},{12... | collective-permute-start | bytes 1572872 | tf_op jit(solution)/shard_map/ppermute | solution.py:58
  96.0 22.1 %copy-start = (f32[8,128,128]{2,1,0:T(8,128)}, f32[8,128,128]{2,1,0:T(8,128)S(1)}, u32[]{:S(2)}) copy-start(f32[8,128,128]{2,1,0:T(8,128)S(1)} %collective-permute-done.7) | copy-start | bytes 1572868
  96.0 13.6 %collective-permute-start.8 = (f32[8,128,128]{2,1,0:T(8,128)S(1)}, f32[8,128,128]{2,1,0:T(8,128)S(1)}, u32[]{:S(2)}, u32[]{:S(2)}) collective-permute-start(f32[8,128,128]{2,1,0:T(8,128)S(1)} %collective-permute-done.7), channel_id=1, source_target_pairs={{0,1},{1,2},{2,3},{3,4},{4,5},{5,6},{6,7},{8,9},{9,10},{10,11},{11... | collective-permute-start | bytes 1572872 | tf_op jit(solution)/shard_map/ppermute | solution.py:57
  98.2 13.9 %collective-permute-start.15 = (f32[8,128,128]{2,1,0:T(8,128)S(1)}, f32[8,128,128]{2,1,0:T(8,128)S(1)}, u32[]{:S(2)}, u32[]{:S(2)}) collective-permute-start(f32[8,128,128]{2,1,0:T(8,128)S(1)} %collective-permute-done.14), channel_id=1, source_target_pairs={{1,0},{2,1},{3,2},{4,3},{5,4},{6,5},{7,6},{9,8},{10,9},{11,10},{12... | collective-permute-start | bytes 1572872 | tf_op jit(solution)/shard_map/ppermute | solution.py:58
  109.6 11.2 %copy-start.1 = (f32[8,128,128]{2,1,0:T(8,128)}, f32[8,128,128]{2,1,0:T(8,128)S(1)}, u32[]{:S(2)}) copy-start(f32[8,128,128]{2,1,0:T(8,128)S(1)} %collective-permute-done.8) | copy-start | bytes 1572868
  109.6 15.0 %collective-permute-start.9 = (f32[8,128,128]{2,1,0:T(8,128)S(1)}, f32[8,128,128]{2,1,0:T(8,128)}, u32[]{:S(2)}, u32[]{:S(2)}) collective-permute-start(f32[8,128,128]{2,1,0:T(8,128)S(1)} %collective-permute-done.8), channel_id=1, source_target_pairs={{0,1},{1,2},{2,3},{3,4},{4,5},{5,6},{6,7},{8,9},{9,10},{10,11},{11... | collective-permute-start | bytes 1572872 | tf_op jit(solution)/shard_map/ppermute | solution.py:57
  112.2 15.8 %collective-permute-start.16 = (f32[8,128,128]{2,1,0:T(8,128)S(1)}, f32[8,128,128]{2,1,0:T(8,128)}, u32[]{:S(2)}, u32[]{:S(2)}) collective-permute-start(f32[8,128,128]{2,1,0:T(8,128)S(1)} %collective-permute-done.15), channel_id=1, source_target_pairs={{1,0},{2,1},{3,2},{4,3},{5,4},{6,5},{7,6},{9,8},{10,9},{11,10},{12... | collective-permute-start | bytes 1572872 | tf_op jit(solution)/shard_map/ppermute | solution.py:58
  114.9 37.9 %collective-permute-start.4 = (f32[12,2,128,128]{3,2,1,0:T(8,128)S(1)}, f32[12,2,128,128]{3,2,1,0:T(8,128)}, u32[]{:S(2)}, u32[]{:S(2)}) collective-permute-start(f32[12,2,128,128]{3,2,1,0:T(8,128)S(1)} %pad_maximum_fusion.1), channel_id=1, source_target_pairs={{0,128},{32,160},{64,192},{96,224},{128,256},{160,288},{192,320},{... | collective-permute-start | bytes 4718600 | tf_op jit(solution)/shard_map/ppermute | solution.py:27
  118.0 36.0 %collective-permute-start.5 = (f32[12,2,128,128]{3,2,1,0:T(8,128)S(1)}, f32[12,2,128,128]{3,2,1,0:T(8,128)}, u32[]{:S(2)}, u32[]{:S(2)}) collective-permute-start(f32[12,2,128,128]{3,2,1,0:T(8,128)S(1)} %pad_maximum_fusion.1), channel_id=1, source_target_pairs={{0,256},{32,288},{64,320},{96,352},{128,384},{160,416},{192,448},{... | collective-permute-start | bytes 4718600 | tf_op jit(solution)/shard_map/ppermute | solution.py:27
  120.8 70.8 %collective-permute-start.6 = (f32[12,2,128,128]{3,2,1,0:T(8,128)S(1)}, f32[12,2,128,128]{3,2,1,0:T(8,128)}, u32[]{:S(2)}, u32[]{:S(2)}) collective-permute-start(f32[12,2,128,128]{3,2,1,0:T(8,128)S(1)} %pad_maximum_fusion.1), channel_id=1, source_target_pairs={{0,384},{32,416},{64,448},{96,480},{128,0},{160,32},{192,64},{224,... | collective-permute-start | bytes 4718600 | tf_op jit(solution)/shard_map/ppermute | solution.py:27
  124.6 11.6 %collective-permute-start.10 = (f32[8,128,128]{2,1,0:T(8,128)}, f32[8,128,128]{2,1,0:T(8,128)}, u32[]{:S(2)}, u32[]{:S(2)}) collective-permute-start(f32[8,128,128]{2,1,0:T(8,128)} %collective-permute-done.9), channel_id=1, source_target_pairs={{0,1},{1,2},{2,3},{3,4},{4,5},{5,6},{6,7},{8,9},{9,10},{10,11},{11... | collective-permute-start | bytes 1572872 | tf_op jit(solution)/shard_map/ppermute | solution.py:57
  128.0 12.9 %collective-permute-start.17 = (f32[8,128,128]{2,1,0:T(8,128)}, f32[8,128,128]{2,1,0:T(8,128)}, u32[]{:S(2)}, u32[]{:S(2)}) collective-permute-start(f32[8,128,128]{2,1,0:T(8,128)} %collective-permute-done.16), channel_id=1, source_target_pairs={{1,0},{2,1},{3,2},{4,3},{5,4},{6,5},{7,6},{9,8},{10,9},{11,10},{12... | collective-permute-start | bytes 1572872 | tf_op jit(solution)/shard_map/ppermute | solution.py:58
  136.2 10.7 %collective-permute-start.11 = (f32[8,128,128]{2,1,0:T(8,128)}, f32[8,128,128]{2,1,0:T(8,128)}, u32[]{:S(2)}, u32[]{:S(2)}) collective-permute-start(f32[8,128,128]{2,1,0:T(8,128)} %collective-permute-done.10), channel_id=1, source_target_pairs={{0,1},{1,2},{2,3},{3,4},{4,5},{5,6},{6,7},{8,9},{9,10},{10,11},{11... | collective-permute-start | bytes 1572872 | tf_op jit(solution)/shard_map/ppermute | solution.py:57
  140.9 55.3 %collective-permute-start.18 = (f32[8,128,128]{2,1,0:T(8,128)}, f32[8,128,128]{2,1,0:T(8,128)S(1)}, u32[]{:S(2)}, u32[]{:S(2)}) collective-permute-start(f32[8,128,128]{2,1,0:T(8,128)} %collective-permute-done.17), channel_id=1, source_target_pairs={{1,0},{2,1},{3,2},{4,3},{5,4},{6,5},{7,6},{9,8},{10,9},{11,10},{12... | collective-permute-start | bytes 1572872 | tf_op jit(solution)/shard_map/ppermute | solution.py:58
  146.9 53.1 %collective-permute-start.12 = (f32[8,128,128]{2,1,0:T(8,128)}, f32[8,128,128]{2,1,0:T(8,128)S(1)}, u32[]{:S(2)}, u32[]{:S(2)}) collective-permute-start(f32[8,128,128]{2,1,0:T(8,128)} %collective-permute-done.11), channel_id=1, source_target_pairs={{0,1},{1,2},{2,3},{3,4},{4,5},{5,6},{6,7},{8,9},{9,10},{10,11},{11... | collective-permute-start | bytes 1572872 | tf_op jit(solution)/shard_map/ppermute | solution.py:57
  196.2 14.9 %collective-permute-start.19 = (f32[8,128,128]{2,1,0:T(8,128)S(1)}, f32[8,128,128]{2,1,0:T(8,128)S(1)}, u32[]{:S(2)}, u32[]{:S(2)}) collective-permute-start(f32[8,128,128]{2,1,0:T(8,128)S(1)} %collective-permute-done.18), channel_id=1, source_target_pairs={{1,0},{2,1},{3,2},{4,3},{5,4},{6,5},{7,6},{9,8},{10,9},{11,10},{12... | collective-permute-start | bytes 1572872 | tf_op jit(solution)/shard_map/ppermute | solution.py:58
  200.0 14.6 %collective-permute-start.13 = (f32[8,128,128]{2,1,0:T(8,128)S(1)}, f32[8,128,128]{2,1,0:T(8,128)S(1)}, u32[]{:S(2)}, u32[]{:S(2)}) collective-permute-start(f32[8,128,128]{2,1,0:T(8,128)S(1)} %collective-permute-done.12), channel_id=1, source_target_pairs={{0,1},{1,2},{2,3},{3,4},{4,5},{5,6},{6,7},{8,9},{9,10},{10,11},{11... | collective-permute-start | bytes 1572872 | tf_op jit(solution)/shard_map/ppermute | solution.py:57
  211.0 14.0 %collective-permute-start.20 = (f32[8,128,128]{2,1,0:T(8,128)S(1)}, f32[8,128,128]{2,1,0:T(8,128)S(1)}, u32[]{:S(2)}, u32[]{:S(2)}) collective-permute-start(f32[8,128,128]{2,1,0:T(8,128)S(1)} %collective-permute-done.19), channel_id=1, source_target_pairs={{1,0},{2,1},{3,2},{4,3},{5,4},{6,5},{7,6},{9,8},{10,9},{11,10},{12... | collective-permute-start | bytes 1572872 | tf_op jit(solution)/shard_map/ppermute | solution.py:58
  225.9 14.9 %copy-start.2 = (s32[12,16]{1,0:T(8,128)S(1)}, s32[12,16]{1,0:T(8,128)}, u32[]{:S(2)}) copy-start(s32[12,16]{1,0:T(8,128)} %param.8) | copy-start | bytes 2308
  225.9 14.9 %copy-start.4 = (s32[64]{0:T(128)S(1)}, s32[64]{0:T(128)}, u32[]{:S(2)}) copy-start(s32[64]{0:T(128)} %param.13) | copy-start | bytes 772
  225.9 16.1 %copy-start.3 = (s32[12,4]{0,1:T(4,128)S(1)}, s32[12,4]{0,1:T(4,128)}, u32[]{:S(2)}) copy-start(s32[12,4]{0,1:T(4,128)} %param.12) | copy-start | bytes 580
  225.9 16.2 %copy-start.5 = (s32[64,1]{0,1:T(1,128)S(1)}, s32[64,1]{0,1:T(1,128)}, u32[]{:S(2)}) copy-start(s32[64,1]{0,1:T(1,128)} %param.11) | copy-start | bytes 772
  225.9 16.6 %copy-start.6 = (s32[12]{0:T(128)S(1)}, s32[12]{0:T(128)}, u32[]{:S(2)}) copy-start(s32[12]{0:T(128)} %param.9) | copy-start | bytes 148
  236.5 25.9 %collective-permute-start.21 = (f32[12,8,128,128]{3,2,1,0:T(8,128)}, f32[12,8,128,128]{3,2,1,0:T(8,128)}, u32[]{:S(2)}, u32[]{:S(2)}) collective-permute-start(f32[12,8,128,128]{3,2,1,0:T(8,128)} %pad_maximum_fusion.a_ref), channel_id=1, source_target_pairs={{0,32},{32,0},{64,96},{96,64},{128,160},{160,128},{192,224},{224,1... | collective-permute-start | bytes 18874376 | tf_op jit(solution)/shard_map/ppermute | solution.py:32

commit v5 on v3

--- a/solution.py
+++ b/solution.py
@@ -107,6 +107,16 @@
                         target[:, half:].reshape(-1), pattern_slots, mine)
 
 
+def split_dot(a, b):
+    a_hi = a.astype(jnp.bfloat16)
+    a_lo = (a - a_hi.astype(jnp.float32)).astype(jnp.bfloat16)
+    b_hi = b.astype(jnp.bfloat16)
+    b_lo = (b - b_hi.astype(jnp.float32)).astype(jnp.bfloat16)
+    out = jnp.dot(a_hi, b_lo, preferred_element_type=jnp.float32)
+    out = out + jnp.dot(a_lo, b_hi, preferred_element_type=jnp.float32)
+    return out + jnp.dot(a_hi, b_hi, preferred_element_type=jnp.float32)
+
+
 def product_kernel(pidx_ref, sidx_ref, a_ref, b_ref, *rest):
     i = pl.program_id(0)
     n_slots = a_ref.shape[1]
@@ -122,8 +132,7 @@
         @pl.when(s >= 0)
         def _():
             p = pidx_ref[i * n_slots + j]
-            prod = jnp.dot(a_ref[0, j], b_ref[p], precision=lax.Precision.HIGHEST,
-                           preferred_element_type=jnp.float32)
+            prod = split_dot(a_ref[0, j], b_ref[p])
             o_ref[0, s] += prod
 
         return carry

time: 263 us -> 259 us (0.985)
  the two profiles are of different devices: /device:TPU:97 before, /device:TPU:113 now
where the time goes in v5:
time: 259 us; the launch traced here: 257 us
  waiting for transfers between devices  119 us (46%)
  starting transfers between devices  80.5 us (31%)
  Pallas kernels  32.2 us (12%)
  local copies, waits for them, and re-layouts  17.2 us (7%)
  other arithmetic  7.54 us (3%)
    ppermute x7, waiting for transfers between devices, line_z(): going_right = lax.ppermute(going_right, 'col', right)  63.7 us
    ppermute x3, waiting for transfers between devices, ring_y(): parts.append(lax.ppermute(held, 'col', shift))  38.5 us
    pallas_call x2, Pallas kernels, row_products(): pl.pallas_call(product_kernel, grid_spec=grid_spec, out_shape=jax.ShapeDt...  32.2 us
    ppermute x7, starting transfers between devices, line_z(): going_right = lax.ppermute(going_right, 'col', right)  31.7 us
    ppermute x3, waiting for transfers between devices, ring_x(): parts.append(lax.ppermute(held, 'row', shift))  17.3 us
    ppermute x7, starting transfers between devices, line_z(): going_left = lax.ppermute(going_left, 'col', left)  13.4 us
    ppermute x3, starting transfers between devices, ring_y(): parts.append(lax.ppermute(held, 'col', shift))  12.3 us
    ppermute x1, starting transfers between devices, swap_z(): return jnp.concatenate([chunk, lax.ppermute(chunk, 'row', pairs)], axis=1)  11.4 us
  transfers between devices with their start and end apart: 22, of which 5 were waited for; matrix products, arithmetic and copies ran while one was open for 7% of the time, Pallas kernels for 6%

profile of v5, /device:TPU:113, one launch (start us, length us, event | category | flops | bytes accessed | tf_op | source)
XLA Modules:
  0.0 257.3 jit_solution(6707306060318679188)
XLA Ops:
  0.0 4.9 %collective-permute-start.1 = (f32[2,128,128]{2,1,0:T(8,128)}, f32[2,128,128]{2,1,0:T(8,128)S(1)}, u32[]{:S(2)}, u32[]{:S(2)}) collective-permute-start(f32[2,128,128]{2,1,0:T(8,128)} %bitcast.41), channel_id=1, source_target_pairs={{0,1},{1,2},{2,3},{3,4},{4,5},{5,6},{6,7},{8,9},{9,10},{10,11},{11... | collective-permute-start | bytes 393224 | tf_op jit(solution)/shard_map/ppermute | solution.py:57
  4.9 1.9 collective-permute-start.8
  6.8 11.4 %collective-permute-start = (f32[12,1,128,128]{3,2,1,0:T(8,128)}, f32[12,1,128,128]{3,2,1,0:T(8,128)S(1)}, u32[]{:S(2)}, u32[]{:S(2)}) collective-permute-start(f32[12,1,128,128]{3,2,1,0:T(8,128)} %param.7), channel_id=1, source_target_pairs={{0,64},{32,96},{64,0},{96,32},{128,192},{160,224},{192,128},{224,1... | collective-permute-start | bytes 2359304 | tf_op jit(solution)/shard_map/ppermute | solution.py:21
  18.2 1.6 bitcast_dynamic-update-slice_fusion.14
  19.8 0.1 broadcast_in_dim.53
  19.9 3.9 %collective-permute-start.2 = (f32[2,128,128]{2,1,0:T(8,128)S(1)}, f32[2,128,128]{2,1,0:T(8,128)S(1)}, u32[]{:S(2)}, u32[]{:S(2)}) collective-permute-start(f32[2,128,128]{2,1,0:T(8,128)S(1)} %collective-permute-done.1), channel_id=1, source_target_pairs={{0,1},{1,2},{2,3},{3,4},{4,5},{5,6},{6,7},{8,9},{9,10},{10,11},{11... | collective-permute-start | bytes 393224 | tf_op jit(solution)/shard_map/ppermute | solution.py:57
  23.8 1.9 collective-permute-start.9
  25.8 0.7 bitcast_dynamic-update-slice_fusion.13
  26.4 63.6 %collective-permute-done.2 = f32[2,128,128]{2,1,0:T(8,128)S(1)} collective-permute-done((f32[2,128,128]{2,1,0:T(8,128)S(1)}, f32[2,128,128]{2,1,0:T(8,128)S(1)}, u32[]{:S(2)}, u32[]{:S(2)}) %collective-permute-start.2) | collective-permute-done | bytes 131104 | tf_op jit(solution)/shard_map/ppermute | solution.py:57
  90.1 4.3 %collective-permute-start.3 = (f32[2,128,128]{2,1,0:T(8,128)S(1)}, f32[2,128,128]{2,1,0:T(8,128)S(1)}, u32[]{:S(2)}, u32[]{:S(2)}) collective-permute-start(f32[2,128,128]{2,1,0:T(8,128)S(1)} %collective-permute-done.2), channel_id=1, source_target_pairs={{0,1},{1,2},{2,3},{3,4},{4,5},{5,6},{6,7},{8,9},{9,10},{10,11},{11... | collective-permute-start | bytes 393224 | tf_op jit(solution)/shard_map/ppermute | solution.py:57
  94.3 1.9 collective-permute-start.10
  96.3 0.7 bitcast_dynamic-update-slice_fusion.12
  96.9 5.0 %collective-permute-start.4 = (f32[2,128,128]{2,1,0:T(8,128)S(1)}, f32[2,128,128]{2,1,0:T(8,128)S(1)}, u32[]{:S(2)}, u32[]{:S(2)}) collective-permute-start(f32[2,128,128]{2,1,0:T(8,128)S(1)} %collective-permute-done.3), channel_id=1, source_target_pairs={{0,1},{1,2},{2,3},{3,4},{4,5},{5,6},{6,7},{8,9},{9,10},{10,11},{11... | collective-permute-start | bytes 393224 | tf_op jit(solution)/shard_map/ppermute | solution.py:57
  102.0 1.9 collective-permute-start.11
  103.9 0.7 bitcast_dynamic-update-slice_fusion.11
  104.6 4.6 %collective-permute-start.5 = (f32[2,128,128]{2,1,0:T(8,128)S(1)}, f32[2,128,128]{2,1,0:T(8,128)S(1)}, u32[]{:S(2)}, u32[]{:S(2)}) collective-permute-start(f32[2,128,128]{2,1,0:T(8,128)S(1)} %collective-permute-done.4), channel_id=1, source_target_pairs={{0,1},{1,2},{2,3},{3,4},{4,5},{5,6},{6,7},{8,9},{9,10},{10,11},{11... | collective-permute-start | bytes 393224 | tf_op jit(solution)/shard_map/ppermute | solution.py:57
  109.2 1.9 collective-permute-start.12
  111.1 0.7 bitcast_dynamic-update-slice_fusion.10
  111.8 4.6 %collective-permute-start.6 = (f32[2,128,128]{2,1,0:T(8,128)S(1)}, f32[2,128,128]{2,1,0:T(8,128)S(1)}, u32[]{:S(2)}, u32[]{:S(2)}) collective-permute-start(f32[2,128,128]{2,1,0:T(8,128)S(1)} %collective-permute-done.5), channel_id=1, source_target_pairs={{0,1},{1,2},{2,3},{3,4},{4,5},{5,6},{6,7},{8,9},{9,10},{10,11},{11... | collective-permute-start | bytes 393224 | tf_op jit(solution)/shard_map/ppermute | solution.py:57
  116.4 1.9 collective-permute-start.13
  118.3 0.7 bitcast_dynamic-update-slice_fusion.9
  119.0 4.6 %collective-permute-start.7 = (f32[2,128,128]{2,1,0:T(8,128)S(1)}, f32[2,128,128]{2,1,0:T(8,128)S(1)}, u32[]{:S(2)}, u32[]{:S(2)}) collective-permute-start(f32[2,128,128]{2,1,0:T(8,128)S(1)} %collective-permute-done.6), channel_id=1, source_target_pairs={{0,1},{1,2},{2,3},{3,4},{4,5},{5,6},{6,7},{8,9},{9,10},{10,11},{11... | collective-permute-start | bytes 393224 | tf_op jit(solution)/shard_map/ppermute | solution.py:57
  123.5 1.9 collective-permute-start.14
  125.5 0.7 bitcast_dynamic-update-slice_fusion.8
  126.1 0.1 pad_maximum_fusion.2
  126.3 0.7 bitcast_dynamic-update-slice_fusion.7
  127.0 0.7 bitcast_dynamic-update-slice_fusion.6
  127.6 0.7 bitcast_dynamic-update-slice_fusion.5
  128.3 0.7 bitcast_dynamic-update-slice_fusion.4
  129.0 0.7 bitcast_dynamic-update-slice_fusion.3
  129.6 0.7 bitcast_dynamic-update-slice_fusion.2
  130.3 0.7 bitcast_dynamic-update-slice_fusion.1
  131.0 0.7 bitcast_dynamic-update-slice_fusion
  131.6 2.2 gather_fusion.1
  133.8 0.1 bitcast_select_fusion
  133.9 2.1 collective-permute-start.20
  136.0 4.4 %collective-permute-start.17 = (f32[12,2,128,128]{3,2,1,0:T(8,128)S(1)}, f32[12,2,128,128]{3,2,1,0:T(8,128)S(1)}, u32[]{:S(2)}, u32[]{:S(2)}) collective-permute-start(f32[12,2,128,128]{3,2,1,0:T(8,128)S(1)} %pad_maximum_fusion.2), channel_id=1, source_target_pairs={{0,384},{32,416},{64,448},{96,480},{128,0},{160,32},{192,64},{224,... | collective-permute-start | bytes 4718600 | tf_op jit(solution)/shard_map/ppermute | solution.py:27
  140.4 2.4 collective-permute-start.16
  142.9 2.5 collective-permute-start.15
  145.4 4.5 %collective-permute-start.19 = (f32[16,128,128]{2,1,0:T(8,128)S(1)}, f32[16,128,128]{2,1,0:T(8,128)S(1)}, u32[]{:S(2)}, u32[]{:S(2)}) collective-permute-start(f32[16,128,128]{2,1,0:T(8,128)S(1)} %bitcast_select_fusion), channel_id=1, source_target_pairs={{0,16},{1,17},{2,18},{3,19},{4,20},{5,21},{6,22},{7,23},{8,24},{9,... | collective-permute-start | bytes 3145736 | tf_op jit(solution)/shard_map/ppermute | solution.py:70
  149.9 5.7 %collective-permute-done.20 = f32[16,128,128]{2,1,0:T(8,128)S(1)} collective-permute-done((f32[16,128,128]{2,1,0:T(8,128)S(1)}, f32[16,128,128]{2,1,0:T(8,128)S(1)}, u32[]{:S(2)}, u32[]{:S(2)}) %collective-permute-start.20) | collective-permute-done | bytes 1048608 | tf_op jit(solution)/shard_map/ppermute | solution.py:70
  155.6 5.7 %collective-permute-start.18 = (f32[16,128,128]{2,1,0:T(8,128)S(1)}, f32[16,128,128]{2,1,0:T(8,128)S(1)}, u32[]{:S(2)}, u32[]{:S(2)}) collective-permute-start(f32[16,128,128]{2,1,0:T(8,128)S(1)} %bitcast_select_fusion), channel_id=1, source_target_pairs={{0,8},{1,9},{2,10},{3,11},{4,12},{5,13},{6,14},{7,15},{8,16},{9,17... | collective-permute-start | bytes 3145736 | tf_op jit(solution)/shard_map/ppermute | solution.py:70
  161.2 6.2 %collective-permute-done.19 = f32[16,128,128]{2,1,0:T(8,128)S(1)} collective-permute-done((f32[16,128,128]{2,1,0:T(8,128)S(1)}, f32[16,128,128]{2,1,0:T(8,128)S(1)}, u32[]{:S(2)}, u32[]{:S(2)}) %collective-permute-start.19) | collective-permute-done | bytes 1048608 | tf_op jit(solution)/shard_map/ppermute | solution.py:70
  167.4 26.7 %collective-permute-done.18 = f32[16,128,128]{2,1,0:T(8,128)S(1)} collective-permute-done((f32[16,128,128]{2,1,0:T(8,128)S(1)}, f32[16,128,128]{2,1,0:T(8,128)S(1)}, u32[]{:S(2)}, u32[]{:S(2)}) %collective-permute-start.18) | collective-permute-done | bytes 1048608 | tf_op jit(solution)/shard_map/ppermute | solution.py:70
  194.1 2.4 pad_maximum_fusion.1.b_ref
  196.6 17.3 %collective-permute-done.15 = f32[12,2,128,128]{3,2,1,0:T(8,128)S(1)} collective-permute-done((f32[12,2,128,128]{3,2,1,0:T(8,128)S(1)}, f32[12,2,128,128]{3,2,1,0:T(8,128)S(1)}, u32[]{:S(2)}, u32[]{:S(2)}) %collective-permute-start.15) | collective-permute-done | bytes 1572896 | tf_op jit(solution)/shard_map/ppermute | solution.py:27
  213.8 3.0 %pad_maximum_fusion.a_ref = f32[12,8,128,128]{3,2,1,0:T(8,128)} fusion(f32[12,2,128,128]{3,2,1,0:T(8,128)S(1)} %collective-permute-done.17, f32[12,2,128,128]{3,2,1,0:T(8,128)S(1)} %collective-permute-done.16, f32[12,2,128,128]{3,2,1,0:T(8,128)S(1)} %collective-permute-done.15, f32[12,2,128,128]{3,2,1,0:T(8,128)S(1)} %pad_maximum_fusion.2), kind=kLoop, calls=%fused_computation.2 | loop fusion | flops 4718592 | bytes 12582912 | tf_op jit(solution)/shard_map/concatenate | solution.py:28
  216.8 2.4 collective-permute-start.21
  219.3 0.4 select_reduce_fusion.1
  219.8 0.6 gather_fusion
  220.4 0.1 fusion.5
  220.5 0.1 copy.24
  220.6 0.7 reshape.328.pidx_ref
  221.2 0.1 copy.26
  221.4 0.4 select_reduce_fusion
  221.8 0.1 fusion
  222.0 0.1 copy.27
  222.1 0.8 convert_reduce_fusion
  222.9 0.1 copy.29
  223.0 0.6 reshape.329.sidx_ref
  223.7 0.7 reshape.330.pidx_ref
  224.4 0.7 reshape.331.sidx_ref
  225.1 15.7 %shard_map.73.rest_0_ = f32[12,4,128,128]{3,2,1,0:T(8,128)} custom-call(s32[96]{0:T(128)} %reshape.330.pidx_ref, s32[96]{0:T(128)} %reshape.331.sidx_ref, f32[12,8,128,128]{3,2,1,0:T(8,128)} %pad_maximum_fusion.a_ref, f32[64,128,128]{2,1,0:T(8,128)} %pad_maximum_fusion.1.b_ref), custom_call_target="tpu_custom_call" | custom-call | tf_op jit(solution)/shard_map/pallas_call | solution.py:156
  240.8 16.5 %shard_map.74 = f32[12,4,128,128]{3,2,1,0:T(8,128)} custom-call(s32[96]{0:T(128)} %reshape.328.pidx_ref, s32[96]{0:T(128)} %reshape.329.sidx_ref, f32[12,8,128,128]{3,2,1,0:T(8,128)} %collective-permute-done.21.a_ref, f32[64,128,128]{2,1,0:T(8,128)} %pad_maximum_fusion.1.b_ref, f32[12,4,128,128]{3,2,1,0:T(8,128)} %shard_map.73.rest_0_), custom_call_target="tpu_custom_call", output_to_operand_aliasing={{}: (4, {})} | custom-call | tf_op jit(solution)/shard_map/pallas_call | solution.py:156
  (45 shorter events, 0.7 us)
Async XLA Ops:
  0.0 126.1 %copy-start = (f32[12,1,128,128]{3,2,1,0:T(8,128)S(1)}, f32[12,1,128,128]{3,2,1,0:T(8,128)}, u32[]{:S(2)}) copy-start(f32[12,1,128,128]{3,2,1,0:T(8,128)} %param.7) | copy-start | bytes 2359300
  0.0 19.9 %collective-permute-start.1 = (f32[2,128,128]{2,1,0:T(8,128)}, f32[2,128,128]{2,1,0:T(8,128)S(1)}, u32[]{:S(2)}, u32[]{:S(2)}) collective-permute-start(f32[2,128,128]{2,1,0:T(8,128)} %bitcast.41), channel_id=1, source_target_pairs={{0,1},{1,2},{2,3},{3,4},{4,5},{5,6},{6,7},{8,9},{9,10},{10,11},{11... | collective-permute-start | bytes 393224 | tf_op jit(solution)/shard_map/ppermute | solution.py:57
  4.9 18.9 %collective-permute-start.8 = (f32[2,128,128]{2,1,0:T(8,128)}, f32[2,128,128]{2,1,0:T(8,128)S(1)}, u32[]{:S(2)}, u32[]{:S(2)}) collective-permute-start(f32[2,128,128]{2,1,0:T(8,128)} %bitcast.42), channel_id=1, source_target_pairs={{1,0},{2,1},{3,2},{4,3},{5,4},{6,5},{7,6},{9,8},{10,9},{11,10},{12... | collective-permute-start | bytes 393224 | tf_op jit(solution)/shard_map/ppermute | solution.py:58
  6.8 119.3 %collective-permute-start = (f32[12,1,128,128]{3,2,1,0:T(8,128)}, f32[12,1,128,128]{3,2,1,0:T(8,128)S(1)}, u32[]{:S(2)}, u32[]{:S(2)}) collective-permute-start(f32[12,1,128,128]{3,2,1,0:T(8,128)} %param.7), channel_id=1, source_target_pairs={{0,64},{32,96},{64,0},{96,32},{128,192},{160,224},{192,128},{224,1... | collective-permute-start | bytes 2359304 | tf_op jit(solution)/shard_map/ppermute | solution.py:21
  19.9 70.1 %collective-permute-start.2 = (f32[2,128,128]{2,1,0:T(8,128)S(1)}, f32[2,128,128]{2,1,0:T(8,128)S(1)}, u32[]{:S(2)}, u32[]{:S(2)}) collective-permute-start(f32[2,128,128]{2,1,0:T(8,128)S(1)} %collective-permute-done.1), channel_id=1, source_target_pairs={{0,1},{1,2},{2,3},{3,4},{4,5},{5,6},{6,7},{8,9},{9,10},{10,11},{11... | collective-permute-start | bytes 393224 | tf_op jit(solution)/shard_map/ppermute | solution.py:57
  23.8 70.5 %collective-permute-start.9 = (f32[2,128,128]{2,1,0:T(8,128)S(1)}, f32[2,128,128]{2,1,0:T(8,128)S(1)}, u32[]{:S(2)}, u32[]{:S(2)}) collective-permute-start(f32[2,128,128]{2,1,0:T(8,128)S(1)} %collective-permute-done.8), channel_id=1, source_target_pairs={{1,0},{2,1},{3,2},{4,3},{5,4},{6,5},{7,6},{9,8},{10,9},{11,10},{12... | collective-permute-start | bytes 393224 | tf_op jit(solution)/shard_map/ppermute | solution.py:58
  90.1 6.9 %collective-permute-start.3 = (f32[2,128,128]{2,1,0:T(8,128)S(1)}, f32[2,128,128]{2,1,0:T(8,128)S(1)}, u32[]{:S(2)}, u32[]{:S(2)}) collective-permute-start(f32[2,128,128]{2,1,0:T(8,128)S(1)} %collective-permute-done.2), channel_id=1, source_target_pairs={{0,1},{1,2},{2,3},{3,4},{4,5},{5,6},{6,7},{8,9},{9,10},{10,11},{11... | collective-permute-start | bytes 393224 | tf_op jit(solution)/shard_map/ppermute | solution.py:57
  94.3 7.7 %collective-permute-start.10 = (f32[2,128,128]{2,1,0:T(8,128)S(1)}, f32[2,128,128]{2,1,0:T(8,128)S(1)}, u32[]{:S(2)}, u32[]{:S(2)}) collective-permute-start(f32[2,128,128]{2,1,0:T(8,128)S(1)} %collective-permute-done.9), channel_id=1, source_target_pairs={{1,0},{2,1},{3,2},{4,3},{5,4},{6,5},{7,6},{9,8},{10,9},{11,10},{12... | collective-permute-start | bytes 393224 | tf_op jit(solution)/shard_map/ppermute | solution.py:58
  96.9 7.7 %collective-permute-start.4 = (f32[2,128,128]{2,1,0:T(8,128)S(1)}, f32[2,128,128]{2,1,0:T(8,128)S(1)}, u32[]{:S(2)}, u32[]{:S(2)}) collective-permute-start(f32[2,128,128]{2,1,0:T(8,128)S(1)} %collective-permute-done.3), channel_id=1, source_target_pairs={{0,1},{1,2},{2,3},{3,4},{4,5},{5,6},{6,7},{8,9},{9,10},{10,11},{11... | collective-permute-start | bytes 393224 | tf_op jit(solution)/shard_map/ppermute | solution.py:57
  102.0 7.2 %collective-permute-start.11 = (f32[2,128,128]{2,1,0:T(8,128)S(1)}, f32[2,128,128]{2,1,0:T(8,128)S(1)}, u32[]{:S(2)}, u32[]{:S(2)}) collective-permute-start(f32[2,128,128]{2,1,0:T(8,128)S(1)} %collective-permute-done.10), channel_id=1, source_target_pairs={{1,0},{2,1},{3,2},{4,3},{5,4},{6,5},{7,6},{9,8},{10,9},{11,10},{12... | collective-permute-start | bytes 393224 | tf_op jit(solution)/shard_map/ppermute | solution.py:58
  104.6 7.2 %collective-permute-start.5 = (f32[2,128,128]{2,1,0:T(8,128)S(1)}, f32[2,128,128]{2,1,0:T(8,128)S(1)}, u32[]{:S(2)}, u32[]{:S(2)}) collective-permute-start(f32[2,128,128]{2,1,0:T(8,128)S(1)} %collective-permute-done.4), channel_id=1, source_target_pairs={{0,1},{1,2},{2,3},{3,4},{4,5},{5,6},{6,7},{8,9},{9,10},{10,11},{11... | collective-permute-start | bytes 393224 | tf_op jit(solution)/shard_map/ppermute | solution.py:57
  109.2 7.2 %collective-permute-start.12 = (f32[2,128,128]{2,1,0:T(8,128)S(1)}, f32[2,128,128]{2,1,0:T(8,128)S(1)}, u32[]{:S(2)}, u32[]{:S(2)}) collective-permute-start(f32[2,128,128]{2,1,0:T(8,128)S(1)} %collective-permute-done.11), channel_id=1, source_target_pairs={{1,0},{2,1},{3,2},{4,3},{5,4},{6,5},{7,6},{9,8},{10,9},{11,10},{12... | collective-permute-start | bytes 393224 | tf_op jit(solution)/shard_map/ppermute | solution.py:58
  111.8 7.2 %collective-permute-start.6 = (f32[2,128,128]{2,1,0:T(8,128)S(1)}, f32[2,128,128]{2,1,0:T(8,128)S(1)}, u32[]{:S(2)}, u32[]{:S(2)}) collective-permute-start(f32[2,128,128]{2,1,0:T(8,128)S(1)} %collective-permute-done.5), channel_id=1, source_target_pairs={{0,1},{1,2},{2,3},{3,4},{4,5},{5,6},{6,7},{8,9},{9,10},{10,11},{11... | collective-permute-start | bytes 393224 | tf_op jit(solution)/shard_map/ppermute | solution.py:57
  116.4 7.2 %collective-permute-start.13 = (f32[2,128,128]{2,1,0:T(8,128)S(1)}, f32[2,128,128]{2,1,0:T(8,128)S(1)}, u32[]{:S(2)}, u32[]{:S(2)}) collective-permute-start(f32[2,128,128]{2,1,0:T(8,128)S(1)} %collective-permute-done.12), channel_id=1, source_target_pairs={{1,0},{2,1},{3,2},{4,3},{5,4},{6,5},{7,6},{9,8},{10,9},{11,10},{12... | collective-permute-start | bytes 393224 | tf_op jit(solution)/shard_map/ppermute | solution.py:58
  119.0 7.3 %collective-permute-start.7 = (f32[2,128,128]{2,1,0:T(8,128)S(1)}, f32[2,128,128]{2,1,0:T(8,128)S(1)}, u32[]{:S(2)}, u32[]{:S(2)}) collective-permute-start(f32[2,128,128]{2,1,0:T(8,128)S(1)} %collective-permute-done.6), channel_id=1, source_target_pairs={{0,1},{1,2},{2,3},{3,4},{4,5},{5,6},{6,7},{8,9},{9,10},{10,11},{11... | collective-permute-start | bytes 393224 | tf_op jit(solution)/shard_map/ppermute | solution.py:57
  123.5 7.4 %collective-permute-start.14 = (f32[2,128,128]{2,1,0:T(8,128)S(1)}, f32[2,128,128]{2,1,0:T(8,128)S(1)}, u32[]{:S(2)}, u32[]{:S(2)}) collective-permute-start(f32[2,128,128]{2,1,0:T(8,128)S(1)} %collective-permute-done.13), channel_id=1, source_target_pairs={{1,0},{2,1},{3,2},{4,3},{5,4},{6,5},{7,6},{9,8},{10,9},{11,10},{12... | collective-permute-start | bytes 393224 | tf_op jit(solution)/shard_map/ppermute | solution.py:58
  133.9 21.6 %collective-permute-start.20 = (f32[16,128,128]{2,1,0:T(8,128)S(1)}, f32[16,128,128]{2,1,0:T(8,128)S(1)}, u32[]{:S(2)}, u32[]{:S(2)}) collective-permute-start(f32[16,128,128]{2,1,0:T(8,128)S(1)} %bitcast_select_fusion), channel_id=1, source_target_pairs={{0,24},{1,25},{2,26},{3,27},{4,28},{5,29},{6,30},{7,31},{8,0},{9,1... | collective-permute-start | bytes 3145736 | tf_op jit(solution)/shard_map/ppermute | solution.py:70
  136.0 60.5 %collective-permute-start.17 = (f32[12,2,128,128]{3,2,1,0:T(8,128)S(1)}, f32[12,2,128,128]{3,2,1,0:T(8,128)S(1)}, u32[]{:S(2)}, u32[]{:S(2)}) collective-permute-start(f32[12,2,128,128]{3,2,1,0:T(8,128)S(1)} %pad_maximum_fusion.2), channel_id=1, source_target_pairs={{0,384},{32,416},{64,448},{96,480},{128,0},{160,32},{192,64},{224,... | collective-permute-start | bytes 4718600 | tf_op jit(solution)/shard_map/ppermute | solution.py:27
  140.4 56.1 %collective-permute-start.16 = (f32[12,2,128,128]{3,2,1,0:T(8,128)S(1)}, f32[12,2,128,128]{3,2,1,0:T(8,128)S(1)}, u32[]{:S(2)}, u32[]{:S(2)}) collective-permute-start(f32[12,2,128,128]{3,2,1,0:T(8,128)S(1)} %pad_maximum_fusion.2), channel_id=1, source_target_pairs={{0,256},{32,288},{64,320},{96,352},{128,384},{160,416},{192,448},{... | collective-permute-start | bytes 4718600 | tf_op jit(solution)/shard_map/ppermute | solution.py:27
  142.9 71.0 %collective-permute-start.15 = (f32[12,2,128,128]{3,2,1,0:T(8,128)S(1)}, f32[12,2,128,128]{3,2,1,0:T(8,128)S(1)}, u32[]{:S(2)}, u32[]{:S(2)}) collective-permute-start(f32[12,2,128,128]{3,2,1,0:T(8,128)S(1)} %pad_maximum_fusion.2), channel_id=1, source_target_pairs={{0,128},{32,160},{64,192},{96,224},{128,256},{160,288},{192,320},{... | collective-permute-start | bytes 4718600 | tf_op jit(solution)/shard_map/ppermute | solution.py:27
  145.4 22.1 %collective-permute-start.19 = (f32[16,128,128]{2,1,0:T(8,128)S(1)}, f32[16,128,128]{2,1,0:T(8,128)S(1)}, u32[]{:S(2)}, u32[]{:S(2)}) collective-permute-start(f32[16,128,128]{2,1,0:T(8,128)S(1)} %bitcast_select_fusion), channel_id=1, source_target_pairs={{0,16},{1,17},{2,18},{3,19},{4,20},{5,21},{6,22},{7,23},{8,24},{9,... | collective-permute-start | bytes 3145736 | tf_op jit(solution)/shard_map/ppermute | solution.py:70
  155.6 38.5 %collective-permute-start.18 = (f32[16,128,128]{2,1,0:T(8,128)S(1)}, f32[16,128,128]{2,1,0:T(8,128)S(1)}, u32[]{:S(2)}, u32[]{:S(2)}) collective-permute-start(f32[16,128,128]{2,1,0:T(8,128)S(1)} %bitcast_select_fusion), channel_id=1, source_target_pairs={{0,8},{1,9},{2,10},{3,11},{4,12},{5,13},{6,14},{7,15},{8,16},{9,17... | collective-permute-start | bytes 3145736 | tf_op jit(solution)/shard_map/ppermute | solution.py:70
  196.5 22.8 %copy-start.1 = (s32[12,16]{1,0:T(8,128)S(1)}, s32[12,16]{1,0:T(8,128)}, u32[]{:S(2)}) copy-start(s32[12,16]{1,0:T(8,128)} %param.8) | copy-start | bytes 2308
  196.5 22.8 %copy-start.3 = (s32[64]{0:T(128)S(1)}, s32[64]{0:T(128)}, u32[]{:S(2)}) copy-start(s32[64]{0:T(128)} %param.13) | copy-start | bytes 772
  196.5 24.7 %copy-start.2 = (s32[12,4]{0,1:T(4,128)S(1)}, s32[12,4]{0,1:T(4,128)}, u32[]{:S(2)}) copy-start(s32[12,4]{0,1:T(4,128)} %param.12) | copy-start | bytes 580
  196.5 24.9 %copy-start.4 = (s32[64,1]{0,1:T(1,128)S(1)}, s32[64,1]{0,1:T(1,128)}, u32[]{:S(2)}) copy-start(s32[64,1]{0,1:T(1,128)} %param.11) | copy-start | bytes 772
  196.5 25.2 %copy-start.5 = (s32[12]{0:T(128)S(1)}, s32[12]{0:T(128)}, u32[]{:S(2)}) copy-start(s32[12]{0:T(128)} %param.9) | copy-start | bytes 148
  216.8 24.0 %collective-permute-start.21 = (f32[12,8,128,128]{3,2,1,0:T(8,128)}, f32[12,8,128,128]{3,2,1,0:T(8,128)}, u32[]{:S(2)}, u32[]{:S(2)}) collective-permute-start(f32[12,8,128,128]{3,2,1,0:T(8,128)} %pad_maximum_fusion.a_ref), channel_id=1, source_target_pairs={{0,32},{32,0},{64,96},{96,64},{128,160},{160,128},{192,224},{224,1... | collective-permute-start | bytes 18874376 | tf_op jit(solution)/shard_map/ppermute | solution.py:32

commit v6 on v5

--- a/solution.py
+++ b/solution.py
@@ -85,7 +85,8 @@
     per_dev = b_blocks.shape[0]
     swap_z, ring_x, swap_core = row_stages(n_row)
     line_z, ring_y = col_stages(n_col)
-    a_held, b_held = lax.optimization_barrier((swap_z(a_blocks), line_z(b_blocks[:, 0])))
+    a_held, b_held = lax.optimization_barrier((a_blocks, line_z(b_blocks[:, 0])))
+    a_held, b_held = lax.optimization_barrier((swap_z(a_held), b_held))
     a_held, panels = lax.optimization_barrier((ring_x(a_held), ring_y(b_held)))
     rows_here, slot_all = a_cols.shape
     pattern_slots = c_cols.shape[1]

time: 259 us -> 263 us (1.015)
  the two profiles are of different devices: /device:TPU:113 before, /device:TPU:105 now
where the time goes in v6:
time: 263 us; the launch traced here: 261 us
  waiting for transfers between devices  127 us (48%)
  starting transfers between devices  77.4 us (29%)
  Pallas kernels  31.7 us (12%)
  local copies, waits for them, and re-layouts  17.2 us (7%)
  other arithmetic  7.53 us (3%)
    ppermute x1, waiting for transfers between devices, swap_z(): return jnp.concatenate([chunk, lax.ppermute(chunk, 'row', pairs)], axis=1)  68.4 us
    ppermute x3, waiting for transfers between devices, ring_y(): parts.append(lax.ppermute(held, 'col', shift))  54 us
    ppermute x7, starting transfers between devices, line_z(): going_right = lax.ppermute(going_right, 'col', right)  32.1 us
    pallas_call x2, Pallas kernels, row_products(): pl.pallas_call(product_kernel, grid_spec=grid_spec, out_shape=jax.ShapeDt...  31.7 us
    ppermute x7, starting transfers between devices, line_z(): going_left = lax.ppermute(going_left, 'col', left)  13.4 us
    ppermute x1, starting transfers between devices, swap_z(): return jnp.concatenate([chunk, lax.ppermute(chunk, 'row', pairs)], axis=1)  10.6 us
    unnamed x27, local copies, waits for them, and re-layouts  10.3 us
    ppermute x3, starting transfers between devices, ring_y(): parts.append(lax.ppermute(held, 'col', shift))  9.49 us
  transfers between devices with their start and end apart: 22, of which 5 were waited for; matrix products, arithmetic and copies ran while one was open for 7% of the time, Pallas kernels for 6%

profile of v6, /device:TPU:105, one launch (start us, length us, event | category | flops | bytes accessed | tf_op | source)
XLA Modules:
  0.0 261.4 jit_solution(6677226587004829665)
XLA Ops:
  0.0 4.7 %collective-permute-start = (f32[2,128,128]{2,1,0:T(8,128)}, f32[2,128,128]{2,1,0:T(8,128)S(1)}, u32[]{:S(2)}, u32[]{:S(2)}) collective-permute-start(f32[2,128,128]{2,1,0:T(8,128)} %bitcast.41), channel_id=1, source_target_pairs={{0,1},{1,2},{2,3},{3,4},{4,5},{5,6},{6,7},{8,9},{9,10},{10,11},{11... | collective-permute-start | bytes 393224 | tf_op jit(solution)/shard_map/ppermute | solution.py:57
  4.8 1.9 collective-permute-start.7
  6.7 1.6 bitcast_dynamic-update-slice_fusion.14
  8.4 0.1 broadcast_in_dim.53
  8.5 4.6 %collective-permute-start.1 = (f32[2,128,128]{2,1,0:T(8,128)S(1)}, f32[2,128,128]{2,1,0:T(8,128)S(1)}, u32[]{:S(2)}, u32[]{:S(2)}) collective-permute-start(f32[2,128,128]{2,1,0:T(8,128)S(1)} %collective-permute-done), channel_id=1, source_target_pairs={{0,1},{1,2},{2,3},{3,4},{4,5},{5,6},{6,7},{8,9},{9,10},{10,11},{11... | collective-permute-start | bytes 393224 | tf_op jit(solution)/shard_map/ppermute | solution.py:57
  13.1 1.9 collective-permute-start.8
  15.0 0.7 bitcast_dynamic-update-slice_fusion.13
  15.7 4.6 %collective-permute-start.2 = (f32[2,128,128]{2,1,0:T(8,128)S(1)}, f32[2,128,128]{2,1,0:T(8,128)S(1)}, u32[]{:S(2)}, u32[]{:S(2)}) collective-permute-start(f32[2,128,128]{2,1,0:T(8,128)S(1)} %collective-permute-done.1), channel_id=1, source_target_pairs={{0,1},{1,2},{2,3},{3,4},{4,5},{5,6},{6,7},{8,9},{9,10},{10,11},{11... | collective-permute-start | bytes 393224 | tf_op jit(solution)/shard_map/ppermute | solution.py:57
  20.2 1.9 collective-permute-start.9
  22.2 0.7 bitcast_dynamic-update-slice_fusion.12
  22.8 4.6 %collective-permute-start.3 = (f32[2,128,128]{2,1,0:T(8,128)S(1)}, f32[2,128,128]{2,1,0:T(8,128)S(1)}, u32[]{:S(2)}, u32[]{:S(2)}) collective-permute-start(f32[2,128,128]{2,1,0:T(8,128)S(1)} %collective-permute-done.2), channel_id=1, source_target_pairs={{0,1},{1,2},{2,3},{3,4},{4,5},{5,6},{6,7},{8,9},{9,10},{10,11},{11... | collective-permute-start | bytes 393224 | tf_op jit(solution)/shard_map/ppermute | solution.py:57
  27.4 1.9 collective-permute-start.10
  29.3 0.7 bitcast_dynamic-update-slice_fusion.11
  30.0 4.6 %collective-permute-start.4 = (f32[2,128,128]{2,1,0:T(8,128)S(1)}, f32[2,128,128]{2,1,0:T(8,128)S(1)}, u32[]{:S(2)}, u32[]{:S(2)}) collective-permute-start(f32[2,128,128]{2,1,0:T(8,128)S(1)} %collective-permute-done.3), channel_id=1, source_target_pairs={{0,1},{1,2},{2,3},{3,4},{4,5},{5,6},{6,7},{8,9},{9,10},{10,11},{11... | collective-permute-start | bytes 393224 | tf_op jit(solution)/shard_map/ppermute | solution.py:57
  34.6 1.9 collective-permute-start.11
  36.5 0.7 bitcast_dynamic-update-slice_fusion.10
  37.2 4.6 %collective-permute-start.5 = (f32[2,128,128]{2,1,0:T(8,128)S(1)}, f32[2,128,128]{2,1,0:T(8,128)S(1)}, u32[]{:S(2)}, u32[]{:S(2)}) collective-permute-start(f32[2,128,128]{2,1,0:T(8,128)S(1)} %collective-permute-done.4), channel_id=1, source_target_pairs={{0,1},{1,2},{2,3},{3,4},{4,5},{5,6},{6,7},{8,9},{9,10},{10,11},{11... | collective-permute-start | bytes 393224 | tf_op jit(solution)/shard_map/ppermute | solution.py:57
  41.8 1.9 collective-permute-start.12
  43.7 0.7 bitcast_dynamic-update-slice_fusion.9
  44.4 4.6 %collective-permute-start.6 = (f32[2,128,128]{2,1,0:T(8,128)S(1)}, f32[2,128,128]{2,1,0:T(8,128)S(1)}, u32[]{:S(2)}, u32[]{:S(2)}) collective-permute-start(f32[2,128,128]{2,1,0:T(8,128)S(1)} %collective-permute-done.5), channel_id=1, source_target_pairs={{0,1},{1,2},{2,3},{3,4},{4,5},{5,6},{6,7},{8,9},{9,10},{10,11},{11... | collective-permute-start | bytes 393224 | tf_op jit(solution)/shard_map/ppermute | solution.py:57
  49.0 1.9 collective-permute-start.13
  50.9 0.7 bitcast_dynamic-update-slice_fusion.8
  51.6 0.7 bitcast_dynamic-update-slice_fusion.7
  52.2 0.7 bitcast_dynamic-update-slice_fusion.6
  52.9 0.7 bitcast_dynamic-update-slice_fusion.5
  53.5 0.7 bitcast_dynamic-update-slice_fusion.4
  54.2 0.7 bitcast_dynamic-update-slice_fusion.3
  54.9 0.7 bitcast_dynamic-update-slice_fusion.2
  55.5 0.7 bitcast_dynamic-update-slice_fusion.1
  56.2 0.7 bitcast_dynamic-update-slice_fusion
  56.9 2.2 gather_fusion.1
  59.1 0.1 bitcast_select_fusion
  59.3 10.6 %collective-permute-start.14 = (f32[12,1,128,128]{3,2,1,0:T(8,128)S(1)}, f32[12,1,128,128]{3,2,1,0:T(8,128)S(1)}, u32[]{:S(2)}, u32[]{:S(2)}) collective-permute-start(f32[12,1,128,128]{3,2,1,0:T(8,128)S(1)} %copy-done), channel_id=1, source_target_pairs={{0,64},{32,96},{64,0},{96,32},{128,192},{160,224},{192,128},{224,1... | collective-permute-start | bytes 2359304 | tf_op jit(solution)/shard_map/ppermute | solution.py:21
  69.9 68.4 %collective-permute-done.14 = f32[12,1,128,128]{3,2,1,0:T(8,128)S(1)} collective-permute-done((f32[12,1,128,128]{3,2,1,0:T(8,128)S(1)}, f32[12,1,128,128]{3,2,1,0:T(8,128)S(1)}, u32[]{:S(2)}, u32[]{:S(2)}) %collective-permute-start.14) | collective-permute-done | bytes 786464 | tf_op jit(solution)/shard_map/ppermute | solution.py:21
  138.3 0.1 pad_maximum_fusion.2
  138.5 2.1 collective-permute-start.20
  140.6 4.4 %collective-permute-start.17 = (f32[12,2,128,128]{3,2,1,0:T(8,128)S(1)}, f32[12,2,128,128]{3,2,1,0:T(8,128)S(1)}, u32[]{:S(2)}, u32[]{:S(2)}) collective-permute-start(f32[12,2,128,128]{3,2,1,0:T(8,128)S(1)} %pad_maximum_fusion.2), channel_id=1, source_target_pairs={{0,384},{32,416},{64,448},{96,480},{128,0},{160,32},{192,64},{224,... | collective-permute-start | bytes 4718600 | tf_op jit(solution)/shard_map/ppermute | solution.py:27
  145.0 2.4 collective-permute-start.16
  147.4 2.5 collective-permute-start.15
  149.9 4.2 %collective-permute-start.19 = (f32[16,128,128]{2,1,0:T(8,128)S(1)}, f32[16,128,128]{2,1,0:T(8,128)S(1)}, u32[]{:S(2)}, u32[]{:S(2)}) collective-permute-start(f32[16,128,128]{2,1,0:T(8,128)S(1)} %bitcast_select_fusion), channel_id=1, source_target_pairs={{0,16},{1,17},{2,18},{3,19},{4,20},{5,21},{6,22},{7,23},{8,24},{9,... | collective-permute-start | bytes 3145736 | tf_op jit(solution)/shard_map/ppermute | solution.py:70
  154.1 10.4 %collective-permute-done.20 = f32[16,128,128]{2,1,0:T(8,128)S(1)} collective-permute-done((f32[16,128,128]{2,1,0:T(8,128)S(1)}, f32[16,128,128]{2,1,0:T(8,128)S(1)}, u32[]{:S(2)}, u32[]{:S(2)}) %collective-permute-start.20) | collective-permute-done | bytes 1048608 | tf_op jit(solution)/shard_map/ppermute | solution.py:70
  164.5 3.2 %collective-permute-start.18 = (f32[16,128,128]{2,1,0:T(8,128)S(1)}, f32[16,128,128]{2,1,0:T(8,128)S(1)}, u32[]{:S(2)}, u32[]{:S(2)}) collective-permute-start(f32[16,128,128]{2,1,0:T(8,128)S(1)} %bitcast_select_fusion), channel_id=1, source_target_pairs={{0,8},{1,9},{2,10},{3,11},{4,12},{5,13},{6,14},{7,15},{8,16},{9,17... | collective-permute-start | bytes 3145736 | tf_op jit(solution)/shard_map/ppermute | solution.py:70
  167.7 20.3 %collective-permute-done.19 = f32[16,128,128]{2,1,0:T(8,128)S(1)} collective-permute-done((f32[16,128,128]{2,1,0:T(8,128)S(1)}, f32[16,128,128]{2,1,0:T(8,128)S(1)}, u32[]{:S(2)}, u32[]{:S(2)}) %collective-permute-start.19) | collective-permute-done | bytes 1048608 | tf_op jit(solution)/shard_map/ppermute | solution.py:70
  188.0 23.4 %collective-permute-done.18 = f32[16,128,128]{2,1,0:T(8,128)S(1)} collective-permute-done((f32[16,128,128]{2,1,0:T(8,128)S(1)}, f32[16,128,128]{2,1,0:T(8,128)S(1)}, u32[]{:S(2)}, u32[]{:S(2)}) %collective-permute-start.18) | collective-permute-done | bytes 1048608 | tf_op jit(solution)/shard_map/ppermute | solution.py:70
  211.4 2.4 pad_maximum_fusion.1.b_ref
  213.9 4.5 %collective-permute-done.15 = f32[12,2,128,128]{3,2,1,0:T(8,128)S(1)} collective-permute-done((f32[12,2,128,128]{3,2,1,0:T(8,128)S(1)}, f32[12,2,128,128]{3,2,1,0:T(8,128)S(1)}, u32[]{:S(2)}, u32[]{:S(2)}) %collective-permute-start.15) | collective-permute-done | bytes 1572896 | tf_op jit(solution)/shard_map/ppermute | solution.py:27
  218.4 3.0 %pad_maximum_fusion.a_ref = f32[12,8,128,128]{3,2,1,0:T(8,128)} fusion(f32[12,2,128,128]{3,2,1,0:T(8,128)S(1)} %collective-permute-done.17, f32[12,2,128,128]{3,2,1,0:T(8,128)S(1)} %collective-permute-done.16, f32[12,2,128,128]{3,2,1,0:T(8,128)S(1)} %collective-permute-done.15, f32[12,2,128,128]{3,2,1,0:T(8,128)S(1)} %pad_maximum_fusion.2), kind=kLoop, calls=%fused_computation.2 | loop fusion | flops 4718592 | bytes 12582912 | tf_op jit(solution)/shard_map/concatenate | solution.py:28
  221.4 2.4 collective-permute-start.21
  223.8 0.4 select_reduce_fusion.1
  224.3 0.6 gather_fusion
  224.9 0.1 fusion.5
  225.0 0.1 copy.24
  225.1 0.7 reshape.328.pidx_ref
  225.8 0.1 copy.26
  226.0 0.4 select_reduce_fusion
  226.4 0.1 fusion
  226.5 0.1 copy.27
  226.6 0.8 convert_reduce_fusion
  227.5 0.1 copy.29
  227.5 0.6 reshape.329.sidx_ref
  228.3 0.7 reshape.330.pidx_ref
  229.0 0.7 reshape.331.sidx_ref
  229.7 15.2 %shard_map.73.rest_0_ = f32[12,4,128,128]{3,2,1,0:T(8,128)} custom-call(s32[96]{0:T(128)} %reshape.330.pidx_ref, s32[96]{0:T(128)} %reshape.331.sidx_ref, f32[12,8,128,128]{3,2,1,0:T(8,128)} %pad_maximum_fusion.a_ref, f32[64,128,128]{2,1,0:T(8,128)} %pad_maximum_fusion.1.b_ref), custom_call_target="tpu_custom_call" | custom-call | tf_op jit(solution)/shard_map/pallas_call | solution.py:157
  244.9 16.5 %shard_map.74 = f32[12,4,128,128]{3,2,1,0:T(8,128)} custom-call(s32[96]{0:T(128)} %reshape.328.pidx_ref, s32[96]{0:T(128)} %reshape.329.sidx_ref, f32[12,8,128,128]{3,2,1,0:T(8,128)} %collective-permute-done.21.a_ref, f32[64,128,128]{2,1,0:T(8,128)} %pad_maximum_fusion.1.b_ref, f32[12,4,128,128]{3,2,1,0:T(8,128)} %shard_map.73.rest_0_), custom_call_target="tpu_custom_call", output_to_operand_aliasing={{}: (4, {})} | custom-call | tf_op jit(solution)/shard_map/pallas_call | solution.py:157
  (45 shorter events, 0.7 us)
Async XLA Ops:
  0.0 8.5 %collective-permute-start = (f32[2,128,128]{2,1,0:T(8,128)}, f32[2,128,128]{2,1,0:T(8,128)S(1)}, u32[]{:S(2)}, u32[]{:S(2)}) collective-permute-start(f32[2,128,128]{2,1,0:T(8,128)} %bitcast.41), channel_id=1, source_target_pairs={{0,1},{1,2},{2,3},{3,4},{4,5},{5,6},{6,7},{8,9},{9,10},{10,11},{11... | collective-permute-start | bytes 393224 | tf_op jit(solution)/shard_map/ppermute | solution.py:57
  4.8 8.3 %collective-permute-start.7 = (f32[2,128,128]{2,1,0:T(8,128)}, f32[2,128,128]{2,1,0:T(8,128)S(1)}, u32[]{:S(2)}, u32[]{:S(2)}) collective-permute-start(f32[2,128,128]{2,1,0:T(8,128)} %bitcast.42), channel_id=1, source_target_pairs={{1,0},{2,1},{3,2},{4,3},{5,4},{6,5},{7,6},{9,8},{10,9},{11,10},{12... | collective-permute-start | bytes 393224 | tf_op jit(solution)/shard_map/ppermute | solution.py:58
  8.5 7.2 %collective-permute-start.1 = (f32[2,128,128]{2,1,0:T(8,128)S(1)}, f32[2,128,128]{2,1,0:T(8,128)S(1)}, u32[]{:S(2)}, u32[]{:S(2)}) collective-permute-start(f32[2,128,128]{2,1,0:T(8,128)S(1)} %collective-permute-done), channel_id=1, source_target_pairs={{0,1},{1,2},{2,3},{3,4},{4,5},{5,6},{6,7},{8,9},{9,10},{10,11},{11... | collective-permute-start | bytes 393224 | tf_op jit(solution)/shard_map/ppermute | solution.py:57
  13.1 7.2 %collective-permute-start.8 = (f32[2,128,128]{2,1,0:T(8,128)S(1)}, f32[2,128,128]{2,1,0:T(8,128)S(1)}, u32[]{:S(2)}, u32[]{:S(2)}) collective-permute-start(f32[2,128,128]{2,1,0:T(8,128)S(1)} %collective-permute-done.7), channel_id=1, source_target_pairs={{1,0},{2,1},{3,2},{4,3},{5,4},{6,5},{7,6},{9,8},{10,9},{11,10},{12... | collective-permute-start | bytes 393224 | tf_op jit(solution)/shard_map/ppermute | solution.py:58
  15.7 7.2 %collective-permute-start.2 = (f32[2,128,128]{2,1,0:T(8,128)S(1)}, f32[2,128,128]{2,1,0:T(8,128)S(1)}, u32[]{:S(2)}, u32[]{:S(2)}) collective-permute-start(f32[2,128,128]{2,1,0:T(8,128)S(1)} %collective-permute-done.1), channel_id=1, source_target_pairs={{0,1},{1,2},{2,3},{3,4},{4,5},{5,6},{6,7},{8,9},{9,10},{10,11},{11... | collective-permute-start | bytes 393224 | tf_op jit(solution)/shard_map/ppermute | solution.py:57
  20.2 7.2 %collective-permute-start.9 = (f32[2,128,128]{2,1,0:T(8,128)S(1)}, f32[2,128,128]{2,1,0:T(8,128)S(1)}, u32[]{:S(2)}, u32[]{:S(2)}) collective-permute-start(f32[2,128,128]{2,1,0:T(8,128)S(1)} %collective-permute-done.8), channel_id=1, source_target_pairs={{1,0},{2,1},{3,2},{4,3},{5,4},{6,5},{7,6},{9,8},{10,9},{11,10},{12... | collective-permute-start | bytes 393224 | tf_op jit(solution)/shard_map/ppermute | solution.py:58
  22.8 7.2 %collective-permute-start.3 = (f32[2,128,128]{2,1,0:T(8,128)S(1)}, f32[2,128,128]{2,1,0:T(8,128)S(1)}, u32[]{:S(2)}, u32[]{:S(2)}) collective-permute-start(f32[2,128,128]{2,1,0:T(8,128)S(1)} %collective-permute-done.2), channel_id=1, source_target_pairs={{0,1},{1,2},{2,3},{3,4},{4,5},{5,6},{6,7},{8,9},{9,10},{10,11},{11... | collective-permute-start | bytes 393224 | tf_op jit(solution)/shard_map/ppermute | solution.py:57
  27.4 7.2 %collective-permute-start.10 = (f32[2,128,128]{2,1,0:T(8,128)S(1)}, f32[2,128,128]{2,1,0:T(8,128)S(1)}, u32[]{:S(2)}, u32[]{:S(2)}) collective-permute-start(f32[2,128,128]{2,1,0:T(8,128)S(1)} %collective-permute-done.9), channel_id=1, source_target_pairs={{1,0},{2,1},{3,2},{4,3},{5,4},{6,5},{7,6},{9,8},{10,9},{11,10},{12... | collective-permute-start | bytes 393224 | tf_op jit(solution)/shard_map/ppermute | solution.py:58
  30.0 7.2 %collective-permute-start.4 = (f32[2,128,128]{2,1,0:T(8,128)S(1)}, f32[2,128,128]{2,1,0:T(8,128)S(1)}, u32[]{:S(2)}, u32[]{:S(2)}) collective-permute-start(f32[2,128,128]{2,1,0:T(8,128)S(1)} %collective-permute-done.3), channel_id=1, source_target_pairs={{0,1},{1,2},{2,3},{3,4},{4,5},{5,6},{6,7},{8,9},{9,10},{10,11},{11... | collective-permute-start | bytes 393224 | tf_op jit(solution)/shard_map/ppermute | solution.py:57
  34.6 7.2 %collective-permute-start.11 = (f32[2,128,128]{2,1,0:T(8,128)S(1)}, f32[2,128,128]{2,1,0:T(8,128)S(1)}, u32[]{:S(2)}, u32[]{:S(2)}) collective-permute-start(f32[2,128,128]{2,1,0:T(8,128)S(1)} %collective-permute-done.10), channel_id=1, source_target_pairs={{1,0},{2,1},{3,2},{4,3},{5,4},{6,5},{7,6},{9,8},{10,9},{11,10},{12... | collective-permute-start | bytes 393224 | tf_op jit(solution)/shard_map/ppermute | solution.py:58
  37.2 7.2 %collective-permute-start.5 = (f32[2,128,128]{2,1,0:T(8,128)S(1)}, f32[2,128,128]{2,1,0:T(8,128)S(1)}, u32[]{:S(2)}, u32[]{:S(2)}) collective-permute-start(f32[2,128,128]{2,1,0:T(8,128)S(1)} %collective-permute-done.4), channel_id=1, source_target_pairs={{0,1},{1,2},{2,3},{3,4},{4,5},{5,6},{6,7},{8,9},{9,10},{10,11},{11... | collective-permute-start | bytes 393224 | tf_op jit(solution)/shard_map/ppermute | solution.py:57
  41.8 7.2 %collective-permute-start.12 = (f32[2,128,128]{2,1,0:T(8,128)S(1)}, f32[2,128,128]{2,1,0:T(8,128)S(1)}, u32[]{:S(2)}, u32[]{:S(2)}) collective-permute-start(f32[2,128,128]{2,1,0:T(8,128)S(1)} %collective-permute-done.11), channel_id=1, source_target_pairs={{1,0},{2,1},{3,2},{4,3},{5,4},{6,5},{7,6},{9,8},{10,9},{11,10},{12... | collective-permute-start | bytes 393224 | tf_op jit(solution)/shard_map/ppermute | solution.py:58
  44.4 7.2 %collective-permute-start.6 = (f32[2,128,128]{2,1,0:T(8,128)S(1)}, f32[2,128,128]{2,1,0:T(8,128)S(1)}, u32[]{:S(2)}, u32[]{:S(2)}) collective-permute-start(f32[2,128,128]{2,1,0:T(8,128)S(1)} %collective-permute-done.5), channel_id=1, source_target_pairs={{0,1},{1,2},{2,3},{3,4},{4,5},{5,6},{6,7},{8,9},{9,10},{10,11},{11... | collective-permute-start | bytes 393224 | tf_op jit(solution)/shard_map/ppermute | solution.py:57
  49.0 7.3 %collective-permute-start.13 = (f32[2,128,128]{2,1,0:T(8,128)S(1)}, f32[2,128,128]{2,1,0:T(8,128)S(1)}, u32[]{:S(2)}, u32[]{:S(2)}) collective-permute-start(f32[2,128,128]{2,1,0:T(8,128)S(1)} %collective-permute-done.12), channel_id=1, source_target_pairs={{1,0},{2,1},{3,2},{4,3},{5,4},{6,5},{7,6},{9,8},{10,9},{11,10},{12... | collective-permute-start | bytes 393224 | tf_op jit(solution)/shard_map/ppermute | solution.py:58
  56.9 2.4 copy-start
  59.3 79.1 %collective-permute-start.14 = (f32[12,1,128,128]{3,2,1,0:T(8,128)S(1)}, f32[12,1,128,128]{3,2,1,0:T(8,128)S(1)}, u32[]{:S(2)}, u32[]{:S(2)}) collective-permute-start(f32[12,1,128,128]{3,2,1,0:T(8,128)S(1)} %copy-done), channel_id=1, source_target_pairs={{0,64},{32,96},{64,0},{96,32},{128,192},{160,224},{192,128},{224,1... | collective-permute-start | bytes 2359304 | tf_op jit(solution)/shard_map/ppermute | solution.py:21
  138.5 26.1 %collective-permute-start.20 = (f32[16,128,128]{2,1,0:T(8,128)S(1)}, f32[16,128,128]{2,1,0:T(8,128)S(1)}, u32[]{:S(2)}, u32[]{:S(2)}) collective-permute-start(f32[16,128,128]{2,1,0:T(8,128)S(1)} %bitcast_select_fusion), channel_id=1, source_target_pairs={{0,24},{1,25},{2,26},{3,27},{4,28},{5,29},{6,30},{7,31},{8,0},{9,1... | collective-permute-start | bytes 3145736 | tf_op jit(solution)/shard_map/ppermute | solution.py:70
  140.6 73.3 %collective-permute-start.17 = (f32[12,2,128,128]{3,2,1,0:T(8,128)S(1)}, f32[12,2,128,128]{3,2,1,0:T(8,128)S(1)}, u32[]{:S(2)}, u32[]{:S(2)}) collective-permute-start(f32[12,2,128,128]{3,2,1,0:T(8,128)S(1)} %pad_maximum_fusion.2), channel_id=1, source_target_pairs={{0,384},{32,416},{64,448},{96,480},{128,0},{160,32},{192,64},{224,... | collective-permute-start | bytes 4718600 | tf_op jit(solution)/shard_map/ppermute | solution.py:27
  145.0 68.9 %collective-permute-start.16 = (f32[12,2,128,128]{3,2,1,0:T(8,128)S(1)}, f32[12,2,128,128]{3,2,1,0:T(8,128)S(1)}, u32[]{:S(2)}, u32[]{:S(2)}) collective-permute-start(f32[12,2,128,128]{3,2,1,0:T(8,128)S(1)} %pad_maximum_fusion.2), channel_id=1, source_target_pairs={{0,256},{32,288},{64,320},{96,352},{128,384},{160,416},{192,448},{... | collective-permute-start | bytes 4718600 | tf_op jit(solution)/shard_map/ppermute | solution.py:27
  147.4 71.0 %collective-permute-start.15 = (f32[12,2,128,128]{3,2,1,0:T(8,128)S(1)}, f32[12,2,128,128]{3,2,1,0:T(8,128)S(1)}, u32[]{:S(2)}, u32[]{:S(2)}) collective-permute-start(f32[12,2,128,128]{3,2,1,0:T(8,128)S(1)} %pad_maximum_fusion.2), channel_id=1, source_target_pairs={{0,128},{32,160},{64,192},{96,224},{128,256},{160,288},{192,320},{... | collective-permute-start | bytes 4718600 | tf_op jit(solution)/shard_map/ppermute | solution.py:27
  149.9 38.1 %collective-permute-start.19 = (f32[16,128,128]{2,1,0:T(8,128)S(1)}, f32[16,128,128]{2,1,0:T(8,128)S(1)}, u32[]{:S(2)}, u32[]{:S(2)}) collective-permute-start(f32[16,128,128]{2,1,0:T(8,128)S(1)} %bitcast_select_fusion), channel_id=1, source_target_pairs={{0,16},{1,17},{2,18},{3,19},{4,20},{5,21},{6,22},{7,23},{8,24},{9,... | collective-permute-start | bytes 3145736 | tf_op jit(solution)/shard_map/ppermute | solution.py:70
  164.5 46.8 %collective-permute-start.18 = (f32[16,128,128]{2,1,0:T(8,128)S(1)}, f32[16,128,128]{2,1,0:T(8,128)S(1)}, u32[]{:S(2)}, u32[]{:S(2)}) collective-permute-start(f32[16,128,128]{2,1,0:T(8,128)S(1)} %bitcast_select_fusion), channel_id=1, source_target_pairs={{0,8},{1,9},{2,10},{3,11},{4,12},{5,13},{6,14},{7,15},{8,16},{9,17... | collective-permute-start | bytes 3145736 | tf_op jit(solution)/shard_map/ppermute | solution.py:70
  213.8 10.0 %copy-start.1 = (s32[12,16]{1,0:T(8,128)S(1)}, s32[12,16]{1,0:T(8,128)}, u32[]{:S(2)}) copy-start(s32[12,16]{1,0:T(8,128)} %param.8) | copy-start | bytes 2308
  213.8 10.0 %copy-start.3 = (s32[64]{0:T(128)S(1)}, s32[64]{0:T(128)}, u32[]{:S(2)}) copy-start(s32[64]{0:T(128)} %param.13) | copy-start | bytes 772
  213.8 12.0 %copy-start.2 = (s32[12,4]{0,1:T(4,128)S(1)}, s32[12,4]{0,1:T(4,128)}, u32[]{:S(2)}) copy-start(s32[12,4]{0,1:T(4,128)} %param.12) | copy-start | bytes 580
  213.8 12.1 %copy-start.4 = (s32[64,1]{0,1:T(1,128)S(1)}, s32[64,1]{0,1:T(1,128)}, u32[]{:S(2)}) copy-start(s32[64,1]{0,1:T(1,128)} %param.11) | copy-start | bytes 772
  213.8 12.5 %copy-start.5 = (s32[12]{0:T(128)S(1)}, s32[12]{0:T(128)}, u32[]{:S(2)}) copy-start(s32[12]{0:T(128)} %param.9) | copy-start | bytes 148
  221.4 23.5 %collective-permute-start.21 = (f32[12,8,128,128]{3,2,1,0:T(8,128)}, f32[12,8,128,128]{3,2,1,0:T(8,128)}, u32[]{:S(2)}, u32[]{:S(2)}) collective-permute-start(f32[12,8,128,128]{3,2,1,0:T(8,128)} %pad_maximum_fusion.a_ref), channel_id=1, source_target_pairs={{0,32},{32,0},{64,96},{96,64},{128,160},{160,128},{192,224},{224,1... | collective-permute-start | bytes 18874376 | tf_op jit(solution)/shard_map/ppermute | solution.py:32

commit v7 on v6

--- a/solution.py
+++ b/solution.py
@@ -13,12 +13,24 @@
     return jnp.sum(jnp.where(matched, values_table, 0), axis=-1)
 
 
-def row_stages(n_row):
+def row_stages(n_row, n_col):
     n_x = n_row // 4
 
+    def down_z(k):
+        r, c = k // n_col, k % n_col
+        z = ((r // 2) % 2) * 8 + c % 8 - 4
+        z = z % 16
+        return ((r // 4) * 4 + (z // 8) * 2 + r % 2) * n_col + (c // 8) * 8 + z % 8
+
     def swap_z(chunk):
+        half = chunk.shape[0] // 2
         pairs = [(r, r ^ 2) for r in range(n_row)]
-        return jnp.concatenate([chunk, lax.ppermute(chunk, "row", pairs)], axis=1)
+        direct = lax.ppermute(chunk[:half], "row", pairs)
+        legs = [(k, down_z(k)) for k in range(n_row * n_col)]
+        around = lax.ppermute(chunk[half:], ("row", "col"), legs)
+        around = lax.ppermute(around, ("row", "col"), legs)
+        other = jnp.concatenate([direct, around], axis=0)
+        return jnp.concatenate([chunk, other], axis=1)
 
     def ring_x(held):
         parts = [held]
@@ -83,7 +95,7 @@
 
 def local(a_blocks, a_cols, a_lengths, b_blocks, b_cols, c_cols, order, n_row, n_col):
     per_dev = b_blocks.shape[0]
-    swap_z, ring_x, swap_core = row_stages(n_row)
+    swap_z, ring_x, swap_core = row_stages(n_row, n_col)
     line_z, ring_y = col_stages(n_col)
     a_held, b_held = lax.optimization_barrier((a_blocks, line_z(b_blocks[:, 0])))
     a_held, b_held = lax.optimization_barrier((swap_z(a_held), b_held))

time: 263 us -> 301 us (1.14)
  the two profiles are of different devices: /device:TPU:105 before, /device:TPU:1 now
where the time goes in v7:
time: 301 us; the launch traced here: 299 us
  waiting for transfers between devices  153 us (51%)
  starting transfers between devices  89.5 us (30%)
  Pallas kernels  31.6 us (10%)
  local copies, waits for them, and re-layouts  17.2 us (6%)
  other arithmetic  7.53 us (3%)
    ppermute x1, waiting for transfers between devices, swap_z(): around = lax.ppermute(chunk[half:], ('row', 'col'), legs)  64.4 us
    ppermute x3, waiting for transfers between devices, ring_y(): parts.append(lax.ppermute(held, 'col', shift))  58.4 us
    ppermute x7, starting transfers between devices, line_z(): going_right = lax.ppermute(going_right, 'col', right)  33.7 us
    pallas_call x2, Pallas kernels, row_products(): pl.pallas_call(product_kernel, grid_spec=grid_spec, out_shape=jax.ShapeDt...  31.6 us
    ppermute x1, waiting for transfers between devices, swap_z(): around = lax.ppermute(around, ('row', 'col'), legs)  26.4 us
    ppermute x1, starting transfers between devices, swap_z(): around = lax.ppermute(chunk[half:], ('row', 'col'), legs)  15.7 us
    unnamed x27, local copies, waits for them, and re-layouts  10.3 us
    ppermute x3, starting transfers between devices, ring_x(): parts.append(lax.ppermute(held, 'row', shift))  9.33 us
  transfers between devices with their start and end apart: 24, of which 6 were waited for; matrix products, arithmetic and copies ran while one was open for 6% of the time, Pallas kernels for 5%

profile of v7, /device:TPU:1, one launch (start us, length us, event | category | flops | bytes accessed | tf_op | source)
XLA Modules:
  0.0 299.3 jit_solution(3508346072737973633)
XLA Ops:
  0.0 4.4 %collective-permute-start = (f32[2,128,128]{2,1,0:T(8,128)}, f32[2,128,128]{2,1,0:T(8,128)S(1)}, u32[]{:S(2)}, u32[]{:S(2)}) collective-permute-start(f32[2,128,128]{2,1,0:T(8,128)} %bitcast.41), channel_id=1, source_target_pairs={{0,1},{1,2},{2,3},{3,4},{4,5},{5,6},{6,7},{8,9},{9,10},{10,11},{11... | collective-permute-start | bytes 393224 | tf_op jit(solution)/shard_map/ppermute | solution.py:69
  4.4 1.3 collective-permute-start.7
  5.7 1.6 bitcast_dynamic-update-slice_fusion.14
  7.4 4.2 %collective-permute-start.1 = (f32[2,128,128]{2,1,0:T(8,128)S(1)}, f32[2,128,128]{2,1,0:T(8,128)S(1)}, u32[]{:S(2)}, u32[]{:S(2)}) collective-permute-start(f32[2,128,128]{2,1,0:T(8,128)S(1)} %collective-permute-done), channel_id=1, source_target_pairs={{0,1},{1,2},{2,3},{3,4},{4,5},{5,6},{6,7},{8,9},{9,10},{10,11},{11... | collective-permute-start | bytes 393224 | tf_op jit(solution)/shard_map/ppermute | solution.py:69
  11.6 1.3 collective-permute-start.8
  12.9 0.7 bitcast_dynamic-update-slice_fusion.13
  13.6 4.2 %collective-permute-start.2 = (f32[2,128,128]{2,1,0:T(8,128)S(1)}, f32[2,128,128]{2,1,0:T(8,128)S(1)}, u32[]{:S(2)}, u32[]{:S(2)}) collective-permute-start(f32[2,128,128]{2,1,0:T(8,128)S(1)} %collective-permute-done.1), channel_id=1, source_target_pairs={{0,1},{1,2},{2,3},{3,4},{4,5},{5,6},{6,7},{8,9},{9,10},{10,11},{11... | collective-permute-start | bytes 393224 | tf_op jit(solution)/shard_map/ppermute | solution.py:69
  17.8 1.3 collective-permute-start.9
  19.1 0.7 bitcast_dynamic-update-slice_fusion.12
  19.8 5.4 %collective-permute-start.3 = (f32[2,128,128]{2,1,0:T(8,128)S(1)}, f32[2,128,128]{2,1,0:T(8,128)S(1)}, u32[]{:S(2)}, u32[]{:S(2)}) collective-permute-start(f32[2,128,128]{2,1,0:T(8,128)S(1)} %collective-permute-done.2), channel_id=1, source_target_pairs={{0,1},{1,2},{2,3},{3,4},{4,5},{5,6},{6,7},{8,9},{9,10},{10,11},{11... | collective-permute-start | bytes 393224 | tf_op jit(solution)/shard_map/ppermute | solution.py:69
  25.2 1.3 collective-permute-start.10
  26.5 0.7 bitcast_dynamic-update-slice_fusion.11
  27.1 5.2 %collective-permute-start.4 = (f32[2,128,128]{2,1,0:T(8,128)S(1)}, f32[2,128,128]{2,1,0:T(8,128)S(1)}, u32[]{:S(2)}, u32[]{:S(2)}) collective-permute-start(f32[2,128,128]{2,1,0:T(8,128)S(1)} %collective-permute-done.3), channel_id=1, source_target_pairs={{0,1},{1,2},{2,3},{3,4},{4,5},{5,6},{6,7},{8,9},{9,10},{10,11},{11... | collective-permute-start | bytes 393224 | tf_op jit(solution)/shard_map/ppermute | solution.py:69
  32.3 1.3 collective-permute-start.11
  33.6 0.7 bitcast_dynamic-update-slice_fusion.10
  34.3 5.2 %collective-permute-start.5 = (f32[2,128,128]{2,1,0:T(8,128)S(1)}, f32[2,128,128]{2,1,0:T(8,128)S(1)}, u32[]{:S(2)}, u32[]{:S(2)}) collective-permute-start(f32[2,128,128]{2,1,0:T(8,128)S(1)} %collective-permute-done.4), channel_id=1, source_target_pairs={{0,1},{1,2},{2,3},{3,4},{4,5},{5,6},{6,7},{8,9},{9,10},{10,11},{11... | collective-permute-start | bytes 393224 | tf_op jit(solution)/shard_map/ppermute | solution.py:69
  39.5 1.3 collective-permute-start.12
  40.8 0.7 bitcast_dynamic-update-slice_fusion.9
  41.5 5.2 %collective-permute-start.6 = (f32[2,128,128]{2,1,0:T(8,128)S(1)}, f32[2,128,128]{2,1,0:T(8,128)S(1)}, u32[]{:S(2)}, u32[]{:S(2)}) collective-permute-start(f32[2,128,128]{2,1,0:T(8,128)S(1)} %collective-permute-done.5), channel_id=1, source_target_pairs={{0,1},{1,2},{2,3},{3,4},{4,5},{5,6},{6,7},{8,9},{9,10},{10,11},{11... | collective-permute-start | bytes 393224 | tf_op jit(solution)/shard_map/ppermute | solution.py:69
  46.7 1.3 collective-permute-start.13
  48.0 0.7 bitcast_dynamic-update-slice_fusion.8
  48.7 0.7 bitcast_dynamic-update-slice_fusion.7
  49.3 0.7 bitcast_dynamic-update-slice_fusion.6
  50.0 0.7 bitcast_dynamic-update-slice_fusion.5
  50.7 0.7 bitcast_dynamic-update-slice_fusion.4
  51.3 0.7 bitcast_dynamic-update-slice_fusion.3
  52.0 0.7 bitcast_dynamic-update-slice_fusion.2
  52.7 0.7 bitcast_dynamic-update-slice_fusion.1
  53.3 0.3 collective-permute-done.13
  53.6 0.7 bitcast_dynamic-update-slice_fusion
  54.3 2.2 gather_fusion.1
  56.5 0.1 bitcast_select_fusion
  56.7 15.7 %collective-permute-start.15 = (f32[6,1,128,128]{3,2,1,0:T(8,128)S(1)}, f32[6,1,128,128]{3,2,1,0:T(8,128)S(1)}, u32[]{:S(2)}, u32[]{:S(2)}) collective-permute-start(f32[6,1,128,128]{3,2,1,0:T(8,128)S(1)} %get-tuple-element.24), channel_id=1, source_target_pairs={{0,68},{1,69},{2,70},{3,71},{4,0},{5,1},{6,2},{7,3},{8,76},{9,77},... | collective-permute-start | bytes 1179656 | tf_op jit(solution)/shard_map/ppermute | solution.py:30
  72.4 3.4 %collective-permute-start.14 = (f32[6,1,128,128]{3,2,1,0:T(8,128)S(1)}, f32[6,1,128,128]{3,2,1,0:T(8,128)S(1)}, u32[]{:S(2)}, u32[]{:S(2)}) collective-permute-start(f32[6,1,128,128]{3,2,1,0:T(8,128)S(1)} %get-tuple-element.23), channel_id=1, source_target_pairs={{0,64},{32,96},{64,0},{96,32},{128,192},{160,224},{192,128},{224,1... | collective-permute-start | bytes 1179656 | tf_op jit(solution)/shard_map/ppermute | solution.py:28
  75.8 64.4 %collective-permute-done.15 = f32[6,1,128,128]{3,2,1,0:T(8,128)S(1)} collective-permute-done((f32[6,1,128,128]{3,2,1,0:T(8,128)S(1)}, f32[6,1,128,128]{3,2,1,0:T(8,128)S(1)}, u32[]{:S(2)}, u32[]{:S(2)}) %collective-permute-start.15) | collective-permute-done | bytes 393248 | tf_op jit(solution)/shard_map/ppermute | solution.py:30
  140.2 7.2 %collective-permute-start.16 = (f32[6,1,128,128]{3,2,1,0:T(8,128)S(1)}, f32[6,1,128,128]{3,2,1,0:T(8,128)S(1)}, u32[]{:S(2)}, u32[]{:S(2)}) collective-permute-start(f32[6,1,128,128]{3,2,1,0:T(8,128)S(1)} %collective-permute-done.15), channel_id=1, source_target_pairs={{0,68},{1,69},{2,70},{3,71},{4,0},{5,1},{6,2},{7,3},{8,76},{9,77},... | collective-permute-start | bytes 1179656 | tf_op jit(solution)/shard_map/ppermute | solution.py:31
  147.5 26.4 %collective-permute-done.16 = f32[6,1,128,128]{3,2,1,0:T(8,128)S(1)} collective-permute-done((f32[6,1,128,128]{3,2,1,0:T(8,128)S(1)}, f32[6,1,128,128]{3,2,1,0:T(8,128)S(1)}, u32[]{:S(2)}, u32[]{:S(2)}) %collective-permute-start.16) | collective-permute-done | bytes 393248 | tf_op jit(solution)/shard_map/ppermute | solution.py:31
  173.8 0.1 maximum_maximum_fusion
  174.0 4.6 %collective-permute-start.22 = (f32[16,128,128]{2,1,0:T(8,128)S(1)}, f32[16,128,128]{2,1,0:T(8,128)S(1)}, u32[]{:S(2)}, u32[]{:S(2)}) collective-permute-start(f32[16,128,128]{2,1,0:T(8,128)S(1)} %bitcast_select_fusion), channel_id=1, source_target_pairs={{0,24},{1,25},{2,26},{3,27},{4,28},{5,29},{6,30},{7,31},{8,0},{9,1... | collective-permute-start | bytes 3145736 | tf_op jit(solution)/shard_map/ppermute | solution.py:82
  178.6 4.4 %collective-permute-start.19 = (f32[12,2,128,128]{3,2,1,0:T(8,128)S(1)}, f32[12,2,128,128]{3,2,1,0:T(8,128)S(1)}, u32[]{:S(2)}, u32[]{:S(2)}) collective-permute-start(f32[12,2,128,128]{3,2,1,0:T(8,128)S(1)} %maximum_maximum_fusion), channel_id=1, source_target_pairs={{0,384},{32,416},{64,448},{96,480},{128,0},{160,32},{192,64},{224,... | collective-permute-start | bytes 4718600 | tf_op jit(solution)/shard_map/ppermute | solution.py:39
  183.0 2.4 collective-permute-start.18
  185.5 2.5 collective-permute-start.17
  188.0 2.3 collective-permute-start.21
  190.3 32.8 %collective-permute-done.22 = f32[16,128,128]{2,1,0:T(8,128)S(1)} collective-permute-done((f32[16,128,128]{2,1,0:T(8,128)S(1)}, f32[16,128,128]{2,1,0:T(8,128)S(1)}, u32[]{:S(2)}, u32[]{:S(2)}) %collective-permute-start.22) | collective-permute-done | bytes 1048608 | tf_op jit(solution)/shard_map/ppermute | solution.py:82
  223.0 1.9 collective-permute-start.20
  224.9 25.7 %collective-permute-done.20 = f32[16,128,128]{2,1,0:T(8,128)S(1)} collective-permute-done((f32[16,128,128]{2,1,0:T(8,128)S(1)}, f32[16,128,128]{2,1,0:T(8,128)S(1)}, u32[]{:S(2)}, u32[]{:S(2)}) %collective-permute-start.20) | collective-permute-done | bytes 1048608 | tf_op jit(solution)/shard_map/ppermute | solution.py:82
  250.6 2.4 pad_maximum_fusion.1.b_ref
  253.1 3.4 %collective-permute-done.17 = f32[12,2,128,128]{3,2,1,0:T(8,128)S(1)} collective-permute-done((f32[12,2,128,128]{3,2,1,0:T(8,128)S(1)}, f32[12,2,128,128]{3,2,1,0:T(8,128)S(1)}, u32[]{:S(2)}, u32[]{:S(2)}) %collective-permute-start.17) | collective-permute-done | bytes 1572896 | tf_op jit(solution)/shard_map/ppermute | solution.py:39
  256.5 3.0 pad_maximum_fusion.a_ref
  259.4 2.4 collective-permute-start.23
  261.9 0.4 select_reduce_fusion.1
  262.4 0.6 gather_fusion
  263.0 0.1 fusion.5
  263.2 0.7 reshape.328.pidx_ref
  263.8 0.1 copy.26
  264.0 0.4 select_reduce_fusion
  264.5 0.1 fusion
  264.6 0.1 copy.27
  264.7 0.8 convert_reduce_fusion
  265.6 0.6 reshape.329.sidx_ref
  266.3 0.6 reshape.330.pidx_ref
  267.0 0.7 reshape.331.sidx_ref
  267.7 15.9 %shard_map.73.rest_0_ = f32[12,4,128,128]{3,2,1,0:T(8,128)} custom-call(s32[96]{0:T(128)} %reshape.330.pidx_ref, s32[96]{0:T(128)} %reshape.331.sidx_ref, f32[12,8,128,128]{3,2,1,0:T(8,128)} %pad_maximum_fusion.a_ref, f32[64,128,128]{2,1,0:T(8,128)} %pad_maximum_fusion.1.b_ref), custom_call_target="tpu_custom_call" | custom-call | tf_op jit(solution)/shard_map/pallas_call | solution.py:169
  283.6 15.7 %shard_map.74 = f32[12,4,128,128]{3,2,1,0:T(8,128)} custom-call(s32[96]{0:T(128)} %reshape.328.pidx_ref, s32[96]{0:T(128)} %reshape.329.sidx_ref, f32[12,8,128,128]{3,2,1,0:T(8,128)} %collective-permute-done.23.a_ref, f32[64,128,128]{2,1,0:T(8,128)} %pad_maximum_fusion.1.b_ref, f32[12,4,128,128]{3,2,1,0:T(8,128)} %shard_map.73.rest_0_), custom_call_target="tpu_custom_call", output_to_operand_aliasing={{}: (4, {})} | custom-call | tf_op jit(solution)/shard_map/pallas_call | solution.py:169
  (50 shorter events, 1.0 us)
Async XLA Ops:
  0.0 7.4 %collective-permute-start = (f32[2,128,128]{2,1,0:T(8,128)}, f32[2,128,128]{2,1,0:T(8,128)S(1)}, u32[]{:S(2)}, u32[]{:S(2)}) collective-permute-start(f32[2,128,128]{2,1,0:T(8,128)} %bitcast.41), channel_id=1, source_target_pairs={{0,1},{1,2},{2,3},{3,4},{4,5},{5,6},{6,7},{8,9},{9,10},{10,11},{11... | collective-permute-start | bytes 393224 | tf_op jit(solution)/shard_map/ppermute | solution.py:69
  4.4 7.3 %collective-permute-start.7 = (f32[2,128,128]{2,1,0:T(8,128)}, f32[2,128,128]{2,1,0:T(8,128)S(1)}, u32[]{:S(2)}, u32[]{:S(2)}) collective-permute-start(f32[2,128,128]{2,1,0:T(8,128)} %bitcast.42), channel_id=1, source_target_pairs={{1,0},{2,1},{3,2},{4,3},{5,4},{6,5},{7,6},{9,8},{10,9},{11,10},{12... | collective-permute-start | bytes 393224 | tf_op jit(solution)/shard_map/ppermute | solution.py:70
  7.4 6.2 %collective-permute-start.1 = (f32[2,128,128]{2,1,0:T(8,128)S(1)}, f32[2,128,128]{2,1,0:T(8,128)S(1)}, u32[]{:S(2)}, u32[]{:S(2)}) collective-permute-start(f32[2,128,128]{2,1,0:T(8,128)S(1)} %collective-permute-done), channel_id=1, source_target_pairs={{0,1},{1,2},{2,3},{3,4},{4,5},{5,6},{6,7},{8,9},{9,10},{10,11},{11... | collective-permute-start | bytes 393224 | tf_op jit(solution)/shard_map/ppermute | solution.py:69
  11.6 6.1 %collective-permute-start.8 = (f32[2,128,128]{2,1,0:T(8,128)S(1)}, f32[2,128,128]{2,1,0:T(8,128)S(1)}, u32[]{:S(2)}, u32[]{:S(2)}) collective-permute-start(f32[2,128,128]{2,1,0:T(8,128)S(1)} %collective-permute-done.7), channel_id=1, source_target_pairs={{1,0},{2,1},{3,2},{4,3},{5,4},{6,5},{7,6},{9,8},{10,9},{11,10},{12... | collective-permute-start | bytes 393224 | tf_op jit(solution)/shard_map/ppermute | solution.py:70
  13.6 6.2 %collective-permute-start.2 = (f32[2,128,128]{2,1,0:T(8,128)S(1)}, f32[2,128,128]{2,1,0:T(8,128)S(1)}, u32[]{:S(2)}, u32[]{:S(2)}) collective-permute-start(f32[2,128,128]{2,1,0:T(8,128)S(1)} %collective-permute-done.1), channel_id=1, source_target_pairs={{0,1},{1,2},{2,3},{3,4},{4,5},{5,6},{6,7},{8,9},{9,10},{10,11},{11... | collective-permute-start | bytes 393224 | tf_op jit(solution)/shard_map/ppermute | solution.py:69
  17.8 7.4 %collective-permute-start.9 = (f32[2,128,128]{2,1,0:T(8,128)S(1)}, f32[2,128,128]{2,1,0:T(8,128)S(1)}, u32[]{:S(2)}, u32[]{:S(2)}) collective-permute-start(f32[2,128,128]{2,1,0:T(8,128)S(1)} %collective-permute-done.8), channel_id=1, source_target_pairs={{1,0},{2,1},{3,2},{4,3},{5,4},{6,5},{7,6},{9,8},{10,9},{11,10},{12... | collective-permute-start | bytes 393224 | tf_op jit(solution)/shard_map/ppermute | solution.py:70
  19.8 7.4 %collective-permute-start.3 = (f32[2,128,128]{2,1,0:T(8,128)S(1)}, f32[2,128,128]{2,1,0:T(8,128)S(1)}, u32[]{:S(2)}, u32[]{:S(2)}) collective-permute-start(f32[2,128,128]{2,1,0:T(8,128)S(1)} %collective-permute-done.2), channel_id=1, source_target_pairs={{0,1},{1,2},{2,3},{3,4},{4,5},{5,6},{6,7},{8,9},{9,10},{10,11},{11... | collective-permute-start | bytes 393224 | tf_op jit(solution)/shard_map/ppermute | solution.py:69
  25.2 7.2 %collective-permute-start.10 = (f32[2,128,128]{2,1,0:T(8,128)S(1)}, f32[2,128,128]{2,1,0:T(8,128)S(1)}, u32[]{:S(2)}, u32[]{:S(2)}) collective-permute-start(f32[2,128,128]{2,1,0:T(8,128)S(1)} %collective-permute-done.9), channel_id=1, source_target_pairs={{1,0},{2,1},{3,2},{4,3},{5,4},{6,5},{7,6},{9,8},{10,9},{11,10},{12... | collective-permute-start | bytes 393224 | tf_op jit(solution)/shard_map/ppermute | solution.py:70
  27.1 7.2 %collective-permute-start.4 = (f32[2,128,128]{2,1,0:T(8,128)S(1)}, f32[2,128,128]{2,1,0:T(8,128)S(1)}, u32[]{:S(2)}, u32[]{:S(2)}) collective-permute-start(f32[2,128,128]{2,1,0:T(8,128)S(1)} %collective-permute-done.3), channel_id=1, source_target_pairs={{0,1},{1,2},{2,3},{3,4},{4,5},{5,6},{6,7},{8,9},{9,10},{10,11},{11... | collective-permute-start | bytes 393224 | tf_op jit(solution)/shard_map/ppermute | solution.py:69
  32.3 7.2 %collective-permute-start.11 = (f32[2,128,128]{2,1,0:T(8,128)S(1)}, f32[2,128,128]{2,1,0:T(8,128)S(1)}, u32[]{:S(2)}, u32[]{:S(2)}) collective-permute-start(f32[2,128,128]{2,1,0:T(8,128)S(1)} %collective-permute-done.10), channel_id=1, source_target_pairs={{1,0},{2,1},{3,2},{4,3},{5,4},{6,5},{7,6},{9,8},{10,9},{11,10},{12... | collective-permute-start | bytes 393224 | tf_op jit(solution)/shard_map/ppermute | solution.py:70
  34.3 7.2 %collective-permute-start.5 = (f32[2,128,128]{2,1,0:T(8,128)S(1)}, f32[2,128,128]{2,1,0:T(8,128)S(1)}, u32[]{:S(2)}, u32[]{:S(2)}) collective-permute-start(f32[2,128,128]{2,1,0:T(8,128)S(1)} %collective-permute-done.4), channel_id=1, source_target_pairs={{0,1},{1,2},{2,3},{3,4},{4,5},{5,6},{6,7},{8,9},{9,10},{10,11},{11... | collective-permute-start | bytes 393224 | tf_op jit(solution)/shard_map/ppermute | solution.py:69
  39.5 7.2 %collective-permute-start.12 = (f32[2,128,128]{2,1,0:T(8,128)S(1)}, f32[2,128,128]{2,1,0:T(8,128)S(1)}, u32[]{:S(2)}, u32[]{:S(2)}) collective-permute-start(f32[2,128,128]{2,1,0:T(8,128)S(1)} %collective-permute-done.11), channel_id=1, source_target_pairs={{1,0},{2,1},{3,2},{4,3},{5,4},{6,5},{7,6},{9,8},{10,9},{11,10},{12... | collective-permute-start | bytes 393224 | tf_op jit(solution)/shard_map/ppermute | solution.py:70
  41.5 7.2 %collective-permute-start.6 = (f32[2,128,128]{2,1,0:T(8,128)S(1)}, f32[2,128,128]{2,1,0:T(8,128)S(1)}, u32[]{:S(2)}, u32[]{:S(2)}) collective-permute-start(f32[2,128,128]{2,1,0:T(8,128)S(1)} %collective-permute-done.5), channel_id=1, source_target_pairs={{0,1},{1,2},{2,3},{3,4},{4,5},{5,6},{6,7},{8,9},{9,10},{10,11},{11... | collective-permute-start | bytes 393224 | tf_op jit(solution)/shard_map/ppermute | solution.py:69
  46.7 6.9 %collective-permute-start.13 = (f32[2,128,128]{2,1,0:T(8,128)S(1)}, f32[2,128,128]{2,1,0:T(8,128)S(1)}, u32[]{:S(2)}, u32[]{:S(2)}) collective-permute-start(f32[2,128,128]{2,1,0:T(8,128)S(1)} %collective-permute-done.12), channel_id=1, source_target_pairs={{1,0},{2,1},{3,2},{4,3},{5,4},{6,5},{7,6},{9,8},{10,9},{11,10},{12... | collective-permute-start | bytes 393224 | tf_op jit(solution)/shard_map/ppermute | solution.py:70
  54.3 2.4 copy-start
  56.7 83.5 %collective-permute-start.15 = (f32[6,1,128,128]{3,2,1,0:T(8,128)S(1)}, f32[6,1,128,128]{3,2,1,0:T(8,128)S(1)}, u32[]{:S(2)}, u32[]{:S(2)}) collective-permute-start(f32[6,1,128,128]{3,2,1,0:T(8,128)S(1)} %get-tuple-element.24), channel_id=1, source_target_pairs={{0,68},{1,69},{2,70},{3,71},{4,0},{5,1},{6,2},{7,3},{8,76},{9,77},... | collective-permute-start | bytes 1179656 | tf_op jit(solution)/shard_map/ppermute | solution.py:30
  72.4 75.0 %collective-permute-start.14 = (f32[6,1,128,128]{3,2,1,0:T(8,128)S(1)}, f32[6,1,128,128]{3,2,1,0:T(8,128)S(1)}, u32[]{:S(2)}, u32[]{:S(2)}) collective-permute-start(f32[6,1,128,128]{3,2,1,0:T(8,128)S(1)} %get-tuple-element.23), channel_id=1, source_target_pairs={{0,64},{32,96},{64,0},{96,32},{128,192},{160,224},{192,128},{224,1... | collective-permute-start | bytes 1179656 | tf_op jit(solution)/shard_map/ppermute | solution.py:28
  140.2 33.6 %collective-permute-start.16 = (f32[6,1,128,128]{3,2,1,0:T(8,128)S(1)}, f32[6,1,128,128]{3,2,1,0:T(8,128)S(1)}, u32[]{:S(2)}, u32[]{:S(2)}) collective-permute-start(f32[6,1,128,128]{3,2,1,0:T(8,128)S(1)} %collective-permute-done.15), channel_id=1, source_target_pairs={{0,68},{1,69},{2,70},{3,71},{4,0},{5,1},{6,2},{7,3},{8,76},{9,77},... | collective-permute-start | bytes 1179656 | tf_op jit(solution)/shard_map/ppermute | solution.py:31
  174.0 49.0 %collective-permute-start.22 = (f32[16,128,128]{2,1,0:T(8,128)S(1)}, f32[16,128,128]{2,1,0:T(8,128)S(1)}, u32[]{:S(2)}, u32[]{:S(2)}) collective-permute-start(f32[16,128,128]{2,1,0:T(8,128)S(1)} %bitcast_select_fusion), channel_id=1, source_target_pairs={{0,24},{1,25},{2,26},{3,27},{4,28},{5,29},{6,30},{7,31},{8,0},{9,1... | collective-permute-start | bytes 3145736 | tf_op jit(solution)/shard_map/ppermute | solution.py:82
  178.6 74.4 %collective-permute-start.19 = (f32[12,2,128,128]{3,2,1,0:T(8,128)S(1)}, f32[12,2,128,128]{3,2,1,0:T(8,128)S(1)}, u32[]{:S(2)}, u32[]{:S(2)}) collective-permute-start(f32[12,2,128,128]{3,2,1,0:T(8,128)S(1)} %maximum_maximum_fusion), channel_id=1, source_target_pairs={{0,384},{32,416},{64,448},{96,480},{128,0},{160,32},{192,64},{224,... | collective-permute-start | bytes 4718600 | tf_op jit(solution)/shard_map/ppermute | solution.py:39
  183.0 70.0 %collective-permute-start.18 = (f32[12,2,128,128]{3,2,1,0:T(8,128)S(1)}, f32[12,2,128,128]{3,2,1,0:T(8,128)S(1)}, u32[]{:S(2)}, u32[]{:S(2)}) collective-permute-start(f32[12,2,128,128]{3,2,1,0:T(8,128)S(1)} %maximum_maximum_fusion), channel_id=1, source_target_pairs={{0,256},{32,288},{64,320},{96,352},{128,384},{160,416},{192,448},{... | collective-permute-start | bytes 4718600 | tf_op jit(solution)/shard_map/ppermute | solution.py:39
  185.5 71.0 %collective-permute-start.17 = (f32[12,2,128,128]{3,2,1,0:T(8,128)S(1)}, f32[12,2,128,128]{3,2,1,0:T(8,128)S(1)}, u32[]{:S(2)}, u32[]{:S(2)}) collective-permute-start(f32[12,2,128,128]{3,2,1,0:T(8,128)S(1)} %maximum_maximum_fusion), channel_id=1, source_target_pairs={{0,128},{32,160},{64,192},{96,224},{128,256},{160,288},{192,320},{... | collective-permute-start | bytes 4718600 | tf_op jit(solution)/shard_map/ppermute | solution.py:39
  188.0 36.9 %collective-permute-start.21 = (f32[16,128,128]{2,1,0:T(8,128)S(1)}, f32[16,128,128]{2,1,0:T(8,128)S(1)}, u32[]{:S(2)}, u32[]{:S(2)}) collective-permute-start(f32[16,128,128]{2,1,0:T(8,128)S(1)} %bitcast_select_fusion), channel_id=1, source_target_pairs={{0,16},{1,17},{2,18},{3,19},{4,20},{5,21},{6,22},{7,23},{8,24},{9,... | collective-permute-start | bytes 3145736 | tf_op jit(solution)/shard_map/ppermute | solution.py:82
  223.0 27.6 %collective-permute-start.20 = (f32[16,128,128]{2,1,0:T(8,128)S(1)}, f32[16,128,128]{2,1,0:T(8,128)S(1)}, u32[]{:S(2)}, u32[]{:S(2)}) collective-permute-start(f32[16,128,128]{2,1,0:T(8,128)S(1)} %bitcast_select_fusion), channel_id=1, source_target_pairs={{0,8},{1,9},{2,10},{3,11},{4,12},{5,13},{6,14},{7,15},{8,16},{9,17... | collective-permute-start | bytes 3145736 | tf_op jit(solution)/shard_map/ppermute | solution.py:82
  253.0 8.9 %copy-start.1 = (s32[12,16]{1,0:T(8,128)S(1)}, s32[12,16]{1,0:T(8,128)}, u32[]{:S(2)}) copy-start(s32[12,16]{1,0:T(8,128)} %param.8) | copy-start | bytes 2308
  253.0 8.9 %copy-start.3 = (s32[64]{0:T(128)S(1)}, s32[64]{0:T(128)}, u32[]{:S(2)}) copy-start(s32[64]{0:T(128)} %param.13) | copy-start | bytes 772
  253.0 10.8 %copy-start.2 = (s32[12,4]{0,1:T(4,128)S(1)}, s32[12,4]{0,1:T(4,128)}, u32[]{:S(2)}) copy-start(s32[12,4]{0,1:T(4,128)} %param.12) | copy-start | bytes 580
  253.0 11.0 %copy-start.4 = (s32[64,1]{0,1:T(1,128)S(1)}, s32[64,1]{0,1:T(1,128)}, u32[]{:S(2)}) copy-start(s32[64,1]{0,1:T(1,128)} %param.11) | copy-start | bytes 772
  253.0 11.3 %copy-start.5 = (s32[12]{0:T(128)S(1)}, s32[12]{0:T(128)}, u32[]{:S(2)}) copy-start(s32[12]{0:T(128)} %param.9) | copy-start | bytes 148
  259.4 24.1 %collective-permute-start.23 = (f32[12,8,128,128]{3,2,1,0:T(8,128)}, f32[12,8,128,128]{3,2,1,0:T(8,128)}, u32[]{:S(2)}, u32[]{:S(2)}) collective-permute-start(f32[12,8,128,128]{3,2,1,0:T(8,128)} %pad_maximum_fusion.a_ref), channel_id=1, source_target_pairs={{0,32},{32,0},{64,96},{96,64},{128,160},{160,128},{192,224},{224,1... | collective-permute-start | bytes 18874376 | tf_op jit(solution)/shard_map/ppermute | solution.py:44

commit v8 on v5

--- a/solution.py
+++ b/solution.py
@@ -18,14 +18,14 @@
 
     def swap_z(chunk):
         pairs = [(r, r ^ 2) for r in range(n_row)]
-        return jnp.concatenate([chunk, lax.ppermute(chunk, "row", pairs)], axis=1)
+        return lax.ppermute(chunk, "row", pairs)
 
     def ring_x(held):
         parts = [held]
         for k in range(1, n_x):
             shift = [(r, ((r // 4 + k) % n_x) * 4 + r % 4) for r in range(n_row)]
             parts.append(lax.ppermute(held, "row", shift))
-        return jnp.concatenate(parts, axis=1)
+        return parts
 
     def swap_core(held):
         pairs = [(r, r ^ 1) for r in range(n_row)]
@@ -85,8 +85,10 @@
     per_dev = b_blocks.shape[0]
     swap_z, ring_x, swap_core = row_stages(n_row)
     line_z, ring_y = col_stages(n_col)
-    a_held, b_held = lax.optimization_barrier((swap_z(a_blocks), line_z(b_blocks[:, 0])))
-    a_held, panels = lax.optimization_barrier((ring_x(a_held), ring_y(b_held)))
+    a_own, b_held = lax.optimization_barrier((a_blocks, line_z(b_blocks[:, 0])))
+    a_other, own_x, panels = lax.optimization_barrier((swap_z(a_own), ring_x(a_own), ring_y(b_held)))
+    other_x = ring_x(a_other)
+    a_held = jnp.concatenate([p for pair in zip(own_x, other_x) for p in pair], axis=1)
     rows_here, slot_all = a_cols.shape
     pattern_slots = c_cols.shape[1]
     block_size = panels.shape[-1]

time: 259 us -> 228 us (0.88)
  the two profiles are of different devices: /device:TPU:113 before, /device:TPU:107 now
where the time goes in v8:
time: 228 us; the launch traced here: 227 us
  starting transfers between devices  86.1 us (38%)
  waiting for transfers between devices  84.4 us (37%)
  Pallas kernels  26.8 us (12%)
  local copies, waits for them, and re-layouts  24.9 us (11%)
  other arithmetic  4.4 us (2%)
    ppermute x1, waiting for transfers between devices, swap_z(): return lax.ppermute(chunk, 'row', pairs)  34.4 us
    ppermute x7, starting transfers between devices, line_z(): going_right = lax.ppermute(going_right, 'col', right)  32.1 us
    pallas_call x2, Pallas kernels, row_products(): pl.pallas_call(product_kernel, grid_spec=grid_spec, out_shape=jax.ShapeDt...  26.8 us
    ppermute x6, waiting for transfers between devices, ring_x(): parts.append(lax.ppermute(held, 'row', shift))  26.4 us
    ppermute x3, waiting for transfers between devices, ring_y(): parts.append(lax.ppermute(held, 'col', shift))  23.6 us
    ppermute x6, starting transfers between devices, ring_x(): parts.append(lax.ppermute(held, 'row', shift))  17.7 us
    unnamed x34, local copies, waits for them, and re-layouts  17.1 us
    ppermute x7, starting transfers between devices, line_z(): going_left = lax.ppermute(going_left, 'col', left)  13.4 us
  transfers between devices with their start and end apart: 25, of which 6 were waited for; matrix products, arithmetic and copies ran while one was open for 11% of the time, Pallas kernels for 6%

profile of v8, /device:TPU:107, one launch (start us, length us, event | category | flops | bytes accessed | tf_op | source)
XLA Modules:
  0.0 227.0 jit_solution(8365634200465727159)
XLA Ops:
  0.0 4.7 %collective-permute-start = (f32[2,128,128]{2,1,0:T(8,128)}, f32[2,128,128]{2,1,0:T(8,128)S(1)}, u32[]{:S(2)}, u32[]{:S(2)}) collective-permute-start(f32[2,128,128]{2,1,0:T(8,128)} %bitcast.41), channel_id=1, source_target_pairs={{0,1},{1,2},{2,3},{3,4},{4,5},{5,6},{6,7},{8,9},{9,10},{10,11},{11... | collective-permute-start | bytes 393224 | tf_op jit(solution)/shard_map/ppermute | solution.py:57
  4.8 1.9 collective-permute-start.7
  6.7 1.6 bitcast_dynamic-update-slice_fusion.14
  8.5 4.6 %collective-permute-start.1 = (f32[2,128,128]{2,1,0:T(8,128)S(1)}, f32[2,128,128]{2,1,0:T(8,128)S(1)}, u32[]{:S(2)}, u32[]{:S(2)}) collective-permute-start(f32[2,128,128]{2,1,0:T(8,128)S(1)} %collective-permute-done), channel_id=1, source_target_pairs={{0,1},{1,2},{2,3},{3,4},{4,5},{5,6},{6,7},{8,9},{9,10},{10,11},{11... | collective-permute-start | bytes 393224 | tf_op jit(solution)/shard_map/ppermute | solution.py:57
  13.1 1.9 collective-permute-start.8
  15.0 0.7 bitcast_dynamic-update-slice_fusion.13
  15.7 4.6 %collective-permute-start.2 = (f32[2,128,128]{2,1,0:T(8,128)S(1)}, f32[2,128,128]{2,1,0:T(8,128)S(1)}, u32[]{:S(2)}, u32[]{:S(2)}) collective-permute-start(f32[2,128,128]{2,1,0:T(8,128)S(1)} %collective-permute-done.1), channel_id=1, source_target_pairs={{0,1},{1,2},{2,3},{3,4},{4,5},{5,6},{6,7},{8,9},{9,10},{10,11},{11... | collective-permute-start | bytes 393224 | tf_op jit(solution)/shard_map/ppermute | solution.py:57
  20.2 1.9 collective-permute-start.9
  22.2 0.7 bitcast_dynamic-update-slice_fusion.12
  22.8 4.6 %collective-permute-start.3 = (f32[2,128,128]{2,1,0:T(8,128)S(1)}, f32[2,128,128]{2,1,0:T(8,128)S(1)}, u32[]{:S(2)}, u32[]{:S(2)}) collective-permute-start(f32[2,128,128]{2,1,0:T(8,128)S(1)} %collective-permute-done.2), channel_id=1, source_target_pairs={{0,1},{1,2},{2,3},{3,4},{4,5},{5,6},{6,7},{8,9},{9,10},{10,11},{11... | collective-permute-start | bytes 393224 | tf_op jit(solution)/shard_map/ppermute | solution.py:57
  27.4 1.9 collective-permute-start.10
  29.3 0.7 bitcast_dynamic-update-slice_fusion.11
  30.0 4.6 %collective-permute-start.4 = (f32[2,128,128]{2,1,0:T(8,128)S(1)}, f32[2,128,128]{2,1,0:T(8,128)S(1)}, u32[]{:S(2)}, u32[]{:S(2)}) collective-permute-start(f32[2,128,128]{2,1,0:T(8,128)S(1)} %collective-permute-done.3), channel_id=1, source_target_pairs={{0,1},{1,2},{2,3},{3,4},{4,5},{5,6},{6,7},{8,9},{9,10},{10,11},{11... | collective-permute-start | bytes 393224 | tf_op jit(solution)/shard_map/ppermute | solution.py:57
  34.6 1.9 collective-permute-start.11
  36.5 0.7 bitcast_dynamic-update-slice_fusion.10
  37.2 4.6 %collective-permute-start.5 = (f32[2,128,128]{2,1,0:T(8,128)S(1)}, f32[2,128,128]{2,1,0:T(8,128)S(1)}, u32[]{:S(2)}, u32[]{:S(2)}) collective-permute-start(f32[2,128,128]{2,1,0:T(8,128)S(1)} %collective-permute-done.4), channel_id=1, source_target_pairs={{0,1},{1,2},{2,3},{3,4},{4,5},{5,6},{6,7},{8,9},{9,10},{10,11},{11... | collective-permute-start | bytes 393224 | tf_op jit(solution)/shard_map/ppermute | solution.py:57
  41.8 1.9 collective-permute-start.12
  43.7 0.7 bitcast_dynamic-update-slice_fusion.9
  44.4 4.6 %collective-permute-start.6 = (f32[2,128,128]{2,1,0:T(8,128)S(1)}, f32[2,128,128]{2,1,0:T(8,128)S(1)}, u32[]{:S(2)}, u32[]{:S(2)}) collective-permute-start(f32[2,128,128]{2,1,0:T(8,128)S(1)} %collective-permute-done.5), channel_id=1, source_target_pairs={{0,1},{1,2},{2,3},{3,4},{4,5},{5,6},{6,7},{8,9},{9,10},{10,11},{11... | collective-permute-start | bytes 393224 | tf_op jit(solution)/shard_map/ppermute | solution.py:57
  49.0 1.9 collective-permute-start.13
  50.9 0.7 bitcast_dynamic-update-slice_fusion.8
  51.6 0.7 bitcast_dynamic-update-slice_fusion.7
  52.2 0.7 bitcast_dynamic-update-slice_fusion.6
  52.9 0.7 bitcast_dynamic-update-slice_fusion.5
  53.5 0.7 bitcast_dynamic-update-slice_fusion.4
  54.2 0.7 bitcast_dynamic-update-slice_fusion.3
  54.9 0.7 bitcast_dynamic-update-slice_fusion.2
  55.5 0.7 bitcast_dynamic-update-slice_fusion.1
  56.2 0.7 bitcast_dynamic-update-slice_fusion
  56.9 2.2 gather_fusion.1
  59.3 2.1 collective-permute-start.20
  61.3 4.2 %collective-permute-start.19 = (f32[16,128,128]{2,1,0:T(8,128)S(1)}, f32[16,128,128]{2,1,0:T(8,128)S(1)}, u32[]{:S(2)}, u32[]{:S(2)}) collective-permute-start(f32[16,128,128]{2,1,0:T(8,128)S(1)} %bitcast_select_fusion), channel_id=1, source_target_pairs={{0,16},{1,17},{2,18},{3,19},{4,20},{5,21},{6,22},{7,23},{8,24},{9,... | collective-permute-start | bytes 3145736 | tf_op jit(solution)/shard_map/ppermute | solution.py:70
  65.6 3.5 %collective-permute-start.18 = (f32[16,128,128]{2,1,0:T(8,128)S(1)}, f32[16,128,128]{2,1,0:T(8,128)S(1)}, u32[]{:S(2)}, u32[]{:S(2)}) collective-permute-start(f32[16,128,128]{2,1,0:T(8,128)S(1)} %bitcast_select_fusion), channel_id=1, source_target_pairs={{0,8},{1,9},{2,10},{3,11},{4,12},{5,13},{6,14},{7,15},{8,16},{9,17... | collective-permute-start | bytes 3145736 | tf_op jit(solution)/shard_map/ppermute | solution.py:70
  69.1 10.6 %collective-permute-start.14 = (f32[12,1,128,128]{3,2,1,0:T(8,128)S(1)}, f32[12,1,128,128]{3,2,1,0:T(8,128)S(1)}, u32[]{:S(2)}, u32[]{:S(2)}) collective-permute-start(f32[12,1,128,128]{3,2,1,0:T(8,128)S(1)} %copy-done), channel_id=1, source_target_pairs={{0,64},{32,96},{64,0},{96,32},{128,192},{160,224},{192,128},{224,1... | collective-permute-start | bytes 2359304 | tf_op jit(solution)/shard_map/ppermute | solution.py:21
  79.7 3.1 %collective-permute-start.15 = (f32[12,1,128,128]{3,2,1,0:T(8,128)S(1)}, f32[12,1,128,128]{3,2,1,0:T(8,128)S(1)}, u32[]{:S(2)}, u32[]{:S(2)}) collective-permute-start(f32[12,1,128,128]{3,2,1,0:T(8,128)S(1)} %copy-done), channel_id=1, source_target_pairs={{0,128},{32,160},{64,192},{96,224},{128,256},{160,288},{192,320},{... | collective-permute-start | bytes 2359304 | tf_op jit(solution)/shard_map/ppermute | solution.py:27
  82.9 2.7 %collective-permute-start.16 = (f32[12,1,128,128]{3,2,1,0:T(8,128)S(1)}, f32[12,1,128,128]{3,2,1,0:T(8,128)S(1)}, u32[]{:S(2)}, u32[]{:S(2)}) collective-permute-start(f32[12,1,128,128]{3,2,1,0:T(8,128)S(1)} %copy-done), channel_id=1, source_target_pairs={{0,256},{32,288},{64,320},{96,352},{128,384},{160,416},{192,448},{... | collective-permute-start | bytes 2359304 | tf_op jit(solution)/shard_map/ppermute | solution.py:27
  85.6 16.9 %collective-permute-done.19 = f32[16,128,128]{2,1,0:T(8,128)S(1)} collective-permute-done((f32[16,128,128]{2,1,0:T(8,128)S(1)}, f32[16,128,128]{2,1,0:T(8,128)S(1)}, u32[]{:S(2)}, u32[]{:S(2)}) %collective-permute-start.19) | collective-permute-done | bytes 1048608 | tf_op jit(solution)/shard_map/ppermute | solution.py:70
  102.5 2.2 collective-permute-start.17
  104.7 6.7 %collective-permute-done.18 = f32[16,128,128]{2,1,0:T(8,128)S(1)} collective-permute-done((f32[16,128,128]{2,1,0:T(8,128)S(1)}, f32[16,128,128]{2,1,0:T(8,128)S(1)}, u32[]{:S(2)}, u32[]{:S(2)}) %collective-permute-start.18) | collective-permute-done | bytes 1048608 | tf_op jit(solution)/shard_map/ppermute | solution.py:70
  111.4 2.4 %pad_maximum_fusion.b_ref = f32[64,128,128]{2,1,0:T(8,128)} fusion(f32[16,128,128]{2,1,0:T(8,128)S(1)} %collective-permute-done.20, f32[16,128,128]{2,1,0:T(8,128)S(1)} %collective-permute-done.19, f32[16,128,128]{2,1,0:T(8,128)S(1)} %collective-permute-done.18, f32[16,128,128]{2,1,0:T(8,128)S(1)} %bitcast_select_fusion), kind=kLoop, calls=%fused_computation.2 | loop fusion | flops 3145728 | bytes 8388608 | tf_op jit(solution)/shard_map/concatenate | solution.py:71
  113.8 34.4 %collective-permute-done.14 = f32[12,1,128,128]{3,2,1,0:T(8,128)S(1)} collective-permute-done((f32[12,1,128,128]{3,2,1,0:T(8,128)S(1)}, f32[12,1,128,128]{3,2,1,0:T(8,128)S(1)}, u32[]{:S(2)}, u32[]{:S(2)}) %collective-permute-start.14) | collective-permute-done | bytes 786464 | tf_op jit(solution)/shard_map/ppermute | solution.py:21
  148.2 3.1 %collective-permute-start.21 = (f32[12,1,128,128]{3,2,1,0:T(8,128)S(1)}, f32[12,1,128,128]{3,2,1,0:T(8,128)S(1)}, u32[]{:S(2)}, u32[]{:S(2)}) collective-permute-start(f32[12,1,128,128]{3,2,1,0:T(8,128)S(1)} %collective-permute-done.14), channel_id=1, source_target_pairs={{0,128},{32,160},{64,192},{96,224},{128,256},{160,288},{192,320},{... | collective-permute-start | bytes 2359304 | tf_op jit(solution)/shard_map/ppermute | solution.py:27
  151.3 2.7 %collective-permute-start.22 = (f32[12,1,128,128]{3,2,1,0:T(8,128)S(1)}, f32[12,1,128,128]{3,2,1,0:T(8,128)S(1)}, u32[]{:S(2)}, u32[]{:S(2)}) collective-permute-start(f32[12,1,128,128]{3,2,1,0:T(8,128)S(1)} %collective-permute-done.14), channel_id=1, source_target_pairs={{0,256},{32,288},{64,320},{96,352},{128,384},{160,416},{192,448},{... | collective-permute-start | bytes 2359304 | tf_op jit(solution)/shard_map/ppermute | solution.py:27
  154.1 3.8 %collective-permute-start.23 = (f32[12,1,128,128]{3,2,1,0:T(8,128)S(1)}, f32[12,1,128,128]{3,2,1,0:T(8,128)S(1)}, u32[]{:S(2)}, u32[]{:S(2)}) collective-permute-start(f32[12,1,128,128]{3,2,1,0:T(8,128)S(1)} %collective-permute-done.14), channel_id=1, source_target_pairs={{0,384},{32,416},{64,448},{96,480},{128,0},{160,32},{192,64},{224,... | collective-permute-start | bytes 2359304 | tf_op jit(solution)/shard_map/ppermute | solution.py:27
  157.8 1.0 constant_dynamic-update-slice_fusion.7
  158.8 1.0 constant_dynamic-update-slice_fusion.6
  159.8 1.0 constant_dynamic-update-slice_fusion.5
  160.8 7.8 %collective-permute-done.21 = f32[12,1,128,128]{3,2,1,0:T(8,128)S(1)} collective-permute-done((f32[12,1,128,128]{3,2,1,0:T(8,128)S(1)}, f32[12,1,128,128]{3,2,1,0:T(8,128)S(1)}, u32[]{:S(2)}, u32[]{:S(2)}) %collective-permute-start.21) | collective-permute-done | bytes 786464 | tf_op jit(solution)/shard_map/ppermute | solution.py:27
  168.6 1.0 constant_dynamic-update-slice_fusion.4
  169.6 0.9 constant_dynamic-update-slice_fusion.3
  170.6 2.4 %collective-permute-done.22 = f32[12,1,128,128]{3,2,1,0:T(8,128)S(1)} collective-permute-done((f32[12,1,128,128]{3,2,1,0:T(8,128)S(1)}, f32[12,1,128,128]{3,2,1,0:T(8,128)S(1)}, u32[]{:S(2)}, u32[]{:S(2)}) %collective-permute-start.22) | collective-permute-done | bytes 786464 | tf_op jit(solution)/shard_map/ppermute | solution.py:27
  173.0 0.9 constant_dynamic-update-slice_fusion.2
  173.9 0.9 constant_dynamic-update-slice_fusion.1
  174.9 16.2 %collective-permute-done.23 = f32[12,1,128,128]{3,2,1,0:T(8,128)S(1)} collective-permute-done((f32[12,1,128,128]{3,2,1,0:T(8,128)S(1)}, f32[12,1,128,128]{3,2,1,0:T(8,128)S(1)}, u32[]{:S(2)}, u32[]{:S(2)}) %collective-permute-start.23) | collective-permute-done | bytes 786464 | tf_op jit(solution)/shard_map/ppermute | solution.py:27
  191.0 0.9 constant_dynamic-update-slice_fusion.a_ref
  192.0 2.4 %collective-permute-start.24 = (f32[12,8,128,128]{3,2,1,0:T(8,128)}, f32[12,8,128,128]{3,2,1,0:T(8,128)}, u32[]{:S(2)}, u32[]{:S(2)}) collective-permute-start(f32[12,8,128,128]{3,2,1,0:T(8,128)} %constant_dynamic-update-slice_fusion.a_ref), channel_id=1, source_target_pairs={{0,32},{32,0},{64,96},{96,64},{128,160},{160,128},{192,224},{224,1... | collective-permute-start | bytes 18874376 | tf_op jit(solution)/shard_map/ppermute | solution.py:32
  194.9 0.6 gather_fusion
  195.7 0.7 reshape.328.pidx_ref
  197.2 0.8 convert_reduce_fusion
  198.1 0.6 reshape.329.sidx_ref
  198.8 0.6 reshape.330.pidx_ref
  199.5 0.7 reshape.331.sidx_ref
  200.2 12.8 %shard_map.73.rest_0_ = f32[12,4,128,128]{3,2,1,0:T(8,128)} custom-call(s32[96]{0:T(128)} %reshape.330.pidx_ref, s32[96]{0:T(128)} %reshape.331.sidx_ref, f32[12,8,128,128]{3,2,1,0:T(8,128)} %constant_dynamic-update-slice_fusion.a_ref, f32[64,128,128]{2,1,0:T(8,128)} %pad_maximum_fusion.b_ref), custom_call_target="tpu_custom_call" | custom-call | tf_op jit(solution)/shard_map/pallas_call | solution.py:158
  212.9 14.1 %shard_map.74 = f32[12,4,128,128]{3,2,1,0:T(8,128)} custom-call(s32[96]{0:T(128)} %reshape.328.pidx_ref, s32[96]{0:T(128)} %reshape.329.sidx_ref, f32[12,8,128,128]{3,2,1,0:T(8,128)} %collective-permute-done.24.a_ref, f32[64,128,128]{2,1,0:T(8,128)} %pad_maximum_fusion.b_ref, f32[12,4,128,128]{3,2,1,0:T(8,128)} %shard_map.73.rest_0_), custom_call_target="tpu_custom_call", output_to_operand_aliasing={{}: (4, {})} | custom-call | tf_op jit(solution)/shard_map/pallas_call | solution.py:158
  (57 shorter events, 2.2 us)
Async XLA Ops:
  0.0 8.5 %collective-permute-start = (f32[2,128,128]{2,1,0:T(8,128)}, f32[2,128,128]{2,1,0:T(8,128)S(1)}, u32[]{:S(2)}, u32[]{:S(2)}) collective-permute-start(f32[2,128,128]{2,1,0:T(8,128)} %bitcast.41), channel_id=1, source_target_pairs={{0,1},{1,2},{2,3},{3,4},{4,5},{5,6},{6,7},{8,9},{9,10},{10,11},{11... | collective-permute-start | bytes 393224 | tf_op jit(solution)/shard_map/ppermute | solution.py:57
  4.8 8.3 %collective-permute-start.7 = (f32[2,128,128]{2,1,0:T(8,128)}, f32[2,128,128]{2,1,0:T(8,128)S(1)}, u32[]{:S(2)}, u32[]{:S(2)}) collective-permute-start(f32[2,128,128]{2,1,0:T(8,128)} %bitcast.42), channel_id=1, source_target_pairs={{1,0},{2,1},{3,2},{4,3},{5,4},{6,5},{7,6},{9,8},{10,9},{11,10},{12... | collective-permute-start | bytes 393224 | tf_op jit(solution)/shard_map/ppermute | solution.py:58
  8.5 7.2 %collective-permute-start.1 = (f32[2,128,128]{2,1,0:T(8,128)S(1)}, f32[2,128,128]{2,1,0:T(8,128)S(1)}, u32[]{:S(2)}, u32[]{:S(2)}) collective-permute-start(f32[2,128,128]{2,1,0:T(8,128)S(1)} %collective-permute-done), channel_id=1, source_target_pairs={{0,1},{1,2},{2,3},{3,4},{4,5},{5,6},{6,7},{8,9},{9,10},{10,11},{11... | collective-permute-start | bytes 393224 | tf_op jit(solution)/shard_map/ppermute | solution.py:57
  13.1 7.2 %collective-permute-start.8 = (f32[2,128,128]{2,1,0:T(8,128)S(1)}, f32[2,128,128]{2,1,0:T(8,128)S(1)}, u32[]{:S(2)}, u32[]{:S(2)}) collective-permute-start(f32[2,128,128]{2,1,0:T(8,128)S(1)} %collective-permute-done.7), channel_id=1, source_target_pairs={{1,0},{2,1},{3,2},{4,3},{5,4},{6,5},{7,6},{9,8},{10,9},{11,10},{12... | collective-permute-start | bytes 393224 | tf_op jit(solution)/shard_map/ppermute | solution.py:58
  15.7 7.2 %collective-permute-start.2 = (f32[2,128,128]{2,1,0:T(8,128)S(1)}, f32[2,128,128]{2,1,0:T(8,128)S(1)}, u32[]{:S(2)}, u32[]{:S(2)}) collective-permute-start(f32[2,128,128]{2,1,0:T(8,128)S(1)} %collective-permute-done.1), channel_id=1, source_target_pairs={{0,1},{1,2},{2,3},{3,4},{4,5},{5,6},{6,7},{8,9},{9,10},{10,11},{11... | collective-permute-start | bytes 393224 | tf_op jit(solution)/shard_map/ppermute | solution.py:57
  20.2 7.2 %collective-permute-start.9 = (f32[2,128,128]{2,1,0:T(8,128)S(1)}, f32[2,128,128]{2,1,0:T(8,128)S(1)}, u32[]{:S(2)}, u32[]{:S(2)}) collective-permute-start(f32[2,128,128]{2,1,0:T(8,128)S(1)} %collective-permute-done.8), channel_id=1, source_target_pairs={{1,0},{2,1},{3,2},{4,3},{5,4},{6,5},{7,6},{9,8},{10,9},{11,10},{12... | collective-permute-start | bytes 393224 | tf_op jit(solution)/shard_map/ppermute | solution.py:58
  22.8 7.2 %collective-permute-start.3 = (f32[2,128,128]{2,1,0:T(8,128)S(1)}, f32[2,128,128]{2,1,0:T(8,128)S(1)}, u32[]{:S(2)}, u32[]{:S(2)}) collective-permute-start(f32[2,128,128]{2,1,0:T(8,128)S(1)} %collective-permute-done.2), channel_id=1, source_target_pairs={{0,1},{1,2},{2,3},{3,4},{4,5},{5,6},{6,7},{8,9},{9,10},{10,11},{11... | collective-permute-start | bytes 393224 | tf_op jit(solution)/shard_map/ppermute | solution.py:57
  27.4 7.2 %collective-permute-start.10 = (f32[2,128,128]{2,1,0:T(8,128)S(1)}, f32[2,128,128]{2,1,0:T(8,128)S(1)}, u32[]{:S(2)}, u32[]{:S(2)}) collective-permute-start(f32[2,128,128]{2,1,0:T(8,128)S(1)} %collective-permute-done.9), channel_id=1, source_target_pairs={{1,0},{2,1},{3,2},{4,3},{5,4},{6,5},{7,6},{9,8},{10,9},{11,10},{12... | collective-permute-start | bytes 393224 | tf_op jit(solution)/shard_map/ppermute | solution.py:58
  30.0 7.2 %collective-permute-start.4 = (f32[2,128,128]{2,1,0:T(8,128)S(1)}, f32[2,128,128]{2,1,0:T(8,128)S(1)}, u32[]{:S(2)}, u32[]{:S(2)}) collective-permute-start(f32[2,128,128]{2,1,0:T(8,128)S(1)} %collective-permute-done.3), channel_id=1, source_target_pairs={{0,1},{1,2},{2,3},{3,4},{4,5},{5,6},{6,7},{8,9},{9,10},{10,11},{11... | collective-permute-start | bytes 393224 | tf_op jit(solution)/shard_map/ppermute | solution.py:57
  34.6 7.2 %collective-permute-start.11 = (f32[2,128,128]{2,1,0:T(8,128)S(1)}, f32[2,128,128]{2,1,0:T(8,128)S(1)}, u32[]{:S(2)}, u32[]{:S(2)}) collective-permute-start(f32[2,128,128]{2,1,0:T(8,128)S(1)} %collective-permute-done.10), channel_id=1, source_target_pairs={{1,0},{2,1},{3,2},{4,3},{5,4},{6,5},{7,6},{9,8},{10,9},{11,10},{12... | collective-permute-start | bytes 393224 | tf_op jit(solution)/shard_map/ppermute | solution.py:58
  37.2 7.2 %collective-permute-start.5 = (f32[2,128,128]{2,1,0:T(8,128)S(1)}, f32[2,128,128]{2,1,0:T(8,128)S(1)}, u32[]{:S(2)}, u32[]{:S(2)}) collective-permute-start(f32[2,128,128]{2,1,0:T(8,128)S(1)} %collective-permute-done.4), channel_id=1, source_target_pairs={{0,1},{1,2},{2,3},{3,4},{4,5},{5,6},{6,7},{8,9},{9,10},{10,11},{11... | collective-permute-start | bytes 393224 | tf_op jit(solution)/shard_map/ppermute | solution.py:57
  41.8 7.2 %collective-permute-start.12 = (f32[2,128,128]{2,1,0:T(8,128)S(1)}, f32[2,128,128]{2,1,0:T(8,128)S(1)}, u32[]{:S(2)}, u32[]{:S(2)}) collective-permute-start(f32[2,128,128]{2,1,0:T(8,128)S(1)} %collective-permute-done.11), channel_id=1, source_target_pairs={{1,0},{2,1},{3,2},{4,3},{5,4},{6,5},{7,6},{9,8},{10,9},{11,10},{12... | collective-permute-start | bytes 393224 | tf_op jit(solution)/shard_map/ppermute | solution.py:58
  44.4 7.2 %collective-permute-start.6 = (f32[2,128,128]{2,1,0:T(8,128)S(1)}, f32[2,128,128]{2,1,0:T(8,128)S(1)}, u32[]{:S(2)}, u32[]{:S(2)}) collective-permute-start(f32[2,128,128]{2,1,0:T(8,128)S(1)} %collective-permute-done.5), channel_id=1, source_target_pairs={{0,1},{1,2},{2,3},{3,4},{4,5},{5,6},{6,7},{8,9},{9,10},{10,11},{11... | collective-permute-start | bytes 393224 | tf_op jit(solution)/shard_map/ppermute | solution.py:57
  49.0 7.3 %collective-permute-start.13 = (f32[2,128,128]{2,1,0:T(8,128)S(1)}, f32[2,128,128]{2,1,0:T(8,128)S(1)}, u32[]{:S(2)}, u32[]{:S(2)}) collective-permute-start(f32[2,128,128]{2,1,0:T(8,128)S(1)} %collective-permute-done.12), channel_id=1, source_target_pairs={{1,0},{2,1},{3,2},{4,3},{5,4},{6,5},{7,6},{9,8},{10,9},{11,10},{12... | collective-permute-start | bytes 393224 | tf_op jit(solution)/shard_map/ppermute | solution.py:58
  56.9 12.2 %copy-start = (f32[12,1,128,128]{3,2,1,0:T(8,128)S(1)}, f32[12,1,128,128]{3,2,1,0:T(8,128)}, u32[]{:S(2)}) copy-start(f32[12,1,128,128]{3,2,1,0:T(8,128)} %param.7) | copy-start | bytes 2359300
  59.3 23.6 %collective-permute-start.20 = (f32[16,128,128]{2,1,0:T(8,128)S(1)}, f32[16,128,128]{2,1,0:T(8,128)S(1)}, u32[]{:S(2)}, u32[]{:S(2)}) collective-permute-start(f32[16,128,128]{2,1,0:T(8,128)S(1)} %bitcast_select_fusion), channel_id=1, source_target_pairs={{0,24},{1,25},{2,26},{3,27},{4,28},{5,29},{6,30},{7,31},{8,0},{9,1... | collective-permute-start | bytes 3145736 | tf_op jit(solution)/shard_map/ppermute | solution.py:70
  61.3 41.2 %collective-permute-start.19 = (f32[16,128,128]{2,1,0:T(8,128)S(1)}, f32[16,128,128]{2,1,0:T(8,128)S(1)}, u32[]{:S(2)}, u32[]{:S(2)}) collective-permute-start(f32[16,128,128]{2,1,0:T(8,128)S(1)} %bitcast_select_fusion), channel_id=1, source_target_pairs={{0,16},{1,17},{2,18},{3,19},{4,20},{5,21},{6,22},{7,23},{8,24},{9,... | collective-permute-start | bytes 3145736 | tf_op jit(solution)/shard_map/ppermute | solution.py:70
  65.6 45.8 %collective-permute-start.18 = (f32[16,128,128]{2,1,0:T(8,128)S(1)}, f32[16,128,128]{2,1,0:T(8,128)S(1)}, u32[]{:S(2)}, u32[]{:S(2)}) collective-permute-start(f32[16,128,128]{2,1,0:T(8,128)S(1)} %bitcast_select_fusion), channel_id=1, source_target_pairs={{0,8},{1,9},{2,10},{3,11},{4,12},{5,13},{6,14},{7,15},{8,16},{9,17... | collective-permute-start | bytes 3145736 | tf_op jit(solution)/shard_map/ppermute | solution.py:70
  69.1 79.1 %collective-permute-start.14 = (f32[12,1,128,128]{3,2,1,0:T(8,128)S(1)}, f32[12,1,128,128]{3,2,1,0:T(8,128)S(1)}, u32[]{:S(2)}, u32[]{:S(2)}) collective-permute-start(f32[12,1,128,128]{3,2,1,0:T(8,128)S(1)} %copy-done), channel_id=1, source_target_pairs={{0,64},{32,96},{64,0},{96,32},{128,192},{160,224},{192,128},{224,1... | collective-permute-start | bytes 2359304 | tf_op jit(solution)/shard_map/ppermute | solution.py:21
  79.7 68.4 %collective-permute-start.15 = (f32[12,1,128,128]{3,2,1,0:T(8,128)S(1)}, f32[12,1,128,128]{3,2,1,0:T(8,128)S(1)}, u32[]{:S(2)}, u32[]{:S(2)}) collective-permute-start(f32[12,1,128,128]{3,2,1,0:T(8,128)S(1)} %copy-done), channel_id=1, source_target_pairs={{0,128},{32,160},{64,192},{96,224},{128,256},{160,288},{192,320},{... | collective-permute-start | bytes 2359304 | tf_op jit(solution)/shard_map/ppermute | solution.py:27
  82.9 65.3 %collective-permute-start.16 = (f32[12,1,128,128]{3,2,1,0:T(8,128)S(1)}, f32[12,1,128,128]{3,2,1,0:T(8,128)S(1)}, u32[]{:S(2)}, u32[]{:S(2)}) collective-permute-start(f32[12,1,128,128]{3,2,1,0:T(8,128)S(1)} %copy-done), channel_id=1, source_target_pairs={{0,256},{32,288},{64,320},{96,352},{128,384},{160,416},{192,448},{... | collective-permute-start | bytes 2359304 | tf_op jit(solution)/shard_map/ppermute | solution.py:27
  102.5 45.6 %collective-permute-start.17 = (f32[12,1,128,128]{3,2,1,0:T(8,128)S(1)}, f32[12,1,128,128]{3,2,1,0:T(8,128)S(1)}, u32[]{:S(2)}, u32[]{:S(2)}) collective-permute-start(f32[12,1,128,128]{3,2,1,0:T(8,128)S(1)} %copy-done), channel_id=1, source_target_pairs={{0,384},{32,416},{64,448},{96,480},{128,0},{160,32},{192,64},{224,... | collective-permute-start | bytes 2359304 | tf_op jit(solution)/shard_map/ppermute | solution.py:27
  148.2 20.4 %collective-permute-start.21 = (f32[12,1,128,128]{3,2,1,0:T(8,128)S(1)}, f32[12,1,128,128]{3,2,1,0:T(8,128)S(1)}, u32[]{:S(2)}, u32[]{:S(2)}) collective-permute-start(f32[12,1,128,128]{3,2,1,0:T(8,128)S(1)} %collective-permute-done.14), channel_id=1, source_target_pairs={{0,128},{32,160},{64,192},{96,224},{128,256},{160,288},{192,320},{... | collective-permute-start | bytes 2359304 | tf_op jit(solution)/shard_map/ppermute | solution.py:27
  151.3 21.7 %collective-permute-start.22 = (f32[12,1,128,128]{3,2,1,0:T(8,128)S(1)}, f32[12,1,128,128]{3,2,1,0:T(8,128)S(1)}, u32[]{:S(2)}, u32[]{:S(2)}) collective-permute-start(f32[12,1,128,128]{3,2,1,0:T(8,128)S(1)} %collective-permute-done.14), channel_id=1, source_target_pairs={{0,256},{32,288},{64,320},{96,352},{128,384},{160,416},{192,448},{... | collective-permute-start | bytes 2359304 | tf_op jit(solution)/shard_map/ppermute | solution.py:27
  154.1 37.0 %collective-permute-start.23 = (f32[12,1,128,128]{3,2,1,0:T(8,128)S(1)}, f32[12,1,128,128]{3,2,1,0:T(8,128)S(1)}, u32[]{:S(2)}, u32[]{:S(2)}) collective-permute-start(f32[12,1,128,128]{3,2,1,0:T(8,128)S(1)} %collective-permute-done.14), channel_id=1, source_target_pairs={{0,384},{32,416},{64,448},{96,480},{128,0},{160,32},{192,64},{224,... | collective-permute-start | bytes 2359304 | tf_op jit(solution)/shard_map/ppermute | solution.py:27
  173.9 20.5 %copy-start.1 = (s32[12,16]{1,0:T(8,128)S(1)}, s32[12,16]{1,0:T(8,128)}, u32[]{:S(2)}) copy-start(s32[12,16]{1,0:T(8,128)} %param.8) | copy-start | bytes 2308
  173.9 20.5 %copy-start.3 = (s32[64]{0:T(128)S(1)}, s32[64]{0:T(128)}, u32[]{:S(2)}) copy-start(s32[64]{0:T(128)} %param.13) | copy-start | bytes 772
  173.9 22.4 %copy-start.2 = (s32[12,4]{0,1:T(4,128)S(1)}, s32[12,4]{0,1:T(4,128)}, u32[]{:S(2)}) copy-start(s32[12,4]{0,1:T(4,128)} %param.12) | copy-start | bytes 580
  173.9 22.6 %copy-start.4 = (s32[64,1]{0,1:T(1,128)S(1)}, s32[64,1]{0,1:T(1,128)}, u32[]{:S(2)}) copy-start(s32[64,1]{0,1:T(1,128)} %param.11) | copy-start | bytes 772
  173.9 23.0 %copy-start.5 = (s32[12]{0:T(128)S(1)}, s32[12]{0:T(128)}, u32[]{:S(2)}) copy-start(s32[12]{0:T(128)} %param.9) | copy-start | bytes 148
  192.0 21.0 %collective-permute-start.24 = (f32[12,8,128,128]{3,2,1,0:T(8,128)}, f32[12,8,128,128]{3,2,1,0:T(8,128)}, u32[]{:S(2)}, u32[]{:S(2)}) collective-permute-start(f32[12,8,128,128]{3,2,1,0:T(8,128)} %constant_dynamic-update-slice_fusion.a_ref), channel_id=1, source_target_pairs={{0,32},{32,0},{64,96},{96,64},{128,160},{160,128},{192,224},{224,1... | collective-permute-start | bytes 18874376 | tf_op jit(solution)/shard_map/ppermute | solution.py:32

commit v9 on v8

--- a/solution.py
+++ b/solution.py
@@ -85,8 +85,8 @@
     per_dev = b_blocks.shape[0]
     swap_z, ring_x, swap_core = row_stages(n_row)
     line_z, ring_y = col_stages(n_col)
-    a_own, b_held = lax.optimization_barrier((a_blocks, line_z(b_blocks[:, 0])))
-    a_other, own_x, panels = lax.optimization_barrier((swap_z(a_own), ring_x(a_own), ring_y(b_held)))
+    a_own, own_x, b_held = lax.optimization_barrier((a_blocks, ring_x(a_blocks), line_z(b_blocks[:, 0])))
+    a_other, panels = lax.optimization_barrier((swap_z(a_own), ring_y(b_held)))
     other_x = ring_x(a_other)
     a_held = jnp.concatenate([p for pair in zip(own_x, other_x) for p in pair], axis=1)
     rows_here, slot_all = a_cols.shape

time: 228 us -> 238 us (1.044)
  the two profiles are of different devices: /device:TPU:107 before, /device:TPU:97 now
where the time goes in v9:
time: 238 us; the launch traced here: 236 us
  waiting for transfers between devices  92.8 us (39%)
  starting transfers between devices  88.2 us (37%)
  local copies, waits for them, and re-layouts  26 us (11%)
  Pallas kernels  24.5 us (10%)
  other arithmetic  4.4 us (2%)
    ppermute x3, waiting for transfers between devices, ring_y(): parts.append(lax.ppermute(held, 'col', shift))  35.4 us
    ppermute x7, starting transfers between devices, line_z(): going_right = lax.ppermute(going_right, 'col', right)  32.2 us
    ppermute x1, waiting for transfers between devices, swap_z(): return lax.ppermute(chunk, 'row', pairs)  31.4 us
    ppermute x6, waiting for transfers between devices, ring_x(): parts.append(lax.ppermute(held, 'row', shift))  25.8 us
    pallas_call x2, Pallas kernels, row_products(): pl.pallas_call(product_kernel, grid_spec=grid_spec, out_shape=jax.ShapeDt...  24.5 us
    ppermute x6, starting transfers between devices, ring_x(): parts.append(lax.ppermute(held, 'row', shift))  19.1 us
    unnamed x34, local copies, waits for them, and re-layouts  18.2 us
    ppermute x7, starting transfers between devices, line_z(): going_left = lax.ppermute(going_left, 'col', left)  13.4 us
  transfers between devices with their start and end apart: 25, of which 6 were waited for; matrix products, arithmetic and copies ran while one was open for 12% of the time, Pallas kernels for 5%

profile of v9, /device:TPU:97, one launch (start us, length us, event | category | flops | bytes accessed | tf_op | source)
XLA Modules:
  0.0 236.4 jit_solution(18434266621364309478)
XLA Ops:
  0.0 3.1 %collective-permute-start = (f32[12,1,128,128]{3,2,1,0:T(8,128)}, f32[12,1,128,128]{3,2,1,0:T(8,128)}, u32[]{:S(2)}, u32[]{:S(2)}) collective-permute-start(f32[12,1,128,128]{3,2,1,0:T(8,128)} %param.7), channel_id=1, source_target_pairs={{0,128},{32,160},{64,192},{96,224},{128,256},{160,288},{192,320},{... | collective-permute-start | bytes 2359304 | tf_op jit(solution)/shard_map/ppermute | solution.py:27
  3.1 4.4 %collective-permute-start.1 = (f32[12,1,128,128]{3,2,1,0:T(8,128)}, f32[12,1,128,128]{3,2,1,0:T(8,128)S(1)}, u32[]{:S(2)}, u32[]{:S(2)}) collective-permute-start(f32[12,1,128,128]{3,2,1,0:T(8,128)} %param.7), channel_id=1, source_target_pairs={{0,256},{32,288},{64,320},{96,352},{128,384},{160,416},{192,448},{... | collective-permute-start | bytes 2359304 | tf_op jit(solution)/shard_map/ppermute | solution.py:27
  7.5 3.1 %collective-permute-start.2 = (f32[12,1,128,128]{3,2,1,0:T(8,128)}, f32[12,1,128,128]{3,2,1,0:T(8,128)S(1)}, u32[]{:S(2)}, u32[]{:S(2)}) collective-permute-start(f32[12,1,128,128]{3,2,1,0:T(8,128)} %param.7), channel_id=1, source_target_pairs={{0,384},{32,416},{64,448},{96,480},{128,0},{160,32},{192,64},{224,... | collective-permute-start | bytes 2359304 | tf_op jit(solution)/shard_map/ppermute | solution.py:27
  10.6 4.8 %collective-permute-start.3 = (f32[2,128,128]{2,1,0:T(8,128)}, f32[2,128,128]{2,1,0:T(8,128)S(1)}, u32[]{:S(2)}, u32[]{:S(2)}) collective-permute-start(f32[2,128,128]{2,1,0:T(8,128)} %bitcast.41), channel_id=1, source_target_pairs={{0,1},{1,2},{2,3},{3,4},{4,5},{5,6},{6,7},{8,9},{9,10},{10,11},{11... | collective-permute-start | bytes 393224 | tf_op jit(solution)/shard_map/ppermute | solution.py:57
  15.3 1.9 collective-permute-start.10
  17.3 1.6 bitcast_dynamic-update-slice_fusion.14
  19.0 4.6 %collective-permute-start.4 = (f32[2,128,128]{2,1,0:T(8,128)S(1)}, f32[2,128,128]{2,1,0:T(8,128)S(1)}, u32[]{:S(2)}, u32[]{:S(2)}) collective-permute-start(f32[2,128,128]{2,1,0:T(8,128)S(1)} %collective-permute-done.3), channel_id=1, source_target_pairs={{0,1},{1,2},{2,3},{3,4},{4,5},{5,6},{6,7},{8,9},{9,10},{10,11},{11... | collective-permute-start | bytes 393224 | tf_op jit(solution)/shard_map/ppermute | solution.py:57
  23.6 1.9 collective-permute-start.11
  25.6 0.7 bitcast_dynamic-update-slice_fusion.13
  26.2 4.6 %collective-permute-start.5 = (f32[2,128,128]{2,1,0:T(8,128)S(1)}, f32[2,128,128]{2,1,0:T(8,128)S(1)}, u32[]{:S(2)}, u32[]{:S(2)}) collective-permute-start(f32[2,128,128]{2,1,0:T(8,128)S(1)} %collective-permute-done.4), channel_id=1, source_target_pairs={{0,1},{1,2},{2,3},{3,4},{4,5},{5,6},{6,7},{8,9},{9,10},{10,11},{11... | collective-permute-start | bytes 393224 | tf_op jit(solution)/shard_map/ppermute | solution.py:57
  30.8 1.9 collective-permute-start.12
  32.8 0.7 bitcast_dynamic-update-slice_fusion.12
  33.4 4.6 %collective-permute-start.6 = (f32[2,128,128]{2,1,0:T(8,128)S(1)}, f32[2,128,128]{2,1,0:T(8,128)S(1)}, u32[]{:S(2)}, u32[]{:S(2)}) collective-permute-start(f32[2,128,128]{2,1,0:T(8,128)S(1)} %collective-permute-done.5), channel_id=1, source_target_pairs={{0,1},{1,2},{2,3},{3,4},{4,5},{5,6},{6,7},{8,9},{9,10},{10,11},{11... | collective-permute-start | bytes 393224 | tf_op jit(solution)/shard_map/ppermute | solution.py:57
  38.0 1.9 collective-permute-start.13
  40.0 0.7 bitcast_dynamic-update-slice_fusion.11
  40.6 4.6 %collective-permute-start.7 = (f32[2,128,128]{2,1,0:T(8,128)S(1)}, f32[2,128,128]{2,1,0:T(8,128)S(1)}, u32[]{:S(2)}, u32[]{:S(2)}) collective-permute-start(f32[2,128,128]{2,1,0:T(8,128)S(1)} %collective-permute-done.6), channel_id=1, source_target_pairs={{0,1},{1,2},{2,3},{3,4},{4,5},{5,6},{6,7},{8,9},{9,10},{10,11},{11... | collective-permute-start | bytes 393224 | tf_op jit(solution)/shard_map/ppermute | solution.py:57
  45.2 1.9 collective-permute-start.14
  47.2 0.7 bitcast_dynamic-update-slice_fusion.10
  47.8 4.6 %collective-permute-start.8 = (f32[2,128,128]{2,1,0:T(8,128)S(1)}, f32[2,128,128]{2,1,0:T(8,128)S(1)}, u32[]{:S(2)}, u32[]{:S(2)}) collective-permute-start(f32[2,128,128]{2,1,0:T(8,128)S(1)} %collective-permute-done.7), channel_id=1, source_target_pairs={{0,1},{1,2},{2,3},{3,4},{4,5},{5,6},{6,7},{8,9},{9,10},{10,11},{11... | collective-permute-start | bytes 393224 | tf_op jit(solution)/shard_map/ppermute | solution.py:57
  52.4 1.9 collective-permute-start.15
  54.4 0.7 bitcast_dynamic-update-slice_fusion.9
  55.0 4.6 %collective-permute-start.9 = (f32[2,128,128]{2,1,0:T(8,128)S(1)}, f32[2,128,128]{2,1,0:T(8,128)S(1)}, u32[]{:S(2)}, u32[]{:S(2)}) collective-permute-start(f32[2,128,128]{2,1,0:T(8,128)S(1)} %collective-permute-done.8), channel_id=1, source_target_pairs={{0,1},{1,2},{2,3},{3,4},{4,5},{5,6},{6,7},{8,9},{9,10},{10,11},{11... | collective-permute-start | bytes 393224 | tf_op jit(solution)/shard_map/ppermute | solution.py:57
  59.6 1.9 collective-permute-start.16
  61.5 0.7 bitcast_dynamic-update-slice_fusion.8
  62.2 0.7 bitcast_dynamic-update-slice_fusion.7
  62.9 0.7 bitcast_dynamic-update-slice_fusion.6
  63.5 0.7 bitcast_dynamic-update-slice_fusion.5
  64.2 0.7 bitcast_dynamic-update-slice_fusion.4
  64.9 0.7 bitcast_dynamic-update-slice_fusion.3
  65.5 0.7 bitcast_dynamic-update-slice_fusion.2
  66.2 0.7 bitcast_dynamic-update-slice_fusion.1
  67.0 0.7 bitcast_dynamic-update-slice_fusion
  67.7 2.2 gather_fusion.1
  70.1 4.6 %collective-permute-start.20 = (f32[16,128,128]{2,1,0:T(8,128)S(1)}, f32[16,128,128]{2,1,0:T(8,128)S(1)}, u32[]{:S(2)}, u32[]{:S(2)}) collective-permute-start(f32[16,128,128]{2,1,0:T(8,128)S(1)} %bitcast_select_fusion), channel_id=1, source_target_pairs={{0,24},{1,25},{2,26},{3,27},{4,28},{5,29},{6,30},{7,31},{8,0},{9,1... | collective-permute-start | bytes 3145736 | tf_op jit(solution)/shard_map/ppermute | solution.py:70
  74.7 2.3 collective-permute-start.19
  77.0 2.6 %collective-permute-start.18 = (f32[16,128,128]{2,1,0:T(8,128)S(1)}, f32[16,128,128]{2,1,0:T(8,128)S(1)}, u32[]{:S(2)}, u32[]{:S(2)}) collective-permute-start(f32[16,128,128]{2,1,0:T(8,128)S(1)} %bitcast_select_fusion), channel_id=1, source_target_pairs={{0,8},{1,9},{2,10},{3,11},{4,12},{5,13},{6,14},{7,15},{8,16},{9,17... | collective-permute-start | bytes 3145736 | tf_op jit(solution)/shard_map/ppermute | solution.py:70
  79.6 10.6 %collective-permute-start.17 = (f32[12,1,128,128]{3,2,1,0:T(8,128)S(1)}, f32[12,1,128,128]{3,2,1,0:T(8,128)S(1)}, u32[]{:S(2)}, u32[]{:S(2)}) collective-permute-start(f32[12,1,128,128]{3,2,1,0:T(8,128)S(1)} %copy-done), channel_id=1, source_target_pairs={{0,64},{32,96},{64,0},{96,32},{128,192},{160,224},{192,128},{224,1... | collective-permute-start | bytes 2359304 | tf_op jit(solution)/shard_map/ppermute | solution.py:21
  90.4 4.4 %collective-permute-done.19 = f32[16,128,128]{2,1,0:T(8,128)S(1)} collective-permute-done((f32[16,128,128]{2,1,0:T(8,128)S(1)}, f32[16,128,128]{2,1,0:T(8,128)S(1)}, u32[]{:S(2)}, u32[]{:S(2)}) %collective-permute-start.19) | collective-permute-done | bytes 1048608 | tf_op jit(solution)/shard_map/ppermute | solution.py:70
  94.8 30.9 %collective-permute-done.18 = f32[16,128,128]{2,1,0:T(8,128)S(1)} collective-permute-done((f32[16,128,128]{2,1,0:T(8,128)S(1)}, f32[16,128,128]{2,1,0:T(8,128)S(1)}, u32[]{:S(2)}, u32[]{:S(2)}) %collective-permute-start.18) | collective-permute-done | bytes 1048608 | tf_op jit(solution)/shard_map/ppermute | solution.py:70
  125.7 2.4 %pad_maximum_fusion.b_ref = f32[64,128,128]{2,1,0:T(8,128)} fusion(f32[16,128,128]{2,1,0:T(8,128)S(1)} %collective-permute-done.20, f32[16,128,128]{2,1,0:T(8,128)S(1)} %collective-permute-done.19, f32[16,128,128]{2,1,0:T(8,128)S(1)} %collective-permute-done.18, f32[16,128,128]{2,1,0:T(8,128)S(1)} %bitcast_select_fusion), kind=kLoop, calls=%fused_computation.2 | loop fusion | flops 3145728 | bytes 8388608 | tf_op jit(solution)/shard_map/concatenate | solution.py:71
  128.1 31.4 %collective-permute-done.17 = f32[12,1,128,128]{3,2,1,0:T(8,128)S(1)} collective-permute-done((f32[12,1,128,128]{3,2,1,0:T(8,128)S(1)}, f32[12,1,128,128]{3,2,1,0:T(8,128)S(1)}, u32[]{:S(2)}, u32[]{:S(2)}) %collective-permute-start.17) | collective-permute-done | bytes 786464 | tf_op jit(solution)/shard_map/ppermute | solution.py:21
  159.5 2.4 %collective-permute-start.21 = (f32[12,1,128,128]{3,2,1,0:T(8,128)S(1)}, f32[12,1,128,128]{3,2,1,0:T(8,128)S(1)}, u32[]{:S(2)}, u32[]{:S(2)}) collective-permute-start(f32[12,1,128,128]{3,2,1,0:T(8,128)S(1)} %collective-permute-done.17), channel_id=1, source_target_pairs={{0,128},{32,160},{64,192},{96,224},{128,256},{160,288},{192,320},{... | collective-permute-start | bytes 2359304 | tf_op jit(solution)/shard_map/ppermute | solution.py:27
  161.9 2.1 collective-permute-start.22
  164.1 1.0 constant_dynamic-update-slice_fusion.7
  165.1 4.1 %collective-permute-start.23 = (f32[12,1,128,128]{3,2,1,0:T(8,128)S(1)}, f32[12,1,128,128]{3,2,1,0:T(8,128)S(1)}, u32[]{:S(2)}, u32[]{:S(2)}) collective-permute-start(f32[12,1,128,128]{3,2,1,0:T(8,128)S(1)} %collective-permute-done.17), channel_id=1, source_target_pairs={{0,384},{32,416},{64,448},{96,480},{128,0},{160,32},{192,64},{224,... | collective-permute-start | bytes 2359304 | tf_op jit(solution)/shard_map/ppermute | solution.py:27
  169.1 1.0 constant_dynamic-update-slice_fusion.6
  170.1 2.1 constant_dynamic-update-slice_fusion.5
  172.3 25.7 %collective-permute-done.21 = f32[12,1,128,128]{3,2,1,0:T(8,128)S(1)} collective-permute-done((f32[12,1,128,128]{3,2,1,0:T(8,128)S(1)}, f32[12,1,128,128]{3,2,1,0:T(8,128)S(1)}, u32[]{:S(2)}, u32[]{:S(2)}) %collective-permute-start.21) | collective-permute-done | bytes 786464 | tf_op jit(solution)/shard_map/ppermute | solution.py:27
  198.0 1.0 constant_dynamic-update-slice_fusion.4
  199.0 0.9 constant_dynamic-update-slice_fusion.3
  199.9 0.9 constant_dynamic-update-slice_fusion.2
  200.9 0.9 constant_dynamic-update-slice_fusion.1
  201.8 0.9 constant_dynamic-update-slice_fusion.a_ref
  202.8 3.3 %collective-permute-start.24 = (f32[12,8,128,128]{3,2,1,0:T(8,128)}, f32[12,8,128,128]{3,2,1,0:T(8,128)}, u32[]{:S(2)}, u32[]{:S(2)}) collective-permute-start(f32[12,8,128,128]{3,2,1,0:T(8,128)} %constant_dynamic-update-slice_fusion.a_ref), channel_id=1, source_target_pairs={{0,32},{32,0},{64,96},{96,64},{128,160},{160,128},{192,224},{224,1... | collective-permute-start | bytes 18874376 | tf_op jit(solution)/shard_map/ppermute | solution.py:32
  206.1 0.4 select_reduce_fusion.1
  206.6 0.6 gather_fusion
  207.4 0.7 reshape.328.pidx_ref
  208.2 0.4 select_reduce_fusion
  208.9 0.8 convert_reduce_fusion
  209.8 0.6 reshape.329.sidx_ref
  210.5 0.6 reshape.330.pidx_ref
  211.2 0.7 reshape.331.sidx_ref
  211.9 12.3 %shard_map.73.rest_0_ = f32[12,4,128,128]{3,2,1,0:T(8,128)} custom-call(s32[96]{0:T(128)} %reshape.330.pidx_ref, s32[96]{0:T(128)} %reshape.331.sidx_ref, f32[12,8,128,128]{3,2,1,0:T(8,128)} %constant_dynamic-update-slice_fusion.a_ref, f32[64,128,128]{2,1,0:T(8,128)} %pad_maximum_fusion.b_ref), custom_call_target="tpu_custom_call" | custom-call | tf_op jit(solution)/shard_map/pallas_call | solution.py:158
  224.1 12.3 %shard_map.74 = f32[12,4,128,128]{3,2,1,0:T(8,128)} custom-call(s32[96]{0:T(128)} %reshape.328.pidx_ref, s32[96]{0:T(128)} %reshape.329.sidx_ref, f32[12,8,128,128]{3,2,1,0:T(8,128)} %collective-permute-done.24.a_ref, f32[64,128,128]{2,1,0:T(8,128)} %pad_maximum_fusion.b_ref, f32[12,4,128,128]{3,2,1,0:T(8,128)} %shard_map.73.rest_0_), custom_call_target="tpu_custom_call", output_to_operand_aliasing={{}: (4, {})} | custom-call | tf_op jit(solution)/shard_map/pallas_call | solution.py:158
  (57 shorter events, 1.8 us)
Async XLA Ops:
  0.0 70.1 %collective-permute-start = (f32[12,1,128,128]{3,2,1,0:T(8,128)}, f32[12,1,128,128]{3,2,1,0:T(8,128)}, u32[]{:S(2)}, u32[]{:S(2)}) collective-permute-start(f32[12,1,128,128]{3,2,1,0:T(8,128)} %param.7), channel_id=1, source_target_pairs={{0,128},{32,160},{64,192},{96,224},{128,256},{160,288},{192,320},{... | collective-permute-start | bytes 2359304 | tf_op jit(solution)/shard_map/ppermute | solution.py:27
  3.1 67.0 %collective-permute-start.1 = (f32[12,1,128,128]{3,2,1,0:T(8,128)}, f32[12,1,128,128]{3,2,1,0:T(8,128)S(1)}, u32[]{:S(2)}, u32[]{:S(2)}) collective-permute-start(f32[12,1,128,128]{3,2,1,0:T(8,128)} %param.7), channel_id=1, source_target_pairs={{0,256},{32,288},{64,320},{96,352},{128,384},{160,416},{192,448},{... | collective-permute-start | bytes 2359304 | tf_op jit(solution)/shard_map/ppermute | solution.py:27
  7.5 62.6 %collective-permute-start.2 = (f32[12,1,128,128]{3,2,1,0:T(8,128)}, f32[12,1,128,128]{3,2,1,0:T(8,128)S(1)}, u32[]{:S(2)}, u32[]{:S(2)}) collective-permute-start(f32[12,1,128,128]{3,2,1,0:T(8,128)} %param.7), channel_id=1, source_target_pairs={{0,384},{32,416},{64,448},{96,480},{128,0},{160,32},{192,64},{224,... | collective-permute-start | bytes 2359304 | tf_op jit(solution)/shard_map/ppermute | solution.py:27
  10.6 8.5 %collective-permute-start.3 = (f32[2,128,128]{2,1,0:T(8,128)}, f32[2,128,128]{2,1,0:T(8,128)S(1)}, u32[]{:S(2)}, u32[]{:S(2)}) collective-permute-start(f32[2,128,128]{2,1,0:T(8,128)} %bitcast.41), channel_id=1, source_target_pairs={{0,1},{1,2},{2,3},{3,4},{4,5},{5,6},{6,7},{8,9},{9,10},{10,11},{11... | collective-permute-start | bytes 393224 | tf_op jit(solution)/shard_map/ppermute | solution.py:57
  15.3 8.3 %collective-permute-start.10 = (f32[2,128,128]{2,1,0:T(8,128)}, f32[2,128,128]{2,1,0:T(8,128)S(1)}, u32[]{:S(2)}, u32[]{:S(2)}) collective-permute-start(f32[2,128,128]{2,1,0:T(8,128)} %bitcast.42), channel_id=1, source_target_pairs={{1,0},{2,1},{3,2},{4,3},{5,4},{6,5},{7,6},{9,8},{10,9},{11,10},{12... | collective-permute-start | bytes 393224 | tf_op jit(solution)/shard_map/ppermute | solution.py:58
  19.0 7.2 %collective-permute-start.4 = (f32[2,128,128]{2,1,0:T(8,128)S(1)}, f32[2,128,128]{2,1,0:T(8,128)S(1)}, u32[]{:S(2)}, u32[]{:S(2)}) collective-permute-start(f32[2,128,128]{2,1,0:T(8,128)S(1)} %collective-permute-done.3), channel_id=1, source_target_pairs={{0,1},{1,2},{2,3},{3,4},{4,5},{5,6},{6,7},{8,9},{9,10},{10,11},{11... | collective-permute-start | bytes 393224 | tf_op jit(solution)/shard_map/ppermute | solution.py:57
  23.6 7.2 %collective-permute-start.11 = (f32[2,128,128]{2,1,0:T(8,128)S(1)}, f32[2,128,128]{2,1,0:T(8,128)S(1)}, u32[]{:S(2)}, u32[]{:S(2)}) collective-permute-start(f32[2,128,128]{2,1,0:T(8,128)S(1)} %collective-permute-done.10), channel_id=1, source_target_pairs={{1,0},{2,1},{3,2},{4,3},{5,4},{6,5},{7,6},{9,8},{10,9},{11,10},{12... | collective-permute-start | bytes 393224 | tf_op jit(solution)/shard_map/ppermute | solution.py:58
  26.2 7.2 %collective-permute-start.5 = (f32[2,128,128]{2,1,0:T(8,128)S(1)}, f32[2,128,128]{2,1,0:T(8,128)S(1)}, u32[]{:S(2)}, u32[]{:S(2)}) collective-permute-start(f32[2,128,128]{2,1,0:T(8,128)S(1)} %collective-permute-done.4), channel_id=1, source_target_pairs={{0,1},{1,2},{2,3},{3,4},{4,5},{5,6},{6,7},{8,9},{9,10},{10,11},{11... | collective-permute-start | bytes 393224 | tf_op jit(solution)/shard_map/ppermute | solution.py:57
  30.8 7.2 %collective-permute-start.12 = (f32[2,128,128]{2,1,0:T(8,128)S(1)}, f32[2,128,128]{2,1,0:T(8,128)S(1)}, u32[]{:S(2)}, u32[]{:S(2)}) collective-permute-start(f32[2,128,128]{2,1,0:T(8,128)S(1)} %collective-permute-done.11), channel_id=1, source_target_pairs={{1,0},{2,1},{3,2},{4,3},{5,4},{6,5},{7,6},{9,8},{10,9},{11,10},{12... | collective-permute-start | bytes 393224 | tf_op jit(solution)/shard_map/ppermute | solution.py:58
  33.4 7.2 %collective-permute-start.6 = (f32[2,128,128]{2,1,0:T(8,128)S(1)}, f32[2,128,128]{2,1,0:T(8,128)S(1)}, u32[]{:S(2)}, u32[]{:S(2)}) collective-permute-start(f32[2,128,128]{2,1,0:T(8,128)S(1)} %collective-permute-done.5), channel_id=1, source_target_pairs={{0,1},{1,2},{2,3},{3,4},{4,5},{5,6},{6,7},{8,9},{9,10},{10,11},{11... | collective-permute-start | bytes 393224 | tf_op jit(solution)/shard_map/ppermute | solution.py:57
  38.0 7.2 %collective-permute-start.13 = (f32[2,128,128]{2,1,0:T(8,128)S(1)}, f32[2,128,128]{2,1,0:T(8,128)S(1)}, u32[]{:S(2)}, u32[]{:S(2)}) collective-permute-start(f32[2,128,128]{2,1,0:T(8,128)S(1)} %collective-permute-done.12), channel_id=1, source_target_pairs={{1,0},{2,1},{3,2},{4,3},{5,4},{6,5},{7,6},{9,8},{10,9},{11,10},{12... | collective-permute-start | bytes 393224 | tf_op jit(solution)/shard_map/ppermute | solution.py:58
  40.6 7.2 %collective-permute-start.7 = (f32[2,128,128]{2,1,0:T(8,128)S(1)}, f32[2,128,128]{2,1,0:T(8,128)S(1)}, u32[]{:S(2)}, u32[]{:S(2)}) collective-permute-start(f32[2,128,128]{2,1,0:T(8,128)S(1)} %collective-permute-done.6), channel_id=1, source_target_pairs={{0,1},{1,2},{2,3},{3,4},{4,5},{5,6},{6,7},{8,9},{9,10},{10,11},{11... | collective-permute-start | bytes 393224 | tf_op jit(solution)/shard_map/ppermute | solution.py:57
  45.2 7.2 %collective-permute-start.14 = (f32[2,128,128]{2,1,0:T(8,128)S(1)}, f32[2,128,128]{2,1,0:T(8,128)S(1)}, u32[]{:S(2)}, u32[]{:S(2)}) collective-permute-start(f32[2,128,128]{2,1,0:T(8,128)S(1)} %collective-permute-done.13), channel_id=1, source_target_pairs={{1,0},{2,1},{3,2},{4,3},{5,4},{6,5},{7,6},{9,8},{10,9},{11,10},{12... | collective-permute-start | bytes 393224 | tf_op jit(solution)/shard_map/ppermute | solution.py:58
  47.8 7.2 %collective-permute-start.8 = (f32[2,128,128]{2,1,0:T(8,128)S(1)}, f32[2,128,128]{2,1,0:T(8,128)S(1)}, u32[]{:S(2)}, u32[]{:S(2)}) collective-permute-start(f32[2,128,128]{2,1,0:T(8,128)S(1)} %collective-permute-done.7), channel_id=1, source_target_pairs={{0,1},{1,2},{2,3},{3,4},{4,5},{5,6},{6,7},{8,9},{9,10},{10,11},{11... | collective-permute-start | bytes 393224 | tf_op jit(solution)/shard_map/ppermute | solution.py:57
  52.4 7.2 %collective-permute-start.15 = (f32[2,128,128]{2,1,0:T(8,128)S(1)}, f32[2,128,128]{2,1,0:T(8,128)S(1)}, u32[]{:S(2)}, u32[]{:S(2)}) collective-permute-start(f32[2,128,128]{2,1,0:T(8,128)S(1)} %collective-permute-done.14), channel_id=1, source_target_pairs={{1,0},{2,1},{3,2},{4,3},{5,4},{6,5},{7,6},{9,8},{10,9},{11,10},{12... | collective-permute-start | bytes 393224 | tf_op jit(solution)/shard_map/ppermute | solution.py:58
  55.0 7.2 %collective-permute-start.9 = (f32[2,128,128]{2,1,0:T(8,128)S(1)}, f32[2,128,128]{2,1,0:T(8,128)S(1)}, u32[]{:S(2)}, u32[]{:S(2)}) collective-permute-start(f32[2,128,128]{2,1,0:T(8,128)S(1)} %collective-permute-done.8), channel_id=1, source_target_pairs={{0,1},{1,2},{2,3},{3,4},{4,5},{5,6},{6,7},{8,9},{9,10},{10,11},{11... | collective-permute-start | bytes 393224 | tf_op jit(solution)/shard_map/ppermute | solution.py:57
  59.6 7.4 %collective-permute-start.16 = (f32[2,128,128]{2,1,0:T(8,128)S(1)}, f32[2,128,128]{2,1,0:T(8,128)S(1)}, u32[]{:S(2)}, u32[]{:S(2)}) collective-permute-start(f32[2,128,128]{2,1,0:T(8,128)S(1)} %collective-permute-done.15), channel_id=1, source_target_pairs={{1,0},{2,1},{3,2},{4,3},{5,4},{6,5},{7,6},{9,8},{10,9},{11,10},{12... | collective-permute-start | bytes 393224 | tf_op jit(solution)/shard_map/ppermute | solution.py:58
  67.7 11.9 %copy-start = (f32[12,1,128,128]{3,2,1,0:T(8,128)S(1)}, f32[12,1,128,128]{3,2,1,0:T(8,128)}, u32[]{:S(2)}) copy-start(f32[12,1,128,128]{3,2,1,0:T(8,128)} %param.7) | copy-start | bytes 2359300
  70.1 20.3 %collective-permute-start.20 = (f32[16,128,128]{2,1,0:T(8,128)S(1)}, f32[16,128,128]{2,1,0:T(8,128)S(1)}, u32[]{:S(2)}, u32[]{:S(2)}) collective-permute-start(f32[16,128,128]{2,1,0:T(8,128)S(1)} %bitcast_select_fusion), channel_id=1, source_target_pairs={{0,24},{1,25},{2,26},{3,27},{4,28},{5,29},{6,30},{7,31},{8,0},{9,1... | collective-permute-start | bytes 3145736 | tf_op jit(solution)/shard_map/ppermute | solution.py:70
  74.7 20.0 %collective-permute-start.19 = (f32[16,128,128]{2,1,0:T(8,128)S(1)}, f32[16,128,128]{2,1,0:T(8,128)S(1)}, u32[]{:S(2)}, u32[]{:S(2)}) collective-permute-start(f32[16,128,128]{2,1,0:T(8,128)S(1)} %bitcast_select_fusion), channel_id=1, source_target_pairs={{0,16},{1,17},{2,18},{3,19},{4,20},{5,21},{6,22},{7,23},{8,24},{9,... | collective-permute-start | bytes 3145736 | tf_op jit(solution)/shard_map/ppermute | solution.py:70
  77.0 48.7 %collective-permute-start.18 = (f32[16,128,128]{2,1,0:T(8,128)S(1)}, f32[16,128,128]{2,1,0:T(8,128)S(1)}, u32[]{:S(2)}, u32[]{:S(2)}) collective-permute-start(f32[16,128,128]{2,1,0:T(8,128)S(1)} %bitcast_select_fusion), channel_id=1, source_target_pairs={{0,8},{1,9},{2,10},{3,11},{4,12},{5,13},{6,14},{7,15},{8,16},{9,17... | collective-permute-start | bytes 3145736 | tf_op jit(solution)/shard_map/ppermute | solution.py:70
  79.6 79.9 %collective-permute-start.17 = (f32[12,1,128,128]{3,2,1,0:T(8,128)S(1)}, f32[12,1,128,128]{3,2,1,0:T(8,128)S(1)}, u32[]{:S(2)}, u32[]{:S(2)}) collective-permute-start(f32[12,1,128,128]{3,2,1,0:T(8,128)S(1)} %copy-done), channel_id=1, source_target_pairs={{0,64},{32,96},{64,0},{96,32},{128,192},{160,224},{192,128},{224,1... | collective-permute-start | bytes 2359304 | tf_op jit(solution)/shard_map/ppermute | solution.py:21
  159.5 38.5 %collective-permute-start.21 = (f32[12,1,128,128]{3,2,1,0:T(8,128)S(1)}, f32[12,1,128,128]{3,2,1,0:T(8,128)S(1)}, u32[]{:S(2)}, u32[]{:S(2)}) collective-permute-start(f32[12,1,128,128]{3,2,1,0:T(8,128)S(1)} %collective-permute-done.17), channel_id=1, source_target_pairs={{0,128},{32,160},{64,192},{96,224},{128,256},{160,288},{192,320},{... | collective-permute-start | bytes 2359304 | tf_op jit(solution)/shard_map/ppermute | solution.py:27
  161.9 38.0 %collective-permute-start.22 = (f32[12,1,128,128]{3,2,1,0:T(8,128)S(1)}, f32[12,1,128,128]{3,2,1,0:T(8,128)S(1)}, u32[]{:S(2)}, u32[]{:S(2)}) collective-permute-start(f32[12,1,128,128]{3,2,1,0:T(8,128)S(1)} %collective-permute-done.17), channel_id=1, source_target_pairs={{0,256},{32,288},{64,320},{96,352},{128,384},{160,416},{192,448},{... | collective-permute-start | bytes 2359304 | tf_op jit(solution)/shard_map/ppermute | solution.py:27
  165.1 36.8 %collective-permute-start.23 = (f32[12,1,128,128]{3,2,1,0:T(8,128)S(1)}, f32[12,1,128,128]{3,2,1,0:T(8,128)S(1)}, u32[]{:S(2)}, u32[]{:S(2)}) collective-permute-start(f32[12,1,128,128]{3,2,1,0:T(8,128)S(1)} %collective-permute-done.17), channel_id=1, source_target_pairs={{0,384},{32,416},{64,448},{96,480},{128,0},{160,32},{192,64},{224,... | collective-permute-start | bytes 2359304 | tf_op jit(solution)/shard_map/ppermute | solution.py:27
  200.9 5.3 %copy-start.1 = (s32[12,16]{1,0:T(8,128)S(1)}, s32[12,16]{1,0:T(8,128)}, u32[]{:S(2)}) copy-start(s32[12,16]{1,0:T(8,128)} %param.8) | copy-start | bytes 2308
  200.9 5.3 %copy-start.3 = (s32[64]{0:T(128)S(1)}, s32[64]{0:T(128)}, u32[]{:S(2)}) copy-start(s32[64]{0:T(128)} %param.13) | copy-start | bytes 772
  200.9 7.2 %copy-start.2 = (s32[12,4]{0,1:T(4,128)S(1)}, s32[12,4]{0,1:T(4,128)}, u32[]{:S(2)}) copy-start(s32[12,4]{0,1:T(4,128)} %param.12) | copy-start | bytes 580
  200.9 7.4 %copy-start.4 = (s32[64,1]{0,1:T(1,128)S(1)}, s32[64,1]{0,1:T(1,128)}, u32[]{:S(2)}) copy-start(s32[64,1]{0,1:T(1,128)} %param.11) | copy-start | bytes 772
  200.9 7.7 %copy-start.5 = (s32[12]{0:T(128)S(1)}, s32[12]{0:T(128)}, u32[]{:S(2)}) copy-start(s32[12]{0:T(128)} %param.9) | copy-start | bytes 148
  202.8 21.4 %collective-permute-start.24 = (f32[12,8,128,128]{3,2,1,0:T(8,128)}, f32[12,8,128,128]{3,2,1,0:T(8,128)}, u32[]{:S(2)}, u32[]{:S(2)}) collective-permute-start(f32[12,8,128,128]{3,2,1,0:T(8,128)} %constant_dynamic-update-slice_fusion.a_ref), channel_id=1, source_target_pairs={{0,32},{32,0},{64,96},{96,64},{128,160},{160,128},{192,224},{224,1... | collective-permute-start | bytes 18874376 | tf_op jit(solution)/shard_map/ppermute | solution.py:32

commit v10 on v8

--- a/solution.py
+++ b/solution.py
@@ -103,10 +103,16 @@
     target = jnp.where(jnp.any(weights > 0, axis=-1), jnp.argmax(weights, axis=-1), -1)
     target = target.astype(jnp.int32)
     half = a_held.shape[1]
-    mine = row_products(a_held, panels, panel_index[:, :half].reshape(-1),
-                        target[:, :half].reshape(-1), pattern_slots)
-    return row_products(swap_core(a_held), panels, panel_index[:, half:].reshape(-1),
-                        target[:, half:].reshape(-1), pattern_slots, mine)
+
+    def products(slots, held_ids, acc=None):
+        ids = jnp.array(held_ids, dtype=jnp.int32)
+        return row_products(slots, panels, panel_index[:, ids].reshape(-1),
+                            target[:, ids].reshape(-1), pattern_slots, acc)
+
+    out = products(jnp.concatenate(own_x, axis=1), list(range(0, half, 2)))
+    a_held, out = lax.optimization_barrier((a_held, out))
+    out = products(jnp.concatenate(other_x, axis=1), list(range(1, half, 2)), out)
+    return products(swap_core(a_held), list(range(half, 2 * half)), out)
 
 
 def split_dot(a, b):

time: 228 us -> 235 us (1.031)
  the two profiles are of different devices: /device:TPU:107 before, /device:TPU:449 now
where the time goes in v10:
time: 235 us; the launch traced here: 233 us
  starting transfers between devices  80.1 us (34%)
  waiting for transfers between devices  63.2 us (27%)
  Pallas kernels  41 us (17%)
  local copies, waits for them, and re-layouts  35.3 us (15%)
  other arithmetic  13.1 us (6%)
    pallas_call x3, Pallas kernels, row_products(): pl.pallas_call(product_kernel, grid_spec=grid_spec, out_shape=jax.ShapeDt...  41 us
    ppermute x1, waiting for transfers between devices, swap_z(): return lax.ppermute(chunk, 'row', pairs)  31.3 us
    ppermute x3, waiting for transfers between devices, ring_y(): parts.append(lax.ppermute(held, 'col', shift))  26.6 us
    ppermute x7, starting transfers between devices, line_z(): going_left = lax.ppermute(going_left, 'col', left)  25.2 us
    ppermute x6, starting transfers between devices, ring_x(): parts.append(lax.ppermute(held, 'row', shift))  22.5 us
    unnamed x38, local copies, waits for them, and re-layouts  21.7 us
    ppermute x7, starting transfers between devices, line_z(): going_right = lax.ppermute(going_right, 'col', right)  16.3 us
    ppermute x3, starting transfers between devices, ring_y(): parts.append(lax.ppermute(held, 'col', shift))  9.5 us
  transfers between devices with their start and end apart: 25, of which 4 were waited for; matrix products, arithmetic and copies ran while one was open for 19% of the time, Pallas kernels for 11%

profile of v10, /device:TPU:449, one launch (start us, length us, event | category | flops | bytes accessed | tf_op | source)
XLA Modules:
  0.0 233.2 jit_solution(6997833875002361553)
XLA Ops:
  0.0 2.6 %collective-permute-start = (f32[2,128,128]{2,1,0:T(8,128)}, f32[2,128,128]{2,1,0:T(8,128)S(1)}, u32[]{:S(2)}, u32[]{:S(2)}) collective-permute-start(f32[2,128,128]{2,1,0:T(8,128)} %bitcast.47), channel_id=1, source_target_pairs={{0,1},{1,2},{2,3},{3,4},{4,5},{5,6},{6,7},{8,9},{9,10},{10,11},{11... | collective-permute-start | bytes 393224 | tf_op jit(solution)/shard_map/ppermute | solution.py:57
  2.6 2.6 %collective-permute-start.7 = (f32[2,128,128]{2,1,0:T(8,128)}, f32[2,128,128]{2,1,0:T(8,128)S(1)}, u32[]{:S(2)}, u32[]{:S(2)}) collective-permute-start(f32[2,128,128]{2,1,0:T(8,128)} %bitcast.48), channel_id=1, source_target_pairs={{1,0},{2,1},{3,2},{4,3},{5,4},{6,5},{7,6},{9,8},{10,9},{11,10},{12... | collective-permute-start | bytes 393224 | tf_op jit(solution)/shard_map/ppermute | solution.py:58
  5.3 1.6 bitcast_dynamic-update-slice_fusion.14
  7.1 2.6 %collective-permute-start.1 = (f32[2,128,128]{2,1,0:T(8,128)S(1)}, f32[2,128,128]{2,1,0:T(8,128)S(1)}, u32[]{:S(2)}, u32[]{:S(2)}) collective-permute-start(f32[2,128,128]{2,1,0:T(8,128)S(1)} %collective-permute-done), channel_id=1, source_target_pairs={{0,1},{1,2},{2,3},{3,4},{4,5},{5,6},{6,7},{8,9},{9,10},{10,11},{11... | collective-permute-start | bytes 393224 | tf_op jit(solution)/shard_map/ppermute | solution.py:57
  9.7 2.6 %collective-permute-start.8 = (f32[2,128,128]{2,1,0:T(8,128)S(1)}, f32[2,128,128]{2,1,0:T(8,128)S(1)}, u32[]{:S(2)}, u32[]{:S(2)}) collective-permute-start(f32[2,128,128]{2,1,0:T(8,128)S(1)} %collective-permute-done.7), channel_id=1, source_target_pairs={{1,0},{2,1},{3,2},{4,3},{5,4},{6,5},{7,6},{9,8},{10,9},{11,10},{12... | collective-permute-start | bytes 393224 | tf_op jit(solution)/shard_map/ppermute | solution.py:58
  12.4 0.7 bitcast_dynamic-update-slice_fusion.13
  13.0 2.6 %collective-permute-start.2 = (f32[2,128,128]{2,1,0:T(8,128)S(1)}, f32[2,128,128]{2,1,0:T(8,128)S(1)}, u32[]{:S(2)}, u32[]{:S(2)}) collective-permute-start(f32[2,128,128]{2,1,0:T(8,128)S(1)} %collective-permute-done.1), channel_id=1, source_target_pairs={{0,1},{1,2},{2,3},{3,4},{4,5},{5,6},{6,7},{8,9},{9,10},{10,11},{11... | collective-permute-start | bytes 393224 | tf_op jit(solution)/shard_map/ppermute | solution.py:57
  15.7 2.6 %collective-permute-start.9 = (f32[2,128,128]{2,1,0:T(8,128)S(1)}, f32[2,128,128]{2,1,0:T(8,128)S(1)}, u32[]{:S(2)}, u32[]{:S(2)}) collective-permute-start(f32[2,128,128]{2,1,0:T(8,128)S(1)} %collective-permute-done.8), channel_id=1, source_target_pairs={{1,0},{2,1},{3,2},{4,3},{5,4},{6,5},{7,6},{9,8},{10,9},{11,10},{12... | collective-permute-start | bytes 393224 | tf_op jit(solution)/shard_map/ppermute | solution.py:58
  18.3 0.7 bitcast_dynamic-update-slice_fusion.12
  19.0 2.6 %collective-permute-start.3 = (f32[2,128,128]{2,1,0:T(8,128)S(1)}, f32[2,128,128]{2,1,0:T(8,128)S(1)}, u32[]{:S(2)}, u32[]{:S(2)}) collective-permute-start(f32[2,128,128]{2,1,0:T(8,128)S(1)} %collective-permute-done.2), channel_id=1, source_target_pairs={{0,1},{1,2},{2,3},{3,4},{4,5},{5,6},{6,7},{8,9},{9,10},{10,11},{11... | collective-permute-start | bytes 393224 | tf_op jit(solution)/shard_map/ppermute | solution.py:57
  21.7 3.6 %collective-permute-start.10 = (f32[2,128,128]{2,1,0:T(8,128)S(1)}, f32[2,128,128]{2,1,0:T(8,128)S(1)}, u32[]{:S(2)}, u32[]{:S(2)}) collective-permute-start(f32[2,128,128]{2,1,0:T(8,128)S(1)} %collective-permute-done.9), channel_id=1, source_target_pairs={{1,0},{2,1},{3,2},{4,3},{5,4},{6,5},{7,6},{9,8},{10,9},{11,10},{12... | collective-permute-start | bytes 393224 | tf_op jit(solution)/shard_map/ppermute | solution.py:58
  25.3 0.7 bitcast_dynamic-update-slice_fusion.11
  26.0 1.9 collective-permute-start.4
  27.9 4.6 %collective-permute-start.11 = (f32[2,128,128]{2,1,0:T(8,128)S(1)}, f32[2,128,128]{2,1,0:T(8,128)S(1)}, u32[]{:S(2)}, u32[]{:S(2)}) collective-permute-start(f32[2,128,128]{2,1,0:T(8,128)S(1)} %collective-permute-done.10), channel_id=1, source_target_pairs={{1,0},{2,1},{3,2},{4,3},{5,4},{6,5},{7,6},{9,8},{10,9},{11,10},{12... | collective-permute-start | bytes 393224 | tf_op jit(solution)/shard_map/ppermute | solution.py:58
  32.5 0.7 bitcast_dynamic-update-slice_fusion.10
  33.1 1.9 collective-permute-start.5
  35.1 4.6 %collective-permute-start.12 = (f32[2,128,128]{2,1,0:T(8,128)S(1)}, f32[2,128,128]{2,1,0:T(8,128)S(1)}, u32[]{:S(2)}, u32[]{:S(2)}) collective-permute-start(f32[2,128,128]{2,1,0:T(8,128)S(1)} %collective-permute-done.11), channel_id=1, source_target_pairs={{1,0},{2,1},{3,2},{4,3},{5,4},{6,5},{7,6},{9,8},{10,9},{11,10},{12... | collective-permute-start | bytes 393224 | tf_op jit(solution)/shard_map/ppermute | solution.py:58
  39.6 0.7 bitcast_dynamic-update-slice_fusion.9
  40.3 1.9 collective-permute-start.6
  42.2 4.6 %collective-permute-start.13 = (f32[2,128,128]{2,1,0:T(8,128)S(1)}, f32[2,128,128]{2,1,0:T(8,128)S(1)}, u32[]{:S(2)}, u32[]{:S(2)}) collective-permute-start(f32[2,128,128]{2,1,0:T(8,128)S(1)} %collective-permute-done.12), channel_id=1, source_target_pairs={{1,0},{2,1},{3,2},{4,3},{5,4},{6,5},{7,6},{9,8},{10,9},{11,10},{12... | collective-permute-start | bytes 393224 | tf_op jit(solution)/shard_map/ppermute | solution.py:58
  46.8 0.7 bitcast_dynamic-update-slice_fusion.8
  47.5 0.7 bitcast_dynamic-update-slice_fusion.7
  48.2 0.7 bitcast_dynamic-update-slice_fusion.6
  48.9 0.7 bitcast_dynamic-update-slice_fusion.5
  49.5 0.7 bitcast_dynamic-update-slice_fusion.4
  50.2 0.7 bitcast_dynamic-update-slice_fusion.3
  50.9 0.7 bitcast_dynamic-update-slice_fusion.2
  51.5 0.7 bitcast_dynamic-update-slice_fusion.1
  52.2 0.7 bitcast_dynamic-update-slice_fusion
  52.9 2.2 gather_fusion.3
  55.2 4.6 %collective-permute-start.20 = (f32[16,128,128]{2,1,0:T(8,128)S(1)}, f32[16,128,128]{2,1,0:T(8,128)}, u32[]{:S(2)}, u32[]{:S(2)}) collective-permute-start(f32[16,128,128]{2,1,0:T(8,128)S(1)} %bitcast_select_fusion), channel_id=1, source_target_pairs={{0,24},{1,25},{2,26},{3,27},{4,28},{5,29},{6,30},{7,31},{8,0},{9,1... | collective-permute-start | bytes 3145736 | tf_op jit(solution)/shard_map/ppermute | solution.py:70
  59.8 2.3 collective-permute-start.19
  63.2 2.6 %collective-permute-start.18 = (f32[16,128,128]{2,1,0:T(8,128)S(1)}, f32[16,128,128]{2,1,0:T(8,128)}, u32[]{:S(2)}, u32[]{:S(2)}) collective-permute-start(f32[16,128,128]{2,1,0:T(8,128)S(1)} %bitcast_select_fusion), channel_id=1, source_target_pairs={{0,8},{1,9},{2,10},{3,11},{4,12},{5,13},{6,14},{7,15},{8,16},{9,17... | collective-permute-start | bytes 3145736 | tf_op jit(solution)/shard_map/ppermute | solution.py:70
  66.1 3.4 %collective-permute-start.14 = (f32[12,1,128,128]{3,2,1,0:T(8,128)S(1)}, f32[12,1,128,128]{3,2,1,0:T(8,128)S(1)}, u32[]{:S(2)}, u32[]{:S(2)}) collective-permute-start(f32[12,1,128,128]{3,2,1,0:T(8,128)S(1)} %copy-done), channel_id=1, source_target_pairs={{0,64},{32,96},{64,0},{96,32},{128,192},{160,224},{192,128},{224,1... | collective-permute-start | bytes 2359304 | tf_op jit(solution)/shard_map/ppermute | solution.py:21
  69.5 3.1 %collective-permute-start.15 = (f32[12,1,128,128]{3,2,1,0:T(8,128)S(1)}, f32[12,1,128,128]{3,2,1,0:T(8,128)}, u32[]{:S(2)}, u32[]{:S(2)}) collective-permute-start(f32[12,1,128,128]{3,2,1,0:T(8,128)S(1)} %copy-done), channel_id=1, source_target_pairs={{0,128},{32,160},{64,192},{96,224},{128,256},{160,288},{192,320},{... | collective-permute-start | bytes 2359304 | tf_op jit(solution)/shard_map/ppermute | solution.py:27
  72.6 4.7 %collective-permute-done.20 = f32[16,128,128]{2,1,0:T(8,128)} collective-permute-done((f32[16,128,128]{2,1,0:T(8,128)S(1)}, f32[16,128,128]{2,1,0:T(8,128)}, u32[]{:S(2)}, u32[]{:S(2)}) %collective-permute-start.20) | collective-permute-done | bytes 1048608 | tf_op jit(solution)/shard_map/ppermute | solution.py:70
  77.3 4.6 %collective-permute-start.16 = (f32[12,1,128,128]{3,2,1,0:T(8,128)S(1)}, f32[12,1,128,128]{3,2,1,0:T(8,128)}, u32[]{:S(2)}, u32[]{:S(2)}) collective-permute-start(f32[12,1,128,128]{3,2,1,0:T(8,128)S(1)} %copy-done), channel_id=1, source_target_pairs={{0,256},{32,288},{64,320},{96,352},{128,384},{160,416},{192,448},{... | collective-permute-start | bytes 2359304 | tf_op jit(solution)/shard_map/ppermute | solution.py:27
  82.0 4.2 %collective-permute-start.17 = (f32[12,1,128,128]{3,2,1,0:T(8,128)S(1)}, f32[12,1,128,128]{3,2,1,0:T(8,128)}, u32[]{:S(2)}, u32[]{:S(2)}) collective-permute-start(f32[12,1,128,128]{3,2,1,0:T(8,128)S(1)} %copy-done), channel_id=1, source_target_pairs={{0,384},{32,416},{64,448},{96,480},{128,0},{160,32},{192,64},{224,... | collective-permute-start | bytes 2359304 | tf_op jit(solution)/shard_map/ppermute | solution.py:27
  86.9 0.8 convert_reduce_fusion
  88.4 0.6 reshape.336.pidx_ref
  89.0 21.9 %collective-permute-done.18 = f32[16,128,128]{2,1,0:T(8,128)} collective-permute-done((f32[16,128,128]{2,1,0:T(8,128)S(1)}, f32[16,128,128]{2,1,0:T(8,128)}, u32[]{:S(2)}, u32[]{:S(2)}) %collective-permute-start.18) | collective-permute-done | bytes 1048608 | tf_op jit(solution)/shard_map/ppermute | solution.py:70
  110.9 4.2 %pad_maximum_fusion.b_ref = f32[64,128,128]{2,1,0:T(8,128)} fusion(f32[16,128,128]{2,1,0:T(8,128)} %collective-permute-done.20, f32[16,128,128]{2,1,0:T(8,128)} %collective-permute-done.19, f32[16,128,128]{2,1,0:T(8,128)} %collective-permute-done.18, f32[16,128,128]{2,1,0:T(8,128)S(1)} %bitcast_select_fusion), kind=kLoop, calls=%fused_computation.8 | loop fusion | flops 3145728 | bytes 8388608 | tf_op jit(solution)/shard_map/concatenate | solution.py:71
  115.1 31.3 %collective-permute-done.14 = f32[12,1,128,128]{3,2,1,0:T(8,128)S(1)} collective-permute-done((f32[12,1,128,128]{3,2,1,0:T(8,128)S(1)}, f32[12,1,128,128]{3,2,1,0:T(8,128)S(1)}, u32[]{:S(2)}, u32[]{:S(2)}) %collective-permute-start.14) | collective-permute-done | bytes 786464 | tf_op jit(solution)/shard_map/ppermute | solution.py:21
  146.4 3.1 %collective-permute-start.21 = (f32[12,1,128,128]{3,2,1,0:T(8,128)S(1)}, f32[12,1,128,128]{3,2,1,0:T(8,128)S(1)}, u32[]{:S(2)}, u32[]{:S(2)}) collective-permute-start(f32[12,1,128,128]{3,2,1,0:T(8,128)S(1)} %collective-permute-done.14), channel_id=1, source_target_pairs={{0,128},{32,160},{64,192},{96,224},{128,256},{160,288},{192,320},{... | collective-permute-start | bytes 2359304 | tf_op jit(solution)/shard_map/ppermute | solution.py:27
  150.2 0.7 reshape.337.sidx_ref
  150.9 4.3 %collective-permute-start.22 = (f32[12,1,128,128]{3,2,1,0:T(8,128)S(1)}, f32[12,1,128,128]{3,2,1,0:T(8,128)}, u32[]{:S(2)}, u32[]{:S(2)}) collective-permute-start(f32[12,1,128,128]{3,2,1,0:T(8,128)S(1)} %collective-permute-done.14), channel_id=1, source_target_pairs={{0,256},{32,288},{64,320},{96,352},{128,384},{160,416},{192,448},{... | collective-permute-start | bytes 2359304 | tf_op jit(solution)/shard_map/ppermute | solution.py:27
  155.2 3.1 %collective-permute-start.23 = (f32[12,1,128,128]{3,2,1,0:T(8,128)S(1)}, f32[12,1,128,128]{3,2,1,0:T(8,128)}, u32[]{:S(2)}, u32[]{:S(2)}) collective-permute-start(f32[12,1,128,128]{3,2,1,0:T(8,128)S(1)} %collective-permute-done.14), channel_id=1, source_target_pairs={{0,384},{32,416},{64,448},{96,480},{128,0},{160,32},{192,64},{224,... | collective-permute-start | bytes 2359304 | tf_op jit(solution)/shard_map/ppermute | solution.py:27
  158.3 3.6 %pad_maximum_fusion.1.a_ref = f32[12,4,128,128]{3,2,1,0:T(8,128)} fusion(f32[12,1,128,128]{3,2,1,0:T(8,128)} %collective-permute-done.17, f32[12,1,128,128]{3,2,1,0:T(8,128)} %collective-permute-done.16, f32[12,1,128,128]{3,2,1,0:T(8,128)} %collective-permute-done.15, f32[12,1,128,128]{3,2,1,0:T(8,128)S(1)} %copy-done), kind=kLoop, calls=%fused_computation.9 | loop fusion | flops 2359296 | bytes 6291456 | tf_op jit(solution)/shard_map/concatenate | solution.py:112
  161.9 11.8 %shard_map.100.rest_0_ = f32[12,4,128,128]{3,2,1,0:T(8,128)} custom-call(s32[48]{0:T(128)} %reshape.336.pidx_ref, s32[48]{0:T(128)} %reshape.337.sidx_ref, f32[12,4,128,128]{3,2,1,0:T(8,128)} %pad_maximum_fusion.1.a_ref, f32[64,128,128]{2,1,0:T(8,128)} %pad_maximum_fusion.b_ref), custom_call_target="tpu_custom_call" | custom-call | tf_op jit(solution)/shard_map/pallas_call | solution.py:164
  173.6 1.0 constant_dynamic-update-slice_fusion.7
  174.6 1.0 constant_dynamic-update-slice_fusion.6
  175.6 2.1 constant_dynamic-update-slice_fusion.5
  177.7 1.0 constant_dynamic-update-slice_fusion.4
  178.7 2.1 constant_dynamic-update-slice_fusion.3
  180.8 5.3 %collective-permute-done.22 = f32[12,1,128,128]{3,2,1,0:T(8,128)} collective-permute-done((f32[12,1,128,128]{3,2,1,0:T(8,128)S(1)}, f32[12,1,128,128]{3,2,1,0:T(8,128)}, u32[]{:S(2)}, u32[]{:S(2)}) %collective-permute-start.22) | collective-permute-done | bytes 786464 | tf_op jit(solution)/shard_map/ppermute | solution.py:27
  186.1 2.1 constant_dynamic-update-slice_fusion.2
  188.1 2.1 constant_dynamic-update-slice_fusion.1
  190.2 2.1 constant_dynamic-update-slice_fusion
  192.3 3.2 %collective-permute-start.24 = (f32[12,8,128,128]{3,2,1,0:T(8,128)}, f32[12,8,128,128]{3,2,1,0:T(8,128)}, u32[]{:S(2)}, u32[]{:S(2)}) collective-permute-start(f32[12,8,128,128]{3,2,1,0:T(8,128)} %constant_dynamic-update-slice_fusion), channel_id=1, source_target_pairs={{0,32},{32,0},{64,96},{96,64},{128,160},{160,128},{192,224},{224,1... | collective-permute-start | bytes 18874376 | tf_op jit(solution)/shard_map/ppermute | solution.py:32
  197.9 0.7 reshape.334.pidx_ref
  198.6 0.6 reshape.335.sidx_ref
  200.6 3.4 %pad_maximum_fusion.2.a_ref = f32[12,4,128,128]{3,2,1,0:T(8,128)} fusion(f32[12,1,128,128]{3,2,1,0:T(8,128)} %collective-permute-done.23, f32[12,1,128,128]{3,2,1,0:T(8,128)} %collective-permute-done.22, f32[12,1,128,128]{3,2,1,0:T(8,128)S(1)} %collective-permute-done.21, f32[12,1,128,128]{3,2,1,0:T(8,128)S(1)} %collective-permute-done.14), kind=kLoop, calls=%fused_computation.10 | loop fusion | flops 2359296 | bytes 6291456 | tf_op jit(solution)/shard_map/concatenate | solution.py:114
  203.9 13.1 %shard_map.101.rest_0_ = f32[12,4,128,128]{3,2,1,0:T(8,128)} custom-call(s32[48]{0:T(128)} %reshape.338.pidx_ref, s32[48]{0:T(128)} %reshape.339.sidx_ref, f32[12,4,128,128]{3,2,1,0:T(8,128)} %pad_maximum_fusion.2.a_ref, f32[64,128,128]{2,1,0:T(8,128)} %pad_maximum_fusion.b_ref, f32[12,4,128,128]{3,2,1,0:T(8,128)} %shard_map.100.rest_0_), custom_call_target="tpu_custom_call", output_to_operand_aliasing={{}: (4, {})} | custom-call | tf_op jit(solution)/shard_map/pallas_call | solution.py:164
  217.0 16.2 %shard_map.102 = f32[12,4,128,128]{3,2,1,0:T(8,128)} custom-call(s32[96]{0:T(128)} %reshape.334.pidx_ref, s32[96]{0:T(128)} %reshape.335.sidx_ref, f32[12,8,128,128]{3,2,1,0:T(8,128)} %collective-permute-done.24.a_ref, f32[64,128,128]{2,1,0:T(8,128)} %pad_maximum_fusion.b_ref, f32[12,4,128,128]{3,2,1,0:T(8,128)} %shard_map.101.rest_0_), custom_call_target="tpu_custom_call", output_to_operand_aliasing={{}: (4, {})} | custom-call | tf_op jit(solution)/shard_map/pallas_call | solution.py:164
  (74 shorter events, 7.5 us)
Async XLA Ops:
  0.0 7.1 %collective-permute-start = (f32[2,128,128]{2,1,0:T(8,128)}, f32[2,128,128]{2,1,0:T(8,128)S(1)}, u32[]{:S(2)}, u32[]{:S(2)}) collective-permute-start(f32[2,128,128]{2,1,0:T(8,128)} %bitcast.47), channel_id=1, source_target_pairs={{0,1},{1,2},{2,3},{3,4},{4,5},{5,6},{6,7},{8,9},{9,10},{10,11},{11... | collective-permute-start | bytes 393224 | tf_op jit(solution)/shard_map/ppermute | solution.py:57
  2.6 7.1 %collective-permute-start.7 = (f32[2,128,128]{2,1,0:T(8,128)}, f32[2,128,128]{2,1,0:T(8,128)S(1)}, u32[]{:S(2)}, u32[]{:S(2)}) collective-permute-start(f32[2,128,128]{2,1,0:T(8,128)} %bitcast.48), channel_id=1, source_target_pairs={{1,0},{2,1},{3,2},{4,3},{5,4},{6,5},{7,6},{9,8},{10,9},{11,10},{12... | collective-permute-start | bytes 393224 | tf_op jit(solution)/shard_map/ppermute | solution.py:58
  7.1 6.0 %collective-permute-start.1 = (f32[2,128,128]{2,1,0:T(8,128)S(1)}, f32[2,128,128]{2,1,0:T(8,128)S(1)}, u32[]{:S(2)}, u32[]{:S(2)}) collective-permute-start(f32[2,128,128]{2,1,0:T(8,128)S(1)} %collective-permute-done), channel_id=1, source_target_pairs={{0,1},{1,2},{2,3},{3,4},{4,5},{5,6},{6,7},{8,9},{9,10},{10,11},{11... | collective-permute-start | bytes 393224 | tf_op jit(solution)/shard_map/ppermute | solution.py:57
  9.7 6.0 %collective-permute-start.8 = (f32[2,128,128]{2,1,0:T(8,128)S(1)}, f32[2,128,128]{2,1,0:T(8,128)S(1)}, u32[]{:S(2)}, u32[]{:S(2)}) collective-permute-start(f32[2,128,128]{2,1,0:T(8,128)S(1)} %collective-permute-done.7), channel_id=1, source_target_pairs={{1,0},{2,1},{3,2},{4,3},{5,4},{6,5},{7,6},{9,8},{10,9},{11,10},{12... | collective-permute-start | bytes 393224 | tf_op jit(solution)/shard_map/ppermute | solution.py:58
  13.0 6.0 %collective-permute-start.2 = (f32[2,128,128]{2,1,0:T(8,128)S(1)}, f32[2,128,128]{2,1,0:T(8,128)S(1)}, u32[]{:S(2)}, u32[]{:S(2)}) collective-permute-start(f32[2,128,128]{2,1,0:T(8,128)S(1)} %collective-permute-done.1), channel_id=1, source_target_pairs={{0,1},{1,2},{2,3},{3,4},{4,5},{5,6},{6,7},{8,9},{9,10},{10,11},{11... | collective-permute-start | bytes 393224 | tf_op jit(solution)/shard_map/ppermute | solution.py:57
  15.7 6.0 %collective-permute-start.9 = (f32[2,128,128]{2,1,0:T(8,128)S(1)}, f32[2,128,128]{2,1,0:T(8,128)S(1)}, u32[]{:S(2)}, u32[]{:S(2)}) collective-permute-start(f32[2,128,128]{2,1,0:T(8,128)S(1)} %collective-permute-done.8), channel_id=1, source_target_pairs={{1,0},{2,1},{3,2},{4,3},{5,4},{6,5},{7,6},{9,8},{10,9},{11,10},{12... | collective-permute-start | bytes 393224 | tf_op jit(solution)/shard_map/ppermute | solution.py:58
  19.0 6.9 %collective-permute-start.3 = (f32[2,128,128]{2,1,0:T(8,128)S(1)}, f32[2,128,128]{2,1,0:T(8,128)S(1)}, u32[]{:S(2)}, u32[]{:S(2)}) collective-permute-start(f32[2,128,128]{2,1,0:T(8,128)S(1)} %collective-permute-done.2), channel_id=1, source_target_pairs={{0,1},{1,2},{2,3},{3,4},{4,5},{5,6},{6,7},{8,9},{9,10},{10,11},{11... | collective-permute-start | bytes 393224 | tf_op jit(solution)/shard_map/ppermute | solution.py:57
  21.7 6.2 %collective-permute-start.10 = (f32[2,128,128]{2,1,0:T(8,128)S(1)}, f32[2,128,128]{2,1,0:T(8,128)S(1)}, u32[]{:S(2)}, u32[]{:S(2)}) collective-permute-start(f32[2,128,128]{2,1,0:T(8,128)S(1)} %collective-permute-done.9), channel_id=1, source_target_pairs={{1,0},{2,1},{3,2},{4,3},{5,4},{6,5},{7,6},{9,8},{10,9},{11,10},{12... | collective-permute-start | bytes 393224 | tf_op jit(solution)/shard_map/ppermute | solution.py:58
  26.0 7.2 %collective-permute-start.4 = (f32[2,128,128]{2,1,0:T(8,128)S(1)}, f32[2,128,128]{2,1,0:T(8,128)S(1)}, u32[]{:S(2)}, u32[]{:S(2)}) collective-permute-start(f32[2,128,128]{2,1,0:T(8,128)S(1)} %collective-permute-done.3), channel_id=1, source_target_pairs={{0,1},{1,2},{2,3},{3,4},{4,5},{5,6},{6,7},{8,9},{9,10},{10,11},{11... | collective-permute-start | bytes 393224 | tf_op jit(solution)/shard_map/ppermute | solution.py:57
  27.9 7.2 %collective-permute-start.11 = (f32[2,128,128]{2,1,0:T(8,128)S(1)}, f32[2,128,128]{2,1,0:T(8,128)S(1)}, u32[]{:S(2)}, u32[]{:S(2)}) collective-permute-start(f32[2,128,128]{2,1,0:T(8,128)S(1)} %collective-permute-done.10), channel_id=1, source_target_pairs={{1,0},{2,1},{3,2},{4,3},{5,4},{6,5},{7,6},{9,8},{10,9},{11,10},{12... | collective-permute-start | bytes 393224 | tf_op jit(solution)/shard_map/ppermute | solution.py:58
  33.1 7.2 %collective-permute-start.5 = (f32[2,128,128]{2,1,0:T(8,128)S(1)}, f32[2,128,128]{2,1,0:T(8,128)S(1)}, u32[]{:S(2)}, u32[]{:S(2)}) collective-permute-start(f32[2,128,128]{2,1,0:T(8,128)S(1)} %collective-permute-done.4), channel_id=1, source_target_pairs={{0,1},{1,2},{2,3},{3,4},{4,5},{5,6},{6,7},{8,9},{9,10},{10,11},{11... | collective-permute-start | bytes 393224 | tf_op jit(solution)/shard_map/ppermute | solution.py:57
  35.1 7.2 %collective-permute-start.12 = (f32[2,128,128]{2,1,0:T(8,128)S(1)}, f32[2,128,128]{2,1,0:T(8,128)S(1)}, u32[]{:S(2)}, u32[]{:S(2)}) collective-permute-start(f32[2,128,128]{2,1,0:T(8,128)S(1)} %collective-permute-done.11), channel_id=1, source_target_pairs={{1,0},{2,1},{3,2},{4,3},{5,4},{6,5},{7,6},{9,8},{10,9},{11,10},{12... | collective-permute-start | bytes 393224 | tf_op jit(solution)/shard_map/ppermute | solution.py:58
  40.3 7.2 %collective-permute-start.6 = (f32[2,128,128]{2,1,0:T(8,128)S(1)}, f32[2,128,128]{2,1,0:T(8,128)S(1)}, u32[]{:S(2)}, u32[]{:S(2)}) collective-permute-start(f32[2,128,128]{2,1,0:T(8,128)S(1)} %collective-permute-done.5), channel_id=1, source_target_pairs={{0,1},{1,2},{2,3},{3,4},{4,5},{5,6},{6,7},{8,9},{9,10},{10,11},{11... | collective-permute-start | bytes 393224 | tf_op jit(solution)/shard_map/ppermute | solution.py:57
  42.2 9.9 %collective-permute-start.13 = (f32[2,128,128]{2,1,0:T(8,128)S(1)}, f32[2,128,128]{2,1,0:T(8,128)S(1)}, u32[]{:S(2)}, u32[]{:S(2)}) collective-permute-start(f32[2,128,128]{2,1,0:T(8,128)S(1)} %collective-permute-done.12), channel_id=1, source_target_pairs={{1,0},{2,1},{3,2},{4,3},{5,4},{6,5},{7,6},{9,8},{10,9},{11,10},{12... | collective-permute-start | bytes 393224 | tf_op jit(solution)/shard_map/ppermute | solution.py:58
  47.5 14.6 %copy-start.1 = (s32[12,16]{1,0:T(8,128)S(1)}, s32[12,16]{1,0:T(8,128)}, u32[]{:S(2)}) copy-start(s32[12,16]{1,0:T(8,128)} %param.11) | copy-start | bytes 2308
  47.5 14.6 %copy-start.3 = (s32[64]{0:T(128)S(1)}, s32[64]{0:T(128)}, u32[]{:S(2)}) copy-start(s32[64]{0:T(128)} %param.16) | copy-start | bytes 772
  48.2 14.5 %copy-start.6 = (s32[8]{0:T(128)S(1)}, s32[8]{0:T(128)}, u32[]{:S(2)}) copy-start(s32[8]{0:T(128)} %constant.237) | copy-start | bytes 100
  48.2 17.9 %copy-start.7 = (s32[12]{0:T(128)S(1)}, s32[12]{0:T(128)}, u32[]{:S(2)}) copy-start(s32[12]{0:T(128)} %param.12) | copy-start | bytes 148
  48.2 17.9 %copy-start = (f32[12,1,128,128]{3,2,1,0:T(8,128)S(1)}, f32[12,1,128,128]{3,2,1,0:T(8,128)}, u32[]{:S(2)}) copy-start(f32[12,1,128,128]{3,2,1,0:T(8,128)} %param.10) | copy-start | bytes 2359300
  48.2 38.0 %copy-start.4 = (s32[64,1]{0,1:T(1,128)S(1)}, s32[64,1]{0,1:T(1,128)}, u32[]{:S(2)}) copy-start(s32[64,1]{0,1:T(1,128)} %param.14) | copy-start | bytes 772
  48.2 38.4 %copy-start.2 = (s32[12,4]{0,1:T(4,128)S(1)}, s32[12,4]{0,1:T(4,128)}, u32[]{:S(2)}) copy-start(s32[12,4]{0,1:T(4,128)} %param.15) | copy-start | bytes 580
  48.2 39.5 %copy-start.5 = (s32[4]{0:T(128)S(1)}, s32[4]{0:T(128)}, u32[]{:S(2)}) copy-start(s32[4]{0:T(128)} %constant.239) | copy-start | bytes 52
  55.2 22.2 %collective-permute-start.20 = (f32[16,128,128]{2,1,0:T(8,128)S(1)}, f32[16,128,128]{2,1,0:T(8,128)}, u32[]{:S(2)}, u32[]{:S(2)}) collective-permute-start(f32[16,128,128]{2,1,0:T(8,128)S(1)} %bitcast_select_fusion), channel_id=1, source_target_pairs={{0,24},{1,25},{2,26},{3,27},{4,28},{5,29},{6,30},{7,31},{8,0},{9,1... | collective-permute-start | bytes 3145736 | tf_op jit(solution)/shard_map/ppermute | solution.py:70
  59.8 22.2 %collective-permute-start.19 = (f32[16,128,128]{2,1,0:T(8,128)S(1)}, f32[16,128,128]{2,1,0:T(8,128)}, u32[]{:S(2)}, u32[]{:S(2)}) collective-permute-start(f32[16,128,128]{2,1,0:T(8,128)S(1)} %bitcast_select_fusion), channel_id=1, source_target_pairs={{0,16},{1,17},{2,18},{3,19},{4,20},{5,21},{6,22},{7,23},{8,24},{9,... | collective-permute-start | bytes 3145736 | tf_op jit(solution)/shard_map/ppermute | solution.py:70
  63.2 47.6 %collective-permute-start.18 = (f32[16,128,128]{2,1,0:T(8,128)S(1)}, f32[16,128,128]{2,1,0:T(8,128)}, u32[]{:S(2)}, u32[]{:S(2)}) collective-permute-start(f32[16,128,128]{2,1,0:T(8,128)S(1)} %bitcast_select_fusion), channel_id=1, source_target_pairs={{0,8},{1,9},{2,10},{3,11},{4,12},{5,13},{6,14},{7,15},{8,16},{9,17... | collective-permute-start | bytes 3145736 | tf_op jit(solution)/shard_map/ppermute | solution.py:70
  66.1 80.3 %collective-permute-start.14 = (f32[12,1,128,128]{3,2,1,0:T(8,128)S(1)}, f32[12,1,128,128]{3,2,1,0:T(8,128)S(1)}, u32[]{:S(2)}, u32[]{:S(2)}) collective-permute-start(f32[12,1,128,128]{3,2,1,0:T(8,128)S(1)} %copy-done), channel_id=1, source_target_pairs={{0,64},{32,96},{64,0},{96,32},{128,192},{160,224},{192,128},{224,1... | collective-permute-start | bytes 2359304 | tf_op jit(solution)/shard_map/ppermute | solution.py:21
  69.5 76.9 %collective-permute-start.15 = (f32[12,1,128,128]{3,2,1,0:T(8,128)S(1)}, f32[12,1,128,128]{3,2,1,0:T(8,128)}, u32[]{:S(2)}, u32[]{:S(2)}) collective-permute-start(f32[12,1,128,128]{3,2,1,0:T(8,128)S(1)} %copy-done), channel_id=1, source_target_pairs={{0,128},{32,160},{64,192},{96,224},{128,256},{160,288},{192,320},{... | collective-permute-start | bytes 2359304 | tf_op jit(solution)/shard_map/ppermute | solution.py:27
  77.3 69.1 %collective-permute-start.16 = (f32[12,1,128,128]{3,2,1,0:T(8,128)S(1)}, f32[12,1,128,128]{3,2,1,0:T(8,128)}, u32[]{:S(2)}, u32[]{:S(2)}) collective-permute-start(f32[12,1,128,128]{3,2,1,0:T(8,128)S(1)} %copy-done), channel_id=1, source_target_pairs={{0,256},{32,288},{64,320},{96,352},{128,384},{160,416},{192,448},{... | collective-permute-start | bytes 2359304 | tf_op jit(solution)/shard_map/ppermute | solution.py:27
  82.0 64.4 %collective-permute-start.17 = (f32[12,1,128,128]{3,2,1,0:T(8,128)S(1)}, f32[12,1,128,128]{3,2,1,0:T(8,128)}, u32[]{:S(2)}, u32[]{:S(2)}) collective-permute-start(f32[12,1,128,128]{3,2,1,0:T(8,128)S(1)} %copy-done), channel_id=1, source_target_pairs={{0,384},{32,416},{64,448},{96,480},{128,0},{160,32},{192,64},{224,... | collective-permute-start | bytes 2359304 | tf_op jit(solution)/shard_map/ppermute | solution.py:27
  146.4 31.3 %collective-permute-start.21 = (f32[12,1,128,128]{3,2,1,0:T(8,128)S(1)}, f32[12,1,128,128]{3,2,1,0:T(8,128)S(1)}, u32[]{:S(2)}, u32[]{:S(2)}) collective-permute-start(f32[12,1,128,128]{3,2,1,0:T(8,128)S(1)} %collective-permute-done.14), channel_id=1, source_target_pairs={{0,128},{32,160},{64,192},{96,224},{128,256},{160,288},{192,320},{... | collective-permute-start | bytes 2359304 | tf_op jit(solution)/shard_map/ppermute | solution.py:27
  150.9 35.2 %collective-permute-start.22 = (f32[12,1,128,128]{3,2,1,0:T(8,128)S(1)}, f32[12,1,128,128]{3,2,1,0:T(8,128)}, u32[]{:S(2)}, u32[]{:S(2)}) collective-permute-start(f32[12,1,128,128]{3,2,1,0:T(8,128)S(1)} %collective-permute-done.14), channel_id=1, source_target_pairs={{0,256},{32,288},{64,320},{96,352},{128,384},{160,416},{192,448},{... | collective-permute-start | bytes 2359304 | tf_op jit(solution)/shard_map/ppermute | solution.py:27
  155.2 35.0 %collective-permute-start.23 = (f32[12,1,128,128]{3,2,1,0:T(8,128)S(1)}, f32[12,1,128,128]{3,2,1,0:T(8,128)}, u32[]{:S(2)}, u32[]{:S(2)}) collective-permute-start(f32[12,1,128,128]{3,2,1,0:T(8,128)S(1)} %collective-permute-done.14), channel_id=1, source_target_pairs={{0,384},{32,416},{64,448},{96,480},{128,0},{160,32},{192,64},{224,... | collective-permute-start | bytes 2359304 | tf_op jit(solution)/shard_map/ppermute | solution.py:27
  192.3 24.7 %collective-permute-start.24 = (f32[12,8,128,128]{3,2,1,0:T(8,128)}, f32[12,8,128,128]{3,2,1,0:T(8,128)}, u32[]{:S(2)}, u32[]{:S(2)}) collective-permute-start(f32[12,8,128,128]{3,2,1,0:T(8,128)} %constant_dynamic-update-slice_fusion), channel_id=1, source_target_pairs={{0,32},{32,0},{64,96},{96,64},{128,160},{160,128},{192,224},{224,1... | collective-permute-start | bytes 18874376 | tf_op jit(solution)/shard_map/ppermute | solution.py:32

commit v11 on v8

--- a/solution.py
+++ b/solution.py
@@ -86,8 +86,8 @@
     swap_z, ring_x, swap_core = row_stages(n_row)
     line_z, ring_y = col_stages(n_col)
     a_own, b_held = lax.optimization_barrier((a_blocks, line_z(b_blocks[:, 0])))
-    a_other, own_x, panels = lax.optimization_barrier((swap_z(a_own), ring_x(a_own), ring_y(b_held)))
-    other_x = ring_x(a_other)
+    a_other, own_x, b_held = lax.optimization_barrier((swap_z(a_own), ring_x(a_own), b_held))
+    other_x, panels = lax.optimization_barrier((ring_x(a_other), ring_y(b_held)))
     a_held = jnp.concatenate([p for pair in zip(own_x, other_x) for p in pair], axis=1)
     rows_here, slot_all = a_cols.shape
     pattern_slots = c_cols.shape[1]

time: 228 us -> 269 us (1.18)
  the two profiles are of different devices: /device:TPU:107 before, /device:TPU:97 now
where the time goes in v11:
time: 269 us; the launch traced here: 267 us
  waiting for transfers between devices  114 us (42%)
  starting transfers between devices  91.9 us (34%)
  Pallas kernels  31.3 us (12%)
  local copies, waits for them, and re-layouts  24.9 us (9%)
  other arithmetic  4.39 us (2%)
    ppermute x1, waiting for transfers between devices, swap_z(): return lax.ppermute(chunk, 'row', pairs)  45.1 us
    ppermute x3, waiting for transfers between devices, ring_y(): parts.append(lax.ppermute(held, 'col', shift))  34.5 us
    ppermute x6, waiting for transfers between devices, ring_x(): parts.append(lax.ppermute(held, 'row', shift))  33.6 us
    ppermute x7, starting transfers between devices, line_z(): going_right = lax.ppermute(going_right, 'col', right)  32.2 us
    pallas_call x2, Pallas kernels, row_products(): pl.pallas_call(product_kernel, grid_spec=grid_spec, out_shape=jax.ShapeDt...  31.3 us
    ppermute x6, starting transfers between devices, ring_x(): parts.append(lax.ppermute(held, 'row', shift))  19.9 us
    unnamed x34, local copies, waits for them, and re-layouts  17.1 us
    ppermute x7, starting transfers between devices, line_z(): going_left = lax.ppermute(going_left, 'col', left)  13.4 us
  transfers between devices with their start and end apart: 25, of which 6 were waited for; matrix products, arithmetic and copies ran while one was open for 7% of the time, Pallas kernels for 6%

profile of v11, /device:TPU:97, one launch (start us, length us, event | category | flops | bytes accessed | tf_op | source)
XLA Modules:
  0.0 267.4 jit_solution(2327807814723988418)
XLA Ops:
  0.0 1.9 collective-permute-start.7
  1.9 4.8 %collective-permute-start = (f32[2,128,128]{2,1,0:T(8,128)}, f32[2,128,128]{2,1,0:T(8,128)S(1)}, u32[]{:S(2)}, u32[]{:S(2)}) collective-permute-start(f32[2,128,128]{2,1,0:T(8,128)} %bitcast.42), channel_id=1, source_target_pairs={{0,1},{1,2},{2,3},{3,4},{4,5},{5,6},{6,7},{8,9},{9,10},{10,11},{11... | collective-permute-start | bytes 393224 | tf_op jit(solution)/shard_map/ppermute | solution.py:57
  6.7 1.6 bitcast_dynamic-update-slice_fusion.14
  8.5 1.9 collective-permute-start.8
  10.4 4.6 %collective-permute-start.1 = (f32[2,128,128]{2,1,0:T(8,128)S(1)}, f32[2,128,128]{2,1,0:T(8,128)S(1)}, u32[]{:S(2)}, u32[]{:S(2)}) collective-permute-start(f32[2,128,128]{2,1,0:T(8,128)S(1)} %collective-permute-done), channel_id=1, source_target_pairs={{0,1},{1,2},{2,3},{3,4},{4,5},{5,6},{6,7},{8,9},{9,10},{10,11},{11... | collective-permute-start | bytes 393224 | tf_op jit(solution)/shard_map/ppermute | solution.py:57
  15.0 0.7 bitcast_dynamic-update-slice_fusion.13
  15.7 1.9 collective-permute-start.9
  17.6 4.6 %collective-permute-start.2 = (f32[2,128,128]{2,1,0:T(8,128)S(1)}, f32[2,128,128]{2,1,0:T(8,128)S(1)}, u32[]{:S(2)}, u32[]{:S(2)}) collective-permute-start(f32[2,128,128]{2,1,0:T(8,128)S(1)} %collective-permute-done.1), channel_id=1, source_target_pairs={{0,1},{1,2},{2,3},{3,4},{4,5},{5,6},{6,7},{8,9},{9,10},{10,11},{11... | collective-permute-start | bytes 393224 | tf_op jit(solution)/shard_map/ppermute | solution.py:57
  22.2 0.7 bitcast_dynamic-update-slice_fusion.12
  22.9 1.9 collective-permute-start.10
  24.8 4.6 %collective-permute-start.3 = (f32[2,128,128]{2,1,0:T(8,128)S(1)}, f32[2,128,128]{2,1,0:T(8,128)S(1)}, u32[]{:S(2)}, u32[]{:S(2)}) collective-permute-start(f32[2,128,128]{2,1,0:T(8,128)S(1)} %collective-permute-done.2), channel_id=1, source_target_pairs={{0,1},{1,2},{2,3},{3,4},{4,5},{5,6},{6,7},{8,9},{9,10},{10,11},{11... | collective-permute-start | bytes 393224 | tf_op jit(solution)/shard_map/ppermute | solution.py:57
  29.4 0.7 bitcast_dynamic-update-slice_fusion.11
  30.1 1.9 collective-permute-start.11
  32.0 4.6 %collective-permute-start.4 = (f32[2,128,128]{2,1,0:T(8,128)S(1)}, f32[2,128,128]{2,1,0:T(8,128)S(1)}, u32[]{:S(2)}, u32[]{:S(2)}) collective-permute-start(f32[2,128,128]{2,1,0:T(8,128)S(1)} %collective-permute-done.3), channel_id=1, source_target_pairs={{0,1},{1,2},{2,3},{3,4},{4,5},{5,6},{6,7},{8,9},{9,10},{10,11},{11... | collective-permute-start | bytes 393224 | tf_op jit(solution)/shard_map/ppermute | solution.py:57
  36.6 0.7 bitcast_dynamic-update-slice_fusion.10
  37.2 1.9 collective-permute-start.12
  39.2 4.6 %collective-permute-start.5 = (f32[2,128,128]{2,1,0:T(8,128)S(1)}, f32[2,128,128]{2,1,0:T(8,128)S(1)}, u32[]{:S(2)}, u32[]{:S(2)}) collective-permute-start(f32[2,128,128]{2,1,0:T(8,128)S(1)} %collective-permute-done.4), channel_id=1, source_target_pairs={{0,1},{1,2},{2,3},{3,4},{4,5},{5,6},{6,7},{8,9},{9,10},{10,11},{11... | collective-permute-start | bytes 393224 | tf_op jit(solution)/shard_map/ppermute | solution.py:57
  43.7 0.7 bitcast_dynamic-update-slice_fusion.9
  44.4 1.9 collective-permute-start.13
  46.3 4.6 %collective-permute-start.6 = (f32[2,128,128]{2,1,0:T(8,128)S(1)}, f32[2,128,128]{2,1,0:T(8,128)S(1)}, u32[]{:S(2)}, u32[]{:S(2)}) collective-permute-start(f32[2,128,128]{2,1,0:T(8,128)S(1)} %collective-permute-done.5), channel_id=1, source_target_pairs={{0,1},{1,2},{2,3},{3,4},{4,5},{5,6},{6,7},{8,9},{9,10},{10,11},{11... | collective-permute-start | bytes 393224 | tf_op jit(solution)/shard_map/ppermute | solution.py:57
  50.9 0.7 bitcast_dynamic-update-slice_fusion.8
  51.6 1.3 collective-permute-done.6
  52.8 0.7 bitcast_dynamic-update-slice_fusion.7
  53.5 0.7 bitcast_dynamic-update-slice_fusion.6
  54.2 0.7 bitcast_dynamic-update-slice_fusion.5
  54.8 0.7 bitcast_dynamic-update-slice_fusion.4
  55.5 0.7 bitcast_dynamic-update-slice_fusion.3
  56.2 0.7 bitcast_dynamic-update-slice_fusion.2
  56.8 0.7 bitcast_dynamic-update-slice_fusion.1
  57.5 0.7 bitcast_dynamic-update-slice_fusion
  58.2 2.2 gather_fusion.1
  60.6 4.4 %collective-permute-start.17 = (f32[12,1,128,128]{3,2,1,0:T(8,128)S(1)}, f32[12,1,128,128]{3,2,1,0:T(8,128)S(1)}, u32[]{:S(2)}, u32[]{:S(2)}) collective-permute-start(f32[12,1,128,128]{3,2,1,0:T(8,128)S(1)} %copy-done), channel_id=1, source_target_pairs={{0,384},{32,416},{64,448},{96,480},{128,0},{160,32},{192,64},{224,... | collective-permute-start | bytes 2359304 | tf_op jit(solution)/shard_map/ppermute | solution.py:27
  65.0 2.4 collective-permute-start.16
  67.4 2.5 collective-permute-start.15
  69.9 12.6 %collective-permute-start.14 = (f32[12,1,128,128]{3,2,1,0:T(8,128)S(1)}, f32[12,1,128,128]{3,2,1,0:T(8,128)S(1)}, u32[]{:S(2)}, u32[]{:S(2)}) collective-permute-start(f32[12,1,128,128]{3,2,1,0:T(8,128)S(1)} %copy-done), channel_id=1, source_target_pairs={{0,64},{32,96},{64,0},{96,32},{128,192},{160,224},{192,128},{224,1... | collective-permute-start | bytes 2359304 | tf_op jit(solution)/shard_map/ppermute | solution.py:21
  82.5 22.1 %collective-permute-done.15 = f32[12,1,128,128]{3,2,1,0:T(8,128)S(1)} collective-permute-done((f32[12,1,128,128]{3,2,1,0:T(8,128)S(1)}, f32[12,1,128,128]{3,2,1,0:T(8,128)S(1)}, u32[]{:S(2)}, u32[]{:S(2)}) %collective-permute-start.15) | collective-permute-done | bytes 786464 | tf_op jit(solution)/shard_map/ppermute | solution.py:27
  104.6 45.1 %collective-permute-done.14 = f32[12,1,128,128]{3,2,1,0:T(8,128)S(1)} collective-permute-done((f32[12,1,128,128]{3,2,1,0:T(8,128)S(1)}, f32[12,1,128,128]{3,2,1,0:T(8,128)S(1)}, u32[]{:S(2)}, u32[]{:S(2)}) %collective-permute-start.14) | collective-permute-done | bytes 786464 | tf_op jit(solution)/shard_map/ppermute | solution.py:21
  149.7 4.6 %collective-permute-start.23 = (f32[16,128,128]{2,1,0:T(8,128)S(1)}, f32[16,128,128]{2,1,0:T(8,128)S(1)}, u32[]{:S(2)}, u32[]{:S(2)}) collective-permute-start(f32[16,128,128]{2,1,0:T(8,128)S(1)} %bitcast_select_fusion), channel_id=1, source_target_pairs={{0,24},{1,25},{2,26},{3,27},{4,28},{5,29},{6,30},{7,31},{8,0},{9,1... | collective-permute-start | bytes 3145736 | tf_op jit(solution)/shard_map/ppermute | solution.py:70
  154.3 2.3 collective-permute-start.22
  156.6 2.6 collective-permute-start.21
  159.2 4.0 %collective-permute-start.20 = (f32[12,1,128,128]{3,2,1,0:T(8,128)S(1)}, f32[12,1,128,128]{3,2,1,0:T(8,128)S(1)}, u32[]{:S(2)}, u32[]{:S(2)}) collective-permute-start(f32[12,1,128,128]{3,2,1,0:T(8,128)S(1)} %collective-permute-done.14), channel_id=1, source_target_pairs={{0,384},{32,416},{64,448},{96,480},{128,0},{160,32},{192,64},{224,... | collective-permute-start | bytes 2359304 | tf_op jit(solution)/shard_map/ppermute | solution.py:27
  163.2 3.1 %collective-permute-start.19 = (f32[12,1,128,128]{3,2,1,0:T(8,128)S(1)}, f32[12,1,128,128]{3,2,1,0:T(8,128)S(1)}, u32[]{:S(2)}, u32[]{:S(2)}) collective-permute-start(f32[12,1,128,128]{3,2,1,0:T(8,128)S(1)} %collective-permute-done.14), channel_id=1, source_target_pairs={{0,256},{32,288},{64,320},{96,352},{128,384},{160,416},{192,448},{... | collective-permute-start | bytes 2359304 | tf_op jit(solution)/shard_map/ppermute | solution.py:27
  166.3 32.3 %collective-permute-done.23 = f32[16,128,128]{2,1,0:T(8,128)S(1)} collective-permute-done((f32[16,128,128]{2,1,0:T(8,128)S(1)}, f32[16,128,128]{2,1,0:T(8,128)S(1)}, u32[]{:S(2)}, u32[]{:S(2)}) %collective-permute-start.23) | collective-permute-done | bytes 1048608 | tf_op jit(solution)/shard_map/ppermute | solution.py:70
  198.6 3.4 %collective-permute-start.18 = (f32[12,1,128,128]{3,2,1,0:T(8,128)S(1)}, f32[12,1,128,128]{3,2,1,0:T(8,128)S(1)}, u32[]{:S(2)}, u32[]{:S(2)}) collective-permute-start(f32[12,1,128,128]{3,2,1,0:T(8,128)S(1)} %collective-permute-done.14), channel_id=1, source_target_pairs={{0,128},{32,160},{64,192},{96,224},{128,256},{160,288},{192,320},{... | collective-permute-start | bytes 2359304 | tf_op jit(solution)/shard_map/ppermute | solution.py:27
  202.0 1.0 constant_dynamic-update-slice_fusion.7
  203.0 2.2 collective-permute-done.21
  205.3 2.4 pad_maximum_fusion.b_ref
  207.7 11.5 %collective-permute-done.18 = f32[12,1,128,128]{3,2,1,0:T(8,128)S(1)} collective-permute-done((f32[12,1,128,128]{3,2,1,0:T(8,128)S(1)}, f32[12,1,128,128]{3,2,1,0:T(8,128)S(1)}, u32[]{:S(2)}, u32[]{:S(2)}) %collective-permute-start.18) | collective-permute-done | bytes 786464 | tf_op jit(solution)/shard_map/ppermute | solution.py:27
  219.2 1.0 constant_dynamic-update-slice_fusion.6
  220.2 1.0 constant_dynamic-update-slice_fusion.5
  221.2 1.0 constant_dynamic-update-slice_fusion.4
  222.2 0.9 constant_dynamic-update-slice_fusion.3
  223.1 0.9 constant_dynamic-update-slice_fusion.2
  224.1 0.9 constant_dynamic-update-slice_fusion.1
  225.0 0.9 constant_dynamic-update-slice_fusion.a_ref
  225.9 4.4 %collective-permute-start.24 = (f32[12,8,128,128]{3,2,1,0:T(8,128)}, f32[12,8,128,128]{3,2,1,0:T(8,128)}, u32[]{:S(2)}, u32[]{:S(2)}) collective-permute-start(f32[12,8,128,128]{3,2,1,0:T(8,128)} %constant_dynamic-update-slice_fusion.a_ref), channel_id=1, source_target_pairs={{0,32},{32,0},{64,96},{96,64},{128,160},{160,128},{192,224},{224,1... | collective-permute-start | bytes 18874376 | tf_op jit(solution)/shard_map/ppermute | solution.py:32
  231.0 0.6 gather_fusion
  231.7 0.6 reshape.330.pidx_ref
  232.4 0.7 reshape.328.pidx_ref
  233.6 0.8 convert_reduce_fusion
  234.8 0.7 reshape.331.sidx_ref
  235.5 0.6 reshape.329.sidx_ref
  236.1 16.0 %shard_map.73.rest_0_ = f32[12,4,128,128]{3,2,1,0:T(8,128)} custom-call(s32[96]{0:T(128)} %reshape.330.pidx_ref, s32[96]{0:T(128)} %reshape.331.sidx_ref, f32[12,8,128,128]{3,2,1,0:T(8,128)} %constant_dynamic-update-slice_fusion.a_ref, f32[64,128,128]{2,1,0:T(8,128)} %pad_maximum_fusion.b_ref), custom_call_target="tpu_custom_call" | custom-call | tf_op jit(solution)/shard_map/pallas_call | solution.py:158
  252.1 15.3 %shard_map.74 = f32[12,4,128,128]{3,2,1,0:T(8,128)} custom-call(s32[96]{0:T(128)} %reshape.328.pidx_ref, s32[96]{0:T(128)} %reshape.329.sidx_ref, f32[12,8,128,128]{3,2,1,0:T(8,128)} %collective-permute-done.24.a_ref, f32[64,128,128]{2,1,0:T(8,128)} %pad_maximum_fusion.b_ref, f32[12,4,128,128]{3,2,1,0:T(8,128)} %shard_map.73.rest_0_), custom_call_target="tpu_custom_call", output_to_operand_aliasing={{}: (4, {})} | custom-call | tf_op jit(solution)/shard_map/pallas_call | solution.py:158
  (57 shorter events, 2.2 us)
Async XLA Ops:
  0.0 8.5 %collective-permute-start.7 = (f32[2,128,128]{2,1,0:T(8,128)}, f32[2,128,128]{2,1,0:T(8,128)S(1)}, u32[]{:S(2)}, u32[]{:S(2)}) collective-permute-start(f32[2,128,128]{2,1,0:T(8,128)} %bitcast.41), channel_id=1, source_target_pairs={{1,0},{2,1},{3,2},{4,3},{5,4},{6,5},{7,6},{9,8},{10,9},{11,10},{12... | collective-permute-start | bytes 393224 | tf_op jit(solution)/shard_map/ppermute | solution.py:58
  1.9 8.5 %collective-permute-start = (f32[2,128,128]{2,1,0:T(8,128)}, f32[2,128,128]{2,1,0:T(8,128)S(1)}, u32[]{:S(2)}, u32[]{:S(2)}) collective-permute-start(f32[2,128,128]{2,1,0:T(8,128)} %bitcast.42), channel_id=1, source_target_pairs={{0,1},{1,2},{2,3},{3,4},{4,5},{5,6},{6,7},{8,9},{9,10},{10,11},{11... | collective-permute-start | bytes 393224 | tf_op jit(solution)/shard_map/ppermute | solution.py:57
  8.5 7.2 %collective-permute-start.8 = (f32[2,128,128]{2,1,0:T(8,128)S(1)}, f32[2,128,128]{2,1,0:T(8,128)S(1)}, u32[]{:S(2)}, u32[]{:S(2)}) collective-permute-start(f32[2,128,128]{2,1,0:T(8,128)S(1)} %collective-permute-done.7), channel_id=1, source_target_pairs={{1,0},{2,1},{3,2},{4,3},{5,4},{6,5},{7,6},{9,8},{10,9},{11,10},{12... | collective-permute-start | bytes 393224 | tf_op jit(solution)/shard_map/ppermute | solution.py:58
  10.4 7.2 %collective-permute-start.1 = (f32[2,128,128]{2,1,0:T(8,128)S(1)}, f32[2,128,128]{2,1,0:T(8,128)S(1)}, u32[]{:S(2)}, u32[]{:S(2)}) collective-permute-start(f32[2,128,128]{2,1,0:T(8,128)S(1)} %collective-permute-done), channel_id=1, source_target_pairs={{0,1},{1,2},{2,3},{3,4},{4,5},{5,6},{6,7},{8,9},{9,10},{10,11},{11... | collective-permute-start | bytes 393224 | tf_op jit(solution)/shard_map/ppermute | solution.py:57
  15.7 7.2 %collective-permute-start.9 = (f32[2,128,128]{2,1,0:T(8,128)S(1)}, f32[2,128,128]{2,1,0:T(8,128)S(1)}, u32[]{:S(2)}, u32[]{:S(2)}) collective-permute-start(f32[2,128,128]{2,1,0:T(8,128)S(1)} %collective-permute-done.8), channel_id=1, source_target_pairs={{1,0},{2,1},{3,2},{4,3},{5,4},{6,5},{7,6},{9,8},{10,9},{11,10},{12... | collective-permute-start | bytes 393224 | tf_op jit(solution)/shard_map/ppermute | solution.py:58
  17.6 7.2 %collective-permute-start.2 = (f32[2,128,128]{2,1,0:T(8,128)S(1)}, f32[2,128,128]{2,1,0:T(8,128)S(1)}, u32[]{:S(2)}, u32[]{:S(2)}) collective-permute-start(f32[2,128,128]{2,1,0:T(8,128)S(1)} %collective-permute-done.1), channel_id=1, source_target_pairs={{0,1},{1,2},{2,3},{3,4},{4,5},{5,6},{6,7},{8,9},{9,10},{10,11},{11... | collective-permute-start | bytes 393224 | tf_op jit(solution)/shard_map/ppermute | solution.py:57
  22.9 7.2 %collective-permute-start.10 = (f32[2,128,128]{2,1,0:T(8,128)S(1)}, f32[2,128,128]{2,1,0:T(8,128)S(1)}, u32[]{:S(2)}, u32[]{:S(2)}) collective-permute-start(f32[2,128,128]{2,1,0:T(8,128)S(1)} %collective-permute-done.9), channel_id=1, source_target_pairs={{1,0},{2,1},{3,2},{4,3},{5,4},{6,5},{7,6},{9,8},{10,9},{11,10},{12... | collective-permute-start | bytes 393224 | tf_op jit(solution)/shard_map/ppermute | solution.py:58
  24.8 7.2 %collective-permute-start.3 = (f32[2,128,128]{2,1,0:T(8,128)S(1)}, f32[2,128,128]{2,1,0:T(8,128)S(1)}, u32[]{:S(2)}, u32[]{:S(2)}) collective-permute-start(f32[2,128,128]{2,1,0:T(8,128)S(1)} %collective-permute-done.2), channel_id=1, source_target_pairs={{0,1},{1,2},{2,3},{3,4},{4,5},{5,6},{6,7},{8,9},{9,10},{10,11},{11... | collective-permute-start | bytes 393224 | tf_op jit(solution)/shard_map/ppermute | solution.py:57
  30.1 7.2 %collective-permute-start.11 = (f32[2,128,128]{2,1,0:T(8,128)S(1)}, f32[2,128,128]{2,1,0:T(8,128)S(1)}, u32[]{:S(2)}, u32[]{:S(2)}) collective-permute-start(f32[2,128,128]{2,1,0:T(8,128)S(1)} %collective-permute-done.10), channel_id=1, source_target_pairs={{1,0},{2,1},{3,2},{4,3},{5,4},{6,5},{7,6},{9,8},{10,9},{11,10},{12... | collective-permute-start | bytes 393224 | tf_op jit(solution)/shard_map/ppermute | solution.py:58
  32.0 7.2 %collective-permute-start.4 = (f32[2,128,128]{2,1,0:T(8,128)S(1)}, f32[2,128,128]{2,1,0:T(8,128)S(1)}, u32[]{:S(2)}, u32[]{:S(2)}) collective-permute-start(f32[2,128,128]{2,1,0:T(8,128)S(1)} %collective-permute-done.3), channel_id=1, source_target_pairs={{0,1},{1,2},{2,3},{3,4},{4,5},{5,6},{6,7},{8,9},{9,10},{10,11},{11... | collective-permute-start | bytes 393224 | tf_op jit(solution)/shard_map/ppermute | solution.py:57
  37.2 7.2 %collective-permute-start.12 = (f32[2,128,128]{2,1,0:T(8,128)S(1)}, f32[2,128,128]{2,1,0:T(8,128)S(1)}, u32[]{:S(2)}, u32[]{:S(2)}) collective-permute-start(f32[2,128,128]{2,1,0:T(8,128)S(1)} %collective-permute-done.11), channel_id=1, source_target_pairs={{1,0},{2,1},{3,2},{4,3},{5,4},{6,5},{7,6},{9,8},{10,9},{11,10},{12... | collective-permute-start | bytes 393224 | tf_op jit(solution)/shard_map/ppermute | solution.py:58
  39.2 7.2 %collective-permute-start.5 = (f32[2,128,128]{2,1,0:T(8,128)S(1)}, f32[2,128,128]{2,1,0:T(8,128)S(1)}, u32[]{:S(2)}, u32[]{:S(2)}) collective-permute-start(f32[2,128,128]{2,1,0:T(8,128)S(1)} %collective-permute-done.4), channel_id=1, source_target_pairs={{0,1},{1,2},{2,3},{3,4},{4,5},{5,6},{6,7},{8,9},{9,10},{10,11},{11... | collective-permute-start | bytes 393224 | tf_op jit(solution)/shard_map/ppermute | solution.py:57
  44.4 13.1 %collective-permute-start.13 = (f32[2,128,128]{2,1,0:T(8,128)S(1)}, f32[2,128,128]{2,1,0:T(8,128)S(1)}, u32[]{:S(2)}, u32[]{:S(2)}) collective-permute-start(f32[2,128,128]{2,1,0:T(8,128)S(1)} %collective-permute-done.12), channel_id=1, source_target_pairs={{1,0},{2,1},{3,2},{4,3},{5,4},{6,5},{7,6},{9,8},{10,9},{11,10},{12... | collective-permute-start | bytes 393224 | tf_op jit(solution)/shard_map/ppermute | solution.py:58
  46.3 6.5 %collective-permute-start.6 = (f32[2,128,128]{2,1,0:T(8,128)S(1)}, f32[2,128,128]{2,1,0:T(8,128)S(1)}, u32[]{:S(2)}, u32[]{:S(2)}) collective-permute-start(f32[2,128,128]{2,1,0:T(8,128)S(1)} %collective-permute-done.5), channel_id=1, source_target_pairs={{0,1},{1,2},{2,3},{3,4},{4,5},{5,6},{6,7},{8,9},{9,10},{10,11},{11... | collective-permute-start | bytes 393224 | tf_op jit(solution)/shard_map/ppermute | solution.py:57
  58.2 2.4 copy-start
  60.6 21.9 %collective-permute-start.17 = (f32[12,1,128,128]{3,2,1,0:T(8,128)S(1)}, f32[12,1,128,128]{3,2,1,0:T(8,128)S(1)}, u32[]{:S(2)}, u32[]{:S(2)}) collective-permute-start(f32[12,1,128,128]{3,2,1,0:T(8,128)S(1)} %copy-done), channel_id=1, source_target_pairs={{0,384},{32,416},{64,448},{96,480},{128,0},{160,32},{192,64},{224,... | collective-permute-start | bytes 2359304 | tf_op jit(solution)/shard_map/ppermute | solution.py:27
  65.0 17.5 %collective-permute-start.16 = (f32[12,1,128,128]{3,2,1,0:T(8,128)S(1)}, f32[12,1,128,128]{3,2,1,0:T(8,128)S(1)}, u32[]{:S(2)}, u32[]{:S(2)}) collective-permute-start(f32[12,1,128,128]{3,2,1,0:T(8,128)S(1)} %copy-done), channel_id=1, source_target_pairs={{0,256},{32,288},{64,320},{96,352},{128,384},{160,416},{192,448},{... | collective-permute-start | bytes 2359304 | tf_op jit(solution)/shard_map/ppermute | solution.py:27
  67.4 37.2 %collective-permute-start.15 = (f32[12,1,128,128]{3,2,1,0:T(8,128)S(1)}, f32[12,1,128,128]{3,2,1,0:T(8,128)S(1)}, u32[]{:S(2)}, u32[]{:S(2)}) collective-permute-start(f32[12,1,128,128]{3,2,1,0:T(8,128)S(1)} %copy-done), channel_id=1, source_target_pairs={{0,128},{32,160},{64,192},{96,224},{128,256},{160,288},{192,320},{... | collective-permute-start | bytes 2359304 | tf_op jit(solution)/shard_map/ppermute | solution.py:27
  69.9 79.8 %collective-permute-start.14 = (f32[12,1,128,128]{3,2,1,0:T(8,128)S(1)}, f32[12,1,128,128]{3,2,1,0:T(8,128)S(1)}, u32[]{:S(2)}, u32[]{:S(2)}) collective-permute-start(f32[12,1,128,128]{3,2,1,0:T(8,128)S(1)} %copy-done), channel_id=1, source_target_pairs={{0,64},{32,96},{64,0},{96,32},{128,192},{160,224},{192,128},{224,1... | collective-permute-start | bytes 2359304 | tf_op jit(solution)/shard_map/ppermute | solution.py:21
  149.7 48.9 %collective-permute-start.23 = (f32[16,128,128]{2,1,0:T(8,128)S(1)}, f32[16,128,128]{2,1,0:T(8,128)S(1)}, u32[]{:S(2)}, u32[]{:S(2)}) collective-permute-start(f32[16,128,128]{2,1,0:T(8,128)S(1)} %bitcast_select_fusion), channel_id=1, source_target_pairs={{0,24},{1,25},{2,26},{3,27},{4,28},{5,29},{6,30},{7,31},{8,0},{9,1... | collective-permute-start | bytes 3145736 | tf_op jit(solution)/shard_map/ppermute | solution.py:70
  154.3 48.7 %collective-permute-start.22 = (f32[16,128,128]{2,1,0:T(8,128)S(1)}, f32[16,128,128]{2,1,0:T(8,128)S(1)}, u32[]{:S(2)}, u32[]{:S(2)}) collective-permute-start(f32[16,128,128]{2,1,0:T(8,128)S(1)} %bitcast_select_fusion), channel_id=1, source_target_pairs={{0,16},{1,17},{2,18},{3,19},{4,20},{5,21},{6,22},{7,23},{8,24},{9,... | collective-permute-start | bytes 3145736 | tf_op jit(solution)/shard_map/ppermute | solution.py:70
  156.6 48.7 %collective-permute-start.21 = (f32[16,128,128]{2,1,0:T(8,128)S(1)}, f32[16,128,128]{2,1,0:T(8,128)S(1)}, u32[]{:S(2)}, u32[]{:S(2)}) collective-permute-start(f32[16,128,128]{2,1,0:T(8,128)S(1)} %bitcast_select_fusion), channel_id=1, source_target_pairs={{0,8},{1,9},{2,10},{3,11},{4,12},{5,13},{6,14},{7,15},{8,16},{9,17... | collective-permute-start | bytes 3145736 | tf_op jit(solution)/shard_map/ppermute | solution.py:70
  159.2 48.5 %collective-permute-start.20 = (f32[12,1,128,128]{3,2,1,0:T(8,128)S(1)}, f32[12,1,128,128]{3,2,1,0:T(8,128)S(1)}, u32[]{:S(2)}, u32[]{:S(2)}) collective-permute-start(f32[12,1,128,128]{3,2,1,0:T(8,128)S(1)} %collective-permute-done.14), channel_id=1, source_target_pairs={{0,384},{32,416},{64,448},{96,480},{128,0},{160,32},{192,64},{224,... | collective-permute-start | bytes 2359304 | tf_op jit(solution)/shard_map/ppermute | solution.py:27
  163.2 44.5 %collective-permute-start.19 = (f32[12,1,128,128]{3,2,1,0:T(8,128)S(1)}, f32[12,1,128,128]{3,2,1,0:T(8,128)S(1)}, u32[]{:S(2)}, u32[]{:S(2)}) collective-permute-start(f32[12,1,128,128]{3,2,1,0:T(8,128)S(1)} %collective-permute-done.14), channel_id=1, source_target_pairs={{0,256},{32,288},{64,320},{96,352},{128,384},{160,416},{192,448},{... | collective-permute-start | bytes 2359304 | tf_op jit(solution)/shard_map/ppermute | solution.py:27
  198.6 20.6 %collective-permute-start.18 = (f32[12,1,128,128]{3,2,1,0:T(8,128)S(1)}, f32[12,1,128,128]{3,2,1,0:T(8,128)S(1)}, u32[]{:S(2)}, u32[]{:S(2)}) collective-permute-start(f32[12,1,128,128]{3,2,1,0:T(8,128)S(1)} %collective-permute-done.14), channel_id=1, source_target_pairs={{0,128},{32,160},{64,192},{96,224},{128,256},{160,288},{192,320},{... | collective-permute-start | bytes 2359304 | tf_op jit(solution)/shard_map/ppermute | solution.py:27
  224.0 6.3 %copy-start.2 = (s32[12,4]{0,1:T(4,128)S(1)}, s32[12,4]{0,1:T(4,128)}, u32[]{:S(2)}) copy-start(s32[12,4]{0,1:T(4,128)} %param.12) | copy-start | bytes 580
  224.0 6.4 %copy-start.1 = (s32[12,16]{1,0:T(8,128)S(1)}, s32[12,16]{1,0:T(8,128)}, u32[]{:S(2)}) copy-start(s32[12,16]{1,0:T(8,128)} %param.8) | copy-start | bytes 2308
  224.0 6.4 %copy-start.3 = (s32[64]{0:T(128)S(1)}, s32[64]{0:T(128)}, u32[]{:S(2)}) copy-start(s32[64]{0:T(128)} %param.13) | copy-start | bytes 772
  224.0 9.1 %copy-start.4 = (s32[64,1]{0,1:T(1,128)S(1)}, s32[64,1]{0,1:T(1,128)}, u32[]{:S(2)}) copy-start(s32[64,1]{0,1:T(1,128)} %param.11) | copy-start | bytes 772
  224.0 9.5 %copy-start.5 = (s32[12]{0:T(128)S(1)}, s32[12]{0:T(128)}, u32[]{:S(2)}) copy-start(s32[12]{0:T(128)} %param.9) | copy-start | bytes 148
  225.9 26.2 %collective-permute-start.24 = (f32[12,8,128,128]{3,2,1,0:T(8,128)}, f32[12,8,128,128]{3,2,1,0:T(8,128)}, u32[]{:S(2)}, u32[]{:S(2)}) collective-permute-start(f32[12,8,128,128]{3,2,1,0:T(8,128)} %constant_dynamic-update-slice_fusion.a_ref), channel_id=1, source_target_pairs={{0,32},{32,0},{64,96},{96,64},{128,160},{160,128},{192,224},{224,1... | collective-permute-start | bytes 18874376 | tf_op jit(solution)/shard_map/ppermute | solution.py:32

commit v12 on v8

--- a/solution.py
+++ b/solution.py
@@ -139,7 +139,7 @@
 
         return carry
 
-    lax.fori_loop(0, n_slots, body, 0)
+    lax.fori_loop(0, n_slots, body, 0, unroll=True)
 
 
 def row_products(whole_slots, panels, panel_index, target, pattern_slots, acc=None, interpret=False):

time: 228 us -> 229 us (level)
  the two profiles are of different devices: /device:TPU:107 before, /device:TPU:99 now
where the time goes in v12:
time: 229 us; the launch traced here: 227 us
  starting transfers between devices  87.4 us (38%)
  waiting for transfers between devices  82.7 us (36%)
  Pallas kernels  27 us (12%)
  local copies, waits for them, and re-layouts  24.9 us (11%)
  other arithmetic  4.4 us (2%)
    ppermute x7, starting transfers between devices, line_z(): going_right = lax.ppermute(going_right, 'col', right)  32.1 us
    ppermute x1, waiting for transfers between devices, swap_z(): return lax.ppermute(chunk, 'row', pairs)  30.6 us
    pallas_call x2, Pallas kernels, row_products(): pl.pallas_call(product_kernel, grid_spec=grid_spec, out_shape=jax.ShapeDt...  27 us
    ppermute x6, waiting for transfers between devices, ring_x(): parts.append(lax.ppermute(held, 'row', shift))  26.4 us
    ppermute x3, waiting for transfers between devices, ring_y(): parts.append(lax.ppermute(held, 'col', shift))  25.7 us
    ppermute x6, starting transfers between devices, ring_x(): parts.append(lax.ppermute(held, 'row', shift))  19.3 us
    unnamed x34, local copies, waits for them, and re-layouts  17.1 us
    ppermute x7, starting transfers between devices, line_z(): going_left = lax.ppermute(going_left, 'col', left)  13.4 us
  transfers between devices with their start and end apart: 25, of which 5 were waited for; matrix products, arithmetic and copies ran while one was open for 11% of the time, Pallas kernels for 6%

profile of v12, /device:TPU:99, one launch (start us, length us, event | category | flops | bytes accessed | tf_op | source)
XLA Modules:
  0.0 226.8 jit_solution(4913381304813132765)
XLA Ops:
  0.0 4.7 %collective-permute-start = (f32[2,128,128]{2,1,0:T(8,128)}, f32[2,128,128]{2,1,0:T(8,128)S(1)}, u32[]{:S(2)}, u32[]{:S(2)}) collective-permute-start(f32[2,128,128]{2,1,0:T(8,128)} %bitcast.41), channel_id=1, source_target_pairs={{0,1},{1,2},{2,3},{3,4},{4,5},{5,6},{6,7},{8,9},{9,10},{10,11},{11... | collective-permute-start | bytes 393224 | tf_op jit(solution)/shard_map/ppermute | solution.py:57
  4.8 1.9 collective-permute-start.7
  6.7 1.6 bitcast_dynamic-update-slice_fusion.14
  8.5 4.6 %collective-permute-start.1 = (f32[2,128,128]{2,1,0:T(8,128)S(1)}, f32[2,128,128]{2,1,0:T(8,128)S(1)}, u32[]{:S(2)}, u32[]{:S(2)}) collective-permute-start(f32[2,128,128]{2,1,0:T(8,128)S(1)} %collective-permute-done), channel_id=1, source_target_pairs={{0,1},{1,2},{2,3},{3,4},{4,5},{5,6},{6,7},{8,9},{9,10},{10,11},{11... | collective-permute-start | bytes 393224 | tf_op jit(solution)/shard_map/ppermute | solution.py:57
  13.1 1.9 collective-permute-start.8
  15.0 0.7 bitcast_dynamic-update-slice_fusion.13
  15.7 4.6 %collective-permute-start.2 = (f32[2,128,128]{2,1,0:T(8,128)S(1)}, f32[2,128,128]{2,1,0:T(8,128)S(1)}, u32[]{:S(2)}, u32[]{:S(2)}) collective-permute-start(f32[2,128,128]{2,1,0:T(8,128)S(1)} %collective-permute-done.1), channel_id=1, source_target_pairs={{0,1},{1,2},{2,3},{3,4},{4,5},{5,6},{6,7},{8,9},{9,10},{10,11},{11... | collective-permute-start | bytes 393224 | tf_op jit(solution)/shard_map/ppermute | solution.py:57
  20.2 1.9 collective-permute-start.9
  22.2 0.7 bitcast_dynamic-update-slice_fusion.12
  22.8 4.6 %collective-permute-start.3 = (f32[2,128,128]{2,1,0:T(8,128)S(1)}, f32[2,128,128]{2,1,0:T(8,128)S(1)}, u32[]{:S(2)}, u32[]{:S(2)}) collective-permute-start(f32[2,128,128]{2,1,0:T(8,128)S(1)} %collective-permute-done.2), channel_id=1, source_target_pairs={{0,1},{1,2},{2,3},{3,4},{4,5},{5,6},{6,7},{8,9},{9,10},{10,11},{11... | collective-permute-start | bytes 393224 | tf_op jit(solution)/shard_map/ppermute | solution.py:57
  27.4 1.9 collective-permute-start.10
  29.3 0.7 bitcast_dynamic-update-slice_fusion.11
  30.0 4.6 %collective-permute-start.4 = (f32[2,128,128]{2,1,0:T(8,128)S(1)}, f32[2,128,128]{2,1,0:T(8,128)S(1)}, u32[]{:S(2)}, u32[]{:S(2)}) collective-permute-start(f32[2,128,128]{2,1,0:T(8,128)S(1)} %collective-permute-done.3), channel_id=1, source_target_pairs={{0,1},{1,2},{2,3},{3,4},{4,5},{5,6},{6,7},{8,9},{9,10},{10,11},{11... | collective-permute-start | bytes 393224 | tf_op jit(solution)/shard_map/ppermute | solution.py:57
  34.6 1.9 collective-permute-start.11
  36.5 0.7 bitcast_dynamic-update-slice_fusion.10
  37.2 4.6 %collective-permute-start.5 = (f32[2,128,128]{2,1,0:T(8,128)S(1)}, f32[2,128,128]{2,1,0:T(8,128)S(1)}, u32[]{:S(2)}, u32[]{:S(2)}) collective-permute-start(f32[2,128,128]{2,1,0:T(8,128)S(1)} %collective-permute-done.4), channel_id=1, source_target_pairs={{0,1},{1,2},{2,3},{3,4},{4,5},{5,6},{6,7},{8,9},{9,10},{10,11},{11... | collective-permute-start | bytes 393224 | tf_op jit(solution)/shard_map/ppermute | solution.py:57
  41.8 1.9 collective-permute-start.12
  43.7 0.7 bitcast_dynamic-update-slice_fusion.9
  44.4 4.6 %collective-permute-start.6 = (f32[2,128,128]{2,1,0:T(8,128)S(1)}, f32[2,128,128]{2,1,0:T(8,128)S(1)}, u32[]{:S(2)}, u32[]{:S(2)}) collective-permute-start(f32[2,128,128]{2,1,0:T(8,128)S(1)} %collective-permute-done.5), channel_id=1, source_target_pairs={{0,1},{1,2},{2,3},{3,4},{4,5},{5,6},{6,7},{8,9},{9,10},{10,11},{11... | collective-permute-start | bytes 393224 | tf_op jit(solution)/shard_map/ppermute | solution.py:57
  49.0 1.9 collective-permute-start.13
  50.9 0.7 bitcast_dynamic-update-slice_fusion.8
  51.6 0.7 bitcast_dynamic-update-slice_fusion.7
  52.2 0.7 bitcast_dynamic-update-slice_fusion.6
  52.9 0.7 bitcast_dynamic-update-slice_fusion.5
  53.5 0.7 bitcast_dynamic-update-slice_fusion.4
  54.2 0.7 bitcast_dynamic-update-slice_fusion.3
  54.9 0.7 bitcast_dynamic-update-slice_fusion.2
  55.5 0.7 bitcast_dynamic-update-slice_fusion.1
  56.2 0.7 bitcast_dynamic-update-slice_fusion
  56.9 2.2 gather_fusion.1
  59.3 4.6 %collective-permute-start.20 = (f32[16,128,128]{2,1,0:T(8,128)S(1)}, f32[16,128,128]{2,1,0:T(8,128)S(1)}, u32[]{:S(2)}, u32[]{:S(2)}) collective-permute-start(f32[16,128,128]{2,1,0:T(8,128)S(1)} %bitcast_select_fusion), channel_id=1, source_target_pairs={{0,24},{1,25},{2,26},{3,27},{4,28},{5,29},{6,30},{7,31},{8,0},{9,1... | collective-permute-start | bytes 3145736 | tf_op jit(solution)/shard_map/ppermute | solution.py:70
  63.9 2.3 collective-permute-start.19
  66.2 2.6 %collective-permute-start.18 = (f32[16,128,128]{2,1,0:T(8,128)S(1)}, f32[16,128,128]{2,1,0:T(8,128)S(1)}, u32[]{:S(2)}, u32[]{:S(2)}) collective-permute-start(f32[16,128,128]{2,1,0:T(8,128)S(1)} %bitcast_select_fusion), channel_id=1, source_target_pairs={{0,8},{1,9},{2,10},{3,11},{4,12},{5,13},{6,14},{7,15},{8,16},{9,17... | collective-permute-start | bytes 3145736 | tf_op jit(solution)/shard_map/ppermute | solution.py:70
  68.8 10.6 %collective-permute-start.14 = (f32[12,1,128,128]{3,2,1,0:T(8,128)S(1)}, f32[12,1,128,128]{3,2,1,0:T(8,128)S(1)}, u32[]{:S(2)}, u32[]{:S(2)}) collective-permute-start(f32[12,1,128,128]{3,2,1,0:T(8,128)S(1)} %copy-done), channel_id=1, source_target_pairs={{0,64},{32,96},{64,0},{96,32},{128,192},{160,224},{192,128},{224,1... | collective-permute-start | bytes 2359304 | tf_op jit(solution)/shard_map/ppermute | solution.py:21
  79.4 3.1 %collective-permute-start.15 = (f32[12,1,128,128]{3,2,1,0:T(8,128)S(1)}, f32[12,1,128,128]{3,2,1,0:T(8,128)S(1)}, u32[]{:S(2)}, u32[]{:S(2)}) collective-permute-start(f32[12,1,128,128]{3,2,1,0:T(8,128)S(1)} %copy-done), channel_id=1, source_target_pairs={{0,128},{32,160},{64,192},{96,224},{128,256},{160,288},{192,320},{... | collective-permute-start | bytes 2359304 | tf_op jit(solution)/shard_map/ppermute | solution.py:27
  82.6 2.7 %collective-permute-start.16 = (f32[12,1,128,128]{3,2,1,0:T(8,128)S(1)}, f32[12,1,128,128]{3,2,1,0:T(8,128)S(1)}, u32[]{:S(2)}, u32[]{:S(2)}) collective-permute-start(f32[12,1,128,128]{3,2,1,0:T(8,128)S(1)} %copy-done), channel_id=1, source_target_pairs={{0,256},{32,288},{64,320},{96,352},{128,384},{160,416},{192,448},{... | collective-permute-start | bytes 2359304 | tf_op jit(solution)/shard_map/ppermute | solution.py:27
  85.3 3.8 %collective-permute-start.17 = (f32[12,1,128,128]{3,2,1,0:T(8,128)S(1)}, f32[12,1,128,128]{3,2,1,0:T(8,128)S(1)}, u32[]{:S(2)}, u32[]{:S(2)}) collective-permute-start(f32[12,1,128,128]{3,2,1,0:T(8,128)S(1)} %copy-done), channel_id=1, source_target_pairs={{0,384},{32,416},{64,448},{96,480},{128,0},{160,32},{192,64},{224,... | collective-permute-start | bytes 2359304 | tf_op jit(solution)/shard_map/ppermute | solution.py:27
  89.1 25.7 %collective-permute-done.18 = f32[16,128,128]{2,1,0:T(8,128)S(1)} collective-permute-done((f32[16,128,128]{2,1,0:T(8,128)S(1)}, f32[16,128,128]{2,1,0:T(8,128)S(1)}, u32[]{:S(2)}, u32[]{:S(2)}) %collective-permute-start.18) | collective-permute-done | bytes 1048608 | tf_op jit(solution)/shard_map/ppermute | solution.py:70
  114.9 2.4 %pad_maximum_fusion.b_ref = f32[64,128,128]{2,1,0:T(8,128)} fusion(f32[16,128,128]{2,1,0:T(8,128)S(1)} %collective-permute-done.20, f32[16,128,128]{2,1,0:T(8,128)S(1)} %collective-permute-done.19, f32[16,128,128]{2,1,0:T(8,128)S(1)} %collective-permute-done.18, f32[16,128,128]{2,1,0:T(8,128)S(1)} %bitcast_select_fusion), kind=kLoop, calls=%fused_computation.2 | loop fusion | flops 3145728 | bytes 8388608 | tf_op jit(solution)/shard_map/concatenate | solution.py:71
  117.3 30.6 %collective-permute-done.14 = f32[12,1,128,128]{3,2,1,0:T(8,128)S(1)} collective-permute-done((f32[12,1,128,128]{3,2,1,0:T(8,128)S(1)}, f32[12,1,128,128]{3,2,1,0:T(8,128)S(1)}, u32[]{:S(2)}, u32[]{:S(2)}) %collective-permute-start.14) | collective-permute-done | bytes 786464 | tf_op jit(solution)/shard_map/ppermute | solution.py:21
  147.9 3.1 %collective-permute-start.21 = (f32[12,1,128,128]{3,2,1,0:T(8,128)S(1)}, f32[12,1,128,128]{3,2,1,0:T(8,128)S(1)}, u32[]{:S(2)}, u32[]{:S(2)}) collective-permute-start(f32[12,1,128,128]{3,2,1,0:T(8,128)S(1)} %collective-permute-done.14), channel_id=1, source_target_pairs={{0,128},{32,160},{64,192},{96,224},{128,256},{160,288},{192,320},{... | collective-permute-start | bytes 2359304 | tf_op jit(solution)/shard_map/ppermute | solution.py:27
  151.0 2.7 %collective-permute-start.22 = (f32[12,1,128,128]{3,2,1,0:T(8,128)S(1)}, f32[12,1,128,128]{3,2,1,0:T(8,128)S(1)}, u32[]{:S(2)}, u32[]{:S(2)}) collective-permute-start(f32[12,1,128,128]{3,2,1,0:T(8,128)S(1)} %collective-permute-done.14), channel_id=1, source_target_pairs={{0,256},{32,288},{64,320},{96,352},{128,384},{160,416},{192,448},{... | collective-permute-start | bytes 2359304 | tf_op jit(solution)/shard_map/ppermute | solution.py:27
  153.7 3.8 %collective-permute-start.23 = (f32[12,1,128,128]{3,2,1,0:T(8,128)S(1)}, f32[12,1,128,128]{3,2,1,0:T(8,128)S(1)}, u32[]{:S(2)}, u32[]{:S(2)}) collective-permute-start(f32[12,1,128,128]{3,2,1,0:T(8,128)S(1)} %collective-permute-done.14), channel_id=1, source_target_pairs={{0,384},{32,416},{64,448},{96,480},{128,0},{160,32},{192,64},{224,... | collective-permute-start | bytes 2359304 | tf_op jit(solution)/shard_map/ppermute | solution.py:27
  157.5 1.0 constant_dynamic-update-slice_fusion.7
  158.5 1.0 constant_dynamic-update-slice_fusion.6
  159.5 1.0 constant_dynamic-update-slice_fusion.5
  160.5 7.8 %collective-permute-done.21 = f32[12,1,128,128]{3,2,1,0:T(8,128)S(1)} collective-permute-done((f32[12,1,128,128]{3,2,1,0:T(8,128)S(1)}, f32[12,1,128,128]{3,2,1,0:T(8,128)S(1)}, u32[]{:S(2)}, u32[]{:S(2)}) %collective-permute-start.21) | collective-permute-done | bytes 786464 | tf_op jit(solution)/shard_map/ppermute | solution.py:27
  168.3 1.0 constant_dynamic-update-slice_fusion.4
  169.3 0.9 constant_dynamic-update-slice_fusion.3
  170.2 2.4 %collective-permute-done.22 = f32[12,1,128,128]{3,2,1,0:T(8,128)S(1)} collective-permute-done((f32[12,1,128,128]{3,2,1,0:T(8,128)S(1)}, f32[12,1,128,128]{3,2,1,0:T(8,128)S(1)}, u32[]{:S(2)}, u32[]{:S(2)}) %collective-permute-start.22) | collective-permute-done | bytes 786464 | tf_op jit(solution)/shard_map/ppermute | solution.py:27
  172.7 0.9 constant_dynamic-update-slice_fusion.2
  173.6 0.9 constant_dynamic-update-slice_fusion.1
  174.5 16.2 %collective-permute-done.23 = f32[12,1,128,128]{3,2,1,0:T(8,128)S(1)} collective-permute-done((f32[12,1,128,128]{3,2,1,0:T(8,128)S(1)}, f32[12,1,128,128]{3,2,1,0:T(8,128)S(1)}, u32[]{:S(2)}, u32[]{:S(2)}) %collective-permute-start.23) | collective-permute-done | bytes 786464 | tf_op jit(solution)/shard_map/ppermute | solution.py:27
  190.7 0.9 constant_dynamic-update-slice_fusion.a_ref
  191.6 2.4 %collective-permute-start.24 = (f32[12,8,128,128]{3,2,1,0:T(8,128)}, f32[12,8,128,128]{3,2,1,0:T(8,128)}, u32[]{:S(2)}, u32[]{:S(2)}) collective-permute-start(f32[12,8,128,128]{3,2,1,0:T(8,128)} %constant_dynamic-update-slice_fusion.a_ref), channel_id=1, source_target_pairs={{0,32},{32,0},{64,96},{96,64},{128,160},{160,128},{192,224},{224,1... | collective-permute-start | bytes 18874376 | tf_op jit(solution)/shard_map/ppermute | solution.py:32
  194.6 0.6 gather_fusion
  195.4 0.7 reshape.328.pidx_ref
  196.2 0.4 select_reduce_fusion
  196.9 0.8 convert_reduce_fusion
  197.8 0.6 reshape.329.sidx_ref
  198.5 0.6 reshape.330.pidx_ref
  199.2 0.7 reshape.331.sidx_ref
  199.8 13.2 %shard_map.73.rest_0_ = f32[12,4,128,128]{3,2,1,0:T(8,128)} custom-call(s32[96]{0:T(128)} %reshape.330.pidx_ref, s32[96]{0:T(128)} %reshape.331.sidx_ref, f32[12,8,128,128]{3,2,1,0:T(8,128)} %constant_dynamic-update-slice_fusion.a_ref, f32[64,128,128]{2,1,0:T(8,128)} %pad_maximum_fusion.b_ref), custom_call_target="tpu_custom_call" | custom-call | tf_op jit(solution)/shard_map/pallas_call | solution.py:158
  213.0 13.8 %shard_map.74 = f32[12,4,128,128]{3,2,1,0:T(8,128)} custom-call(s32[96]{0:T(128)} %reshape.328.pidx_ref, s32[96]{0:T(128)} %reshape.329.sidx_ref, f32[12,8,128,128]{3,2,1,0:T(8,128)} %collective-permute-done.24.a_ref, f32[64,128,128]{2,1,0:T(8,128)} %pad_maximum_fusion.b_ref, f32[12,4,128,128]{3,2,1,0:T(8,128)} %shard_map.73.rest_0_), custom_call_target="tpu_custom_call", output_to_operand_aliasing={{}: (4, {})} | custom-call | tf_op jit(solution)/shard_map/pallas_call | solution.py:158
  (57 shorter events, 1.9 us)
Async XLA Ops:
  0.0 8.5 %collective-permute-start = (f32[2,128,128]{2,1,0:T(8,128)}, f32[2,128,128]{2,1,0:T(8,128)S(1)}, u32[]{:S(2)}, u32[]{:S(2)}) collective-permute-start(f32[2,128,128]{2,1,0:T(8,128)} %bitcast.41), channel_id=1, source_target_pairs={{0,1},{1,2},{2,3},{3,4},{4,5},{5,6},{6,7},{8,9},{9,10},{10,11},{11... | collective-permute-start | bytes 393224 | tf_op jit(solution)/shard_map/ppermute | solution.py:57
  4.8 8.3 %collective-permute-start.7 = (f32[2,128,128]{2,1,0:T(8,128)}, f32[2,128,128]{2,1,0:T(8,128)S(1)}, u32[]{:S(2)}, u32[]{:S(2)}) collective-permute-start(f32[2,128,128]{2,1,0:T(8,128)} %bitcast.42), channel_id=1, source_target_pairs={{1,0},{2,1},{3,2},{4,3},{5,4},{6,5},{7,6},{9,8},{10,9},{11,10},{12... | collective-permute-start | bytes 393224 | tf_op jit(solution)/shard_map/ppermute | solution.py:58
  8.5 7.2 %collective-permute-start.1 = (f32[2,128,128]{2,1,0:T(8,128)S(1)}, f32[2,128,128]{2,1,0:T(8,128)S(1)}, u32[]{:S(2)}, u32[]{:S(2)}) collective-permute-start(f32[2,128,128]{2,1,0:T(8,128)S(1)} %collective-permute-done), channel_id=1, source_target_pairs={{0,1},{1,2},{2,3},{3,4},{4,5},{5,6},{6,7},{8,9},{9,10},{10,11},{11... | collective-permute-start | bytes 393224 | tf_op jit(solution)/shard_map/ppermute | solution.py:57
  13.1 7.2 %collective-permute-start.8 = (f32[2,128,128]{2,1,0:T(8,128)S(1)}, f32[2,128,128]{2,1,0:T(8,128)S(1)}, u32[]{:S(2)}, u32[]{:S(2)}) collective-permute-start(f32[2,128,128]{2,1,0:T(8,128)S(1)} %collective-permute-done.7), channel_id=1, source_target_pairs={{1,0},{2,1},{3,2},{4,3},{5,4},{6,5},{7,6},{9,8},{10,9},{11,10},{12... | collective-permute-start | bytes 393224 | tf_op jit(solution)/shard_map/ppermute | solution.py:58
  15.7 7.2 %collective-permute-start.2 = (f32[2,128,128]{2,1,0:T(8,128)S(1)}, f32[2,128,128]{2,1,0:T(8,128)S(1)}, u32[]{:S(2)}, u32[]{:S(2)}) collective-permute-start(f32[2,128,128]{2,1,0:T(8,128)S(1)} %collective-permute-done.1), channel_id=1, source_target_pairs={{0,1},{1,2},{2,3},{3,4},{4,5},{5,6},{6,7},{8,9},{9,10},{10,11},{11... | collective-permute-start | bytes 393224 | tf_op jit(solution)/shard_map/ppermute | solution.py:57
  20.2 7.2 %collective-permute-start.9 = (f32[2,128,128]{2,1,0:T(8,128)S(1)}, f32[2,128,128]{2,1,0:T(8,128)S(1)}, u32[]{:S(2)}, u32[]{:S(2)}) collective-permute-start(f32[2,128,128]{2,1,0:T(8,128)S(1)} %collective-permute-done.8), channel_id=1, source_target_pairs={{1,0},{2,1},{3,2},{4,3},{5,4},{6,5},{7,6},{9,8},{10,9},{11,10},{12... | collective-permute-start | bytes 393224 | tf_op jit(solution)/shard_map/ppermute | solution.py:58
  22.8 7.2 %collective-permute-start.3 = (f32[2,128,128]{2,1,0:T(8,128)S(1)}, f32[2,128,128]{2,1,0:T(8,128)S(1)}, u32[]{:S(2)}, u32[]{:S(2)}) collective-permute-start(f32[2,128,128]{2,1,0:T(8,128)S(1)} %collective-permute-done.2), channel_id=1, source_target_pairs={{0,1},{1,2},{2,3},{3,4},{4,5},{5,6},{6,7},{8,9},{9,10},{10,11},{11... | collective-permute-start | bytes 393224 | tf_op jit(solution)/shard_map/ppermute | solution.py:57
  27.4 7.2 %collective-permute-start.10 = (f32[2,128,128]{2,1,0:T(8,128)S(1)}, f32[2,128,128]{2,1,0:T(8,128)S(1)}, u32[]{:S(2)}, u32[]{:S(2)}) collective-permute-start(f32[2,128,128]{2,1,0:T(8,128)S(1)} %collective-permute-done.9), channel_id=1, source_target_pairs={{1,0},{2,1},{3,2},{4,3},{5,4},{6,5},{7,6},{9,8},{10,9},{11,10},{12... | collective-permute-start | bytes 393224 | tf_op jit(solution)/shard_map/ppermute | solution.py:58
  30.0 7.2 %collective-permute-start.4 = (f32[2,128,128]{2,1,0:T(8,128)S(1)}, f32[2,128,128]{2,1,0:T(8,128)S(1)}, u32[]{:S(2)}, u32[]{:S(2)}) collective-permute-start(f32[2,128,128]{2,1,0:T(8,128)S(1)} %collective-permute-done.3), channel_id=1, source_target_pairs={{0,1},{1,2},{2,3},{3,4},{4,5},{5,6},{6,7},{8,9},{9,10},{10,11},{11... | collective-permute-start | bytes 393224 | tf_op jit(solution)/shard_map/ppermute | solution.py:57
  34.6 7.2 %collective-permute-start.11 = (f32[2,128,128]{2,1,0:T(8,128)S(1)}, f32[2,128,128]{2,1,0:T(8,128)S(1)}, u32[]{:S(2)}, u32[]{:S(2)}) collective-permute-start(f32[2,128,128]{2,1,0:T(8,128)S(1)} %collective-permute-done.10), channel_id=1, source_target_pairs={{1,0},{2,1},{3,2},{4,3},{5,4},{6,5},{7,6},{9,8},{10,9},{11,10},{12... | collective-permute-start | bytes 393224 | tf_op jit(solution)/shard_map/ppermute | solution.py:58
  37.2 7.2 %collective-permute-start.5 = (f32[2,128,128]{2,1,0:T(8,128)S(1)}, f32[2,128,128]{2,1,0:T(8,128)S(1)}, u32[]{:S(2)}, u32[]{:S(2)}) collective-permute-start(f32[2,128,128]{2,1,0:T(8,128)S(1)} %collective-permute-done.4), channel_id=1, source_target_pairs={{0,1},{1,2},{2,3},{3,4},{4,5},{5,6},{6,7},{8,9},{9,10},{10,11},{11... | collective-permute-start | bytes 393224 | tf_op jit(solution)/shard_map/ppermute | solution.py:57
  41.8 7.2 %collective-permute-start.12 = (f32[2,128,128]{2,1,0:T(8,128)S(1)}, f32[2,128,128]{2,1,0:T(8,128)S(1)}, u32[]{:S(2)}, u32[]{:S(2)}) collective-permute-start(f32[2,128,128]{2,1,0:T(8,128)S(1)} %collective-permute-done.11), channel_id=1, source_target_pairs={{1,0},{2,1},{3,2},{4,3},{5,4},{6,5},{7,6},{9,8},{10,9},{11,10},{12... | collective-permute-start | bytes 393224 | tf_op jit(solution)/shard_map/ppermute | solution.py:58
  44.4 7.2 %collective-permute-start.6 = (f32[2,128,128]{2,1,0:T(8,128)S(1)}, f32[2,128,128]{2,1,0:T(8,128)S(1)}, u32[]{:S(2)}, u32[]{:S(2)}) collective-permute-start(f32[2,128,128]{2,1,0:T(8,128)S(1)} %collective-permute-done.5), channel_id=1, source_target_pairs={{0,1},{1,2},{2,3},{3,4},{4,5},{5,6},{6,7},{8,9},{9,10},{10,11},{11... | collective-permute-start | bytes 393224 | tf_op jit(solution)/shard_map/ppermute | solution.py:57
  49.0 7.3 %collective-permute-start.13 = (f32[2,128,128]{2,1,0:T(8,128)S(1)}, f32[2,128,128]{2,1,0:T(8,128)S(1)}, u32[]{:S(2)}, u32[]{:S(2)}) collective-permute-start(f32[2,128,128]{2,1,0:T(8,128)S(1)} %collective-permute-done.12), channel_id=1, source_target_pairs={{1,0},{2,1},{3,2},{4,3},{5,4},{6,5},{7,6},{9,8},{10,9},{11,10},{12... | collective-permute-start | bytes 393224 | tf_op jit(solution)/shard_map/ppermute | solution.py:58
  56.9 11.9 %copy-start = (f32[12,1,128,128]{3,2,1,0:T(8,128)S(1)}, f32[12,1,128,128]{3,2,1,0:T(8,128)}, u32[]{:S(2)}) copy-start(f32[12,1,128,128]{3,2,1,0:T(8,128)} %param.7) | copy-start | bytes 2359300
  59.3 23.3 %collective-permute-start.20 = (f32[16,128,128]{2,1,0:T(8,128)S(1)}, f32[16,128,128]{2,1,0:T(8,128)S(1)}, u32[]{:S(2)}, u32[]{:S(2)}) collective-permute-start(f32[16,128,128]{2,1,0:T(8,128)S(1)} %bitcast_select_fusion), channel_id=1, source_target_pairs={{0,24},{1,25},{2,26},{3,27},{4,28},{5,29},{6,30},{7,31},{8,0},{9,1... | collective-permute-start | bytes 3145736 | tf_op jit(solution)/shard_map/ppermute | solution.py:70
  63.9 21.4 %collective-permute-start.19 = (f32[16,128,128]{2,1,0:T(8,128)S(1)}, f32[16,128,128]{2,1,0:T(8,128)S(1)}, u32[]{:S(2)}, u32[]{:S(2)}) collective-permute-start(f32[16,128,128]{2,1,0:T(8,128)S(1)} %bitcast_select_fusion), channel_id=1, source_target_pairs={{0,16},{1,17},{2,18},{3,19},{4,20},{5,21},{6,22},{7,23},{8,24},{9,... | collective-permute-start | bytes 3145736 | tf_op jit(solution)/shard_map/ppermute | solution.py:70
  66.2 48.7 %collective-permute-start.18 = (f32[16,128,128]{2,1,0:T(8,128)S(1)}, f32[16,128,128]{2,1,0:T(8,128)S(1)}, u32[]{:S(2)}, u32[]{:S(2)}) collective-permute-start(f32[16,128,128]{2,1,0:T(8,128)S(1)} %bitcast_select_fusion), channel_id=1, source_target_pairs={{0,8},{1,9},{2,10},{3,11},{4,12},{5,13},{6,14},{7,15},{8,16},{9,17... | collective-permute-start | bytes 3145736 | tf_op jit(solution)/shard_map/ppermute | solution.py:70
  68.8 79.1 %collective-permute-start.14 = (f32[12,1,128,128]{3,2,1,0:T(8,128)S(1)}, f32[12,1,128,128]{3,2,1,0:T(8,128)S(1)}, u32[]{:S(2)}, u32[]{:S(2)}) collective-permute-start(f32[12,1,128,128]{3,2,1,0:T(8,128)S(1)} %copy-done), channel_id=1, source_target_pairs={{0,64},{32,96},{64,0},{96,32},{128,192},{160,224},{192,128},{224,1... | collective-permute-start | bytes 2359304 | tf_op jit(solution)/shard_map/ppermute | solution.py:21
  79.4 68.4 %collective-permute-start.15 = (f32[12,1,128,128]{3,2,1,0:T(8,128)S(1)}, f32[12,1,128,128]{3,2,1,0:T(8,128)S(1)}, u32[]{:S(2)}, u32[]{:S(2)}) collective-permute-start(f32[12,1,128,128]{3,2,1,0:T(8,128)S(1)} %copy-done), channel_id=1, source_target_pairs={{0,128},{32,160},{64,192},{96,224},{128,256},{160,288},{192,320},{... | collective-permute-start | bytes 2359304 | tf_op jit(solution)/shard_map/ppermute | solution.py:27
  82.6 65.3 %collective-permute-start.16 = (f32[12,1,128,128]{3,2,1,0:T(8,128)S(1)}, f32[12,1,128,128]{3,2,1,0:T(8,128)S(1)}, u32[]{:S(2)}, u32[]{:S(2)}) collective-permute-start(f32[12,1,128,128]{3,2,1,0:T(8,128)S(1)} %copy-done), channel_id=1, source_target_pairs={{0,256},{32,288},{64,320},{96,352},{128,384},{160,416},{192,448},{... | collective-permute-start | bytes 2359304 | tf_op jit(solution)/shard_map/ppermute | solution.py:27
  85.3 62.5 %collective-permute-start.17 = (f32[12,1,128,128]{3,2,1,0:T(8,128)S(1)}, f32[12,1,128,128]{3,2,1,0:T(8,128)S(1)}, u32[]{:S(2)}, u32[]{:S(2)}) collective-permute-start(f32[12,1,128,128]{3,2,1,0:T(8,128)S(1)} %copy-done), channel_id=1, source_target_pairs={{0,384},{32,416},{64,448},{96,480},{128,0},{160,32},{192,64},{224,... | collective-permute-start | bytes 2359304 | tf_op jit(solution)/shard_map/ppermute | solution.py:27
  147.9 20.4 %collective-permute-start.21 = (f32[12,1,128,128]{3,2,1,0:T(8,128)S(1)}, f32[12,1,128,128]{3,2,1,0:T(8,128)S(1)}, u32[]{:S(2)}, u32[]{:S(2)}) collective-permute-start(f32[12,1,128,128]{3,2,1,0:T(8,128)S(1)} %collective-permute-done.14), channel_id=1, source_target_pairs={{0,128},{32,160},{64,192},{96,224},{128,256},{160,288},{192,320},{... | collective-permute-start | bytes 2359304 | tf_op jit(solution)/shard_map/ppermute | solution.py:27
  151.0 21.7 %collective-permute-start.22 = (f32[12,1,128,128]{3,2,1,0:T(8,128)S(1)}, f32[12,1,128,128]{3,2,1,0:T(8,128)S(1)}, u32[]{:S(2)}, u32[]{:S(2)}) collective-permute-start(f32[12,1,128,128]{3,2,1,0:T(8,128)S(1)} %collective-permute-done.14), channel_id=1, source_target_pairs={{0,256},{32,288},{64,320},{96,352},{128,384},{160,416},{192,448},{... | collective-permute-start | bytes 2359304 | tf_op jit(solution)/shard_map/ppermute | solution.py:27
  153.7 37.0 %collective-permute-start.23 = (f32[12,1,128,128]{3,2,1,0:T(8,128)S(1)}, f32[12,1,128,128]{3,2,1,0:T(8,128)S(1)}, u32[]{:S(2)}, u32[]{:S(2)}) collective-permute-start(f32[12,1,128,128]{3,2,1,0:T(8,128)S(1)} %collective-permute-done.14), channel_id=1, source_target_pairs={{0,384},{32,416},{64,448},{96,480},{128,0},{160,32},{192,64},{224,... | collective-permute-start | bytes 2359304 | tf_op jit(solution)/shard_map/ppermute | solution.py:27
  173.6 20.5 %copy-start.1 = (s32[12,16]{1,0:T(8,128)S(1)}, s32[12,16]{1,0:T(8,128)}, u32[]{:S(2)}) copy-start(s32[12,16]{1,0:T(8,128)} %param.8) | copy-start | bytes 2308
  173.6 20.5 %copy-start.3 = (s32[64]{0:T(128)S(1)}, s32[64]{0:T(128)}, u32[]{:S(2)}) copy-start(s32[64]{0:T(128)} %param.13) | copy-start | bytes 772
  173.6 22.4 %copy-start.2 = (s32[12,4]{0,1:T(4,128)S(1)}, s32[12,4]{0,1:T(4,128)}, u32[]{:S(2)}) copy-start(s32[12,4]{0,1:T(4,128)} %param.12) | copy-start | bytes 580
  173.6 22.6 %copy-start.4 = (s32[64,1]{0,1:T(1,128)S(1)}, s32[64,1]{0,1:T(1,128)}, u32[]{:S(2)}) copy-start(s32[64,1]{0,1:T(1,128)} %param.11) | copy-start | bytes 772
  173.6 23.0 %copy-start.5 = (s32[12]{0:T(128)S(1)}, s32[12]{0:T(128)}, u32[]{:S(2)}) copy-start(s32[12]{0:T(128)} %param.9) | copy-start | bytes 148
  191.6 21.4 %collective-permute-start.24 = (f32[12,8,128,128]{3,2,1,0:T(8,128)}, f32[12,8,128,128]{3,2,1,0:T(8,128)}, u32[]{:S(2)}, u32[]{:S(2)}) collective-permute-start(f32[12,8,128,128]{3,2,1,0:T(8,128)} %constant_dynamic-update-slice_fusion.a_ref), channel_id=1, source_target_pairs={{0,32},{32,0},{64,96},{96,64},{128,160},{160,128},{192,224},{224,1... | collective-permute-start | bytes 18874376 | tf_op jit(solution)/shard_map/ppermute | solution.py:32

commit v13 on v12

--- a/solution.py
+++ b/solution.py
@@ -87,8 +87,9 @@
     line_z, ring_y = col_stages(n_col)
     a_own, b_held = lax.optimization_barrier((a_blocks, line_z(b_blocks[:, 0])))
     a_other, own_x, panels = lax.optimization_barrier((swap_z(a_own), ring_x(a_own), ring_y(b_held)))
-    other_x = ring_x(a_other)
-    a_held = jnp.concatenate([p for pair in zip(own_x, other_x) for p in pair], axis=1)
+    own_four = jnp.concatenate(own_x, axis=1)
+    other_x, got_own = lax.optimization_barrier((ring_x(a_other), swap_core(own_four)))
+    half = 2 * len(own_x)
     rows_here, slot_all = a_cols.shape
     pattern_slots = c_cols.shape[1]
     block_size = panels.shape[-1]
@@ -102,11 +103,15 @@
     )
     target = jnp.where(jnp.any(weights > 0, axis=-1), jnp.argmax(weights, axis=-1), -1)
     target = target.astype(jnp.int32)
-    half = a_held.shape[1]
-    mine = row_products(a_held, panels, panel_index[:, :half].reshape(-1),
-                        target[:, :half].reshape(-1), pattern_slots)
-    return row_products(swap_core(a_held), panels, panel_index[:, half:].reshape(-1),
-                        target[:, half:].reshape(-1), pattern_slots, mine)
+    def products(a_list, held_ids, acc=None):
+        ids = jnp.array(held_ids, dtype=jnp.int32)
+        return row_products(a_list, panels, panel_index[:, ids].reshape(-1),
+                            target[:, ids].reshape(-1), pattern_slots, acc)
+
+    order = list(range(0, half, 2)) + list(range(1, half, 2))
+    mine = products([own_four] + other_x, order)
+    got_other = swap_core(jnp.concatenate(other_x, axis=1))
+    return products([got_own, got_other], [half + h for h in order], mine)
 
 
 def split_dot(a, b):
@@ -119,49 +124,48 @@
     return out + jnp.dot(a_hi, b_hi, preferred_element_type=jnp.float32)
 
 
-def product_kernel(pidx_ref, sidx_ref, a_ref, b_ref, *rest):
+def product_kernel(n_a, pidx_ref, sidx_ref, *refs):
     i = pl.program_id(0)
-    n_slots = a_ref.shape[1]
+    a_refs, b_ref, rest = refs[:n_a], refs[n_a], refs[n_a + 1:]
+    n_slots = sum(a.shape[1] for a in a_refs)
     o_ref = rest[-1]
     if len(rest) == 2:
         o_ref[...] = rest[0][...]
     else:
         o_ref[...] = jnp.zeros_like(o_ref)
+    j = 0
+    for a_ref in a_refs:
+        for k in range(a_ref.shape[1]):
+            s = sidx_ref[i * n_slots + j]
 
-    def body(j, carry):
-        s = sidx_ref[i * n_slots + j]
+            @pl.when(s >= 0)
+            def _():
+                p = pidx_ref[i * n_slots + j]
+                o_ref[0, s] += split_dot(a_ref[0, k], b_ref[p])
 
-        @pl.when(s >= 0)
-        def _():
-            p = pidx_ref[i * n_slots + j]
-            prod = split_dot(a_ref[0, j], b_ref[p])
-            o_ref[0, s] += prod
-
-        return carry
-
-    lax.fori_loop(0, n_slots, body, 0, unroll=True)
+            j += 1
 
 
-def row_products(whole_slots, panels, panel_index, target, pattern_slots, acc=None, interpret=False):
-    rows, slots, bs, _ = whole_slots.shape
+def row_products(a_list, panels, panel_index, target, pattern_slots, acc=None, interpret=False):
+    rows, _, bs, _ = a_list[0].shape
     out_spec = pl.BlockSpec((1, pattern_slots, bs, bs), lambda i, pidx, sidx: (i, 0, 0, 0))
     extra = [] if acc is None else [acc]
+    a_specs = [pl.BlockSpec((1, a.shape[1], bs, bs), lambda i, pidx, sidx: (i, 0, 0, 0)) for a in a_list]
     grid_spec = pltpu.PrefetchScalarGridSpec(
         num_scalar_prefetch=2,
         grid=(rows,),
-        in_specs=[
-            pl.BlockSpec((1, slots, bs, bs), lambda i, pidx, sidx: (i, 0, 0, 0)),
+        in_specs=a_specs + [
             pl.BlockSpec(panels.shape, lambda i, pidx, sidx: (0, 0, 0)),
         ] + [out_spec] * len(extra),
         out_specs=out_spec,
     )
     return pl.pallas_call(
-        product_kernel,
+        functools.partial(product_kernel, len(a_list)),
         grid_spec=grid_spec,
         out_shape=jax.ShapeDtypeStruct((rows, pattern_slots, bs, bs), jnp.float32),
-        input_output_aliases={} if acc is None else {4: 0},
+        input_output_aliases={} if acc is None else {3 + len(a_list): 0},
         interpret=interpret,
-    )(panel_index, target, whole_slots, panels, *extra)
+    )(panel_index, target, *a_list, panels, *extra)
 
 
 def solution(mesh):

time: 229 us -> 270 us (1.18)
  the two profiles are of different devices: /device:TPU:99 before, /device:TPU:264 now
where the time goes in v13:
time: 270 us; the launch traced here: 269 us
  waiting for transfers between devices  132 us (49%)
  starting transfers between devices  79.3 us (29%)
  Pallas kernels  30.4 us (11%)
  local copies, waits for them, and re-layouts  19.7 us (7%)
  other arithmetic  6.45 us (2%)
    ppermute x1, waiting for transfers between devices, swap_z(): return lax.ppermute(chunk, 'row', pairs)  68.9 us
    ppermute x6, waiting for transfers between devices, ring_x(): parts.append(lax.ppermute(held, 'row', shift))  34.4 us
    ppermute x7, starting transfers between devices, line_z(): going_right = lax.ppermute(going_right, 'col', right)  32.7 us
    pallas_call x2, Pallas kernels, row_products(): pl.pallas_call(functools.partial(product_kernel, len(a_list)), grid_spec=...  30.4 us
    ppermute x3, waiting for transfers between devices, ring_y(): parts.append(lax.ppermute(held, 'col', shift))  24.4 us
    ppermute x6, starting transfers between devices, ring_x(): parts.append(lax.ppermute(held, 'row', shift))  20.9 us
    ppermute x3, starting transfers between devices, ring_y(): parts.append(lax.ppermute(held, 'col', shift))  10.8 us
    unnamed x46, local copies, waits for them, and re-layouts  10.6 us
  transfers between devices with their start and end apart: 26, of which 17 were waited for; matrix products, arithmetic and copies ran while one was open for 8% of the time, Pallas kernels for 6%

profile of v13, /device:TPU:264, one launch (start us, length us, event | category | flops | bytes accessed | tf_op | source)
XLA Modules:
  0.0 268.5 jit_solution(13938783211476104986)
XLA Ops:
  0.0 1.3 collective-permute-start.7
  1.3 4.6 %collective-permute-start = (f32[2,128,128]{2,1,0:T(8,128)}, f32[2,128,128]{2,1,0:T(8,128)S(1)}, u32[]{:S(2)}, u32[]{:S(2)}) collective-permute-start(f32[2,128,128]{2,1,0:T(8,128)} %bitcast.46), channel_id=1, source_target_pairs={{0,1},{1,2},{2,3},{3,4},{4,5},{5,6},{6,7},{8,9},{9,10},{10,11},{11... | collective-permute-start | bytes 393224 | tf_op jit(solution)/shard_map/ppermute | solution.py:57
  5.9 1.6 bitcast_dynamic-update-slice_fusion.14
  7.7 1.3 collective-permute-start.8
  9.0 4.6 %collective-permute-start.1 = (f32[2,128,128]{2,1,0:T(8,128)S(1)}, f32[2,128,128]{2,1,0:T(8,128)S(1)}, u32[]{:S(2)}, u32[]{:S(2)}) collective-permute-start(f32[2,128,128]{2,1,0:T(8,128)S(1)} %collective-permute-done), channel_id=1, source_target_pairs={{0,1},{1,2},{2,3},{3,4},{4,5},{5,6},{6,7},{8,9},{9,10},{10,11},{11... | collective-permute-start | bytes 393224 | tf_op jit(solution)/shard_map/ppermute | solution.py:57
  13.5 0.7 bitcast_dynamic-update-slice_fusion.13
  14.5 1.3 collective-permute-start.9
  16.0 4.3 %collective-permute-start.2 = (f32[2,128,128]{2,1,0:T(8,128)S(1)}, f32[2,128,128]{2,1,0:T(8,128)S(1)}, u32[]{:S(2)}, u32[]{:S(2)}) collective-permute-start(f32[2,128,128]{2,1,0:T(8,128)S(1)} %collective-permute-done.1), channel_id=1, source_target_pairs={{0,1},{1,2},{2,3},{3,4},{4,5},{5,6},{6,7},{8,9},{9,10},{10,11},{11... | collective-permute-start | bytes 393224 | tf_op jit(solution)/shard_map/ppermute | solution.py:57
  20.4 0.7 bitcast_dynamic-update-slice_fusion.12
  21.4 1.3 collective-permute-start.10
  22.9 4.3 %collective-permute-start.3 = (f32[2,128,128]{2,1,0:T(8,128)S(1)}, f32[2,128,128]{2,1,0:T(8,128)S(1)}, u32[]{:S(2)}, u32[]{:S(2)}) collective-permute-start(f32[2,128,128]{2,1,0:T(8,128)S(1)} %collective-permute-done.2), channel_id=1, source_target_pairs={{0,1},{1,2},{2,3},{3,4},{4,5},{5,6},{6,7},{8,9},{9,10},{10,11},{11... | collective-permute-start | bytes 393224 | tf_op jit(solution)/shard_map/ppermute | solution.py:57
  27.2 0.7 bitcast_dynamic-update-slice_fusion.11
  28.2 1.3 collective-permute-start.11
  29.7 4.3 %collective-permute-start.4 = (f32[2,128,128]{2,1,0:T(8,128)S(1)}, f32[2,128,128]{2,1,0:T(8,128)S(1)}, u32[]{:S(2)}, u32[]{:S(2)}) collective-permute-start(f32[2,128,128]{2,1,0:T(8,128)S(1)} %collective-permute-done.3), channel_id=1, source_target_pairs={{0,1},{1,2},{2,3},{3,4},{4,5},{5,6},{6,7},{8,9},{9,10},{10,11},{11... | collective-permute-start | bytes 393224 | tf_op jit(solution)/shard_map/ppermute | solution.py:57
  34.1 0.7 bitcast_dynamic-update-slice_fusion.10
  35.1 1.3 collective-permute-start.12
  36.6 5.0 %collective-permute-start.5 = (f32[2,128,128]{2,1,0:T(8,128)S(1)}, f32[2,128,128]{2,1,0:T(8,128)S(1)}, u32[]{:S(2)}, u32[]{:S(2)}) collective-permute-start(f32[2,128,128]{2,1,0:T(8,128)S(1)} %collective-permute-done.4), channel_id=1, source_target_pairs={{0,1},{1,2},{2,3},{3,4},{4,5},{5,6},{6,7},{8,9},{9,10},{10,11},{11... | collective-permute-start | bytes 393224 | tf_op jit(solution)/shard_map/ppermute | solution.py:57
  41.6 0.7 bitcast_dynamic-update-slice_fusion.9
  42.6 1.3 collective-permute-start.13
  44.1 5.6 %collective-permute-start.6 = (f32[2,128,128]{2,1,0:T(8,128)S(1)}, f32[2,128,128]{2,1,0:T(8,128)S(1)}, u32[]{:S(2)}, u32[]{:S(2)}) collective-permute-start(f32[2,128,128]{2,1,0:T(8,128)S(1)} %collective-permute-done.5), channel_id=1, source_target_pairs={{0,1},{1,2},{2,3},{3,4},{4,5},{5,6},{6,7},{8,9},{9,10},{10,11},{11... | collective-permute-start | bytes 393224 | tf_op jit(solution)/shard_map/ppermute | solution.py:57
  49.6 0.7 bitcast_dynamic-update-slice_fusion.8
  50.3 1.8 collective-permute-done.6
  52.1 0.7 bitcast_dynamic-update-slice_fusion.7
  52.8 0.7 bitcast_dynamic-update-slice_fusion.6
  53.5 0.7 bitcast_dynamic-update-slice_fusion.5
  54.1 0.7 bitcast_dynamic-update-slice_fusion.4
  54.8 0.7 bitcast_dynamic-update-slice_fusion.3
  55.5 0.7 bitcast_dynamic-update-slice_fusion.2
  56.1 0.7 bitcast_dynamic-update-slice_fusion.1
  56.8 0.7 bitcast_dynamic-update-slice_fusion
  57.5 2.2 gather_fusion.3
  59.9 2.5 collective-permute-start.20
  62.4 4.5 %collective-permute-start.19 = (f32[16,128,128]{2,1,0:T(8,128)S(1)}, f32[16,128,128]{2,1,0:T(8,128)S(1)}, u32[]{:S(2)}, u32[]{:S(2)}) collective-permute-start(f32[16,128,128]{2,1,0:T(8,128)S(1)} %bitcast_select_fusion), channel_id=1, source_target_pairs={{0,16},{1,17},{2,18},{3,19},{4,20},{5,21},{6,22},{7,23},{8,24},{9,... | collective-permute-start | bytes 3145736 | tf_op jit(solution)/shard_map/ppermute | solution.py:70
  66.9 3.8 %collective-permute-start.18 = (f32[16,128,128]{2,1,0:T(8,128)S(1)}, f32[16,128,128]{2,1,0:T(8,128)S(1)}, u32[]{:S(2)}, u32[]{:S(2)}) collective-permute-start(f32[16,128,128]{2,1,0:T(8,128)S(1)} %bitcast_select_fusion), channel_id=1, source_target_pairs={{0,8},{1,9},{2,10},{3,11},{4,12},{5,13},{6,14},{7,15},{8,16},{9,17... | collective-permute-start | bytes 3145736 | tf_op jit(solution)/shard_map/ppermute | solution.py:70
  70.7 4.7 %collective-permute-start.17 = (f32[12,1,128,128]{3,2,1,0:T(8,128)S(1)}, f32[12,1,128,128]{3,2,1,0:T(8,128)S(1)}, u32[]{:S(2)}, u32[]{:S(2)}) collective-permute-start(f32[12,1,128,128]{3,2,1,0:T(8,128)S(1)} %copy-done.5), channel_id=1, source_target_pairs={{0,384},{32,416},{64,448},{96,480},{128,0},{160,32},{192,64},{224,... | collective-permute-start | bytes 2359304 | tf_op jit(solution)/shard_map/ppermute | solution.py:27
  75.3 2.7 %collective-permute-start.16 = (f32[12,1,128,128]{3,2,1,0:T(8,128)S(1)}, f32[12,1,128,128]{3,2,1,0:T(8,128)S(1)}, u32[]{:S(2)}, u32[]{:S(2)}) collective-permute-start(f32[12,1,128,128]{3,2,1,0:T(8,128)S(1)} %copy-done.5), channel_id=1, source_target_pairs={{0,256},{32,288},{64,320},{96,352},{128,384},{160,416},{192,448},{... | collective-permute-start | bytes 2359304 | tf_op jit(solution)/shard_map/ppermute | solution.py:27
  78.1 8.9 %collective-permute-done.20 = f32[16,128,128]{2,1,0:T(8,128)S(1)} collective-permute-done((f32[16,128,128]{2,1,0:T(8,128)S(1)}, f32[16,128,128]{2,1,0:T(8,128)S(1)}, u32[]{:S(2)}, u32[]{:S(2)}) %collective-permute-start.20) | collective-permute-done | bytes 1048608 | tf_op jit(solution)/shard_map/ppermute | solution.py:70
  87.0 3.4 %collective-permute-start.15 = (f32[12,1,128,128]{3,2,1,0:T(8,128)S(1)}, f32[12,1,128,128]{3,2,1,0:T(8,128)S(1)}, u32[]{:S(2)}, u32[]{:S(2)}) collective-permute-start(f32[12,1,128,128]{3,2,1,0:T(8,128)S(1)} %copy-done.5), channel_id=1, source_target_pairs={{0,128},{32,160},{64,192},{96,224},{128,256},{160,288},{192,320},{... | collective-permute-start | bytes 2359304 | tf_op jit(solution)/shard_map/ppermute | solution.py:27
  90.4 14.6 %collective-permute-done.19 = f32[16,128,128]{2,1,0:T(8,128)S(1)} collective-permute-done((f32[16,128,128]{2,1,0:T(8,128)S(1)}, f32[16,128,128]{2,1,0:T(8,128)S(1)}, u32[]{:S(2)}, u32[]{:S(2)}) %collective-permute-start.19) | collective-permute-done | bytes 1048608 | tf_op jit(solution)/shard_map/ppermute | solution.py:70
  105.0 1.9 collective-permute-start.14
  106.9 0.8 collective-permute-done.18
  107.7 2.4 pad_maximum_fusion.refs_5_.refs_2_
  110.2 68.9 %collective-permute-done.14.refs_1_ = f32[12,1,128,128]{3,2,1,0:T(8,128)S(1)} collective-permute-done((f32[12,1,128,128]{3,2,1,0:T(8,128)S(1)}, f32[12,1,128,128]{3,2,1,0:T(8,128)S(1)}, u32[]{:S(2)}, u32[]{:S(2)}) %collective-permute-start.14) | collective-permute-done | bytes 786464 | tf_op jit(solution)/shard_map/ppermute | solution.py:21
  179.4 2.1 collective-permute-start.24
  181.5 4.7 %collective-permute-start.23 = (f32[12,1,128,128]{3,2,1,0:T(8,128)S(1)}, f32[12,1,128,128]{3,2,1,0:T(8,128)S(1)}, u32[]{:S(2)}, u32[]{:S(2)}) collective-permute-start(f32[12,1,128,128]{3,2,1,0:T(8,128)S(1)} %collective-permute-done.14.refs_1_), channel_id=1, source_target_pairs={{0,384},{32,416},{64,448},{96,480},{128,0},{160,32},{192,64},{224,... | collective-permute-start | bytes 2359304 | tf_op jit(solution)/shard_map/ppermute | solution.py:27
  186.1 2.7 %collective-permute-start.22 = (f32[12,1,128,128]{3,2,1,0:T(8,128)S(1)}, f32[12,1,128,128]{3,2,1,0:T(8,128)S(1)}, u32[]{:S(2)}, u32[]{:S(2)}) collective-permute-start(f32[12,1,128,128]{3,2,1,0:T(8,128)S(1)} %collective-permute-done.14.refs_1_), channel_id=1, source_target_pairs={{0,256},{32,288},{64,320},{96,352},{128,384},{160,416},{192,448},{... | collective-permute-start | bytes 2359304 | tf_op jit(solution)/shard_map/ppermute | solution.py:27
  188.9 2.8 %collective-permute-start.21 = (f32[12,1,128,128]{3,2,1,0:T(8,128)S(1)}, f32[12,1,128,128]{3,2,1,0:T(8,128)S(1)}, u32[]{:S(2)}, u32[]{:S(2)}) collective-permute-start(f32[12,1,128,128]{3,2,1,0:T(8,128)S(1)} %collective-permute-done.14.refs_1_), channel_id=1, source_target_pairs={{0,128},{32,160},{64,192},{96,224},{128,256},{160,288},{192,320},{... | collective-permute-start | bytes 2359304 | tf_op jit(solution)/shard_map/ppermute | solution.py:27
  191.7 28.8 %collective-permute-done.23.refs_4_ = f32[12,1,128,128]{3,2,1,0:T(8,128)S(1)} collective-permute-done((f32[12,1,128,128]{3,2,1,0:T(8,128)S(1)}, f32[12,1,128,128]{3,2,1,0:T(8,128)S(1)}, u32[]{:S(2)}, u32[]{:S(2)}) %collective-permute-start.23) | collective-permute-done | bytes 786464 | tf_op jit(solution)/shard_map/ppermute | solution.py:27
  220.5 5.6 %collective-permute-done.21.refs_2_ = f32[12,1,128,128]{3,2,1,0:T(8,128)S(1)} collective-permute-done((f32[12,1,128,128]{3,2,1,0:T(8,128)S(1)}, f32[12,1,128,128]{3,2,1,0:T(8,128)S(1)}, u32[]{:S(2)}, u32[]{:S(2)}) %collective-permute-start.21) | collective-permute-done | bytes 786464 | tf_op jit(solution)/shard_map/ppermute | solution.py:27
  226.1 2.0 pad_maximum_fusion.1
  228.1 1.9 collective-permute-start.25
  230.7 0.6 gather_fusion
  231.5 0.4 select_reduce_fusion
  231.9 0.8 convert_reduce_fusion
  233.0 0.6 gather_fusion.5
  233.6 0.6 gather_fusion.2
  234.1 0.6 gather_fusion.1
  234.7 0.6 gather_fusion.4
  235.3 0.7 reshape.331.sidx_ref
  236.1 0.7 reshape.329.sidx_ref
  236.8 0.6 reshape.328.pidx_ref
  237.5 0.6 reshape.330.pidx_ref
  238.1 15.1 %shard_map.91.refs_3_ = f32[12,4,128,128]{3,2,1,0:T(8,128)} custom-call(s32[96]{0:T(128)} %reshape.330.pidx_ref, s32[96]{0:T(128)} %reshape.331.sidx_ref, f32[12,4,128,128]{3,2,1,0:T(8,128)} %copy-done, f32[12,1,128,128]{3,2,1,0:T(8,128)} %copy-done.1, f32[12,1,128,128]{3,2,1,0:T(8,128)} %copy-done.4, f32[12,1,128,128]{3,2,1,0:T(8,128)} %copy-done.3, ...), custom_call_target="tpu_custom_call" | custom-call | tf_op jit(solution)/shard_map/pallas_call | solution.py:162
  253.2 15.3 %shard_map.92 = f32[12,4,128,128]{3,2,1,0:T(8,128)} custom-call(s32[96]{0:T(128)} %reshape.328.pidx_ref, s32[96]{0:T(128)} %reshape.329.sidx_ref, f32[12,4,128,128]{3,2,1,0:T(8,128)} %collective-permute-done.24.refs_0_, f32[12,4,128,128]{3,2,1,0:T(8,128)} %collective-permute-done.25.refs_1_, ...), custom_call_target="tpu_custom_call", output_to_operand_aliasing={{}: (5, {})} | custom-call | tf_op jit(solution)/shard_map/pallas_call | solution.py:162
  (75 shorter events, 4.8 us)
Async XLA Ops:
  0.0 7.7 %collective-permute-start.7 = (f32[2,128,128]{2,1,0:T(8,128)}, f32[2,128,128]{2,1,0:T(8,128)S(1)}, u32[]{:S(2)}, u32[]{:S(2)}) collective-permute-start(f32[2,128,128]{2,1,0:T(8,128)} %bitcast.45), channel_id=1, source_target_pairs={{1,0},{2,1},{3,2},{4,3},{5,4},{6,5},{7,6},{9,8},{10,9},{11,10},{12... | collective-permute-start | bytes 393224 | tf_op jit(solution)/shard_map/ppermute | solution.py:58
  1.3 7.7 %collective-permute-start = (f32[2,128,128]{2,1,0:T(8,128)}, f32[2,128,128]{2,1,0:T(8,128)S(1)}, u32[]{:S(2)}, u32[]{:S(2)}) collective-permute-start(f32[2,128,128]{2,1,0:T(8,128)} %bitcast.46), channel_id=1, source_target_pairs={{0,1},{1,2},{2,3},{3,4},{4,5},{5,6},{6,7},{8,9},{9,10},{10,11},{11... | collective-permute-start | bytes 393224 | tf_op jit(solution)/shard_map/ppermute | solution.py:57
  7.7 6.9 %collective-permute-start.8 = (f32[2,128,128]{2,1,0:T(8,128)S(1)}, f32[2,128,128]{2,1,0:T(8,128)S(1)}, u32[]{:S(2)}, u32[]{:S(2)}) collective-permute-start(f32[2,128,128]{2,1,0:T(8,128)S(1)} %collective-permute-done.7), channel_id=1, source_target_pairs={{1,0},{2,1},{3,2},{4,3},{5,4},{6,5},{7,6},{9,8},{10,9},{11,10},{12... | collective-permute-start | bytes 393224 | tf_op jit(solution)/shard_map/ppermute | solution.py:58
  9.0 7.1 %collective-permute-start.1 = (f32[2,128,128]{2,1,0:T(8,128)S(1)}, f32[2,128,128]{2,1,0:T(8,128)S(1)}, u32[]{:S(2)}, u32[]{:S(2)}) collective-permute-start(f32[2,128,128]{2,1,0:T(8,128)S(1)} %collective-permute-done), channel_id=1, source_target_pairs={{0,1},{1,2},{2,3},{3,4},{4,5},{5,6},{6,7},{8,9},{9,10},{10,11},{11... | collective-permute-start | bytes 393224 | tf_op jit(solution)/shard_map/ppermute | solution.py:57
  14.5 6.8 %collective-permute-start.9 = (f32[2,128,128]{2,1,0:T(8,128)S(1)}, f32[2,128,128]{2,1,0:T(8,128)S(1)}, u32[]{:S(2)}, u32[]{:S(2)}) collective-permute-start(f32[2,128,128]{2,1,0:T(8,128)S(1)} %collective-permute-done.8), channel_id=1, source_target_pairs={{1,0},{2,1},{3,2},{4,3},{5,4},{6,5},{7,6},{9,8},{10,9},{11,10},{12... | collective-permute-start | bytes 393224 | tf_op jit(solution)/shard_map/ppermute | solution.py:58
  16.0 6.8 %collective-permute-start.2 = (f32[2,128,128]{2,1,0:T(8,128)S(1)}, f32[2,128,128]{2,1,0:T(8,128)S(1)}, u32[]{:S(2)}, u32[]{:S(2)}) collective-permute-start(f32[2,128,128]{2,1,0:T(8,128)S(1)} %collective-permute-done.1), channel_id=1, source_target_pairs={{0,1},{1,2},{2,3},{3,4},{4,5},{5,6},{6,7},{8,9},{9,10},{10,11},{11... | collective-permute-start | bytes 393224 | tf_op jit(solution)/shard_map/ppermute | solution.py:57
  21.4 6.8 %collective-permute-start.10 = (f32[2,128,128]{2,1,0:T(8,128)S(1)}, f32[2,128,128]{2,1,0:T(8,128)S(1)}, u32[]{:S(2)}, u32[]{:S(2)}) collective-permute-start(f32[2,128,128]{2,1,0:T(8,128)S(1)} %collective-permute-done.9), channel_id=1, source_target_pairs={{1,0},{2,1},{3,2},{4,3},{5,4},{6,5},{7,6},{9,8},{10,9},{11,10},{12... | collective-permute-start | bytes 393224 | tf_op jit(solution)/shard_map/ppermute | solution.py:58
  22.9 6.8 %collective-permute-start.3 = (f32[2,128,128]{2,1,0:T(8,128)S(1)}, f32[2,128,128]{2,1,0:T(8,128)S(1)}, u32[]{:S(2)}, u32[]{:S(2)}) collective-permute-start(f32[2,128,128]{2,1,0:T(8,128)S(1)} %collective-permute-done.2), channel_id=1, source_target_pairs={{0,1},{1,2},{2,3},{3,4},{4,5},{5,6},{6,7},{8,9},{9,10},{10,11},{11... | collective-permute-start | bytes 393224 | tf_op jit(solution)/shard_map/ppermute | solution.py:57
  28.2 6.8 %collective-permute-start.11 = (f32[2,128,128]{2,1,0:T(8,128)S(1)}, f32[2,128,128]{2,1,0:T(8,128)S(1)}, u32[]{:S(2)}, u32[]{:S(2)}) collective-permute-start(f32[2,128,128]{2,1,0:T(8,128)S(1)} %collective-permute-done.10), channel_id=1, source_target_pairs={{1,0},{2,1},{3,2},{4,3},{5,4},{6,5},{7,6},{9,8},{10,9},{11,10},{12... | collective-permute-start | bytes 393224 | tf_op jit(solution)/shard_map/ppermute | solution.py:58
  29.7 6.8 %collective-permute-start.4 = (f32[2,128,128]{2,1,0:T(8,128)S(1)}, f32[2,128,128]{2,1,0:T(8,128)S(1)}, u32[]{:S(2)}, u32[]{:S(2)}) collective-permute-start(f32[2,128,128]{2,1,0:T(8,128)S(1)} %collective-permute-done.3), channel_id=1, source_target_pairs={{0,1},{1,2},{2,3},{3,4},{4,5},{5,6},{6,7},{8,9},{9,10},{10,11},{11... | collective-permute-start | bytes 393224 | tf_op jit(solution)/shard_map/ppermute | solution.py:57
  35.1 7.5 %collective-permute-start.12 = (f32[2,128,128]{2,1,0:T(8,128)S(1)}, f32[2,128,128]{2,1,0:T(8,128)S(1)}, u32[]{:S(2)}, u32[]{:S(2)}) collective-permute-start(f32[2,128,128]{2,1,0:T(8,128)S(1)} %collective-permute-done.11), channel_id=1, source_target_pairs={{1,0},{2,1},{3,2},{4,3},{5,4},{6,5},{7,6},{9,8},{10,9},{11,10},{12... | collective-permute-start | bytes 393224 | tf_op jit(solution)/shard_map/ppermute | solution.py:58
  36.6 7.5 %collective-permute-start.5 = (f32[2,128,128]{2,1,0:T(8,128)S(1)}, f32[2,128,128]{2,1,0:T(8,128)S(1)}, u32[]{:S(2)}, u32[]{:S(2)}) collective-permute-start(f32[2,128,128]{2,1,0:T(8,128)S(1)} %collective-permute-done.4), channel_id=1, source_target_pairs={{0,1},{1,2},{2,3},{3,4},{4,5},{5,6},{6,7},{8,9},{9,10},{10,11},{11... | collective-permute-start | bytes 393224 | tf_op jit(solution)/shard_map/ppermute | solution.py:57
  42.6 14.2 %collective-permute-start.13 = (f32[2,128,128]{2,1,0:T(8,128)S(1)}, f32[2,128,128]{2,1,0:T(8,128)S(1)}, u32[]{:S(2)}, u32[]{:S(2)}) collective-permute-start(f32[2,128,128]{2,1,0:T(8,128)S(1)} %collective-permute-done.12), channel_id=1, source_target_pairs={{1,0},{2,1},{3,2},{4,3},{5,4},{6,5},{7,6},{9,8},{10,9},{11,10},{12... | collective-permute-start | bytes 393224 | tf_op jit(solution)/shard_map/ppermute | solution.py:58
  44.1 8.1 %collective-permute-start.6 = (f32[2,128,128]{2,1,0:T(8,128)S(1)}, f32[2,128,128]{2,1,0:T(8,128)S(1)}, u32[]{:S(2)}, u32[]{:S(2)}) collective-permute-start(f32[2,128,128]{2,1,0:T(8,128)S(1)} %collective-permute-done.5), channel_id=1, source_target_pairs={{0,1},{1,2},{2,3},{3,4},{4,5},{5,6},{6,7},{8,9},{9,10},{10,11},{11... | collective-permute-start | bytes 393224 | tf_op jit(solution)/shard_map/ppermute | solution.py:57
  57.5 13.2 %copy-start.5 = (f32[12,1,128,128]{3,2,1,0:T(8,128)S(1)}, f32[12,1,128,128]{3,2,1,0:T(8,128)}, u32[]{:S(2)}) copy-start(f32[12,1,128,128]{3,2,1,0:T(8,128)} %param.9) | copy-start | bytes 2359300
  59.8 119.2 %copy-start.6 = (f32[12,1,128,128]{3,2,1,0:T(8,128)S(1)}, f32[12,1,128,128]{3,2,1,0:T(8,128)}, u32[]{:S(2)}) copy-start(f32[12,1,128,128]{3,2,1,0:T(8,128)} %param.9) | copy-start | bytes 2359300
  59.9 27.1 %collective-permute-start.20 = (f32[16,128,128]{2,1,0:T(8,128)S(1)}, f32[16,128,128]{2,1,0:T(8,128)S(1)}, u32[]{:S(2)}, u32[]{:S(2)}) collective-permute-start(f32[16,128,128]{2,1,0:T(8,128)S(1)} %bitcast_select_fusion), channel_id=1, source_target_pairs={{0,24},{1,25},{2,26},{3,27},{4,28},{5,29},{6,30},{7,31},{8,0},{9,1... | collective-permute-start | bytes 3145736 | tf_op jit(solution)/shard_map/ppermute | solution.py:70
  62.4 42.7 %collective-permute-start.19 = (f32[16,128,128]{2,1,0:T(8,128)S(1)}, f32[16,128,128]{2,1,0:T(8,128)S(1)}, u32[]{:S(2)}, u32[]{:S(2)}) collective-permute-start(f32[16,128,128]{2,1,0:T(8,128)S(1)} %bitcast_select_fusion), channel_id=1, source_target_pairs={{0,16},{1,17},{2,18},{3,19},{4,20},{5,21},{6,22},{7,23},{8,24},{9,... | collective-permute-start | bytes 3145736 | tf_op jit(solution)/shard_map/ppermute | solution.py:70
  66.9 40.9 %collective-permute-start.18 = (f32[16,128,128]{2,1,0:T(8,128)S(1)}, f32[16,128,128]{2,1,0:T(8,128)S(1)}, u32[]{:S(2)}, u32[]{:S(2)}) collective-permute-start(f32[16,128,128]{2,1,0:T(8,128)S(1)} %bitcast_select_fusion), channel_id=1, source_target_pairs={{0,8},{1,9},{2,10},{3,11},{4,12},{5,13},{6,14},{7,15},{8,16},{9,17... | collective-permute-start | bytes 3145736 | tf_op jit(solution)/shard_map/ppermute | solution.py:70
  70.7 39.5 %collective-permute-start.17 = (f32[12,1,128,128]{3,2,1,0:T(8,128)S(1)}, f32[12,1,128,128]{3,2,1,0:T(8,128)S(1)}, u32[]{:S(2)}, u32[]{:S(2)}) collective-permute-start(f32[12,1,128,128]{3,2,1,0:T(8,128)S(1)} %copy-done.5), channel_id=1, source_target_pairs={{0,384},{32,416},{64,448},{96,480},{128,0},{160,32},{192,64},{224,... | collective-permute-start | bytes 2359304 | tf_op jit(solution)/shard_map/ppermute | solution.py:27
  75.3 34.8 %collective-permute-start.16 = (f32[12,1,128,128]{3,2,1,0:T(8,128)S(1)}, f32[12,1,128,128]{3,2,1,0:T(8,128)S(1)}, u32[]{:S(2)}, u32[]{:S(2)}) collective-permute-start(f32[12,1,128,128]{3,2,1,0:T(8,128)S(1)} %copy-done.5), channel_id=1, source_target_pairs={{0,256},{32,288},{64,320},{96,352},{128,384},{160,416},{192,448},{... | collective-permute-start | bytes 2359304 | tf_op jit(solution)/shard_map/ppermute | solution.py:27
  87.0 23.2 %collective-permute-start.15 = (f32[12,1,128,128]{3,2,1,0:T(8,128)S(1)}, f32[12,1,128,128]{3,2,1,0:T(8,128)S(1)}, u32[]{:S(2)}, u32[]{:S(2)}) collective-permute-start(f32[12,1,128,128]{3,2,1,0:T(8,128)S(1)} %copy-done.5), channel_id=1, source_target_pairs={{0,128},{32,160},{64,192},{96,224},{128,256},{160,288},{192,320},{... | collective-permute-start | bytes 2359304 | tf_op jit(solution)/shard_map/ppermute | solution.py:27
  105.0 74.0 %collective-permute-start.14 = (f32[12,1,128,128]{3,2,1,0:T(8,128)S(1)}, f32[12,1,128,128]{3,2,1,0:T(8,128)S(1)}, u32[]{:S(2)}, u32[]{:S(2)}) collective-permute-start(f32[12,1,128,128]{3,2,1,0:T(8,128)S(1)} %copy-done.5), channel_id=1, source_target_pairs={{0,64},{32,96},{64,0},{96,32},{128,192},{160,224},{192,128},{224,1... | collective-permute-start | bytes 2359304 | tf_op jit(solution)/shard_map/ppermute | solution.py:21
  179.1 47.0 %copy-start.1 = (f32[12,1,128,128]{3,2,1,0:T(8,128)}, f32[12,1,128,128]{3,2,1,0:T(8,128)S(1)}, u32[]{:S(2)}) copy-start(f32[12,1,128,128]{3,2,1,0:T(8,128)S(1)} %collective-permute-done.14.refs_1_) | copy-start | bytes 2359300
  179.3 48.8 %copy-start = (f32[12,4,128,128]{3,2,1,0:T(8,128)}, f32[12,4,128,128]{3,2,1,0:T(8,128)S(1)}, u32[]{:S(2)}) copy-start(f32[12,4,128,128]{3,2,1,0:T(8,128)S(1)} %constant_dynamic-update-slice_fusion.refs_0_) | copy-start | bytes 9437188
  179.3 50.8 %copy-start.8 = (s32[12,4]{0,1:T(4,128)S(1)}, s32[12,4]{0,1:T(4,128)}, u32[]{:S(2)}) copy-start(s32[12,4]{0,1:T(4,128)} %param.14) | copy-start | bytes 580
  179.3 50.9 %copy-start.7 = (s32[12,16]{1,0:T(8,128)S(1)}, s32[12,16]{1,0:T(8,128)}, u32[]{:S(2)}) copy-start(s32[12,16]{1,0:T(8,128)} %param.10) | copy-start | bytes 2308
  179.3 50.9 %copy-start.9 = (s32[64]{0:T(128)S(1)}, s32[64]{0:T(128)}, u32[]{:S(2)}) copy-start(s32[64]{0:T(128)} %param.15) | copy-start | bytes 772
  179.4 52.1 %copy-start.10 = (s32[64,1]{0,1:T(1,128)S(1)}, s32[64,1]{0,1:T(1,128)}, u32[]{:S(2)}) copy-start(s32[64,1]{0,1:T(1,128)} %param.13) | copy-start | bytes 772
  179.4 52.5 %copy-start.13 = (s32[12]{0:T(128)S(1)}, s32[12]{0:T(128)}, u32[]{:S(2)}) copy-start(s32[12]{0:T(128)} %param.11) | copy-start | bytes 148
  179.4 53.6 %copy-start.11 = (s32[8]{0:T(128)S(1)}, s32[8]{0:T(128)}, u32[]{:S(2)}) copy-start(s32[8]{0:T(128)} %constant.233) | copy-start | bytes 100
  179.4 53.6 %copy-start.12 = (s32[8]{0:T(128)S(1)}, s32[8]{0:T(128)}, u32[]{:S(2)}) copy-start(s32[8]{0:T(128)} %constant.231) | copy-start | bytes 100
  179.4 46.7 %collective-permute-start.24 = (f32[12,4,128,128]{3,2,1,0:T(8,128)S(1)}, f32[12,4,128,128]{3,2,1,0:T(8,128)}, u32[]{:S(2)}, u32[]{:S(2)}) collective-permute-start(f32[12,4,128,128]{3,2,1,0:T(8,128)S(1)} %constant_dynamic-update-slice_fusion.refs_0_), channel_id=1, source_target_pairs={{0,32},{32,0},{64,96},{96,64},{128,160},{160,128},{192,224},{224,1... | collective-permute-start | bytes 9437192 | tf_op jit(solution)/shard_map/ppermute | solution.py:32
  181.5 39.0 %collective-permute-start.23 = (f32[12,1,128,128]{3,2,1,0:T(8,128)S(1)}, f32[12,1,128,128]{3,2,1,0:T(8,128)S(1)}, u32[]{:S(2)}, u32[]{:S(2)}) collective-permute-start(f32[12,1,128,128]{3,2,1,0:T(8,128)S(1)} %collective-permute-done.14.refs_1_), channel_id=1, source_target_pairs={{0,384},{32,416},{64,448},{96,480},{128,0},{160,32},{192,64},{224,... | collective-permute-start | bytes 2359304 | tf_op jit(solution)/shard_map/ppermute | solution.py:27
  186.1 34.3 %collective-permute-start.22 = (f32[12,1,128,128]{3,2,1,0:T(8,128)S(1)}, f32[12,1,128,128]{3,2,1,0:T(8,128)S(1)}, u32[]{:S(2)}, u32[]{:S(2)}) collective-permute-start(f32[12,1,128,128]{3,2,1,0:T(8,128)S(1)} %collective-permute-done.14.refs_1_), channel_id=1, source_target_pairs={{0,256},{32,288},{64,320},{96,352},{128,384},{160,416},{192,448},{... | collective-permute-start | bytes 2359304 | tf_op jit(solution)/shard_map/ppermute | solution.py:27
  188.9 37.2 %collective-permute-start.21 = (f32[12,1,128,128]{3,2,1,0:T(8,128)S(1)}, f32[12,1,128,128]{3,2,1,0:T(8,128)S(1)}, u32[]{:S(2)}, u32[]{:S(2)}) collective-permute-start(f32[12,1,128,128]{3,2,1,0:T(8,128)S(1)} %collective-permute-done.14.refs_1_), channel_id=1, source_target_pairs={{0,128},{32,160},{64,192},{96,224},{128,256},{160,288},{192,320},{... | collective-permute-start | bytes 2359304 | tf_op jit(solution)/shard_map/ppermute | solution.py:27
  220.5 7.6 %copy-start.2 = (f32[12,1,128,128]{3,2,1,0:T(8,128)}, f32[12,1,128,128]{3,2,1,0:T(8,128)S(1)}, u32[]{:S(2)}) copy-start(f32[12,1,128,128]{3,2,1,0:T(8,128)S(1)} %collective-permute-done.23.refs_4_) | copy-start | bytes 2359300
  220.5 7.6 %copy-start.3 = (f32[12,1,128,128]{3,2,1,0:T(8,128)}, f32[12,1,128,128]{3,2,1,0:T(8,128)S(1)}, u32[]{:S(2)}) copy-start(f32[12,1,128,128]{3,2,1,0:T(8,128)S(1)} %collective-permute-done.22.refs_3_) | copy-start | bytes 2359300
  226.1 2.1 copy-start.4
  228.1 25.1 %collective-permute-start.25 = (f32[12,4,128,128]{3,2,1,0:T(8,128)}, f32[12,4,128,128]{3,2,1,0:T(8,128)}, u32[]{:S(2)}, u32[]{:S(2)}) collective-permute-start(f32[12,4,128,128]{3,2,1,0:T(8,128)} %pad_maximum_fusion.1), channel_id=1, source_target_pairs={{0,32},{32,0},{64,96},{96,64},{128,160},{160,128},{192,224},{224,1... | collective-permute-start | bytes 9437192 | tf_op jit(solution)/shard_map/ppermute | solution.py:32

commit v14 on v13

--- a/solution.py
+++ b/solution.py
@@ -87,8 +87,8 @@
     line_z, ring_y = col_stages(n_col)
     a_own, b_held = lax.optimization_barrier((a_blocks, line_z(b_blocks[:, 0])))
     a_other, own_x, panels = lax.optimization_barrier((swap_z(a_own), ring_x(a_own), ring_y(b_held)))
-    own_four = jnp.concatenate(own_x, axis=1)
-    other_x, got_own = lax.optimization_barrier((ring_x(a_other), swap_core(own_four)))
+    own_four, other_x = lax.optimization_barrier((jnp.concatenate(own_x, axis=1), ring_x(a_other)))
+    got_own = swap_core(own_four)
     half = 2 * len(own_x)
     rows_here, slot_all = a_cols.shape
     pattern_slots = c_cols.shape[1]

time: 270 us -> 269 us (level)
  the two profiles are of different devices: /device:TPU:264 before, /device:TPU:456 now
where the time goes in v14:
time: 269 us; the launch traced here: 268 us
  waiting for transfers between devices  133 us (49%)
  starting transfers between devices  81.1 us (30%)
  Pallas kernels  26.9 us (10%)
  local copies, waits for them, and re-layouts  19.5 us (7%)
  other arithmetic  6.67 us (2%)
    ppermute x1, waiting for transfers between devices, swap_z(): return lax.ppermute(chunk, 'row', pairs)  68.4 us
    ppermute x6, waiting for transfers between devices, ring_x(): parts.append(lax.ppermute(held, 'row', shift))  33.4 us
    pallas_call x2, Pallas kernels, row_products(): pl.pallas_call(functools.partial(product_kernel, len(a_list)), grid_spec=...  26.9 us
    ppermute x7, starting transfers between devices, line_z(): going_left = lax.ppermute(going_left, 'col', left)  26.1 us
    ppermute x3, waiting for transfers between devices, ring_y(): parts.append(lax.ppermute(held, 'col', shift))  23.8 us
    ppermute x6, starting transfers between devices, ring_x(): parts.append(lax.ppermute(held, 'row', shift))  20.9 us
    ppermute x7, starting transfers between devices, line_z(): going_right = lax.ppermute(going_right, 'col', right)  17 us
    ppermute x3, starting transfers between devices, ring_y(): parts.append(lax.ppermute(held, 'col', shift))  10.8 us
  transfers between devices with their start and end apart: 26, of which 14 were waited for; matrix products, arithmetic and copies ran while one was open for 8% of the time, Pallas kernels for 5%

profile of v14, /device:TPU:456, one launch (start us, length us, event | category | flops | bytes accessed | tf_op | source)
XLA Modules:
  0.0 268.1 jit_solution(10916632442108892165)
XLA Ops:
  0.0 2.9 %collective-permute-start.7 = (f32[2,128,128]{2,1,0:T(8,128)}, f32[2,128,128]{2,1,0:T(8,128)S(1)}, u32[]{:S(2)}, u32[]{:S(2)}) collective-permute-start(f32[2,128,128]{2,1,0:T(8,128)} %bitcast.45), channel_id=1, source_target_pairs={{1,0},{2,1},{3,2},{4,3},{5,4},{6,5},{7,6},{9,8},{10,9},{11,10},{12... | collective-permute-start | bytes 393224 | tf_op jit(solution)/shard_map/ppermute | solution.py:58
  2.9 2.9 %collective-permute-start = (f32[2,128,128]{2,1,0:T(8,128)}, f32[2,128,128]{2,1,0:T(8,128)S(1)}, u32[]{:S(2)}, u32[]{:S(2)}) collective-permute-start(f32[2,128,128]{2,1,0:T(8,128)} %bitcast.46), channel_id=1, source_target_pairs={{0,1},{1,2},{2,3},{3,4},{4,5},{5,6},{6,7},{8,9},{9,10},{10,11},{11... | collective-permute-start | bytes 393224 | tf_op jit(solution)/shard_map/ppermute | solution.py:57
  5.9 1.6 bitcast_dynamic-update-slice_fusion.14
  7.7 2.9 %collective-permute-start.8 = (f32[2,128,128]{2,1,0:T(8,128)S(1)}, f32[2,128,128]{2,1,0:T(8,128)S(1)}, u32[]{:S(2)}, u32[]{:S(2)}) collective-permute-start(f32[2,128,128]{2,1,0:T(8,128)S(1)} %collective-permute-done.7), channel_id=1, source_target_pairs={{1,0},{2,1},{3,2},{4,3},{5,4},{6,5},{7,6},{9,8},{10,9},{11,10},{12... | collective-permute-start | bytes 393224 | tf_op jit(solution)/shard_map/ppermute | solution.py:58
  10.6 2.9 %collective-permute-start.1 = (f32[2,128,128]{2,1,0:T(8,128)S(1)}, f32[2,128,128]{2,1,0:T(8,128)S(1)}, u32[]{:S(2)}, u32[]{:S(2)}) collective-permute-start(f32[2,128,128]{2,1,0:T(8,128)S(1)} %collective-permute-done), channel_id=1, source_target_pairs={{0,1},{1,2},{2,3},{3,4},{4,5},{5,6},{6,7},{8,9},{9,10},{10,11},{11... | collective-permute-start | bytes 393224 | tf_op jit(solution)/shard_map/ppermute | solution.py:57
  13.5 0.7 bitcast_dynamic-update-slice_fusion.13
  14.5 2.9 %collective-permute-start.9 = (f32[2,128,128]{2,1,0:T(8,128)S(1)}, f32[2,128,128]{2,1,0:T(8,128)S(1)}, u32[]{:S(2)}, u32[]{:S(2)}) collective-permute-start(f32[2,128,128]{2,1,0:T(8,128)S(1)} %collective-permute-done.8), channel_id=1, source_target_pairs={{1,0},{2,1},{3,2},{4,3},{5,4},{6,5},{7,6},{9,8},{10,9},{11,10},{12... | collective-permute-start | bytes 393224 | tf_op jit(solution)/shard_map/ppermute | solution.py:58
  17.5 2.9 %collective-permute-start.2 = (f32[2,128,128]{2,1,0:T(8,128)S(1)}, f32[2,128,128]{2,1,0:T(8,128)S(1)}, u32[]{:S(2)}, u32[]{:S(2)}) collective-permute-start(f32[2,128,128]{2,1,0:T(8,128)S(1)} %collective-permute-done.1), channel_id=1, source_target_pairs={{0,1},{1,2},{2,3},{3,4},{4,5},{5,6},{6,7},{8,9},{9,10},{10,11},{11... | collective-permute-start | bytes 393224 | tf_op jit(solution)/shard_map/ppermute | solution.py:57
  20.4 0.7 bitcast_dynamic-update-slice_fusion.12
  21.4 3.0 %collective-permute-start.10 = (f32[2,128,128]{2,1,0:T(8,128)S(1)}, f32[2,128,128]{2,1,0:T(8,128)S(1)}, u32[]{:S(2)}, u32[]{:S(2)}) collective-permute-start(f32[2,128,128]{2,1,0:T(8,128)S(1)} %collective-permute-done.9), channel_id=1, source_target_pairs={{1,0},{2,1},{3,2},{4,3},{5,4},{6,5},{7,6},{9,8},{10,9},{11,10},{12... | collective-permute-start | bytes 393224 | tf_op jit(solution)/shard_map/ppermute | solution.py:58
  24.7 2.5 collective-permute-start.3
  27.2 0.7 bitcast_dynamic-update-slice_fusion.11
  28.2 4.2 %collective-permute-start.11 = (f32[2,128,128]{2,1,0:T(8,128)S(1)}, f32[2,128,128]{2,1,0:T(8,128)S(1)}, u32[]{:S(2)}, u32[]{:S(2)}) collective-permute-start(f32[2,128,128]{2,1,0:T(8,128)S(1)} %collective-permute-done.10), channel_id=1, source_target_pairs={{1,0},{2,1},{3,2},{4,3},{5,4},{6,5},{7,6},{9,8},{10,9},{11,10},{12... | collective-permute-start | bytes 393224 | tf_op jit(solution)/shard_map/ppermute | solution.py:58
  32.8 1.9 collective-permute-start.4
  34.7 0.7 bitcast_dynamic-update-slice_fusion.10
  35.4 5.1 %collective-permute-start.12 = (f32[2,128,128]{2,1,0:T(8,128)S(1)}, f32[2,128,128]{2,1,0:T(8,128)S(1)}, u32[]{:S(2)}, u32[]{:S(2)}) collective-permute-start(f32[2,128,128]{2,1,0:T(8,128)S(1)} %collective-permute-done.11), channel_id=1, source_target_pairs={{1,0},{2,1},{3,2},{4,3},{5,4},{6,5},{7,6},{9,8},{10,9},{11,10},{12... | collective-permute-start | bytes 393224 | tf_op jit(solution)/shard_map/ppermute | solution.py:58
  40.8 1.9 collective-permute-start.5
  42.8 0.7 bitcast_dynamic-update-slice_fusion.9
  43.4 5.1 %collective-permute-start.13 = (f32[2,128,128]{2,1,0:T(8,128)S(1)}, f32[2,128,128]{2,1,0:T(8,128)S(1)}, u32[]{:S(2)}, u32[]{:S(2)}) collective-permute-start(f32[2,128,128]{2,1,0:T(8,128)S(1)} %collective-permute-done.12), channel_id=1, source_target_pairs={{1,0},{2,1},{3,2},{4,3},{5,4},{6,5},{7,6},{9,8},{10,9},{11,10},{12... | collective-permute-start | bytes 393224 | tf_op jit(solution)/shard_map/ppermute | solution.py:58
  48.9 1.9 collective-permute-start.6
  50.8 0.7 bitcast_dynamic-update-slice_fusion.8
  51.5 5.5 %collective-permute-done.6 = f32[2,128,128]{2,1,0:T(8,128)S(1)} collective-permute-done((f32[2,128,128]{2,1,0:T(8,128)S(1)}, f32[2,128,128]{2,1,0:T(8,128)S(1)}, u32[]{:S(2)}, u32[]{:S(2)}) %collective-permute-start.6) | collective-permute-done | bytes 131104 | tf_op jit(solution)/shard_map/ppermute | solution.py:57
  57.0 0.7 bitcast_dynamic-update-slice_fusion.7
  57.6 0.7 bitcast_dynamic-update-slice_fusion.6
  58.3 0.7 bitcast_dynamic-update-slice_fusion.5
  59.0 0.7 bitcast_dynamic-update-slice_fusion.4
  59.6 0.7 bitcast_dynamic-update-slice_fusion.3
  60.3 0.7 bitcast_dynamic-update-slice_fusion.2
  61.0 0.7 bitcast_dynamic-update-slice_fusion.1
  61.6 0.7 bitcast_dynamic-update-slice_fusion
  62.3 2.2 gather_fusion.3
  64.7 2.5 collective-permute-start.20
  67.2 4.5 %collective-permute-start.19 = (f32[16,128,128]{2,1,0:T(8,128)S(1)}, f32[16,128,128]{2,1,0:T(8,128)S(1)}, u32[]{:S(2)}, u32[]{:S(2)}) collective-permute-start(f32[16,128,128]{2,1,0:T(8,128)S(1)} %bitcast_select_fusion), channel_id=1, source_target_pairs={{0,16},{1,17},{2,18},{3,19},{4,20},{5,21},{6,22},{7,23},{8,24},{9,... | collective-permute-start | bytes 3145736 | tf_op jit(solution)/shard_map/ppermute | solution.py:70
  71.7 3.8 %collective-permute-start.18 = (f32[16,128,128]{2,1,0:T(8,128)S(1)}, f32[16,128,128]{2,1,0:T(8,128)S(1)}, u32[]{:S(2)}, u32[]{:S(2)}) collective-permute-start(f32[16,128,128]{2,1,0:T(8,128)S(1)} %bitcast_select_fusion), channel_id=1, source_target_pairs={{0,8},{1,9},{2,10},{3,11},{4,12},{5,13},{6,14},{7,15},{8,16},{9,17... | collective-permute-start | bytes 3145736 | tf_op jit(solution)/shard_map/ppermute | solution.py:70
  75.5 4.7 %collective-permute-start.17 = (f32[12,1,128,128]{3,2,1,0:T(8,128)S(1)}, f32[12,1,128,128]{3,2,1,0:T(8,128)S(1)}, u32[]{:S(2)}, u32[]{:S(2)}) collective-permute-start(f32[12,1,128,128]{3,2,1,0:T(8,128)S(1)} %copy-done.5), channel_id=1, source_target_pairs={{0,384},{32,416},{64,448},{96,480},{128,0},{160,32},{192,64},{224,... | collective-permute-start | bytes 2359304 | tf_op jit(solution)/shard_map/ppermute | solution.py:27
  80.2 2.7 %collective-permute-start.16 = (f32[12,1,128,128]{3,2,1,0:T(8,128)S(1)}, f32[12,1,128,128]{3,2,1,0:T(8,128)S(1)}, u32[]{:S(2)}, u32[]{:S(2)}) collective-permute-start(f32[12,1,128,128]{3,2,1,0:T(8,128)S(1)} %copy-done.5), channel_id=1, source_target_pairs={{0,256},{32,288},{64,320},{96,352},{128,384},{160,416},{192,448},{... | collective-permute-start | bytes 2359304 | tf_op jit(solution)/shard_map/ppermute | solution.py:27
  82.9 8.9 %collective-permute-done.20 = f32[16,128,128]{2,1,0:T(8,128)S(1)} collective-permute-done((f32[16,128,128]{2,1,0:T(8,128)S(1)}, f32[16,128,128]{2,1,0:T(8,128)S(1)}, u32[]{:S(2)}, u32[]{:S(2)}) %collective-permute-start.20) | collective-permute-done | bytes 1048608 | tf_op jit(solution)/shard_map/ppermute | solution.py:70
  91.8 3.4 %collective-permute-start.15 = (f32[12,1,128,128]{3,2,1,0:T(8,128)S(1)}, f32[12,1,128,128]{3,2,1,0:T(8,128)S(1)}, u32[]{:S(2)}, u32[]{:S(2)}) collective-permute-start(f32[12,1,128,128]{3,2,1,0:T(8,128)S(1)} %copy-done.5), channel_id=1, source_target_pairs={{0,128},{32,160},{64,192},{96,224},{128,256},{160,288},{192,320},{... | collective-permute-start | bytes 2359304 | tf_op jit(solution)/shard_map/ppermute | solution.py:27
  95.2 14.1 %collective-permute-done.19 = f32[16,128,128]{2,1,0:T(8,128)S(1)} collective-permute-done((f32[16,128,128]{2,1,0:T(8,128)S(1)}, f32[16,128,128]{2,1,0:T(8,128)S(1)}, u32[]{:S(2)}, u32[]{:S(2)}) %collective-permute-start.19) | collective-permute-done | bytes 1048608 | tf_op jit(solution)/shard_map/ppermute | solution.py:70
  109.3 1.9 collective-permute-start.14
  111.2 0.8 collective-permute-done.18
  112.0 2.4 pad_maximum_fusion.refs_5_.refs_2_
  114.4 68.4 %collective-permute-done.14.refs_1_ = f32[12,1,128,128]{3,2,1,0:T(8,128)S(1)} collective-permute-done((f32[12,1,128,128]{3,2,1,0:T(8,128)S(1)}, f32[12,1,128,128]{3,2,1,0:T(8,128)S(1)}, u32[]{:S(2)}, u32[]{:S(2)}) %collective-permute-start.14) | collective-permute-done | bytes 786464 | tf_op jit(solution)/shard_map/ppermute | solution.py:21
  182.9 4.7 %collective-permute-start.23 = (f32[12,1,128,128]{3,2,1,0:T(8,128)S(1)}, f32[12,1,128,128]{3,2,1,0:T(8,128)S(1)}, u32[]{:S(2)}, u32[]{:S(2)}) collective-permute-start(f32[12,1,128,128]{3,2,1,0:T(8,128)S(1)} %collective-permute-done.14.refs_1_), channel_id=1, source_target_pairs={{0,384},{32,416},{64,448},{96,480},{128,0},{160,32},{192,64},{224,... | collective-permute-start | bytes 2359304 | tf_op jit(solution)/shard_map/ppermute | solution.py:27
  187.5 2.7 %collective-permute-start.22 = (f32[12,1,128,128]{3,2,1,0:T(8,128)S(1)}, f32[12,1,128,128]{3,2,1,0:T(8,128)S(1)}, u32[]{:S(2)}, u32[]{:S(2)}) collective-permute-start(f32[12,1,128,128]{3,2,1,0:T(8,128)S(1)} %collective-permute-done.14.refs_1_), channel_id=1, source_target_pairs={{0,256},{32,288},{64,320},{96,352},{128,384},{160,416},{192,448},{... | collective-permute-start | bytes 2359304 | tf_op jit(solution)/shard_map/ppermute | solution.py:27
  190.3 2.8 %collective-permute-start.21 = (f32[12,1,128,128]{3,2,1,0:T(8,128)S(1)}, f32[12,1,128,128]{3,2,1,0:T(8,128)S(1)}, u32[]{:S(2)}, u32[]{:S(2)}) collective-permute-start(f32[12,1,128,128]{3,2,1,0:T(8,128)S(1)} %collective-permute-done.14.refs_1_), channel_id=1, source_target_pairs={{0,128},{32,160},{64,192},{96,224},{128,256},{160,288},{192,320},{... | collective-permute-start | bytes 2359304 | tf_op jit(solution)/shard_map/ppermute | solution.py:27
  193.4 27.8 %collective-permute-done.23.refs_4_ = f32[12,1,128,128]{3,2,1,0:T(8,128)S(1)} collective-permute-done((f32[12,1,128,128]{3,2,1,0:T(8,128)S(1)}, f32[12,1,128,128]{3,2,1,0:T(8,128)S(1)}, u32[]{:S(2)}, u32[]{:S(2)}) %collective-permute-start.23) | collective-permute-done | bytes 786464 | tf_op jit(solution)/shard_map/ppermute | solution.py:27
  221.2 5.6 %collective-permute-done.21.refs_2_ = f32[12,1,128,128]{3,2,1,0:T(8,128)S(1)} collective-permute-done((f32[12,1,128,128]{3,2,1,0:T(8,128)S(1)}, f32[12,1,128,128]{3,2,1,0:T(8,128)S(1)}, u32[]{:S(2)}, u32[]{:S(2)}) %collective-permute-start.21) | collective-permute-done | bytes 786464 | tf_op jit(solution)/shard_map/ppermute | solution.py:27
  226.8 2.0 pad_maximum_fusion.2
  228.8 1.9 collective-permute-start.25
  230.8 2.4 collective-permute-start.24
  233.8 0.6 gather_fusion
  234.6 0.4 select_reduce_fusion
  235.0 0.8 convert_reduce_fusion
  236.1 0.6 gather_fusion.5
  236.7 0.6 gather_fusion.2
  237.2 0.6 gather_fusion.1
  237.8 0.6 gather_fusion.4
  238.4 0.7 reshape.331.sidx_ref
  239.2 0.7 reshape.329.sidx_ref
  239.9 0.6 reshape.328.pidx_ref
  240.6 0.6 reshape.330.pidx_ref
  241.2 12.9 %shard_map.91.refs_3_ = f32[12,4,128,128]{3,2,1,0:T(8,128)} custom-call(s32[96]{0:T(128)} %reshape.330.pidx_ref, s32[96]{0:T(128)} %reshape.331.sidx_ref, f32[12,4,128,128]{3,2,1,0:T(8,128)} %copy-done, f32[12,1,128,128]{3,2,1,0:T(8,128)} %copy-done.1, f32[12,1,128,128]{3,2,1,0:T(8,128)} %copy-done.4, f32[12,1,128,128]{3,2,1,0:T(8,128)} %copy-done.3, ...), custom_call_target="tpu_custom_call" | custom-call | tf_op jit(solution)/shard_map/pallas_call | solution.py:162
  254.2 13.9 %shard_map.92 = f32[12,4,128,128]{3,2,1,0:T(8,128)} custom-call(s32[96]{0:T(128)} %reshape.328.pidx_ref, s32[96]{0:T(128)} %reshape.329.sidx_ref, f32[12,4,128,128]{3,2,1,0:T(8,128)} %collective-permute-done.24.refs_0_, f32[12,4,128,128]{3,2,1,0:T(8,128)} %collective-permute-done.25.refs_1_, ...), custom_call_target="tpu_custom_call", output_to_operand_aliasing={{}: (5, {})} | custom-call | tf_op jit(solution)/shard_map/pallas_call | solution.py:162
  (72 shorter events, 4.5 us)
Async XLA Ops:
  0.0 7.7 %collective-permute-start.7 = (f32[2,128,128]{2,1,0:T(8,128)}, f32[2,128,128]{2,1,0:T(8,128)S(1)}, u32[]{:S(2)}, u32[]{:S(2)}) collective-permute-start(f32[2,128,128]{2,1,0:T(8,128)} %bitcast.45), channel_id=1, source_target_pairs={{1,0},{2,1},{3,2},{4,3},{5,4},{6,5},{7,6},{9,8},{10,9},{11,10},{12... | collective-permute-start | bytes 393224 | tf_op jit(solution)/shard_map/ppermute | solution.py:58
  2.9 7.7 %collective-permute-start = (f32[2,128,128]{2,1,0:T(8,128)}, f32[2,128,128]{2,1,0:T(8,128)S(1)}, u32[]{:S(2)}, u32[]{:S(2)}) collective-permute-start(f32[2,128,128]{2,1,0:T(8,128)} %bitcast.46), channel_id=1, source_target_pairs={{0,1},{1,2},{2,3},{3,4},{4,5},{5,6},{6,7},{8,9},{9,10},{10,11},{11... | collective-permute-start | bytes 393224 | tf_op jit(solution)/shard_map/ppermute | solution.py:57
  7.7 6.9 %collective-permute-start.8 = (f32[2,128,128]{2,1,0:T(8,128)S(1)}, f32[2,128,128]{2,1,0:T(8,128)S(1)}, u32[]{:S(2)}, u32[]{:S(2)}) collective-permute-start(f32[2,128,128]{2,1,0:T(8,128)S(1)} %collective-permute-done.7), channel_id=1, source_target_pairs={{1,0},{2,1},{3,2},{4,3},{5,4},{6,5},{7,6},{9,8},{10,9},{11,10},{12... | collective-permute-start | bytes 393224 | tf_op jit(solution)/shard_map/ppermute | solution.py:58
  10.6 6.9 %collective-permute-start.1 = (f32[2,128,128]{2,1,0:T(8,128)S(1)}, f32[2,128,128]{2,1,0:T(8,128)S(1)}, u32[]{:S(2)}, u32[]{:S(2)}) collective-permute-start(f32[2,128,128]{2,1,0:T(8,128)S(1)} %collective-permute-done), channel_id=1, source_target_pairs={{0,1},{1,2},{2,3},{3,4},{4,5},{5,6},{6,7},{8,9},{9,10},{10,11},{11... | collective-permute-start | bytes 393224 | tf_op jit(solution)/shard_map/ppermute | solution.py:57
  14.5 6.8 %collective-permute-start.9 = (f32[2,128,128]{2,1,0:T(8,128)S(1)}, f32[2,128,128]{2,1,0:T(8,128)S(1)}, u32[]{:S(2)}, u32[]{:S(2)}) collective-permute-start(f32[2,128,128]{2,1,0:T(8,128)S(1)} %collective-permute-done.8), channel_id=1, source_target_pairs={{1,0},{2,1},{3,2},{4,3},{5,4},{6,5},{7,6},{9,8},{10,9},{11,10},{12... | collective-permute-start | bytes 393224 | tf_op jit(solution)/shard_map/ppermute | solution.py:58
  17.5 7.3 %collective-permute-start.2 = (f32[2,128,128]{2,1,0:T(8,128)S(1)}, f32[2,128,128]{2,1,0:T(8,128)S(1)}, u32[]{:S(2)}, u32[]{:S(2)}) collective-permute-start(f32[2,128,128]{2,1,0:T(8,128)S(1)} %collective-permute-done.1), channel_id=1, source_target_pairs={{0,1},{1,2},{2,3},{3,4},{4,5},{5,6},{6,7},{8,9},{9,10},{10,11},{11... | collective-permute-start | bytes 393224 | tf_op jit(solution)/shard_map/ppermute | solution.py:57
  21.4 6.8 %collective-permute-start.10 = (f32[2,128,128]{2,1,0:T(8,128)S(1)}, f32[2,128,128]{2,1,0:T(8,128)S(1)}, u32[]{:S(2)}, u32[]{:S(2)}) collective-permute-start(f32[2,128,128]{2,1,0:T(8,128)S(1)} %collective-permute-done.9), channel_id=1, source_target_pairs={{1,0},{2,1},{3,2},{4,3},{5,4},{6,5},{7,6},{9,8},{10,9},{11,10},{12... | collective-permute-start | bytes 393224 | tf_op jit(solution)/shard_map/ppermute | solution.py:58
  24.7 8.1 %collective-permute-start.3 = (f32[2,128,128]{2,1,0:T(8,128)S(1)}, f32[2,128,128]{2,1,0:T(8,128)S(1)}, u32[]{:S(2)}, u32[]{:S(2)}) collective-permute-start(f32[2,128,128]{2,1,0:T(8,128)S(1)} %collective-permute-done.2), channel_id=1, source_target_pairs={{0,1},{1,2},{2,3},{3,4},{4,5},{5,6},{6,7},{8,9},{9,10},{10,11},{11... | collective-permute-start | bytes 393224 | tf_op jit(solution)/shard_map/ppermute | solution.py:57
  28.2 7.1 %collective-permute-start.11 = (f32[2,128,128]{2,1,0:T(8,128)S(1)}, f32[2,128,128]{2,1,0:T(8,128)S(1)}, u32[]{:S(2)}, u32[]{:S(2)}) collective-permute-start(f32[2,128,128]{2,1,0:T(8,128)S(1)} %collective-permute-done.10), channel_id=1, source_target_pairs={{1,0},{2,1},{3,2},{4,3},{5,4},{6,5},{7,6},{9,8},{10,9},{11,10},{12... | collective-permute-start | bytes 393224 | tf_op jit(solution)/shard_map/ppermute | solution.py:58
  32.8 8.1 %collective-permute-start.4 = (f32[2,128,128]{2,1,0:T(8,128)S(1)}, f32[2,128,128]{2,1,0:T(8,128)S(1)}, u32[]{:S(2)}, u32[]{:S(2)}) collective-permute-start(f32[2,128,128]{2,1,0:T(8,128)S(1)} %collective-permute-done.3), channel_id=1, source_target_pairs={{0,1},{1,2},{2,3},{3,4},{4,5},{5,6},{6,7},{8,9},{9,10},{10,11},{11... | collective-permute-start | bytes 393224 | tf_op jit(solution)/shard_map/ppermute | solution.py:57
  35.4 8.1 %collective-permute-start.12 = (f32[2,128,128]{2,1,0:T(8,128)S(1)}, f32[2,128,128]{2,1,0:T(8,128)S(1)}, u32[]{:S(2)}, u32[]{:S(2)}) collective-permute-start(f32[2,128,128]{2,1,0:T(8,128)S(1)} %collective-permute-done.11), channel_id=1, source_target_pairs={{1,0},{2,1},{3,2},{4,3},{5,4},{6,5},{7,6},{9,8},{10,9},{11,10},{12... | collective-permute-start | bytes 393224 | tf_op jit(solution)/shard_map/ppermute | solution.py:58
  40.8 8.1 %collective-permute-start.5 = (f32[2,128,128]{2,1,0:T(8,128)S(1)}, f32[2,128,128]{2,1,0:T(8,128)S(1)}, u32[]{:S(2)}, u32[]{:S(2)}) collective-permute-start(f32[2,128,128]{2,1,0:T(8,128)S(1)} %collective-permute-done.4), channel_id=1, source_target_pairs={{0,1},{1,2},{2,3},{3,4},{4,5},{5,6},{6,7},{8,9},{9,10},{10,11},{11... | collective-permute-start | bytes 393224 | tf_op jit(solution)/shard_map/ppermute | solution.py:57
  43.4 18.2 %collective-permute-start.13 = (f32[2,128,128]{2,1,0:T(8,128)S(1)}, f32[2,128,128]{2,1,0:T(8,128)S(1)}, u32[]{:S(2)}, u32[]{:S(2)}) collective-permute-start(f32[2,128,128]{2,1,0:T(8,128)S(1)} %collective-permute-done.12), channel_id=1, source_target_pairs={{1,0},{2,1},{3,2},{4,3},{5,4},{6,5},{7,6},{9,8},{10,9},{11,10},{12... | collective-permute-start | bytes 393224 | tf_op jit(solution)/shard_map/ppermute | solution.py:58
  48.9 8.1 %collective-permute-start.6 = (f32[2,128,128]{2,1,0:T(8,128)S(1)}, f32[2,128,128]{2,1,0:T(8,128)S(1)}, u32[]{:S(2)}, u32[]{:S(2)}) collective-permute-start(f32[2,128,128]{2,1,0:T(8,128)S(1)} %collective-permute-done.5), channel_id=1, source_target_pairs={{0,1},{1,2},{2,3},{3,4},{4,5},{5,6},{6,7},{8,9},{9,10},{10,11},{11... | collective-permute-start | bytes 393224 | tf_op jit(solution)/shard_map/ppermute | solution.py:57
  62.3 13.2 %copy-start.5 = (f32[12,1,128,128]{3,2,1,0:T(8,128)S(1)}, f32[12,1,128,128]{3,2,1,0:T(8,128)}, u32[]{:S(2)}) copy-start(f32[12,1,128,128]{3,2,1,0:T(8,128)} %param.9) | copy-start | bytes 2359300
  64.7 128.4 %copy-start.6 = (f32[12,1,128,128]{3,2,1,0:T(8,128)S(1)}, f32[12,1,128,128]{3,2,1,0:T(8,128)}, u32[]{:S(2)}) copy-start(f32[12,1,128,128]{3,2,1,0:T(8,128)} %param.9) | copy-start | bytes 2359300
  64.7 27.1 %collective-permute-start.20 = (f32[16,128,128]{2,1,0:T(8,128)S(1)}, f32[16,128,128]{2,1,0:T(8,128)S(1)}, u32[]{:S(2)}, u32[]{:S(2)}) collective-permute-start(f32[16,128,128]{2,1,0:T(8,128)S(1)} %bitcast_select_fusion), channel_id=1, source_target_pairs={{0,24},{1,25},{2,26},{3,27},{4,28},{5,29},{6,30},{7,31},{8,0},{9,1... | collective-permute-start | bytes 3145736 | tf_op jit(solution)/shard_map/ppermute | solution.py:70
  67.2 42.1 %collective-permute-start.19 = (f32[16,128,128]{2,1,0:T(8,128)S(1)}, f32[16,128,128]{2,1,0:T(8,128)S(1)}, u32[]{:S(2)}, u32[]{:S(2)}) collective-permute-start(f32[16,128,128]{2,1,0:T(8,128)S(1)} %bitcast_select_fusion), channel_id=1, source_target_pairs={{0,16},{1,17},{2,18},{3,19},{4,20},{5,21},{6,22},{7,23},{8,24},{9,... | collective-permute-start | bytes 3145736 | tf_op jit(solution)/shard_map/ppermute | solution.py:70
  71.7 40.3 %collective-permute-start.18 = (f32[16,128,128]{2,1,0:T(8,128)S(1)}, f32[16,128,128]{2,1,0:T(8,128)S(1)}, u32[]{:S(2)}, u32[]{:S(2)}) collective-permute-start(f32[16,128,128]{2,1,0:T(8,128)S(1)} %bitcast_select_fusion), channel_id=1, source_target_pairs={{0,8},{1,9},{2,10},{3,11},{4,12},{5,13},{6,14},{7,15},{8,16},{9,17... | collective-permute-start | bytes 3145736 | tf_op jit(solution)/shard_map/ppermute | solution.py:70
  75.5 38.9 %collective-permute-start.17 = (f32[12,1,128,128]{3,2,1,0:T(8,128)S(1)}, f32[12,1,128,128]{3,2,1,0:T(8,128)S(1)}, u32[]{:S(2)}, u32[]{:S(2)}) collective-permute-start(f32[12,1,128,128]{3,2,1,0:T(8,128)S(1)} %copy-done.5), channel_id=1, source_target_pairs={{0,384},{32,416},{64,448},{96,480},{128,0},{160,32},{192,64},{224,... | collective-permute-start | bytes 2359304 | tf_op jit(solution)/shard_map/ppermute | solution.py:27
  80.2 34.3 %collective-permute-start.16 = (f32[12,1,128,128]{3,2,1,0:T(8,128)S(1)}, f32[12,1,128,128]{3,2,1,0:T(8,128)S(1)}, u32[]{:S(2)}, u32[]{:S(2)}) collective-permute-start(f32[12,1,128,128]{3,2,1,0:T(8,128)S(1)} %copy-done.5), channel_id=1, source_target_pairs={{0,256},{32,288},{64,320},{96,352},{128,384},{160,416},{192,448},{... | collective-permute-start | bytes 2359304 | tf_op jit(solution)/shard_map/ppermute | solution.py:27
  91.8 22.7 %collective-permute-start.15 = (f32[12,1,128,128]{3,2,1,0:T(8,128)S(1)}, f32[12,1,128,128]{3,2,1,0:T(8,128)S(1)}, u32[]{:S(2)}, u32[]{:S(2)}) collective-permute-start(f32[12,1,128,128]{3,2,1,0:T(8,128)S(1)} %copy-done.5), channel_id=1, source_target_pairs={{0,128},{32,160},{64,192},{96,224},{128,256},{160,288},{192,320},{... | collective-permute-start | bytes 2359304 | tf_op jit(solution)/shard_map/ppermute | solution.py:27
  109.3 73.6 %collective-permute-start.14 = (f32[12,1,128,128]{3,2,1,0:T(8,128)S(1)}, f32[12,1,128,128]{3,2,1,0:T(8,128)S(1)}, u32[]{:S(2)}, u32[]{:S(2)}) collective-permute-start(f32[12,1,128,128]{3,2,1,0:T(8,128)S(1)} %copy-done.5), channel_id=1, source_target_pairs={{0,64},{32,96},{64,0},{96,32},{128,192},{160,224},{192,128},{224,1... | collective-permute-start | bytes 2359304 | tf_op jit(solution)/shard_map/ppermute | solution.py:21
  182.9 43.9 %copy-start.1 = (f32[12,1,128,128]{3,2,1,0:T(8,128)}, f32[12,1,128,128]{3,2,1,0:T(8,128)S(1)}, u32[]{:S(2)}) copy-start(f32[12,1,128,128]{3,2,1,0:T(8,128)S(1)} %collective-permute-done.14.refs_1_) | copy-start | bytes 2359300
  182.9 38.3 %collective-permute-start.23 = (f32[12,1,128,128]{3,2,1,0:T(8,128)S(1)}, f32[12,1,128,128]{3,2,1,0:T(8,128)S(1)}, u32[]{:S(2)}, u32[]{:S(2)}) collective-permute-start(f32[12,1,128,128]{3,2,1,0:T(8,128)S(1)} %collective-permute-done.14.refs_1_), channel_id=1, source_target_pairs={{0,384},{32,416},{64,448},{96,480},{128,0},{160,32},{192,64},{224,... | collective-permute-start | bytes 2359304 | tf_op jit(solution)/shard_map/ppermute | solution.py:27
  187.5 33.6 %collective-permute-start.22 = (f32[12,1,128,128]{3,2,1,0:T(8,128)S(1)}, f32[12,1,128,128]{3,2,1,0:T(8,128)S(1)}, u32[]{:S(2)}, u32[]{:S(2)}) collective-permute-start(f32[12,1,128,128]{3,2,1,0:T(8,128)S(1)} %collective-permute-done.14.refs_1_), channel_id=1, source_target_pairs={{0,256},{32,288},{64,320},{96,352},{128,384},{160,416},{192,448},{... | collective-permute-start | bytes 2359304 | tf_op jit(solution)/shard_map/ppermute | solution.py:27
  190.3 36.5 %collective-permute-start.21 = (f32[12,1,128,128]{3,2,1,0:T(8,128)S(1)}, f32[12,1,128,128]{3,2,1,0:T(8,128)S(1)}, u32[]{:S(2)}, u32[]{:S(2)}) collective-permute-start(f32[12,1,128,128]{3,2,1,0:T(8,128)S(1)} %collective-permute-done.14.refs_1_), channel_id=1, source_target_pairs={{0,128},{32,160},{64,192},{96,224},{128,256},{160,288},{192,320},{... | collective-permute-start | bytes 2359304 | tf_op jit(solution)/shard_map/ppermute | solution.py:27
  193.3 37.5 %copy-start = (f32[12,4,128,128]{3,2,1,0:T(8,128)}, f32[12,4,128,128]{3,2,1,0:T(8,128)S(1)}, u32[]{:S(2)}) copy-start(f32[12,4,128,128]{3,2,1,0:T(8,128)S(1)} %pad_maximum_fusion.1.refs_0_) | copy-start | bytes 9437188
  193.3 39.9 %copy-start.8 = (s32[12,4]{0,1:T(4,128)S(1)}, s32[12,4]{0,1:T(4,128)}, u32[]{:S(2)}) copy-start(s32[12,4]{0,1:T(4,128)} %param.14) | copy-start | bytes 580
  193.3 40.0 %copy-start.7 = (s32[12,16]{1,0:T(8,128)S(1)}, s32[12,16]{1,0:T(8,128)}, u32[]{:S(2)}) copy-start(s32[12,16]{1,0:T(8,128)} %param.10) | copy-start | bytes 2308
  193.3 40.0 %copy-start.9 = (s32[64]{0:T(128)S(1)}, s32[64]{0:T(128)}, u32[]{:S(2)}) copy-start(s32[64]{0:T(128)} %param.15) | copy-start | bytes 772
  193.3 41.3 %copy-start.10 = (s32[64,1]{0,1:T(1,128)S(1)}, s32[64,1]{0,1:T(1,128)}, u32[]{:S(2)}) copy-start(s32[64,1]{0,1:T(1,128)} %param.13) | copy-start | bytes 772
  193.3 41.6 %copy-start.13 = (s32[12]{0:T(128)S(1)}, s32[12]{0:T(128)}, u32[]{:S(2)}) copy-start(s32[12]{0:T(128)} %param.11) | copy-start | bytes 148
  193.3 42.7 %copy-start.11 = (s32[8]{0:T(128)S(1)}, s32[8]{0:T(128)}, u32[]{:S(2)}) copy-start(s32[8]{0:T(128)} %constant.233) | copy-start | bytes 100
  193.4 42.7 %copy-start.12 = (s32[8]{0:T(128)S(1)}, s32[8]{0:T(128)}, u32[]{:S(2)}) copy-start(s32[8]{0:T(128)} %constant.231) | copy-start | bytes 100
  221.2 7.6 %copy-start.2 = (f32[12,1,128,128]{3,2,1,0:T(8,128)}, f32[12,1,128,128]{3,2,1,0:T(8,128)S(1)}, u32[]{:S(2)}) copy-start(f32[12,1,128,128]{3,2,1,0:T(8,128)S(1)} %collective-permute-done.23.refs_4_) | copy-start | bytes 2359300
  221.2 7.6 %copy-start.3 = (f32[12,1,128,128]{3,2,1,0:T(8,128)}, f32[12,1,128,128]{3,2,1,0:T(8,128)S(1)}, u32[]{:S(2)}) copy-start(f32[12,1,128,128]{3,2,1,0:T(8,128)S(1)} %collective-permute-done.22.refs_3_) | copy-start | bytes 2359300
  226.8 2.1 copy-start.4
  228.8 25.4 %collective-permute-start.25 = (f32[12,4,128,128]{3,2,1,0:T(8,128)}, f32[12,4,128,128]{3,2,1,0:T(8,128)}, u32[]{:S(2)}, u32[]{:S(2)}) collective-permute-start(f32[12,4,128,128]{3,2,1,0:T(8,128)} %pad_maximum_fusion.2), channel_id=1, source_target_pairs={{0,32},{32,0},{64,96},{96,64},{128,160},{160,128},{192,224},{224,1... | collective-permute-start | bytes 9437192 | tf_op jit(solution)/shard_map/ppermute | solution.py:32
  230.8 23.4 %collective-permute-start.24 = (f32[12,4,128,128]{3,2,1,0:T(8,128)S(1)}, f32[12,4,128,128]{3,2,1,0:T(8,128)}, u32[]{:S(2)}, u32[]{:S(2)}) collective-permute-start(f32[12,4,128,128]{3,2,1,0:T(8,128)S(1)} %pad_maximum_fusion.1.refs_0_), channel_id=1, source_target_pairs={{0,32},{32,0},{64,96},{96,64},{128,160},{160,128},{192,224},{224,1... | collective-permute-start | bytes 9437192 | tf_op jit(solution)/shard_map/ppermute | solution.py:32

commit v15 on v12

--- a/solution.py
+++ b/solution.py
@@ -120,37 +120,40 @@
 
 
 def product_kernel(pidx_ref, sidx_ref, a_ref, b_ref, *rest):
-    i = pl.program_id(0)
-    n_slots = a_ref.shape[1]
+    per_step, n_slots = a_ref.shape[0], a_ref.shape[1]
     o_ref = rest[-1]
     if len(rest) == 2:
         o_ref[...] = rest[0][...]
     else:
         o_ref[...] = jnp.zeros_like(o_ref)
 
-    def body(j, carry):
-        s = sidx_ref[i * n_slots + j]
+    for r in range(per_step):
+        i = pl.program_id(0) * per_step + r
 
-        @pl.when(s >= 0)
-        def _():
-            p = pidx_ref[i * n_slots + j]
-            prod = split_dot(a_ref[0, j], b_ref[p])
-            o_ref[0, s] += prod
+        def body(j, carry):
+            s = sidx_ref[i * n_slots + j]
 
-        return carry
+            @pl.when(s >= 0)
+            def _():
+                p = pidx_ref[i * n_slots + j]
+                prod = split_dot(a_ref[r, j], b_ref[p])
+                o_ref[r, s] += prod
 
-    lax.fori_loop(0, n_slots, body, 0, unroll=True)
+            return carry
+
+        lax.fori_loop(0, n_slots, body, 0, unroll=True)
 
 
 def row_products(whole_slots, panels, panel_index, target, pattern_slots, acc=None, interpret=False):
     rows, slots, bs, _ = whole_slots.shape
-    out_spec = pl.BlockSpec((1, pattern_slots, bs, bs), lambda i, pidx, sidx: (i, 0, 0, 0))
+    per_step = 2 if rows % 2 == 0 else 1
+    out_spec = pl.BlockSpec((per_step, pattern_slots, bs, bs), lambda i, pidx, sidx: (i, 0, 0, 0))
     extra = [] if acc is None else [acc]
     grid_spec = pltpu.PrefetchScalarGridSpec(
         num_scalar_prefetch=2,
-        grid=(rows,),
+        grid=(rows // per_step,),
         in_specs=[
-            pl.BlockSpec((1, slots, bs, bs), lambda i, pidx, sidx: (i, 0, 0, 0)),
+            pl.BlockSpec((per_step, slots, bs, bs), lambda i, pidx, sidx: (i, 0, 0, 0)),
             pl.BlockSpec(panels.shape, lambda i, pidx, sidx: (0, 0, 0)),
         ] + [out_spec] * len(extra),
         out_specs=out_spec,

time: 229 us -> 221 us (0.965)
  the two profiles are of different devices: /device:TPU:99 before, /device:TPU:107 now
where the time goes in v15:
time: 221 us; the launch traced here: 219 us
  starting transfers between devices  86.1 us (39%)
  waiting for transfers between devices  84.4 us (38%)
  local copies, waits for them, and re-layouts  24.9 us (11%)
  Pallas kernels  18.8 us (9%)
  other arithmetic  4.4 us (2%)
    ppermute x1, waiting for transfers between devices, swap_z(): return lax.ppermute(chunk, 'row', pairs)  34.4 us
    ppermute x7, starting transfers between devices, line_z(): going_right = lax.ppermute(going_right, 'col', right)  32.1 us
    ppermute x6, waiting for transfers between devices, ring_x(): parts.append(lax.ppermute(held, 'row', shift))  26.4 us
    ppermute x3, waiting for transfers between devices, ring_y(): parts.append(lax.ppermute(held, 'col', shift))  23.6 us
    pallas_call x2, Pallas kernels, row_products(): pl.pallas_call(product_kernel, grid_spec=grid_spec, out_shape=jax.ShapeDt...  18.8 us
    ppermute x6, starting transfers between devices, ring_x(): parts.append(lax.ppermute(held, 'row', shift))  17.7 us
    unnamed x34, local copies, waits for them, and re-layouts  17.1 us
    ppermute x7, starting transfers between devices, line_z(): going_left = lax.ppermute(going_left, 'col', left)  13.4 us
  transfers between devices with their start and end apart: 25, of which 6 were waited for; matrix products, arithmetic and copies ran while one was open for 12% of the time, Pallas kernels for 4%

profile of v15, /device:TPU:107, one launch (start us, length us, event | category | flops | bytes accessed | tf_op | source)
XLA Modules:
  0.0 219.0 jit_solution(983678033245113517)
XLA Ops:
  0.0 4.7 %collective-permute-start = (f32[2,128,128]{2,1,0:T(8,128)}, f32[2,128,128]{2,1,0:T(8,128)S(1)}, u32[]{:S(2)}, u32[]{:S(2)}) collective-permute-start(f32[2,128,128]{2,1,0:T(8,128)} %bitcast.41), channel_id=1, source_target_pairs={{0,1},{1,2},{2,3},{3,4},{4,5},{5,6},{6,7},{8,9},{9,10},{10,11},{11... | collective-permute-start | bytes 393224 | tf_op jit(solution)/shard_map/ppermute | solution.py:57
  4.8 1.9 collective-permute-start.7
  6.7 1.6 bitcast_dynamic-update-slice_fusion.14
  8.5 4.6 %collective-permute-start.1 = (f32[2,128,128]{2,1,0:T(8,128)S(1)}, f32[2,128,128]{2,1,0:T(8,128)S(1)}, u32[]{:S(2)}, u32[]{:S(2)}) collective-permute-start(f32[2,128,128]{2,1,0:T(8,128)S(1)} %collective-permute-done), channel_id=1, source_target_pairs={{0,1},{1,2},{2,3},{3,4},{4,5},{5,6},{6,7},{8,9},{9,10},{10,11},{11... | collective-permute-start | bytes 393224 | tf_op jit(solution)/shard_map/ppermute | solution.py:57
  13.1 1.9 collective-permute-start.8
  15.0 0.7 bitcast_dynamic-update-slice_fusion.13
  15.7 4.6 %collective-permute-start.2 = (f32[2,128,128]{2,1,0:T(8,128)S(1)}, f32[2,128,128]{2,1,0:T(8,128)S(1)}, u32[]{:S(2)}, u32[]{:S(2)}) collective-permute-start(f32[2,128,128]{2,1,0:T(8,128)S(1)} %collective-permute-done.1), channel_id=1, source_target_pairs={{0,1},{1,2},{2,3},{3,4},{4,5},{5,6},{6,7},{8,9},{9,10},{10,11},{11... | collective-permute-start | bytes 393224 | tf_op jit(solution)/shard_map/ppermute | solution.py:57
  20.2 1.9 collective-permute-start.9
  22.2 0.7 bitcast_dynamic-update-slice_fusion.12
  22.8 4.6 %collective-permute-start.3 = (f32[2,128,128]{2,1,0:T(8,128)S(1)}, f32[2,128,128]{2,1,0:T(8,128)S(1)}, u32[]{:S(2)}, u32[]{:S(2)}) collective-permute-start(f32[2,128,128]{2,1,0:T(8,128)S(1)} %collective-permute-done.2), channel_id=1, source_target_pairs={{0,1},{1,2},{2,3},{3,4},{4,5},{5,6},{6,7},{8,9},{9,10},{10,11},{11... | collective-permute-start | bytes 393224 | tf_op jit(solution)/shard_map/ppermute | solution.py:57
  27.4 1.9 collective-permute-start.10
  29.3 0.7 bitcast_dynamic-update-slice_fusion.11
  30.0 4.6 %collective-permute-start.4 = (f32[2,128,128]{2,1,0:T(8,128)S(1)}, f32[2,128,128]{2,1,0:T(8,128)S(1)}, u32[]{:S(2)}, u32[]{:S(2)}) collective-permute-start(f32[2,128,128]{2,1,0:T(8,128)S(1)} %collective-permute-done.3), channel_id=1, source_target_pairs={{0,1},{1,2},{2,3},{3,4},{4,5},{5,6},{6,7},{8,9},{9,10},{10,11},{11... | collective-permute-start | bytes 393224 | tf_op jit(solution)/shard_map/ppermute | solution.py:57
  34.6 1.9 collective-permute-start.11
  36.5 0.7 bitcast_dynamic-update-slice_fusion.10
  37.2 4.6 %collective-permute-start.5 = (f32[2,128,128]{2,1,0:T(8,128)S(1)}, f32[2,128,128]{2,1,0:T(8,128)S(1)}, u32[]{:S(2)}, u32[]{:S(2)}) collective-permute-start(f32[2,128,128]{2,1,0:T(8,128)S(1)} %collective-permute-done.4), channel_id=1, source_target_pairs={{0,1},{1,2},{2,3},{3,4},{4,5},{5,6},{6,7},{8,9},{9,10},{10,11},{11... | collective-permute-start | bytes 393224 | tf_op jit(solution)/shard_map/ppermute | solution.py:57
  41.8 1.9 collective-permute-start.12
  43.7 0.7 bitcast_dynamic-update-slice_fusion.9
  44.4 4.6 %collective-permute-start.6 = (f32[2,128,128]{2,1,0:T(8,128)S(1)}, f32[2,128,128]{2,1,0:T(8,128)S(1)}, u32[]{:S(2)}, u32[]{:S(2)}) collective-permute-start(f32[2,128,128]{2,1,0:T(8,128)S(1)} %collective-permute-done.5), channel_id=1, source_target_pairs={{0,1},{1,2},{2,3},{3,4},{4,5},{5,6},{6,7},{8,9},{9,10},{10,11},{11... | collective-permute-start | bytes 393224 | tf_op jit(solution)/shard_map/ppermute | solution.py:57
  49.0 1.9 collective-permute-start.13
  50.9 0.7 bitcast_dynamic-update-slice_fusion.8
  51.6 0.7 bitcast_dynamic-update-slice_fusion.7
  52.2 0.7 bitcast_dynamic-update-slice_fusion.6
  52.9 0.7 bitcast_dynamic-update-slice_fusion.5
  53.5 0.7 bitcast_dynamic-update-slice_fusion.4
  54.2 0.7 bitcast_dynamic-update-slice_fusion.3
  54.9 0.7 bitcast_dynamic-update-slice_fusion.2
  55.5 0.7 bitcast_dynamic-update-slice_fusion.1
  56.2 0.7 bitcast_dynamic-update-slice_fusion
  56.9 2.2 %gather_fusion.1 = f32[8,2,128,128]{3,2,1,0:T(8,128)S(1)} fusion(f32[15,2,128,128]{3,2,1,0:T(8,128)} %bitcast_dynamic-update-slice_fusion, s32[1024]{0:T(1024)S(1)} %pad_clamp_fusion), kind=kCustom, calls=%fused_computation.1 | custom fusion | bytes 2097184 | tf_op jit(solution)/shard_map/jit(_take)/gather | solution.py:64
  59.3 2.1 collective-permute-start.20
  61.3 4.2 %collective-permute-start.19 = (f32[16,128,128]{2,1,0:T(8,128)S(1)}, f32[16,128,128]{2,1,0:T(8,128)S(1)}, u32[]{:S(2)}, u32[]{:S(2)}) collective-permute-start(f32[16,128,128]{2,1,0:T(8,128)S(1)} %bitcast_select_fusion), channel_id=1, source_target_pairs={{0,16},{1,17},{2,18},{3,19},{4,20},{5,21},{6,22},{7,23},{8,24},{9,... | collective-permute-start | bytes 3145736 | tf_op jit(solution)/shard_map/ppermute | solution.py:70
  65.6 3.5 %collective-permute-start.18 = (f32[16,128,128]{2,1,0:T(8,128)S(1)}, f32[16,128,128]{2,1,0:T(8,128)S(1)}, u32[]{:S(2)}, u32[]{:S(2)}) collective-permute-start(f32[16,128,128]{2,1,0:T(8,128)S(1)} %bitcast_select_fusion), channel_id=1, source_target_pairs={{0,8},{1,9},{2,10},{3,11},{4,12},{5,13},{6,14},{7,15},{8,16},{9,17... | collective-permute-start | bytes 3145736 | tf_op jit(solution)/shard_map/ppermute | solution.py:70
  69.1 10.6 %collective-permute-start.14 = (f32[12,1,128,128]{3,2,1,0:T(8,128)S(1)}, f32[12,1,128,128]{3,2,1,0:T(8,128)S(1)}, u32[]{:S(2)}, u32[]{:S(2)}) collective-permute-start(f32[12,1,128,128]{3,2,1,0:T(8,128)S(1)} %copy-done), channel_id=1, source_target_pairs={{0,64},{32,96},{64,0},{96,32},{128,192},{160,224},{192,128},{224,1... | collective-permute-start | bytes 2359304 | tf_op jit(solution)/shard_map/ppermute | solution.py:21
  79.7 3.1 %collective-permute-start.15 = (f32[12,1,128,128]{3,2,1,0:T(8,128)S(1)}, f32[12,1,128,128]{3,2,1,0:T(8,128)S(1)}, u32[]{:S(2)}, u32[]{:S(2)}) collective-permute-start(f32[12,1,128,128]{3,2,1,0:T(8,128)S(1)} %copy-done), channel_id=1, source_target_pairs={{0,128},{32,160},{64,192},{96,224},{128,256},{160,288},{192,320},{... | collective-permute-start | bytes 2359304 | tf_op jit(solution)/shard_map/ppermute | solution.py:27
  82.9 2.7 %collective-permute-start.16 = (f32[12,1,128,128]{3,2,1,0:T(8,128)S(1)}, f32[12,1,128,128]{3,2,1,0:T(8,128)S(1)}, u32[]{:S(2)}, u32[]{:S(2)}) collective-permute-start(f32[12,1,128,128]{3,2,1,0:T(8,128)S(1)} %copy-done), channel_id=1, source_target_pairs={{0,256},{32,288},{64,320},{96,352},{128,384},{160,416},{192,448},{... | collective-permute-start | bytes 2359304 | tf_op jit(solution)/shard_map/ppermute | solution.py:27
  85.6 16.9 %collective-permute-done.19 = f32[16,128,128]{2,1,0:T(8,128)S(1)} collective-permute-done((f32[16,128,128]{2,1,0:T(8,128)S(1)}, f32[16,128,128]{2,1,0:T(8,128)S(1)}, u32[]{:S(2)}, u32[]{:S(2)}) %collective-permute-start.19) | collective-permute-done | bytes 1048608 | tf_op jit(solution)/shard_map/ppermute | solution.py:70
  102.5 2.2 collective-permute-start.17
  104.7 6.7 %collective-permute-done.18 = f32[16,128,128]{2,1,0:T(8,128)S(1)} collective-permute-done((f32[16,128,128]{2,1,0:T(8,128)S(1)}, f32[16,128,128]{2,1,0:T(8,128)S(1)}, u32[]{:S(2)}, u32[]{:S(2)}) %collective-permute-start.18) | collective-permute-done | bytes 1048608 | tf_op jit(solution)/shard_map/ppermute | solution.py:70
  111.4 2.4 %pad_maximum_fusion.b_ref = f32[64,128,128]{2,1,0:T(8,128)} fusion(f32[16,128,128]{2,1,0:T(8,128)S(1)} %collective-permute-done.20, f32[16,128,128]{2,1,0:T(8,128)S(1)} %collective-permute-done.19, f32[16,128,128]{2,1,0:T(8,128)S(1)} %collective-permute-done.18, f32[16,128,128]{2,1,0:T(8,128)S(1)} %bitcast_select_fusion), kind=kLoop, calls=%fused_computation.2 | loop fusion | flops 3145728 | bytes 8388608 | tf_op jit(solution)/shard_map/concatenate | solution.py:71
  113.8 34.4 %collective-permute-done.14 = f32[12,1,128,128]{3,2,1,0:T(8,128)S(1)} collective-permute-done((f32[12,1,128,128]{3,2,1,0:T(8,128)S(1)}, f32[12,1,128,128]{3,2,1,0:T(8,128)S(1)}, u32[]{:S(2)}, u32[]{:S(2)}) %collective-permute-start.14) | collective-permute-done | bytes 786464 | tf_op jit(solution)/shard_map/ppermute | solution.py:21
  148.2 3.1 %collective-permute-start.21 = (f32[12,1,128,128]{3,2,1,0:T(8,128)S(1)}, f32[12,1,128,128]{3,2,1,0:T(8,128)S(1)}, u32[]{:S(2)}, u32[]{:S(2)}) collective-permute-start(f32[12,1,128,128]{3,2,1,0:T(8,128)S(1)} %collective-permute-done.14), channel_id=1, source_target_pairs={{0,128},{32,160},{64,192},{96,224},{128,256},{160,288},{192,320},{... | collective-permute-start | bytes 2359304 | tf_op jit(solution)/shard_map/ppermute | solution.py:27
  151.3 2.7 %collective-permute-start.22 = (f32[12,1,128,128]{3,2,1,0:T(8,128)S(1)}, f32[12,1,128,128]{3,2,1,0:T(8,128)S(1)}, u32[]{:S(2)}, u32[]{:S(2)}) collective-permute-start(f32[12,1,128,128]{3,2,1,0:T(8,128)S(1)} %collective-permute-done.14), channel_id=1, source_target_pairs={{0,256},{32,288},{64,320},{96,352},{128,384},{160,416},{192,448},{... | collective-permute-start | bytes 2359304 | tf_op jit(solution)/shard_map/ppermute | solution.py:27
  154.1 3.8 %collective-permute-start.23 = (f32[12,1,128,128]{3,2,1,0:T(8,128)S(1)}, f32[12,1,128,128]{3,2,1,0:T(8,128)S(1)}, u32[]{:S(2)}, u32[]{:S(2)}) collective-permute-start(f32[12,1,128,128]{3,2,1,0:T(8,128)S(1)} %collective-permute-done.14), channel_id=1, source_target_pairs={{0,384},{32,416},{64,448},{96,480},{128,0},{160,32},{192,64},{224,... | collective-permute-start | bytes 2359304 | tf_op jit(solution)/shard_map/ppermute | solution.py:27
  157.8 1.0 constant_dynamic-update-slice_fusion.7
  158.8 1.0 constant_dynamic-update-slice_fusion.6
  159.8 1.0 constant_dynamic-update-slice_fusion.5
  160.8 7.8 %collective-permute-done.21 = f32[12,1,128,128]{3,2,1,0:T(8,128)S(1)} collective-permute-done((f32[12,1,128,128]{3,2,1,0:T(8,128)S(1)}, f32[12,1,128,128]{3,2,1,0:T(8,128)S(1)}, u32[]{:S(2)}, u32[]{:S(2)}) %collective-permute-start.21) | collective-permute-done | bytes 786464 | tf_op jit(solution)/shard_map/ppermute | solution.py:27
  168.6 1.0 constant_dynamic-update-slice_fusion.4
  169.6 0.9 constant_dynamic-update-slice_fusion.3
  170.6 2.4 %collective-permute-done.22 = f32[12,1,128,128]{3,2,1,0:T(8,128)S(1)} collective-permute-done((f32[12,1,128,128]{3,2,1,0:T(8,128)S(1)}, f32[12,1,128,128]{3,2,1,0:T(8,128)S(1)}, u32[]{:S(2)}, u32[]{:S(2)}) %collective-permute-start.22) | collective-permute-done | bytes 786464 | tf_op jit(solution)/shard_map/ppermute | solution.py:27
  173.0 0.9 constant_dynamic-update-slice_fusion.2
  173.9 0.9 constant_dynamic-update-slice_fusion.1
  174.9 16.2 %collective-permute-done.23 = f32[12,1,128,128]{3,2,1,0:T(8,128)S(1)} collective-permute-done((f32[12,1,128,128]{3,2,1,0:T(8,128)S(1)}, f32[12,1,128,128]{3,2,1,0:T(8,128)S(1)}, u32[]{:S(2)}, u32[]{:S(2)}) %collective-permute-start.23) | collective-permute-done | bytes 786464 | tf_op jit(solution)/shard_map/ppermute | solution.py:27
  191.0 0.9 constant_dynamic-update-slice_fusion.a_ref
  192.0 2.4 %collective-permute-start.24 = (f32[12,8,128,128]{3,2,1,0:T(8,128)}, f32[12,8,128,128]{3,2,1,0:T(8,128)}, u32[]{:S(2)}, u32[]{:S(2)}) collective-permute-start(f32[12,8,128,128]{3,2,1,0:T(8,128)} %constant_dynamic-update-slice_fusion.a_ref), channel_id=1, source_target_pairs={{0,32},{32,0},{64,96},{96,64},{128,160},{160,128},{192,224},{224,1... | collective-permute-start | bytes 18874376 | tf_op jit(solution)/shard_map/ppermute | solution.py:32
  194.9 0.6 gather_fusion
  195.7 0.7 reshape.328.pidx_ref
  197.2 0.8 convert_reduce_fusion
  198.1 0.6 reshape.329.sidx_ref
  198.8 0.6 reshape.330.pidx_ref
  199.5 0.7 reshape.331.sidx_ref
  200.2 8.8 %shard_map.73.rest_0_ = f32[12,4,128,128]{3,2,1,0:T(8,128)} custom-call(s32[96]{0:T(128)} %reshape.330.pidx_ref, s32[96]{0:T(128)} %reshape.331.sidx_ref, f32[12,8,128,128]{3,2,1,0:T(8,128)} %constant_dynamic-update-slice_fusion.a_ref, f32[64,128,128]{2,1,0:T(8,128)} %pad_maximum_fusion.b_ref), custom_call_target="tpu_custom_call" | custom-call | tf_op jit(solution)/shard_map/pallas_call | solution.py:161
  209.0 10.0 %shard_map.74 = f32[12,4,128,128]{3,2,1,0:T(8,128)} custom-call(s32[96]{0:T(128)} %reshape.328.pidx_ref, s32[96]{0:T(128)} %reshape.329.sidx_ref, f32[12,8,128,128]{3,2,1,0:T(8,128)} %collective-permute-done.24.a_ref, f32[64,128,128]{2,1,0:T(8,128)} %pad_maximum_fusion.b_ref, f32[12,4,128,128]{3,2,1,0:T(8,128)} %shard_map.73.rest_0_), custom_call_target="tpu_custom_call", output_to_operand_aliasing={{}: (4, {})} | custom-call | tf_op jit(solution)/shard_map/pallas_call | solution.py:161
  (57 shorter events, 2.2 us)
Async XLA Ops:
  0.0 8.5 %collective-permute-start = (f32[2,128,128]{2,1,0:T(8,128)}, f32[2,128,128]{2,1,0:T(8,128)S(1)}, u32[]{:S(2)}, u32[]{:S(2)}) collective-permute-start(f32[2,128,128]{2,1,0:T(8,128)} %bitcast.41), channel_id=1, source_target_pairs={{0,1},{1,2},{2,3},{3,4},{4,5},{5,6},{6,7},{8,9},{9,10},{10,11},{11... | collective-permute-start | bytes 393224 | tf_op jit(solution)/shard_map/ppermute | solution.py:57
  4.8 8.3 %collective-permute-start.7 = (f32[2,128,128]{2,1,0:T(8,128)}, f32[2,128,128]{2,1,0:T(8,128)S(1)}, u32[]{:S(2)}, u32[]{:S(2)}) collective-permute-start(f32[2,128,128]{2,1,0:T(8,128)} %bitcast.42), channel_id=1, source_target_pairs={{1,0},{2,1},{3,2},{4,3},{5,4},{6,5},{7,6},{9,8},{10,9},{11,10},{12... | collective-permute-start | bytes 393224 | tf_op jit(solution)/shard_map/ppermute | solution.py:58
  8.5 7.2 %collective-permute-start.1 = (f32[2,128,128]{2,1,0:T(8,128)S(1)}, f32[2,128,128]{2,1,0:T(8,128)S(1)}, u32[]{:S(2)}, u32[]{:S(2)}) collective-permute-start(f32[2,128,128]{2,1,0:T(8,128)S(1)} %collective-permute-done), channel_id=1, source_target_pairs={{0,1},{1,2},{2,3},{3,4},{4,5},{5,6},{6,7},{8,9},{9,10},{10,11},{11... | collective-permute-start | bytes 393224 | tf_op jit(solution)/shard_map/ppermute | solution.py:57
  13.1 7.2 %collective-permute-start.8 = (f32[2,128,128]{2,1,0:T(8,128)S(1)}, f32[2,128,128]{2,1,0:T(8,128)S(1)}, u32[]{:S(2)}, u32[]{:S(2)}) collective-permute-start(f32[2,128,128]{2,1,0:T(8,128)S(1)} %collective-permute-done.7), channel_id=1, source_target_pairs={{1,0},{2,1},{3,2},{4,3},{5,4},{6,5},{7,6},{9,8},{10,9},{11,10},{12... | collective-permute-start | bytes 393224 | tf_op jit(solution)/shard_map/ppermute | solution.py:58
  15.7 7.2 %collective-permute-start.2 = (f32[2,128,128]{2,1,0:T(8,128)S(1)}, f32[2,128,128]{2,1,0:T(8,128)S(1)}, u32[]{:S(2)}, u32[]{:S(2)}) collective-permute-start(f32[2,128,128]{2,1,0:T(8,128)S(1)} %collective-permute-done.1), channel_id=1, source_target_pairs={{0,1},{1,2},{2,3},{3,4},{4,5},{5,6},{6,7},{8,9},{9,10},{10,11},{11... | collective-permute-start | bytes 393224 | tf_op jit(solution)/shard_map/ppermute | solution.py:57
  20.2 7.2 %collective-permute-start.9 = (f32[2,128,128]{2,1,0:T(8,128)S(1)}, f32[2,128,128]{2,1,0:T(8,128)S(1)}, u32[]{:S(2)}, u32[]{:S(2)}) collective-permute-start(f32[2,128,128]{2,1,0:T(8,128)S(1)} %collective-permute-done.8), channel_id=1, source_target_pairs={{1,0},{2,1},{3,2},{4,3},{5,4},{6,5},{7,6},{9,8},{10,9},{11,10},{12... | collective-permute-start | bytes 393224 | tf_op jit(solution)/shard_map/ppermute | solution.py:58
  22.8 7.2 %collective-permute-start.3 = (f32[2,128,128]{2,1,0:T(8,128)S(1)}, f32[2,128,128]{2,1,0:T(8,128)S(1)}, u32[]{:S(2)}, u32[]{:S(2)}) collective-permute-start(f32[2,128,128]{2,1,0:T(8,128)S(1)} %collective-permute-done.2), channel_id=1, source_target_pairs={{0,1},{1,2},{2,3},{3,4},{4,5},{5,6},{6,7},{8,9},{9,10},{10,11},{11... | collective-permute-start | bytes 393224 | tf_op jit(solution)/shard_map/ppermute | solution.py:57
  27.4 7.2 %collective-permute-start.10 = (f32[2,128,128]{2,1,0:T(8,128)S(1)}, f32[2,128,128]{2,1,0:T(8,128)S(1)}, u32[]{:S(2)}, u32[]{:S(2)}) collective-permute-start(f32[2,128,128]{2,1,0:T(8,128)S(1)} %collective-permute-done.9), channel_id=1, source_target_pairs={{1,0},{2,1},{3,2},{4,3},{5,4},{6,5},{7,6},{9,8},{10,9},{11,10},{12... | collective-permute-start | bytes 393224 | tf_op jit(solution)/shard_map/ppermute | solution.py:58
  30.0 7.2 %collective-permute-start.4 = (f32[2,128,128]{2,1,0:T(8,128)S(1)}, f32[2,128,128]{2,1,0:T(8,128)S(1)}, u32[]{:S(2)}, u32[]{:S(2)}) collective-permute-start(f32[2,128,128]{2,1,0:T(8,128)S(1)} %collective-permute-done.3), channel_id=1, source_target_pairs={{0,1},{1,2},{2,3},{3,4},{4,5},{5,6},{6,7},{8,9},{9,10},{10,11},{11... | collective-permute-start | bytes 393224 | tf_op jit(solution)/shard_map/ppermute | solution.py:57
  34.6 7.2 %collective-permute-start.11 = (f32[2,128,128]{2,1,0:T(8,128)S(1)}, f32[2,128,128]{2,1,0:T(8,128)S(1)}, u32[]{:S(2)}, u32[]{:S(2)}) collective-permute-start(f32[2,128,128]{2,1,0:T(8,128)S(1)} %collective-permute-done.10), channel_id=1, source_target_pairs={{1,0},{2,1},{3,2},{4,3},{5,4},{6,5},{7,6},{9,8},{10,9},{11,10},{12... | collective-permute-start | bytes 393224 | tf_op jit(solution)/shard_map/ppermute | solution.py:58
  37.2 7.2 %collective-permute-start.5 = (f32[2,128,128]{2,1,0:T(8,128)S(1)}, f32[2,128,128]{2,1,0:T(8,128)S(1)}, u32[]{:S(2)}, u32[]{:S(2)}) collective-permute-start(f32[2,128,128]{2,1,0:T(8,128)S(1)} %collective-permute-done.4), channel_id=1, source_target_pairs={{0,1},{1,2},{2,3},{3,4},{4,5},{5,6},{6,7},{8,9},{9,10},{10,11},{11... | collective-permute-start | bytes 393224 | tf_op jit(solution)/shard_map/ppermute | solution.py:57
  41.8 7.2 %collective-permute-start.12 = (f32[2,128,128]{2,1,0:T(8,128)S(1)}, f32[2,128,128]{2,1,0:T(8,128)S(1)}, u32[]{:S(2)}, u32[]{:S(2)}) collective-permute-start(f32[2,128,128]{2,1,0:T(8,128)S(1)} %collective-permute-done.11), channel_id=1, source_target_pairs={{1,0},{2,1},{3,2},{4,3},{5,4},{6,5},{7,6},{9,8},{10,9},{11,10},{12... | collective-permute-start | bytes 393224 | tf_op jit(solution)/shard_map/ppermute | solution.py:58
  44.4 7.2 %collective-permute-start.6 = (f32[2,128,128]{2,1,0:T(8,128)S(1)}, f32[2,128,128]{2,1,0:T(8,128)S(1)}, u32[]{:S(2)}, u32[]{:S(2)}) collective-permute-start(f32[2,128,128]{2,1,0:T(8,128)S(1)} %collective-permute-done.5), channel_id=1, source_target_pairs={{0,1},{1,2},{2,3},{3,4},{4,5},{5,6},{6,7},{8,9},{9,10},{10,11},{11... | collective-permute-start | bytes 393224 | tf_op jit(solution)/shard_map/ppermute | solution.py:57
  49.0 7.3 %collective-permute-start.13 = (f32[2,128,128]{2,1,0:T(8,128)S(1)}, f32[2,128,128]{2,1,0:T(8,128)S(1)}, u32[]{:S(2)}, u32[]{:S(2)}) collective-permute-start(f32[2,128,128]{2,1,0:T(8,128)S(1)} %collective-permute-done.12), channel_id=1, source_target_pairs={{1,0},{2,1},{3,2},{4,3},{5,4},{6,5},{7,6},{9,8},{10,9},{11,10},{12... | collective-permute-start | bytes 393224 | tf_op jit(solution)/shard_map/ppermute | solution.py:58
  56.9 12.2 %copy-start = (f32[12,1,128,128]{3,2,1,0:T(8,128)S(1)}, f32[12,1,128,128]{3,2,1,0:T(8,128)}, u32[]{:S(2)}) copy-start(f32[12,1,128,128]{3,2,1,0:T(8,128)} %param.7) | copy-start | bytes 2359300
  59.3 23.6 %collective-permute-start.20 = (f32[16,128,128]{2,1,0:T(8,128)S(1)}, f32[16,128,128]{2,1,0:T(8,128)S(1)}, u32[]{:S(2)}, u32[]{:S(2)}) collective-permute-start(f32[16,128,128]{2,1,0:T(8,128)S(1)} %bitcast_select_fusion), channel_id=1, source_target_pairs={{0,24},{1,25},{2,26},{3,27},{4,28},{5,29},{6,30},{7,31},{8,0},{9,1... | collective-permute-start | bytes 3145736 | tf_op jit(solution)/shard_map/ppermute | solution.py:70
  61.3 41.2 %collective-permute-start.19 = (f32[16,128,128]{2,1,0:T(8,128)S(1)}, f32[16,128,128]{2,1,0:T(8,128)S(1)}, u32[]{:S(2)}, u32[]{:S(2)}) collective-permute-start(f32[16,128,128]{2,1,0:T(8,128)S(1)} %bitcast_select_fusion), channel_id=1, source_target_pairs={{0,16},{1,17},{2,18},{3,19},{4,20},{5,21},{6,22},{7,23},{8,24},{9,... | collective-permute-start | bytes 3145736 | tf_op jit(solution)/shard_map/ppermute | solution.py:70
  65.6 45.8 %collective-permute-start.18 = (f32[16,128,128]{2,1,0:T(8,128)S(1)}, f32[16,128,128]{2,1,0:T(8,128)S(1)}, u32[]{:S(2)}, u32[]{:S(2)}) collective-permute-start(f32[16,128,128]{2,1,0:T(8,128)S(1)} %bitcast_select_fusion), channel_id=1, source_target_pairs={{0,8},{1,9},{2,10},{3,11},{4,12},{5,13},{6,14},{7,15},{8,16},{9,17... | collective-permute-start | bytes 3145736 | tf_op jit(solution)/shard_map/ppermute | solution.py:70
  69.1 79.1 %collective-permute-start.14 = (f32[12,1,128,128]{3,2,1,0:T(8,128)S(1)}, f32[12,1,128,128]{3,2,1,0:T(8,128)S(1)}, u32[]{:S(2)}, u32[]{:S(2)}) collective-permute-start(f32[12,1,128,128]{3,2,1,0:T(8,128)S(1)} %copy-done), channel_id=1, source_target_pairs={{0,64},{32,96},{64,0},{96,32},{128,192},{160,224},{192,128},{224,1... | collective-permute-start | bytes 2359304 | tf_op jit(solution)/shard_map/ppermute | solution.py:21
  79.7 68.4 %collective-permute-start.15 = (f32[12,1,128,128]{3,2,1,0:T(8,128)S(1)}, f32[12,1,128,128]{3,2,1,0:T(8,128)S(1)}, u32[]{:S(2)}, u32[]{:S(2)}) collective-permute-start(f32[12,1,128,128]{3,2,1,0:T(8,128)S(1)} %copy-done), channel_id=1, source_target_pairs={{0,128},{32,160},{64,192},{96,224},{128,256},{160,288},{192,320},{... | collective-permute-start | bytes 2359304 | tf_op jit(solution)/shard_map/ppermute | solution.py:27
  82.9 65.3 %collective-permute-start.16 = (f32[12,1,128,128]{3,2,1,0:T(8,128)S(1)}, f32[12,1,128,128]{3,2,1,0:T(8,128)S(1)}, u32[]{:S(2)}, u32[]{:S(2)}) collective-permute-start(f32[12,1,128,128]{3,2,1,0:T(8,128)S(1)} %copy-done), channel_id=1, source_target_pairs={{0,256},{32,288},{64,320},{96,352},{128,384},{160,416},{192,448},{... | collective-permute-start | bytes 2359304 | tf_op jit(solution)/shard_map/ppermute | solution.py:27
  102.5 45.6 %collective-permute-start.17 = (f32[12,1,128,128]{3,2,1,0:T(8,128)S(1)}, f32[12,1,128,128]{3,2,1,0:T(8,128)S(1)}, u32[]{:S(2)}, u32[]{:S(2)}) collective-permute-start(f32[12,1,128,128]{3,2,1,0:T(8,128)S(1)} %copy-done), channel_id=1, source_target_pairs={{0,384},{32,416},{64,448},{96,480},{128,0},{160,32},{192,64},{224,... | collective-permute-start | bytes 2359304 | tf_op jit(solution)/shard_map/ppermute | solution.py:27
  148.2 20.4 %collective-permute-start.21 = (f32[12,1,128,128]{3,2,1,0:T(8,128)S(1)}, f32[12,1,128,128]{3,2,1,0:T(8,128)S(1)}, u32[]{:S(2)}, u32[]{:S(2)}) collective-permute-start(f32[12,1,128,128]{3,2,1,0:T(8,128)S(1)} %collective-permute-done.14), channel_id=1, source_target_pairs={{0,128},{32,160},{64,192},{96,224},{128,256},{160,288},{192,320},{... | collective-permute-start | bytes 2359304 | tf_op jit(solution)/shard_map/ppermute | solution.py:27
  151.3 21.7 %collective-permute-start.22 = (f32[12,1,128,128]{3,2,1,0:T(8,128)S(1)}, f32[12,1,128,128]{3,2,1,0:T(8,128)S(1)}, u32[]{:S(2)}, u32[]{:S(2)}) collective-permute-start(f32[12,1,128,128]{3,2,1,0:T(8,128)S(1)} %collective-permute-done.14), channel_id=1, source_target_pairs={{0,256},{32,288},{64,320},{96,352},{128,384},{160,416},{192,448},{... | collective-permute-start | bytes 2359304 | tf_op jit(solution)/shard_map/ppermute | solution.py:27
  154.1 37.0 %collective-permute-start.23 = (f32[12,1,128,128]{3,2,1,0:T(8,128)S(1)}, f32[12,1,128,128]{3,2,1,0:T(8,128)S(1)}, u32[]{:S(2)}, u32[]{:S(2)}) collective-permute-start(f32[12,1,128,128]{3,2,1,0:T(8,128)S(1)} %collective-permute-done.14), channel_id=1, source_target_pairs={{0,384},{32,416},{64,448},{96,480},{128,0},{160,32},{192,64},{224,... | collective-permute-start | bytes 2359304 | tf_op jit(solution)/shard_map/ppermute | solution.py:27
  173.9 20.5 %copy-start.1 = (s32[12,16]{1,0:T(8,128)S(1)}, s32[12,16]{1,0:T(8,128)}, u32[]{:S(2)}) copy-start(s32[12,16]{1,0:T(8,128)} %param.8) | copy-start | bytes 2308
  173.9 20.5 %copy-start.3 = (s32[64]{0:T(128)S(1)}, s32[64]{0:T(128)}, u32[]{:S(2)}) copy-start(s32[64]{0:T(128)} %param.13) | copy-start | bytes 772
  173.9 22.4 %copy-start.2 = (s32[12,4]{0,1:T(4,128)S(1)}, s32[12,4]{0,1:T(4,128)}, u32[]{:S(2)}) copy-start(s32[12,4]{0,1:T(4,128)} %param.12) | copy-start | bytes 580
  173.9 22.6 %copy-start.4 = (s32[64,1]{0,1:T(1,128)S(1)}, s32[64,1]{0,1:T(1,128)}, u32[]{:S(2)}) copy-start(s32[64,1]{0,1:T(1,128)} %param.11) | copy-start | bytes 772
  173.9 23.0 %copy-start.5 = (s32[12]{0:T(128)S(1)}, s32[12]{0:T(128)}, u32[]{:S(2)}) copy-start(s32[12]{0:T(128)} %param.9) | copy-start | bytes 148
  192.0 17.0 %collective-permute-start.24 = (f32[12,8,128,128]{3,2,1,0:T(8,128)}, f32[12,8,128,128]{3,2,1,0:T(8,128)}, u32[]{:S(2)}, u32[]{:S(2)}) collective-permute-start(f32[12,8,128,128]{3,2,1,0:T(8,128)} %constant_dynamic-update-slice_fusion.a_ref), channel_id=1, source_target_pairs={{0,32},{32,0},{64,96},{96,64},{128,160},{160,128},{192,224},{224,1... | collective-permute-start | bytes 18874376 | tf_op jit(solution)/shard_map/ppermute | solution.py:32
